TPU v7x, 32 devices: a whole 2x2x4 slice. The times are simulated.
32 devices in a mesh: dp: 2 (over x), ctx: 4 (over z), tp: 4 (over y, core).
Axes of the slice: x: 2, y: 2, z: 4, core: 2. Of those that a mesh axis runs over, the one named last changes fastest.
Arguments:
- tokens: bfloat16 [6144, 2048], P(('dp', 'ctx')), may hold values from -6 to 6
- attn_gain: bfloat16 [2048], replicated, may hold values from 0.5 to 1.5
- query_weight: bfloat16 [2048, 2048], P(('dp', 'ctx'), 'tp'), may hold values from -0.125 to 0.125
- key_weight: bfloat16 [2048, 2048], P(('dp', 'ctx'), 'tp'), may hold values from -0.125 to 0.125
- value_weight: bfloat16 [2048, 2048], P(('dp', 'ctx'), 'tp'), may hold values from -0.125 to 0.125
- out_weight: bfloat16 [2048, 2048], P(('dp', 'ctx'), 'tp'), may hold values from -1 to 1
- ffn_gain: bfloat16 [2048], replicated, may hold values from 0.5 to 1.5
- gate_weight: bfloat16 [2048, 8192], P(('dp', 'ctx'), 'tp'), may hold values from -0.125 to 0.125
- up_weight: bfloat16 [2048, 8192], P(('dp', 'ctx'), 'tp'), may hold values from -0.125 to 0.125
- down_weight: bfloat16 [2048, 8192], P(('dp', 'ctx'), 'tp'), may hold values from -0.0625 to 0.0625
- seq_ids: int32 [2, 3072], P('dp'), may hold values from 0 to 8, as said below
- positions: int32 [2, 3072], P('dp'), may hold values from 0 to 1279, as said below
- out_grad: bfloat16 [6144, 2048], P(('dp', 'ctx')), may hold values from -6 to 6
Outputs:
- block_out: bfloat16 [6144, 2048], P(('dp', 'ctx'), 'tp')
- in_grad: bfloat16 [6144, 2048], P(('dp', 'ctx'), 'tp')
- attn_gain_grad: float32 [2048], P(('dp', 'ctx'))
- query_grad: float32 [2048, 2048], P(('dp', 'ctx'), 'tp')
- key_grad: float32 [2048, 2048], P(('dp', 'ctx'), 'tp')
- value_grad: float32 [2048, 2048], P(('dp', 'ctx'), 'tp')
- out_weight_grad: float32 [2048, 2048], P(('dp', 'ctx'), 'tp')
- ffn_gain_grad: float32 [2048], P(('dp', 'ctx'))
- gate_grad: float32 [2048, 8192], P(('dp', 'ctx'), 'tp')
- up_grad: float32 [2048, 8192], P(('dp', 'ctx'), 'tp')
- down_grad: float32 [2048, 8192], P(('dp', 'ctx'), 'tp')
Inputs may be any that keep to these rules, and one draw needn't show every extreme that they name: `seq_ids`: A group's slots form aligned blocks of 256; each block is one piece of the prompt (value 0) or one whole continuation (its number); every continuation has one block, and each aligned block of 768 slots holds exactly one prompt piece. A prompt piece b holds positions b * 256 to b * 256 + 255 in order, each piece once in a group; a continuation's block holds 1024 to 1279 in order.
All inputs are finite; a program needn't handle non-finite values.
Results may differ from a plain program's by a relative error of at most 0.024.
Values may be sent and summed in bfloat16 or wider, within the bound.
No kernel may reach another device: no remote copies, remote signals or barrier semaphores. Data moves between devices by JAX's collectives and lax.ppermute only.
A program may use at most 320 MiB of HBM per device.

v0:
```python
import jax
import jax.numpy as jnp
from jax import lax
from jax.sharding import PartitionSpec as P

HEAD_DIM = 64


EPS = 1e-05
ROPE_BASE = 130000.0
MASKED = -1e30


def rope_angles(where):
    half = HEAD_DIM // 2
    freqs = ROPE_BASE ** (-(jnp.arange(half).astype(jnp.float32) * 2.0) / HEAD_DIM)
    angles = where.astype(jnp.float32)[:, None] * freqs[None, :]
    return (jnp.cos(angles), jnp.sin(angles))


def rotate(values, cosine, sine):
    half = HEAD_DIM // 2
    first_half = values[..., :half]
    second_half = values[..., half:]
    cosine = cosine[:, None, :]
    sine = sine[:, None, :]
    return jnp.concatenate(
        [first_half * cosine - second_half * sine, second_half * cosine + first_half * sine],
        axis=-1,
    )


def unrotate(values, cosine, sine):
    half = HEAD_DIM // 2
    first_half = values[..., :half]
    second_half = values[..., half:]
    cosine = cosine[:, None, :]
    sine = sine[:, None, :]
    return jnp.concatenate(
        [first_half * cosine + second_half * sine, second_half * cosine - first_half * sine],
        axis=-1,
    )


def normalize(values):
    factor = lax.rsqrt(jnp.mean(values * values, axis=-1, keepdims=True) + EPS)
    return (values * factor, factor)


def outer_rows(left, right):
    return jnp.einsum("tc,tf->cf", left, right, preferred_element_type=jnp.float32)


def body(
    tokens,
    attn_gain,
    query_weight,
    key_weight,
    value_weight,
    out_weight,
    ffn_gain,
    gate_weight,
    up_weight,
    down_weight,
    seq_ids,
    positions,
    out_grad,
):
    row_count = tokens.shape[0]
    head_width = query_weight.shape[1]
    local_heads = head_width // HEAD_DIM
    ffn_width = gate_weight.shape[1]
    scale = HEAD_DIM ** (-0.5)
    ctx_index = lax.axis_index("ctx")
    ctx_count = lax.axis_size("ctx")
    group_seq = seq_ids[0]
    group_pos = positions[0]
    own_seq = lax.dynamic_slice_in_dim(group_seq, ctx_index * row_count, row_count)
    own_pos = lax.dynamic_slice_in_dim(group_pos, ctx_index * row_count, row_count)
    cosine, sine = rope_angles(own_pos)
    inputs = tokens.astype(jnp.float32)
    gain_one = attn_gain.astype(jnp.float32)
    gain_two = ffn_gain.astype(jnp.float32)
    first_norm, first_scale = normalize(inputs)
    first = (first_norm * gain_one).astype(jnp.bfloat16)
    query_full, key_full, value_full, out_full = (
        lax.all_gather(query_weight, ("dp", "ctx"), axis=0, tiled=True),
        lax.all_gather(key_weight, ("dp", "ctx"), axis=0, tiled=True),
        lax.all_gather(value_weight, ("dp", "ctx"), axis=0, tiled=True),
        lax.all_gather(out_weight, ("dp", "ctx"), axis=0, tiled=True),
    )
    query = rotate(
        jnp.dot(first, query_full, preferred_element_type=jnp.float32).reshape(
            row_count, local_heads, HEAD_DIM
        ),
        cosine,
        sine,
    ).astype(jnp.bfloat16)
    key_rows = (
        rotate(
            jnp.dot(first, key_full, preferred_element_type=jnp.float32).reshape(
                row_count, local_heads, HEAD_DIM
            ),
            cosine,
            sine,
        )
        .astype(jnp.bfloat16)
        .reshape(row_count, head_width)
    )
    value_rows = jnp.dot(first, value_full, preferred_element_type=jnp.float32).astype(jnp.bfloat16)
    keys_all, values_all = (
        lax.all_gather(key_rows, "ctx", axis=0, tiled=True),
        lax.all_gather(value_rows, "ctx", axis=0, tiled=True),
    )

    def block_scores(block):
        lower = block * row_count
        key_block = keys_all[lower : lower + row_count].reshape(row_count, local_heads, HEAD_DIM)
        value_block = values_all[lower : lower + row_count].reshape(
            row_count, local_heads, HEAD_DIM
        )
        block_pos = group_pos[lower : lower + row_count]
        block_seq = group_seq[lower : lower + row_count]
        visible = (block_pos[None, :] <= own_pos[:, None]) & (
            (block_seq[None, :] == 0) | (block_seq[None, :] == own_seq[:, None])
        )
        raw = (
            jnp.einsum("qhd,khd->hqk", query, key_block, preferred_element_type=jnp.float32) * scale
        )
        return (jnp.where(visible[None], raw, MASKED), key_block, value_block)

    running_max = jnp.full((local_heads, row_count), MASKED, jnp.float32)
    running_sum = jnp.zeros((local_heads, row_count), jnp.float32)
    for block in range(ctx_count):
        scores, key_block, value_block = block_scores(block)
        new_max = jnp.maximum(running_max, jnp.max(scores, axis=-1))
        running_sum = running_sum * jnp.exp(running_max - new_max) + jnp.sum(
            jnp.exp(scores - new_max[..., None]), axis=-1
        )
        running_max = new_max
    log_total = running_max + jnp.log(running_sum)
    accum = jnp.zeros((row_count, local_heads, HEAD_DIM), jnp.float32)
    for block in range(ctx_count):
        scores, key_block, value_block = block_scores(block)
        probs = jnp.exp(scores - log_total[..., None]).astype(jnp.bfloat16)
        accum = accum + jnp.einsum(
            "hqk,khd->qhd", probs, value_block, preferred_element_type=jnp.float32
        )
    mixed = accum.reshape(row_count, head_width).astype(jnp.bfloat16)
    out_part = jnp.einsum("qc,dc->qd", mixed, out_full, preferred_element_type=jnp.float32)
    middle = inputs + lax.psum(out_part.astype(jnp.bfloat16), "tp").astype(jnp.float32)
    second_norm, second_scale = normalize(middle)
    second = (second_norm * gain_two).astype(jnp.bfloat16)
    pieces = (
        lax.all_gather(gate_weight, ("dp", "ctx"), axis=0, tiled=True),
        lax.all_gather(up_weight, ("dp", "ctx"), axis=0, tiled=True),
    )
    columns = second
    gate = jnp.dot(columns, pieces[0], preferred_element_type=jnp.float32)
    upward = jnp.dot(columns, pieces[1], preferred_element_type=jnp.float32)
    sigmoid_gate = jax.nn.sigmoid(gate)
    silu_gate = gate * sigmoid_gate
    hidden = (silu_gate * upward).astype(jnp.bfloat16)
    ffn_part = jnp.einsum(
        "qf,df->qd",
        hidden,
        lax.all_gather(down_weight, ("dp", "ctx"), axis=0, tiled=True),
        preferred_element_type=jnp.float32,
    )
    ffn_share = lax.psum_scatter(
        ffn_part.astype(jnp.bfloat16), "tp", scatter_dimension=1, tiled=True
    ).astype(jnp.float32)
    share_width = ffn_share.shape[1]
    tp_index = lax.axis_index("tp")
    middle_share = lax.dynamic_slice_in_dim(middle, tp_index * share_width, share_width, 1)
    block_out = (middle_share + ffn_share).astype(jnp.bfloat16)
    cotangent = out_grad.astype(jnp.float32)
    columns = out_grad
    dhidden = jnp.dot(
        columns,
        lax.all_gather(down_weight, ("dp", "ctx"), axis=0, tiled=True),
        preferred_element_type=jnp.float32,
    )
    dgate = (dhidden * upward * (sigmoid_gate + gate * sigmoid_gate * (1.0 - sigmoid_gate))).astype(
        jnp.bfloat16
    )
    dupward = (dhidden * silu_gate).astype(jnp.bfloat16)
    pieces = (
        lax.all_gather(gate_weight, ("dp", "ctx"), axis=0, tiled=True),
        lax.all_gather(up_weight, ("dp", "ctx"), axis=0, tiled=True),
    )
    add_part = jnp.einsum(
        "qf,df->qd", dgate, pieces[0], preferred_element_type=jnp.float32
    ) + jnp.einsum("qf,df->qd", dupward, pieces[1], preferred_element_type=jnp.float32)
    dsecond = lax.psum(add_part.astype(jnp.bfloat16), "tp").astype(jnp.float32)
    gain_two_grad = jnp.sum(dsecond * second_norm, axis=0)
    scaled_two = dsecond * gain_two
    dmiddle = cotangent + second_scale * (
        scaled_two - second_norm * jnp.mean(scaled_two * second_norm, axis=-1, keepdims=True)
    )
    dmiddle_low = dmiddle.astype(jnp.bfloat16)
    dmixed = (
        jnp.einsum("qd,dc->qc", dmiddle_low, out_full, preferred_element_type=jnp.float32)
        .astype(jnp.bfloat16)
        .reshape(row_count, local_heads, HEAD_DIM)
    )
    delta = jnp.sum(dmixed.astype(jnp.float32) * accum, axis=-1).T
    dquery = jnp.zeros((row_count, local_heads, HEAD_DIM), jnp.float32)
    key_terms = []
    value_terms = []
    for block in range(ctx_count):
        scores, key_block, value_block = block_scores(block)
        probs = jnp.exp(scores - log_total[..., None])
        dprobs = jnp.einsum("qhd,khd->hqk", dmixed, value_block, preferred_element_type=jnp.float32)
        dscores = (probs * (dprobs - delta[..., None])).astype(jnp.bfloat16)
        dquery = (
            dquery
            + jnp.einsum("hqk,khd->qhd", dscores, key_block, preferred_element_type=jnp.float32)
            * scale
        )
        key_terms.append(
            (
                jnp.einsum("hqk,qhd->khd", dscores, query, preferred_element_type=jnp.float32)
                * scale
            ).reshape(row_count, head_width)
        )
        value_terms.append(
            jnp.einsum(
                "hqk,qhd->khd",
                probs.astype(jnp.bfloat16),
                dmixed,
                preferred_element_type=jnp.float32,
            ).reshape(row_count, head_width)
        )
    dkey, dvalue = (
        lax.psum_scatter(
            jnp.concatenate(key_terms, axis=0).astype(jnp.bfloat16),
            "ctx",
            scatter_dimension=0,
            tiled=True,
        ).astype(jnp.float32),
        lax.psum_scatter(
            jnp.concatenate(value_terms, axis=0).astype(jnp.bfloat16),
            "ctx",
            scatter_dimension=0,
            tiled=True,
        ).astype(jnp.float32),
    )
    dquery_low = unrotate(dquery, cosine, sine).reshape(row_count, head_width).astype(jnp.bfloat16)
    dkey_low = (
        unrotate(dkey.reshape(row_count, local_heads, HEAD_DIM), cosine, sine)
        .reshape(row_count, head_width)
        .astype(jnp.bfloat16)
    )
    dvalue_low = dvalue.astype(jnp.bfloat16)
    dfirst_part = jnp.einsum(
        "qc,dc->qd", dquery_low, query_full, preferred_element_type=jnp.float32
    )
    dfirst_part = dfirst_part + jnp.einsum(
        "qc,dc->qd", dkey_low, key_full, preferred_element_type=jnp.float32
    )
    dfirst_part = dfirst_part + jnp.einsum(
        "qc,dc->qd", dvalue_low, value_full, preferred_element_type=jnp.float32
    )
    dfirst = lax.psum(dfirst_part.astype(jnp.bfloat16), "tp").astype(jnp.float32)
    gain_one_grad = jnp.sum(dfirst * first_norm, axis=0)
    scaled_one = dfirst * gain_one
    dinputs = dmiddle + first_scale * (
        scaled_one - first_norm * jnp.mean(scaled_one * first_norm, axis=-1, keepdims=True)
    )
    in_grad = lax.dynamic_slice_in_dim(dinputs, tp_index * share_width, share_width, 1).astype(
        jnp.bfloat16
    )
    stacked = jnp.concatenate(
        [
            outer_rows(first, dquery_low),
            outer_rows(first, dkey_low),
            outer_rows(first, dvalue_low),
            outer_rows(dmiddle_low, mixed),
        ],
        axis=1,
    )
    first_stack = stacked
    stacked = jnp.concatenate(
        [outer_rows(second, dgate), outer_rows(second, dupward), outer_rows(out_grad, hidden)],
        axis=1,
    )
    whole_stack, attn_gain_grad, ffn_gain_grad = jax.tree.map(
        lambda part: lax.psum_scatter(
            part.astype(jnp.bfloat16), ("dp", "ctx"), scatter_dimension=0, tiled=True
        ).astype(jnp.float32),
        (jnp.concatenate([first_stack, stacked], axis=1), gain_one_grad, gain_two_grad),
    )
    attn_stack = whole_stack[:, : 4 * head_width]
    ffn_stack = whole_stack[:, 4 * head_width :]
    query_grad = attn_stack[:, :head_width]
    key_grad = attn_stack[:, head_width : 2 * head_width]
    value_grad = attn_stack[:, 2 * head_width : 3 * head_width]
    out_weight_grad = attn_stack[:, 3 * head_width :]
    gate_grad = ffn_stack[:, :ffn_width]
    up_grad = ffn_stack[:, ffn_width : 2 * ffn_width]
    down_grad = ffn_stack[:, 2 * ffn_width :]
    return (
        block_out,
        in_grad,
        attn_gain_grad,
        query_grad,
        key_grad,
        value_grad,
        out_weight_grad,
        ffn_gain_grad,
        gate_grad,
        up_grad,
        down_grad,
    )


def solution(mesh):
    placed = (
        P(("dp", "ctx"), None),
        P(),
        P(("dp", "ctx"), "tp"),
        P(("dp", "ctx"), "tp"),
        P(("dp", "ctx"), "tp"),
        P(("dp", "ctx"), "tp"),
        P(),
        P(("dp", "ctx"), "tp"),
        P(("dp", "ctx"), "tp"),
        P(("dp", "ctx"), "tp"),
        P("dp", None),
        P("dp", None),
        P(("dp", "ctx"), None),
    )
    return jax.shard_map(
        body,
        mesh=mesh,
        in_specs=placed,
        out_specs=(
            P(("dp", "ctx"), "tp"),
            P(("dp", "ctx"), "tp"),
            P(("dp", "ctx")),
            P(("dp", "ctx"), "tp"),
            P(("dp", "ctx"), "tp"),
            P(("dp", "ctx"), "tp"),
            P(("dp", "ctx"), "tp"),
            P(("dp", "ctx")),
            P(("dp", "ctx"), "tp"),
            P(("dp", "ctx"), "tp"),
            P(("dp", "ctx"), "tp"),
        ),
        check_vma=False,
    )
```

profile of v0, /device:TPU:1, one launch (start us, length us, event | category | flops | bytes accessed | tf_op | source)
XLA Modules:
  0.0 1870.0 jit_solution(1052963531263670778)
XLA Ops:
  12.8 47.7 %all-gather.10.cloned.1.call-done = bf16[2048,512]{1,0:T(8,128)(2,1)} async-done(((bf16[256,512]{1,0:T(8,128)(2,1)}), bf16[2048,512]{1,0:T(8,128)(2,1)}) %all-gather.10.cloned.1.call-update) | async-done | bytes 2097168 | tf_op jit(solution)/shard_map/all_gather | solution.py:89
  67.6 42.8 %all-gather.16.cloned.1.call-done = bf16[2048,512]{1,0:T(8,128)(2,1)} async-done(((bf16[256,512]{1,0:T(8,128)(2,1)}), bf16[2048,512]{1,0:T(8,128)(2,1)}) %all-gather.16.cloned.1.call-update) | async-done | bytes 2097168 | tf_op jit(solution)/shard_map/all_gather | solution.py:88
  115.1 45.2 %all-gather.14.cloned.1.call-done = bf16[2048,512]{1,0:T(8,128)(2,1)} async-done(((bf16[256,512]{1,0:T(8,128)(2,1)}), bf16[2048,512]{1,0:T(8,128)(2,1)}) %all-gather.14.cloned.1.call-update) | async-done | bytes 2097168 | tf_op jit(solution)/shard_map/all_gather | solution.py:87
  172.8 52.6 %all-gather.12.cloned.1.call-done = bf16[3072,512]{1,0:T(8,128)(2,1)} async-done(((bf16[768,512]{1,0:T(8,128)(2,1)}), bf16[3072,512]{1,0:T(8,128)(2,1)}) %all-gather.12.cloned.1.call-update) | async-done | bytes 3145744 | tf_op jit(solution)/shard_map/all_gather | solution.py:113
  238.2 51.4 %all-gather.18.cloned.1.call-done = bf16[3072,512]{0,1:T(8,128)(2,1)} async-done(((bf16[768,512]{0,1:T(8,128)(2,1)}), bf16[3072,512]{0,1:T(8,128)(2,1)}) %all-gather.18.cloned.1.call-update) | async-done | bytes 3145744 | tf_op jit(solution)/shard_map/all_gather | solution.py:112
  335.5 10.5 exponential_reduce_fusion
  346.0 10.8 exponential_reduce_fusion.1
  367.2 12.7 fusion.37
  379.9 12.8 fusion.34
  399.6 14.4 bitcast_convert_fusion
  421.5 65.0 %all-reduce.7.cloned.1.call-done = bf16[768,2048]{1,0:T(8,128)(2,1)} async-done(((bf16[768,2048]{1,0:T(8,128)(2,1)}), bf16[768,2048]{1,0:T(8,128)(2,1)}) %all-reduce.7.cloned.1.call-update) | async-done | bytes 3145744 | tf_op jit(solution)/shard_map/psum | solution.py:151
  493.1 120.3 %all-gather.24.cloned.1.call-done = bf16[2048,2048]{1,0:T(8,128)(2,1)} async-done(((bf16[256,2048]{1,0:T(8,128)(2,1)}), bf16[2048,2048]{1,0:T(8,128)(2,1)}) %all-gather.24.cloned.1.call-update) | async-done | bytes 8388624 | tf_op jit(solution)/shard_map/all_gather | solution.py:156
  613.4 12.1 fusion.55
  625.5 113.2 %all-gather.22.cloned.1.call-done = bf16[2048,2048]{1,0:T(8,128)(2,1)} async-done(((bf16[256,2048]{1,0:T(8,128)(2,1)}), bf16[2048,2048]{1,0:T(8,128)(2,1)}) %all-gather.22.cloned.1.call-update) | async-done | bytes 8388624 | tf_op jit(solution)/shard_map/all_gather | solution.py:155
  738.7 11.7 fusion.54
  750.4 113.4 %all-gather.26.cloned.1.call-done = bf16[2048,2048]{1,0:T(8,128)(2,1)} async-done(((bf16[256,2048]{1,0:T(8,128)(2,1)}), bf16[2048,2048]{1,0:T(8,128)(2,1)}) %all-gather.26.cloned.1.call-update) | async-done | bytes 8388624 | tf_op jit(solution)/shard_map/all_gather | solution.py:167
  863.8 16.9 multiply_convert_fusion.4
  880.7 11.2 fusion.56
  891.9 12.6 add_convert_fusion.1
  904.6 67.0 %all-reduce.9.cloned.1.call-done = bf16[768,2048]{1,0:T(8,128)(2,1)} async-done(((bf16[768,2048]{1,0:T(8,128)(2,1)}), bf16[768,2048]{1,0:T(8,128)(2,1)}) %all-reduce.9.cloned.1.call-update) | async-done | bytes 3145744 | tf_op jit(solution)/shard_map/psum | solution.py:195
  987.7 12.2 multiply_convert_fusion.1
  999.9 12.0 multiply_convert_fusion.2
  1012.0 12.4 multiply_convert_fusion.3
  1024.4 12.3 multiply_convert_fusion
  1063.4 11.7 convolution_convert_fusion.8
  1104.6 12.0 convolution_convert_fusion
  1156.4 29.8 %reduce-scatter.9.cloned.1.call-done = bf16[768,512]{0,1:T(8,128)(2,1)} async-done(((bf16[3072,512]{0,1:T(8,128)(2,1)}), bf16[768,512]{0,1:T(8,128)(2,1)}) %reduce-scatter.9.cloned.1.call-update) | async-done | bytes 786448 | tf_op jit(solution)/shard_map/reduce_scatter | solution.py:242
  1205.6 11.9 convert_dynamic-update-slice_fusion.1
  1226.8 11.4 bitcast_dynamic-update-slice_fusion
  1242.9 54.6 %all-reduce.11.cloned.1.call-done = bf16[768,2048]{1,0:T(8,128)(2,1)} async-done(((bf16[768,2048]{1,0:T(8,128)(2,1)}), bf16[768,2048]{1,0:T(8,128)(2,1)}) %all-reduce.11.cloned.1.call-update) | async-done | bytes 3145744 | tf_op jit(solution)/shard_map/psum | solution.py:265
  1304.5 19.3 %all-reduce.2 = (bf16[2048]{0:T(1024)(128)(2,1)S(1)}, bf16[2048]{0:T(1024)(128)(2,1)S(1)}) all-reduce(bf16[2048]{0:T(1024)(128)(2,1)S(1)} %get-tuple-element.46, bf16[2048]{0:T(1024)(128)(2,1)S(1)} %copy-done.53), channel_id=5, replica_groups=mesh['dp'=2,'ctx'=4,'tp'=4] {'dp','ctx'}, use_global_device_ids=true, to_apply=%region_20.21.clone | all-reduce | flops 4096 | bytes 16384
  1328.7 517.1 %reduce-scatter.11.cloned.1.call-done = bf16[256,8192]{0,1:T(8,128)(2,1)} async-done(((bf16[2048,8192]{0,1:T(8,128)(2,1)}), bf16[256,8192]{0,1:T(8,128)(2,1)}) %reduce-scatter.11.cloned.1.call-update) | async-done | bytes 4194320 | tf_op jit(solution)/shard_map/reduce_scatter | solution.py:289
  (274 shorter events, 293.3 us)
Async XLA Ops:
  7.2 53.3 %all-gather.10.cloned.1.call-start = ((), (), s32[]{:S(2)}) async-start(), calls=%async_computation.4 | async-start | bytes 2359296 | tf_op jit(solution)/shard_map/all_gather | solution.py:89
  7.9 102.5 %all-gather.16.cloned.1.call-start = ((), (), s32[]{:S(2)}) async-start(), calls=%async_computation.7 | async-start | bytes 2359296 | tf_op jit(solution)/shard_map/all_gather | solution.py:88
  8.7 151.7 %all-gather.14.cloned.1.call-start = ((), (), s32[]{:S(2)}) async-start(), calls=%async_computation.6 | async-start | bytes 2359296 | tf_op jit(solution)/shard_map/all_gather | solution.py:87
  9.4 216.0 %all-gather.12.cloned.1.call-start = ((), (), s32[]{:S(2)}) async-start(), calls=%async_computation.5 | async-start | bytes 3932160 | tf_op jit(solution)/shard_map/all_gather | solution.py:113
  10.1 150.2 %copy-start.50 = (f32[2048]{0:T(1024)}, f32[2048]{0:T(1024)S(1)}, u32[]{:S(2)}) copy-start(f32[2048]{0:T(1024)S(1)} %convert_element_type.153) | copy-start | bytes 24580
  12.7 147.6 %copy-start.48 = (f32[768]{0:T(1024)}, f32[768]{0:T(1024)S(1)}, u32[]{:S(2)}) copy-start(f32[768]{0:T(1024)S(1)} %add_rsqrt_fusion.1) | copy-start | bytes 9220
  12.7 53.0 %copy-start.47 = (s32[1,3072]{1,0:T(1,128)S(1)}, s32[1,3072]{1,0:T(1,128)}, u32[]{:S(2)}) copy-start(s32[1,3072]{1,0:T(1,128)} %param.23) | copy-start | bytes 36868
  12.7 53.0 %copy-start.52 = (s32[1,3072]{1,0:T(1,128)S(1)}, s32[1,3072]{1,0:T(1,128)}, u32[]{:S(2)}) copy-start(s32[1,3072]{1,0:T(1,128)} %param.24) | copy-start | bytes 36868
  12.8 97.6 %copy-start = (bf16[768,2048]{1,0:T(8,128)(2,1)S(1)}, bf16[768,2048]{1,0:T(8,128)(2,1)}, u32[]{:S(2)}) copy-start(bf16[768,2048]{1,0:T(8,128)(2,1)} %param.13) | copy-start | bytes 9437188
  65.7 223.9 %all-gather.18.cloned.1.call-start = ((), (), s32[]{:S(2)}) async-start(), calls=%async_computation.8 | async-start | bytes 3932160 | tf_op jit(solution)/shard_map/all_gather | solution.py:112
  165.3 151.5 %copy-start.3 = (bf16[768,8,32]{0,2,1:T(8,128)(2,1)}, bf16[768,8,32]{0,2,1:T(8,128)(2,1)S(1)}, u32[]{:S(2)}) copy-start(bf16[768,8,32]{0,2,1:T(8,128)(2,1)S(1)} %get-tuple-element.93) | copy-start | bytes 1179652
  166.3 247.7 %all-gather.20.cloned.1.call-start = ((), (), s32[]{:S(2)}) async-start(), calls=%async_computation.9 | async-start | bytes 2359296 | tf_op jit(solution)/shard_map/all_gather | solution.py:90
  166.9 319.6 %all-reduce.7.cloned.1.call-start = ((), (), s32[]{:S(2)}) async-start(), calls=%async_computation.10 | async-start | bytes 6291456 | tf_op jit(solution)/shard_map/psum | solution.py:151
  291.8 16.9 copy-start.15
  291.8 25.0 %copy-start.9 = (bf16[768,512]{0,1:T(8,128)(2,1)}, bf16[768,512]{0,1:T(8,128)(2,1)S(1)}, u32[]{:S(2)}) copy-start(bf16[768,512]{0,1:T(8,128)(2,1)S(1)} %get-tuple-element.86) | copy-start | bytes 2359300
  300.4 24.8 %copy-start.45 = (f32[8,768]{1,0:T(8,128)}, f32[8,768]{1,0:T(8,128)S(1)}, u32[]{:S(2)}) copy-start(f32[8,768]{1,0:T(8,128)S(1)} %get-tuple-element.114) | copy-start | bytes 73732
  367.2 25.6 %slice-start = ((s8[18874368]{0:T(1024)(128)(4,1)}), s8[4194304]{0:T(1024)(128)(4,1)S(1)}, s32[]{:S(2)}) async-start(s8[18874368]{0:T(1024)(128)(4,1)} %bitcast.119), calls=%async_computation.20 | async-start | bytes 8388608
  367.2 25.6 %slice-start.1 = ((s8[18874368]{0:T(1024)(128)(4,1)}), s8[4194304]{0:T(1024)(128)(4,1)S(1)}, s32[]{:S(2)}) async-start(s8[18874368]{0:T(1024)(128)(4,1)} %bitcast.119), calls=%async_computation.21 | async-start | bytes 8388608
  367.2 25.5 %slice-start.2 = ((s8[18874368]{0:T(1024)(128)(4,1)}), s8[4194304]{0:T(1024)(128)(4,1)S(1)}, s32[]{:S(2)}) async-start(s8[18874368]{0:T(1024)(128)(4,1)} %bitcast.119), calls=%async_computation.22 | async-start | bytes 8388608
  419.4 194.0 %all-gather.24.cloned.1.call-start = ((), (), s32[]{:S(2)}) async-start(), calls=%async_computation.12 | async-start | bytes 9437184 | tf_op jit(solution)/shard_map/all_gather | solution.py:156
  420.1 318.5 %all-gather.22.cloned.1.call-start = ((), (), s32[]{:S(2)}) async-start(), calls=%async_computation.11 | async-start | bytes 9437184 | tf_op jit(solution)/shard_map/all_gather | solution.py:155
  420.9 442.9 %all-gather.26.cloned.1.call-start = ((), (), s32[]{:S(2)}) async-start(), calls=%async_computation.13 | async-start | bytes 9437184 | tf_op jit(solution)/shard_map/all_gather | solution.py:167
  421.5 550.1 %all-reduce.9.cloned.1.call-start = ((), (), s32[]{:S(2)}) async-start(), calls=%async_computation.15 | async-start | bytes 6291456 | tf_op jit(solution)/shard_map/psum | solution.py:195
  904.5 232.6 %reduce-scatter.7.cloned.1.call-start = ((), (), s32[]{:S(2)}) async-start(), calls=%async_computation.16 | async-start | bytes 3932160 | tf_op jit(solution)/shard_map/reduce_scatter | solution.py:236
  987.6 24.3 %copy-start.58 = (bf16[768,512]{0,1:T(8,128)(2,1)}, bf16[768,512]{0,1:T(8,128)(2,1)S(1)}, u32[]{:S(2)}) copy-start(bf16[768,512]{0,1:T(8,128)(2,1)S(1)} %get-tuple-element.119) | copy-start | bytes 2359300
  1024.4 27.8 %slice-start.11 = ((s8[9437184]{0:T(1024)(128)(4,1)}), s8[1048576]{0:T(1024)(128)(4,1)S(1)}, s32[]{:S(2)}) async-start(s8[9437184]{0:T(1024)(128)(4,1)} %bitcast.125), calls=%async_computation.31 | async-start | bytes 2097152
  1024.4 27.8 %slice-start.12 = ((s8[9437184]{0:T(1024)(128)(4,1)}), s8[4194304]{0:T(1024)(128)(4,1)S(1)}, s32[]{:S(2)}) async-start(s8[9437184]{0:T(1024)(128)(4,1)} %bitcast.125), calls=%async_computation.32 | async-start | bytes 8388608
  1063.1 123.1 %reduce-scatter.9.cloned.1.call-start = ((), (), s32[]{:S(2)}) async-start(), calls=%async_computation.17 | async-start | bytes 3932160 | tf_op jit(solution)/shard_map/reduce_scatter | solution.py:242
  1104.5 135.6 %reduce-scatter.5.cloned.1.call-start = ((), (), s32[]{:S(2)}) async-start(), calls=%async_computation.14 | async-start | bytes 3932160 | tf_op jit(solution)/shard_map/reduce_scatter | solution.py:170
  1116.6 180.9 %all-reduce.11.cloned.1.call-start = ((), (), s32[]{:S(2)}) async-start(), calls=%async_computation.18 | async-start | bytes 6291456 | tf_op jit(solution)/shard_map/psum | solution.py:265
  1226.7 619.1 %reduce-scatter.11.cloned.1.call-start = ((), (), s32[]{:S(2)}) async-start(), calls=%async_computation.19 | async-start | bytes 37748736 | tf_op jit(solution)/shard_map/reduce_scatter | solution.py:289
  1242.9 61.6 %copy-start.53 = (bf16[2048]{0:T(1024)(128)(2,1)S(1)}, bf16[2048]{0:T(1024)(128)(2,1)}, u32[]{:S(2)}) copy-start(bf16[2048]{0:T(1024)(128)(2,1)} %get-tuple-element.44) | copy-start | bytes 12292
  (62 other events, 484.6 us)
Sparse Core Ops, SparseCore 0:
  10.1 50.2 all-gather.9
  62.6 47.7 all-gather.15
  112.5 47.7 all-gather.13
  162.3 63.0 all-gather.11
  227.4 62.1 all-gather.17
  291.6 46.8 all-gather.19
  419.5 66.9 all-reduce.6
  488.6 124.7 all-gather.23
  615.5 123.1 all-gather.21
  740.7 123.1 all-gather.25
  904.6 66.9 all-reduce.8
  1063.3 60.2 reduce-scatter.6
  1125.9 60.2 reduce-scatter.8
  1188.6 38.1 reduce-scatter.4
  1229.1 68.3 all-reduce.10
  1301.6 544.2 reduce-scatter.10
where the time goes:
time: 1880 us; the launch traced here: 1870 us
  waiting for transfers between devices  1320 us (70%)
  matrix products  378 us (20%)
  other arithmetic  93.9 us (5%)
  local copies, waits for them, and re-layouts  37.1 us (2%)
  blocking collectives  19.3 us (1%)
    reduce_scatter x1, waiting for transfers between devices, body(): lax.psum_scatter(part.astype(jnp.bfloat16), ('dp', 'ctx'), scatter_dimens...  517 us
    all_gather x1, waiting for transfers between devices, body(): lax.all_gather(up_weight, ('dp', 'ctx'), axis=0, tiled=True)  120 us
    all_gather x1, waiting for transfers between devices, body(): lax.all_gather(down_weight, ('dp', 'ctx'), axis=0, tiled=True)  113 us
    all_gather x1, waiting for transfers between devices, body(): lax.all_gather(gate_weight, ('dp', 'ctx'), axis=0, tiled=True)  113 us
    psum x1, waiting for transfers between devices, body(): dsecond = lax.psum(add_part.astype(jnp.bfloat16), 'tp').astype(jnp.float32)  67 us
    psum x1, waiting for transfers between devices, body(): lax.psum(out_part.astype(jnp.bfloat16), 'tp').astype(jnp.float32)  65 us
    psum x1, waiting for transfers between devices, body(): lax.psum(dfirst_part.astype(jnp.bfloat16), 'tp').astype(jnp.float32)  54.6 us
    all_gather x1, waiting for transfers between devices, body(): lax.all_gather(value_rows, 'ctx', axis=0, tiled=True)  52.6 us
  transfers between devices with their start and end apart: 16, of which 13 were waited for; matrix products, arithmetic and copies ran while one was open for 19% of the time, Pallas kernels for 0%

commit v1 on v0

v1 whole, which is shorter than its diff:
```python
import functools
import math

import jax
import jax.numpy as jnp
from jax import lax
from jax.experimental import pallas as pl
from jax.experimental.pallas import tpu as pltpu
from jax.sharding import PartitionSpec as P

HEAD_DIM = 64
CLEN = 256
LANES = 128
EPS = 1e-05
ROPE_BASE = 130000.0
MASKED = -1e30
FFN_CHUNKS = 4
BF16 = jnp.bfloat16
F32 = jnp.float32
VMEM_LIMIT = 56 * 1024 * 1024


def swap(values, axis, mask):
    count = lax.axis_size(axis)
    return lax.ppermute(values, axis, [(i, i ^ mask) for i in range(count)])


def fetch(values, axis, shift):
    count = lax.axis_size(axis)
    return lax.ppermute(values, axis, [(i, (i - shift) % count) for i in range(count)])


def send(values, axis, shift):
    count = lax.axis_size(axis)
    return lax.ppermute(values, axis, [(i, (i + shift) % count) for i in range(count)])


def add_low(left, right):
    return (left.astype(F32) + right.astype(F32)).astype(BF16)


def sum_over_tp(part):
    count = lax.axis_size("tp")
    rows = part.shape[0]
    half = rows // 2
    bit = lax.axis_index("tp") & 1
    keep = lax.dynamic_slice_in_dim(part, bit * half, half)
    give = lax.dynamic_slice_in_dim(part, (1 - bit) * half, half)
    total = add_low(keep, swap(give, "tp", 1))
    mask = 2
    while mask < count:
        total = add_low(total, swap(total, "tp", mask))
        mask *= 2
    back = swap(total, "tp", 1)
    first = jnp.where(bit == 0, total, back)
    last = jnp.where(bit == 0, back, total)
    return jnp.concatenate([first, last], axis=0)


def scatter_over_tp(part, shift):
    count = lax.axis_size("tp")
    width = part.shape[1] // count
    me = lax.axis_index("tp")

    def block(owner):
        start = lax.rem(owner * width - shift + part.shape[1], part.shape[1])
        return lax.dynamic_slice_in_dim(part, start, width, 1)

    held = {other: None for other in range(0, count, 2)}
    for other in held:
        held[other] = add_low(block(me ^ other), swap(block(me ^ other ^ 1), "tp", 1))
    mask = count // 2
    while mask >= 2:
        for other in [o for o in held if o & mask]:
            held[other ^ mask] = add_low(held[other ^ mask], swap(held.pop(other), "tp", mask))
        mask //= 2
    return held[0]


def sum_everywhere(values):
    for axis in ("tp", "ctx", "dp"):
        mask = 1
        while mask < lax.axis_size(axis):
            values = values + swap(values, axis, mask)
            mask *= 2
    return values


def gather_rows(weight):
    own = lax.all_gather(weight, "ctx", axis=0, tiled=True)
    return [own] + [fetch(own, "dp", s) for s in range(1, lax.axis_size("dp"))]


def scatter_rows(blocks):
    total = blocks[0]
    extra = [send(block, "dp", s) for s, block in enumerate(blocks) if s]
    if extra:
        total = total.astype(F32)
        for term in extra:
            total = total + term.astype(F32)
        total = total.astype(BF16)
    return lax.psum_scatter(total, "ctx", scatter_dimension=0, tiled=True)


def dot(left, right, dims):
    return lax.dot_general(left, right, (dims, ((), ())), preferred_element_type=F32)


NN = ((1,), (0,))
NT = ((1,), (1,))
TN = ((0,), (0,))


def half_swap(values):
    lane = lax.broadcasted_iota(jnp.int32, values.shape, 1)
    ahead = pltpu.roll(values, LANES - 32, 1)
    behind = pltpu.roll(values, 32, 1)
    return jnp.where((lane & 63) < 32, ahead, behind)


def project_kernel(count, rope, x_ref, *refs):
    w_refs = refs[:count]
    cos_ref, sin_ref, out_ref = refs[count:]
    depth = w_refs[0].shape[0]
    total = None
    for piece in range(count):
        term = dot(x_ref[:, piece * depth : (piece + 1) * depth], w_refs[piece][...], NN)
        total = term if total is None else total + term
    if rope:
        cosine, sine = cos_ref[...], sin_ref[...]
        for at in range(0, total.shape[1], LANES):
            part = total[:, at : at + LANES]
            out_ref[:, at : at + LANES] = (part * cosine + half_swap(part) * sine).astype(BF16)
    else:
        out_ref[...] = total.astype(BF16)


def project(x, pieces, cosine, sine, rope):
    rows, width = x.shape[0], pieces[0].shape[1]
    count = len(pieces)
    full = lambda i: (0, 0)
    row = lambda i: (i, 0)
    return pl.pallas_call(
        functools.partial(project_kernel, count, rope),
        grid=(rows // CLEN,),
        in_specs=[pl.BlockSpec((CLEN, x.shape[1]), row)]
        + [pl.BlockSpec(p.shape, full) for p in pieces]
        + [pl.BlockSpec((CLEN, LANES), row)] * 2,
        out_specs=pl.BlockSpec((CLEN, width), row),
        out_shape=jax.ShapeDtypeStruct((rows, width), BF16),
        compiler_params=pltpu.CompilerParams(vmem_limit_bytes=VMEM_LIMIT),
        cost_estimate=pl.CostEstimate(
            flops=2 * rows * x.shape[1] * width,
            bytes_accessed=2 * (x.size + x.shape[1] * width + rows * width),
            transcendentals=0,
        ),
        name="project",
    )(x, *pieces, cosine, sine)


SCALE = HEAD_DIM**-0.5
SCALE_LOG2 = SCALE * math.log2(math.e)


def forward_kernel(pieces, order_ref, rank_ref, q_ref, ks_ref, vs_ref, *refs):
    kp_refs, vp_refs = refs[:pieces], refs[pieces : 2 * pieces]
    o_ref, lse_ref = refs[2 * pieces :]
    q = q_ref[...]
    size = q.shape[0]
    prompt = pl.program_id(1) == 0
    low_lane = lax.broadcasted_iota(jnp.int32, q.shape, 1) < HEAD_DIM
    causal = lax.broadcasted_iota(jnp.int32, (size, size), 0) >= lax.broadcasted_iota(
        jnp.int32, (size, size), 1
    )
    outs = []
    for head in range(2):
        own = low_lane if head == 0 else jnp.logical_not(low_lane)
        qh = jnp.where(own, q, jnp.zeros_like(q))
        raw = [jnp.where(causal, dot(qh, ks_ref[...], NT), MASKED)]
        for s in range(pieces):
            hidden = jnp.logical_and(prompt, rank_ref[s] >= rank_ref[0])
            raw.append(dot(qh, kp_refs[s][...], NT) + jnp.where(hidden, MASKED, 0.0))
        top = raw[0]
        for r in raw[1:]:
            top = jnp.maximum(top, r)
        top = jnp.max(top, axis=-1, keepdims=True) * SCALE_LOG2
        sums, acc = None, None
        for s, r in enumerate(raw):
            e = jnp.exp2(r * SCALE_LOG2 - top)
            v = vs_ref if s == 0 else vp_refs[s - 1]
            term = dot(e.astype(BF16), v[...], NN)
            sums = e if sums is None else sums + e
            acc = term if acc is None else acc + term
        total = jnp.sum(sums, axis=-1, keepdims=True)
        outs.append((acc / total, top + jnp.log2(total)))
    o_ref[...] = jnp.where(low_lane, outs[0][0], outs[1][0]).astype(BF16)
    lse_ref[...] = jnp.where(low_lane, outs[0][1], outs[1][1])


def backward_kernel(
    pieces, order_ref, rank_ref, q_ref, ks_ref, vs_ref, o_ref, lse_ref, do_ref, cos_ref, sin_ref, *refs
):
    kp_refs, vp_refs = refs[:pieces], refs[pieces : 2 * pieces]
    dq_ref, dks_ref, dvs_ref, dkp_ref, dvp_ref = refs[2 * pieces :]
    step = pl.program_id(1)
    prompt = step == 0
    q, do = q_ref[...], do_ref[...]
    size = q.shape[0]
    low_lane = lax.broadcasted_iota(jnp.int32, q.shape, 1) < HEAD_DIM
    causal = lax.broadcasted_iota(jnp.int32, (size, size), 0) >= lax.broadcasted_iota(
        jnp.int32, (size, size), 1
    )
    product = do.astype(F32) * o_ref[...].astype(F32)
    lse = lse_ref[...]
    dq_heads = []
    dk_all = [None] * (pieces + 1)
    dv_all = [None] * (pieces + 1)
    for head in range(2):
        own = low_lane if head == 0 else jnp.logical_not(low_lane)
        qh = jnp.where(own, q, jnp.zeros_like(q))
        doh = jnp.where(own, do, jnp.zeros_like(do))
        delta = jnp.sum(jnp.where(own, product, 0.0), axis=-1, keepdims=True)
        log_sum = lse[:, head * HEAD_DIM : head * HEAD_DIM + 1]
        dq = None
        for s in range(pieces + 1):
            k = (ks_ref if s == 0 else kp_refs[s - 1])[...]
            v = (vs_ref if s == 0 else vp_refs[s - 1])[...]
            raw = dot(qh, k, NT)
            if s == 0:
                raw = jnp.where(causal, raw, MASKED)
            else:
                hidden = jnp.logical_and(prompt, rank_ref[s - 1] >= rank_ref[0])
                raw = raw + jnp.where(hidden, MASKED, 0.0)
            prob = jnp.exp2(raw * SCALE_LOG2 - log_sum)
            ds = (prob * (dot(doh, v, NT) - delta)).astype(BF16)
            term = dot(ds, k, NN)
            dq = term if dq is None else dq + term
            dk = dot(ds, qh, TN)
            dv = dot(prob.astype(BF16), doh, TN)
            dk_all[s] = dk if dk_all[s] is None else dk_all[s] + dk
            dv_all[s] = dv if dv_all[s] is None else dv_all[s] + dv
        dq_heads.append(dq)
    dq = jnp.where(low_lane, dq_heads[0], dq_heads[1]) * SCALE
    cosine, sine = cos_ref[...], sin_ref[...]
    dq_ref[...] = (dq * cosine - half_swap(dq) * sine).astype(BF16)
    dks_ref[...] = dk_all[0] * SCALE
    dvs_ref[...] = dv_all[0]
    for s in range(pieces):
        at = slice(s * size, (s + 1) * size)

        @pl.when(prompt)
        def _():
            dkp_ref[at, :] = dk_all[s + 1] * SCALE
            dvp_ref[at, :] = dv_all[s + 1]

        @pl.when(jnp.logical_not(prompt))
        def _():
            dkp_ref[at, :] += dk_all[s + 1] * SCALE
            dvp_ref[at, :] += dv_all[s + 1]


def attention_specs(pieces, key_pairs):
    own = pl.BlockSpec((CLEN, LANES), lambda h, j, order, rank: (order[j], h))
    key = pl.BlockSpec((CLEN, LANES), lambda h, j, order, rank: (0, h))
    value = pl.BlockSpec((CLEN, LANES), lambda h, j, order, rank: (0, key_pairs + h))
    trig = pl.BlockSpec((CLEN, LANES), lambda h, j, order, rank: (order[j], 0))
    prompt = pl.BlockSpec((pieces * CLEN, LANES), lambda h, j, order, rank: (0, h))
    return own, key, value, trig, prompt


def attention_forward(order, rank, query, keys, values, prompts):
    rows, width = query.shape
    pieces, pairs = len(prompts), width // LANES
    own, key, value, _, _ = attention_specs(pieces, pairs)
    scores = rows * (pieces + 1) * CLEN * (width // HEAD_DIM)
    return pl.pallas_call(
        functools.partial(forward_kernel, pieces),
        grid_spec=pltpu.PrefetchScalarGridSpec(
            num_scalar_prefetch=2,
            grid=(pairs, rows // CLEN),
            in_specs=[own] * 3 + [key] * pieces + [value] * pieces,
            out_specs=[own, own],
        ),
        out_shape=[jax.ShapeDtypeStruct((rows, width), BF16), jax.ShapeDtypeStruct((rows, width), F32)],
        compiler_params=pltpu.CompilerParams(vmem_limit_bytes=VMEM_LIMIT),
        cost_estimate=pl.CostEstimate(
            flops=16 * scores * HEAD_DIM, bytes_accessed=16 * rows * width, transcendentals=scores
        ),
        name="attend",
    )(order, rank, query, keys, values, *prompts, *prompts)


def attention_backward(order, rank, query, keys, values, mixed, lse, dmixed, cosine, sine, prompts):
    rows, width = query.shape
    pieces, pairs = len(prompts), width // LANES
    own, key, value, trig, prompt = attention_specs(pieces, pairs)
    scores = rows * (pieces + 1) * CLEN * (width // HEAD_DIM)
    return pl.pallas_call(
        functools.partial(backward_kernel, pieces),
        grid_spec=pltpu.PrefetchScalarGridSpec(
            num_scalar_prefetch=2,
            grid=(pairs, rows // CLEN),
            in_specs=[own] * 6 + [trig] * 2 + [key] * pieces + [value] * pieces,
            out_specs=[own, own, own, prompt, prompt],
        ),
        out_shape=[
            jax.ShapeDtypeStruct((rows, width), BF16),
            jax.ShapeDtypeStruct((rows, width), F32),
            jax.ShapeDtypeStruct((rows, width), F32),
            jax.ShapeDtypeStruct((pieces * CLEN, width), F32),
            jax.ShapeDtypeStruct((pieces * CLEN, width), F32),
        ],
        compiler_params=pltpu.CompilerParams(vmem_limit_bytes=VMEM_LIMIT),
        cost_estimate=pl.CostEstimate(
            flops=40 * scores * HEAD_DIM, bytes_accessed=32 * rows * width, transcendentals=scores
        ),
        name="attend_back",
    )(order, rank, query, keys, values, mixed, lse, dmixed, cosine, sine, *prompts, *prompts)


def normalize(values):
    factor = lax.rsqrt(jnp.mean(values * values, axis=-1, keepdims=True) + EPS)
    return (values * factor, factor)


def rope_tables(where):
    half = HEAD_DIM // 2
    freqs = ROPE_BASE ** (-(jnp.arange(half).astype(F32) * 2.0) / HEAD_DIM)
    angles = where.astype(F32)[:, None] * freqs[None, :]
    cosine, sine = jnp.cos(angles), jnp.sin(angles)
    return (
        jnp.concatenate([cosine] * 4, axis=1),
        jnp.concatenate([-sine, sine, -sine, sine], axis=1),
    )


def matmul_pieces(left, pieces):
    depth = pieces[0].shape[0]
    total = None
    for s, piece in enumerate(pieces):
        term = jnp.dot(left[:, s * depth : (s + 1) * depth], piece, preferred_element_type=F32)
        total = term if total is None else total + term
    return total


def matmul_back(left, pieces):
    return jnp.concatenate(
        [jnp.einsum("qf,df->qd", left, p, preferred_element_type=F32) for p in pieces], axis=1
    )


def row_grads(left, right, blocks):
    depth = left.shape[1] // blocks
    return [
        jnp.einsum(
            "tc,tf->cf", left[:, s * depth : (s + 1) * depth], right, preferred_element_type=F32
        ).astype(BF16)
        for s in range(blocks)
    ]


def body(
    tokens,
    attn_gain,
    query_weight,
    key_weight,
    value_weight,
    out_weight,
    ffn_gain,
    gate_weight,
    up_weight,
    down_weight,
    seq_ids,
    positions,
    out_grad,
):
    rows, width = tokens.shape
    head_width = query_weight.shape[1]
    ffn_width = gate_weight.shape[1]
    chunk = ffn_width // FFN_CHUNKS
    dp_count = lax.axis_size("dp")
    ctx_count = lax.axis_size("ctx")
    tp_count = lax.axis_size("tp")
    dp_index = lax.axis_index("dp")
    ctx_index = lax.axis_index("ctx")
    tp_index = lax.axis_index("tp")
    shift = dp_index * (width // dp_count)

    def turned(values):
        doubled = jnp.concatenate([values, values], axis=-1)
        return lax.dynamic_slice_in_dim(doubled, shift, width, values.ndim - 1)

    q_pieces = gather_rows(query_weight)
    k_pieces = gather_rows(key_weight)
    v_pieces = gather_rows(value_weight)
    o_pieces = gather_rows(out_weight)
    ffn_pieces = []
    for f in range(FFN_CHUNKS):
        at = slice(f * chunk, (f + 1) * chunk)
        ffn_pieces.append(
            gather_rows(
                jnp.concatenate([gate_weight[:, at], up_weight[:, at], down_weight[:, at]], axis=1)
            )
        )

    group_seq = seq_ids[0].reshape(ctx_count, rows // CLEN, CLEN)[:, :, 0]
    group_pos = positions[0].reshape(ctx_count, rows // CLEN, CLEN)[:, :, 0]
    prompt_at = jnp.argmax(group_seq == 0, axis=1).astype(jnp.int32)
    prompt_rank = jnp.sum(jnp.where(group_seq == 0, group_pos, 0), axis=1).astype(jnp.int32)
    rank = jnp.roll(prompt_rank, -ctx_index)
    mine = prompt_at[ctx_index]
    blocks = jnp.arange(rows // CLEN, dtype=jnp.int32)
    order = jnp.concatenate([mine[None], jnp.sort(jnp.where(blocks == mine, -1, blocks))[1:]])
    own_pos = lax.dynamic_slice_in_dim(positions[0], ctx_index * rows, rows)
    cosine, sine = rope_tables(own_pos)

    inputs = turned(tokens).astype(F32)
    cotangent_low = turned(out_grad)
    gain_one = turned(attn_gain).astype(F32)
    gain_two = turned(ffn_gain).astype(F32)
    first_norm, first_scale = normalize(inputs)
    first = (first_norm * gain_one).astype(BF16)

    query = project(first, q_pieces, cosine, sine, True)
    keys = project(first, k_pieces, cosine, sine, True)
    values = project(first, v_pieces, cosine, sine, False)
    prompt_own = jnp.concatenate(
        [
            lax.dynamic_slice_in_dim(keys, mine * CLEN, CLEN),
            lax.dynamic_slice_in_dim(values, mine * CLEN, CLEN),
        ],
        axis=1,
    )
    prompts = [prompt_own] + [fetch(prompt_own, "ctx", s) for s in range(1, ctx_count)]
    mixed, lse = attention_forward(order, rank, query, keys, values, prompts)
    middle = inputs + sum_over_tp(matmul_back(mixed, o_pieces).astype(BF16)).astype(F32)
    second_norm, second_scale = normalize(middle)
    second = (second_norm * gain_two).astype(BF16)

    ffn_part, dsecond_part = None, None
    ffn_grads = []
    for f in range(FFN_CHUNKS):
        gate_w = [p[:, :chunk] for p in ffn_pieces[f]]
        up_w = [p[:, chunk : 2 * chunk] for p in ffn_pieces[f]]
        down_w = [p[:, 2 * chunk :] for p in ffn_pieces[f]]
        gate = matmul_pieces(second, gate_w)
        upward = matmul_pieces(second, up_w)
        dhidden = matmul_pieces(cotangent_low, down_w)
        sigmoid_gate = jax.nn.sigmoid(gate)
        silu_gate = gate * sigmoid_gate
        hidden = (silu_gate * upward).astype(BF16)
        dgate = (
            dhidden * upward * (sigmoid_gate + gate * sigmoid_gate * (1.0 - sigmoid_gate))
        ).astype(BF16)
        dupward = (dhidden * silu_gate).astype(BF16)
        part = matmul_back(hidden, down_w)
        ffn_part = part if ffn_part is None else ffn_part + part
        part = matmul_back(dgate, gate_w) + matmul_back(dupward, up_w)
        dsecond_part = part if dsecond_part is None else dsecond_part + part
        grads = [
            jnp.concatenate(terms, axis=1)
            for terms in zip(
                row_grads(second, dgate, dp_count),
                row_grads(second, dupward, dp_count),
                row_grads(cotangent_low, hidden, dp_count),
            )
        ]
        ffn_grads.append(scatter_rows(grads))

    share = width // tp_count
    ffn_share = scatter_over_tp(ffn_part.astype(BF16), shift).astype(F32)

    def own_share(values):
        start = lax.rem(tp_index * share - shift + width, width)
        return lax.dynamic_slice_in_dim(values, start, share, values.ndim - 1)

    block_out = (own_share(middle) + ffn_share).astype(BF16)

    cotangent = cotangent_low.astype(F32)
    dsecond = sum_over_tp(dsecond_part.astype(BF16)).astype(F32)
    gain_two_grad = jnp.sum(dsecond * second_norm, axis=0)
    scaled_two = dsecond * gain_two
    dmiddle = cotangent + second_scale * (
        scaled_two - second_norm * jnp.mean(scaled_two * second_norm, axis=-1, keepdims=True)
    )
    dmiddle_low = dmiddle.astype(BF16)
    dmixed = matmul_pieces(dmiddle_low, o_pieces).astype(BF16)
    dquery_low, dkey_own, dvalue_own, dkey_prompt, dvalue_prompt = attention_backward(
        order, rank, query, keys, values, mixed, lse, dmixed, cosine, sine, prompts
    )
    dprompt = jnp.concatenate([dkey_prompt, dvalue_prompt], axis=1)
    extra = dprompt[:CLEN]
    for s in range(1, ctx_count):
        piece = dprompt[s * CLEN : (s + 1) * CLEN].astype(BF16)
        extra = extra + send(piece, "ctx", s).astype(F32)
    is_mine = (jnp.arange(rows, dtype=jnp.int32) // CLEN == mine)[:, None]
    wide = jnp.concatenate([extra] * (rows // CLEN), axis=0)
    dkey = dkey_own + jnp.where(is_mine, wide[:, :head_width], 0.0)
    dvalue_low = (dvalue_own + jnp.where(is_mine, wide[:, head_width:], 0.0)).astype(BF16)
    half = HEAD_DIM // 2
    turned_key = dkey.reshape(rows, head_width // HEAD_DIM, 2, half)[:, :, ::-1].reshape(rows, head_width)
    repeats = head_width // LANES
    dkey_low = (
        dkey * jnp.concatenate([cosine] * repeats, axis=1)
        - turned_key * jnp.concatenate([sine] * repeats, axis=1)
    ).astype(BF16)

    attn_blocks = [
        jnp.concatenate(terms, axis=1)
        for terms in zip(
            row_grads(first, dquery_low, dp_count),
            row_grads(first, dkey_low, dp_count),
            row_grads(first, dvalue_low, dp_count),
            row_grads(dmiddle_low, mixed, dp_count),
        )
    ]
    attn_grads = scatter_rows(attn_blocks)

    dfirst_part = (
        matmul_back(dquery_low, q_pieces)
        + matmul_back(dkey_low, k_pieces)
        + matmul_back(dvalue_low, v_pieces)
    )
    dfirst = scatter_over_tp(dfirst_part.astype(BF16), shift).astype(F32)
    norm_share = own_share(first_norm)
    gain_one_grad = jnp.sum(dfirst * norm_share, axis=0)
    scaled_one = dfirst * own_share(gain_one)
    inner = jnp.sum(scaled_one * norm_share, axis=-1).reshape(1, rows)
    mask = 1
    while mask < tp_count:
        inner = inner + swap(inner, "tp", mask)
        mask *= 2
    inner = inner.reshape(rows, 1) / width
    in_grad = (own_share(dmiddle) + first_scale * (scaled_one - norm_share * inner)).astype(BF16)

    gains = jnp.stack([gain_one_grad, own_share(gain_two_grad)])
    gains = lax.dynamic_update_slice_in_dim(
        jnp.zeros((2, width), F32), gains, tp_index * share, 1
    )
    gains = sum_everywhere(gains)
    part = width // (dp_count * ctx_count)
    gains = lax.dynamic_slice_in_dim(gains, (dp_index * ctx_count + ctx_index) * part, part, 1)

    attn_grads = attn_grads.astype(F32)
    ffn_out = [
        jnp.concatenate([g[:, i * chunk : (i + 1) * chunk].astype(F32) for g in ffn_grads], axis=1)
        for i in range(3)
    ]
    return (
        block_out,
        in_grad,
        gains[0],
        attn_grads[:, :head_width],
        attn_grads[:, head_width : 2 * head_width],
        attn_grads[:, 2 * head_width : 3 * head_width],
        attn_grads[:, 3 * head_width :],
        gains[1],
        ffn_out[0],
        ffn_out[1],
        ffn_out[2],
    )


def solution(mesh):
    split = P(("dp", "ctx"), "tp")
    rows = P(("dp", "ctx"), None)
    vector = P(("dp", "ctx"))
    return jax.shard_map(
        body,
        mesh=mesh,
        in_specs=(rows, P(), split, split, split, split, P(), split, split, split)
        + (P("dp", None), P("dp", None), rows),
        out_specs=(split, split, vector, split, split, split, split, vector, split, split, split),
        check_vma=False,
    )
```

time: 1880 us -> 1200 us (0.64)
  waiting for transfers between devices: 1320 us -> 630 us
  matrix products: 378 us -> 198 us
  Pallas kernels: 0 us -> 82.9 us
  starting transfers between devices: 1.39 us -> 56.8 us
  other arithmetic: 93.9 us -> 145 us
  local copies, waits for them, and re-layouts: 37.1 us -> 62.7 us
  blocking collectives: 19.3 us -> 0 us
    reduce_scatter x4 -> x5, waiting for transfers between devices: 547 us -> 0.03 us  [scatter_rows(): return lax.psum_scatter(total, 'ctx', scatter_dimension=0, tiled=True)]
    ppermute x0 -> x38, waiting for transfers between devices: none -> 415 us  [the longest x8 271 us: send(): lax.ppermute(values, axis, [(i, (i + shift) % count) for i in range(count)])]
    all_gather x9 -> x8, waiting for transfers between devices: 587 us -> 212 us  [gather_rows(): own = lax.all_gather(weight, 'ctx', axis=0, tiled=True)]
    psum x3 -> x0, waiting for transfers between devices: 187 us -> none  [the longest x1 67 us: body(): dsecond = lax.psum(add_part.astype(jnp.bfloat16), 'tp').astype(jnp.float32)]
    dot_general x45 -> x90, matrix products: 378 us -> 198 us  [the longest x32 99.9 us: matmul_back(): jnp.einsum('qf,df->qd', left, p, preferred_element_type=F32)]
    pallas_call x0 -> x5, Pallas kernels: none -> 82.9 us  [the longest x1 43.7 us: attention_backward(): pl.pallas_call(functools.partial(backward_kernel, pieces), grid_spec=pltp...]
    convert_element_type x8 -> x23, other arithmetic: 11.9 us -> 90.5 us  [the longest x5 19.8 us: scatter_rows(): total = total.astype(BF16)]
    ppermute x0 -> x38, starting transfers between devices: none -> 55.5 us  [the longest x19 32.5 us: swap(): return lax.ppermute(values, axis, [(i, i ^ mask) for i in range(count)])]
  transfers between devices with their start and end apart: 16 -> 51, of which waited for: 13 -> 23; matrix products, arithmetic and copies ran while one was open for 19% -> 32% of each run, Pallas kernels for 0% -> 7%
where the time goes in v1:
time: 1200 us; the launch traced here: 1190 us
  waiting for transfers between devices  630 us (52%)
  matrix products  198 us (16%)
  other arithmetic  145 us (12%)
  Pallas kernels  82.9 us (7%)
  local copies, waits for them, and re-layouts  62.7 us (5%)
  starting transfers between devices  56.8 us (5%)
  between operations  16.4 us (1%)
    ppermute x8, waiting for transfers between devices, send(): lax.ppermute(values, axis, [(i, (i + shift) % count) for i in range(count)])  271 us
    all_gather x8, waiting for transfers between devices, gather_rows(): own = lax.all_gather(weight, 'ctx', axis=0, tiled=True)  212 us
    dot_general x32, matrix products, matmul_back(): jnp.einsum('qf,df->qd', left, p, preferred_element_type=F32)  99.9 us
    ppermute x19, waiting for transfers between devices, swap(): return lax.ppermute(values, axis, [(i, i ^ mask) for i in range(count)])  91.7 us
    dot_general x26, matrix products, matmul_pieces(): jnp.dot(left[:, s * depth:(s + 1) * depth], piece, preferred_element_type...  59.1 us
    ppermute x11, waiting for transfers between devices, fetch(): lax.ppermute(values, axis, [(i, (i - shift) % count) for i in range(count)])  51.8 us
    pallas_call x1, Pallas kernels, attention_backward(): pl.pallas_call(functools.partial(backward_kernel, pieces), grid_spec=pltp...  43.7 us
    dot_general x32, matrix products, row_grads(): jnp.einsum('tc,tf->cf', left[:, s * depth:(s + 1) * depth], right, prefer...  39.3 us
  transfers between devices with their start and end apart: 51, of which 23 were waited for; matrix products, arithmetic and copies ran while one was open for 32% of the time, Pallas kernels for 7%

profile of v1, /device:TPU:1, one launch (start us, length us, event | category | flops | bytes accessed | tf_op | source)
XLA Modules:
  0.0 1192.0 jit_solution(2749931047895533748)
XLA Ops:
  26.5 13.0 %all-gather.13.cloned.1.call-done.refs_0_ = bf16[1024,512]{1,0:T(8,128)(2,1)} async-done(((bf16[256,512]{1,0:T(8,128)(2,1)}), bf16[1024,512]{1,0:T(8,128)(2,1)}) %all-gather.13.cloned.1.call-update) | async-done | bytes 1048592 | tf_op jit(solution)/shard_map/all_gather | solution.py:90
  44.5 24.1 %all-gather.11.cloned.1.call-done.refs_0_ = bf16[1024,512]{1,0:T(8,128)(2,1)} async-done(((bf16[256,512]{1,0:T(8,128)(2,1)}), bf16[1024,512]{1,0:T(8,128)(2,1)}) %all-gather.11.cloned.1.call-update) | async-done | bytes 1048592 | tf_op jit(solution)/shard_map/all_gather | solution.py:90
  72.3 4.5 convert_multiply_fusion
  76.8 20.7 %all-gather.9.cloned.1.call-done.refs_0_ = bf16[1024,512]{1,0:T(8,128)(2,1)} async-done(((bf16[256,512]{1,0:T(8,128)(2,1)}), bf16[1024,512]{1,0:T(8,128)(2,1)}) %all-gather.9.cloned.1.call-update) | async-done | bytes 1048592 | tf_op jit(solution)/shard_map/all_gather | solution.py:90
  98.8 5.5 project.5.vs_ref
  105.3 6.2 project.4.ks_ref
  120.3 11.0 all-gather.15.cloned.1.call-done
  133.7 6.1 project.3.q_ref
  139.8 47.3 %collective-permute-done.4.refs_2_.refs_6_ = bf16[256,1024]{1,0:T(8,128)(2,1)} collective-permute-done((bf16[256,1024]{1,0:T(8,128)(2,1)}, bf16[256,1024]{1,0:T(8,128)(2,1)}, u32[]{:S(2)}, u32[]{:S(2)}) %collective-permute-start.4) | collective-permute-done | bytes 524320 | tf_op jit(solution)/shard_map/ppermute | solution.py:30
  187.1 21.3 %attend.1 = (bf16[768,512]{1,0:T(8,128)(2,1)}, f32[768,512]{1,0:T(8,128)}) custom-call(s32[3]{0:T(128)} %pad_add_fusion.order_ref, s32[4]{0:T(128)} %dynamic_slice.84.rank_ref, bf16[768,512]{1,0:T(8,128)(2,1)} %project.3.q_ref, bf16[768,512]{1,0:T(8,128)(2,1)} %project.4.ks_ref, bf16[768,512]{1,0:T(8,128)(2,1)} %project.5.vs_ref, ...), custom_call_target="tpu_custom_call" | custom-call | flops 8053063680 | bytes 6291456 | tf_op jit(solution)/shard_map/attend/pallas_call | solution.py:276
  223.9 34.7 %collective-permute-done.8 = bf16[384,2048]{1,0:T(8,128)(2,1)} collective-permute-done((bf16[384,2048]{1,0:T(8,128)(2,1)}, bf16[384,2048]{1,0:T(8,128)(2,1)}, u32[]{:S(2)}, u32[]{:S(2)}) %collective-permute-start.8) | collective-permute-done | bytes 1572896 | tf_op jit(solution)/shard_map/ppermute | solution.py:25
  268.3 18.3 %all-gather.19.cloned.1.call-done = bf16[1024,1536]{1,0:T(8,128)(2,1)} async-done(((bf16[256,1536]{1,0:T(8,128)(2,1)}), bf16[1024,1536]{1,0:T(8,128)(2,1)}) %all-gather.19.cloned.1.call-update) | async-done | bytes 3145744 | tf_op jit(solution)/shard_map/all_gather | solution.py:90
  287.8 62.6 %all-gather.21.cloned.1.call-done = bf16[1024,1536]{1,0:T(8,128)(2,1)} async-done(((bf16[256,1536]{1,0:T(8,128)(2,1)}), bf16[1024,1536]{1,0:T(8,128)(2,1)}) %all-gather.21.cloned.1.call-update) | async-done | bytes 3145744 | tf_op jit(solution)/shard_map/all_gather | solution.py:90
  351.5 62.6 %all-gather.23.cloned.1.call-done = bf16[1024,1536]{1,0:T(8,128)(2,1)} async-done(((bf16[256,1536]{1,0:T(8,128)(2,1)}), bf16[1024,1536]{1,0:T(8,128)(2,1)}) %all-gather.23.cloned.1.call-update) | async-done | bytes 3145744 | tf_op jit(solution)/shard_map/all_gather | solution.py:90
  467.5 4.4 collective-permute-done.12
  476.3 130.4 %collective-permute-done.34 = bf16[1024,1536]{0,1:T(8,128)(2,1)S(1)} collective-permute-done((bf16[1024,1536]{0,1:T(8,128)(2,1)S(1)}, bf16[1024,1536]{0,1:T(8,128)(2,1)S(1)}, u32[]{:S(2)}, u32[]{:S(2)}) %collective-permute-start.34) | collective-permute-done | bytes 3145760 | tf_op jit(solution)/shard_map/ppermute | solution.py:35
  644.3 29.9 %collective-permute-done.35 = bf16[1024,1536]{0,1:T(8,128)(2,1)} collective-permute-done((bf16[1024,1536]{0,1:T(8,128)(2,1)}, bf16[1024,1536]{0,1:T(8,128)(2,1)}, u32[]{:S(2)}, u32[]{:S(2)}) %collective-permute-start.35) | collective-permute-done | bytes 3145760 | tf_op jit(solution)/shard_map/ppermute | solution.py:35
  680.1 5.1 multiply_convert_fusion.2
  745.7 18.6 %fusion.13 = bf16[768,2048]{1,0:T(8,128)(2,1)} fusion(f32[768,1024]{1,0:T(8,128)} %fusion.152, f32[768,1024]{1,0:T(8,128)} %fusion.156, f32[768,1024]{1,0:T(8,128)} %fusion.141, f32[768,1024]{1,0:T(8,128)} %fusion.145, f32[768,1024]{1,0:T(8,128)} %fusion.123, f32[768,1024]{1,0:T(8,128)} %fusion.127, f32[768,1024]{1,0:T(8,128)} %fusion.112, ...), kind=kLoop, calls=%fused_computation.25 | loop fusion | flops 25165824 | bytes 53477376 | tf_op jit(solution)/shard_map/convert_element_type | solution.py:480
  783.9 27.1 %collective-permute-done.18 = bf16[384,2048]{1,0:T(8,128)(2,1)} collective-permute-done((bf16[384,2048]{1,0:T(8,128)(2,1)S(1)}, bf16[384,2048]{1,0:T(8,128)(2,1)}, u32[]{:S(2)}, u32[]{:S(2)}) %collective-permute-start.18) | collective-permute-done | bytes 1572896 | tf_op jit(solution)/shard_map/ppermute | solution.py:25
  820.0 23.4 %collective-permute-done.37 = bf16[1024,1536]{0,1:T(8,128)(2,1)} collective-permute-done((bf16[1024,1536]{0,1:T(8,128)(2,1)}, bf16[1024,1536]{0,1:T(8,128)(2,1)}, u32[]{:S(2)}, u32[]{:S(2)}) %collective-permute-start.37) | collective-permute-done | bytes 3145760 | tf_op jit(solution)/shard_map/ppermute | solution.py:35
  851.2 4.4 fusion.5
  855.7 9.6 fusion.225
  869.1 43.7 %attend_back.1 = (bf16[768,512]{1,0:T(8,128)(2,1)}, f32[768,512]{1,0:T(8,128)}, f32[768,512]{1,0:T(8,128)}, f32[1024,512]{1,0:T(8,128)}, f32[1024,512]{1,0:T(8,128)}) custom-call(s32[3]{0:T(128)} %pad_add_fusion.order_ref, s32[4]{0:T(128)} %dynamic_slice.84.rank_ref, bf16[768,512]{1,0:T(8,128)(2,1)} %project.3.q_ref, bf16[768,512]{1,0:T(8,128)(2,1)} %project.4.ks_ref, ...), custom_call_target="tpu_custom_call" | custom-call | flops 20132659200 | bytes 12582912 | tf_op jit(solution)/shard_map/attend_back/pallas_call | solution.py:298
  923.5 6.1 collective-permute-done.20
  929.7 22.6 %collective-permute-done.21 = bf16[256,1024]{1,0:T(8,128)(2,1)S(1)} collective-permute-done((bf16[256,1024]{1,0:T(8,128)(2,1)S(1)}, bf16[256,1024]{1,0:T(8,128)(2,1)S(1)}, u32[]{:S(2)}, u32[]{:S(2)}) %collective-permute-start.21) | collective-permute-done | bytes 524320 | tf_op jit(solution)/shard_map/ppermute | solution.py:35
  1007.1 55.3 %collective-permute-done.33 = bf16[1024,2048]{0,1:T(8,128)(2,1)} collective-permute-done((bf16[1024,2048]{0,1:T(8,128)(2,1)}, bf16[1024,2048]{0,1:T(8,128)(2,1)}, u32[]{:S(2)}, u32[]{:S(2)}) %collective-permute-start.33) | collective-permute-done | bytes 4194336 | tf_op jit(solution)/shard_map/ppermute | solution.py:35
  1062.4 5.0 add_convert_fusion
  1092.6 6.8 fusion.9
  1110.4 13.5 %collective-permute-done.25 = bf16[768,512]{1,0:T(8,128)(2,1)} collective-permute-done((bf16[768,512]{1,0:T(8,128)(2,1)}, bf16[768,512]{1,0:T(8,128)(2,1)}, u32[]{:S(2)}, u32[]{:S(2)}) %collective-permute-start.25) | collective-permute-done | bytes 786464 | tf_op jit(solution)/shard_map/ppermute | solution.py:25
  1132.3 8.8 collective-permute-done.29
  1141.1 11.8 collective-permute-start.30
  (514 shorter events, 411.3 us)
Async XLA Ops:
  7.9 60.6 %all-gather.11.cloned.1.call-start = ((), (), s32[]{:S(2)}) async-start(), calls=%async_computation.6 | async-start | bytes 1310720 | tf_op jit(solution)/shard_map/all_gather | solution.py:90
  8.7 88.9 %all-gather.9.cloned.1.call-start = ((), (), s32[]{:S(2)}) async-start(), calls=%async_computation.5 | async-start | bytes 1310720 | tf_op jit(solution)/shard_map/all_gather | solution.py:90
  9.4 121.9 %all-gather.15.cloned.1.call-start = ((), (), s32[]{:S(2)}) async-start(), calls=%async_computation.8 | async-start | bytes 1310720 | tf_op jit(solution)/shard_map/all_gather | solution.py:90
  10.0 257.1 %all-gather.17.cloned.1.call-start = ((), (), s32[]{:S(2)}) async-start(), calls=%async_computation.9 | async-start | bytes 3932160 | tf_op jit(solution)/shard_map/all_gather | solution.py:90
  13.7 272.9 %all-gather.19.cloned.1.call-start = ((), (), s32[]{:S(2)}) async-start(), calls=%async_computation.10 | async-start | bytes 3932160 | tf_op jit(solution)/shard_map/all_gather | solution.py:90
  14.7 335.7 %all-gather.21.cloned.1.call-start = ((), (), s32[]{:S(2)}) async-start(), calls=%async_computation.11 | async-start | bytes 3932160 | tf_op jit(solution)/shard_map/all_gather | solution.py:90
  15.7 398.4 %all-gather.23.cloned.1.call-start = ((), (), s32[]{:S(2)}) async-start(), calls=%async_computation.12 | async-start | bytes 3932160 | tf_op jit(solution)/shard_map/all_gather | solution.py:90
  16.7 1148.1 %reduce-scatter.8.cloned.1.call-start = ((), (), s32[]{:S(2)}) async-start(), calls=%async_computation.14 | async-start | bytes 3932160 | tf_op jit(solution)/shard_map/reduce_scatter | solution.py:102
  39.5 59.3 %collective-permute-start.2 = (bf16[1024,512]{1,0:T(8,128)(2,1)}, bf16[1024,512]{1,0:T(8,128)(2,1)}, u32[]{:S(2)}, u32[]{:S(2)}) collective-permute-start(bf16[1024,512]{1,0:T(8,128)(2,1)} %all-gather.13.cloned.1.call-done.refs_0_), channel_id=1, source_target_pairs={{0,16},{16,0},{1,17},{17,1},{2,18},{18,2},{3,19},{19,3},{4,20},{20... | collective-permute-start | bytes 3145736 | tf_op jit(solution)/shard_map/ppermute | solution.py:30
  68.5 36.7 %collective-permute-start.1 = (bf16[1024,512]{1,0:T(8,128)(2,1)}, bf16[1024,512]{1,0:T(8,128)(2,1)}, u32[]{:S(2)}, u32[]{:S(2)}) collective-permute-start(bf16[1024,512]{1,0:T(8,128)(2,1)} %all-gather.11.cloned.1.call-done.refs_0_), channel_id=1, source_target_pairs={{0,16},{16,0},{1,17},{17,1},{2,18},{18,2},{3,19},{19,3},{4,20},{20... | collective-permute-start | bytes 3145736 | tf_op jit(solution)/shard_map/ppermute | solution.py:30
  97.6 36.1 %collective-permute-start = (bf16[1024,512]{1,0:T(8,128)(2,1)}, bf16[1024,512]{1,0:T(8,128)(2,1)}, u32[]{:S(2)}, u32[]{:S(2)}) collective-permute-start(bf16[1024,512]{1,0:T(8,128)(2,1)} %all-gather.9.cloned.1.call-done.refs_0_), channel_id=1, source_target_pairs={{0,16},{16,0},{1,17},{17,1},{2,18},{18,2},{3,19},{19,3},{4,20},{20... | collective-permute-start | bytes 3145736 | tf_op jit(solution)/shard_map/ppermute | solution.py:30
  115.2 71.9 %collective-permute-start.4 = (bf16[256,1024]{1,0:T(8,128)(2,1)}, bf16[256,1024]{1,0:T(8,128)(2,1)}, u32[]{:S(2)}, u32[]{:S(2)}) collective-permute-start(bf16[256,1024]{1,0:T(8,128)(2,1)} %pad_maximum_fusion.11.refs_0_.refs_4_), channel_id=1, source_target_pairs={{0,8},{4,12},{8,0},{12,4},{1,9},{5,13},{9,1},{13,5},{2,10},{6,14},... | collective-permute-start | bytes 1572872 | tf_op jit(solution)/shard_map/ppermute | solution.py:30
  115.6 71.5 %collective-permute-start.5 = (bf16[256,1024]{1,0:T(8,128)(2,1)}, bf16[256,1024]{1,0:T(8,128)(2,1)}, u32[]{:S(2)}, u32[]{:S(2)}) collective-permute-start(bf16[256,1024]{1,0:T(8,128)(2,1)} %pad_maximum_fusion.11.refs_0_.refs_4_), channel_id=1, source_target_pairs={{0,4},{4,8},{8,12},{12,0},{1,5},{5,9},{9,13},{13,1},{2,6},{6,10},{... | collective-permute-start | bytes 1572872 | tf_op jit(solution)/shard_map/ppermute | solution.py:30
  131.3 79.4 %collective-permute-start.6 = (bf16[1024,512]{1,0:T(8,128)(2,1)}, bf16[1024,512]{1,0:T(8,128)(2,1)S(1)}, u32[]{:S(2)}, u32[]{:S(2)}) collective-permute-start(bf16[1024,512]{1,0:T(8,128)(2,1)} %all-gather.15.cloned.1.call-done), channel_id=1, source_target_pairs={{0,16},{16,0},{1,17},{17,1},{2,18},{18,2},{3,19},{19,3},{4,20},{20... | collective-permute-start | bytes 3145736 | tf_op jit(solution)/shard_map/ppermute | solution.py:30
  262.3 163.8 %collective-permute-start.9 = (bf16[384,2048]{1,0:T(8,128)(2,1)}, bf16[384,2048]{1,0:T(8,128)(2,1)}, u32[]{:S(2)}, u32[]{:S(2)}) collective-permute-start(bf16[384,2048]{1,0:T(8,128)(2,1)} %add_convert_fusion.7), channel_id=1, source_target_pairs={{0,1},{1,0},{2,3},{3,2},{4,5},{5,4},{6,7},{7,6},{8,9},{9,8},{10,11... | collective-permute-start | bytes 4718600 | tf_op jit(solution)/shard_map/ppermute | solution.py:25
  267.1 167.2 %collective-permute-start.10 = (bf16[1024,1536]{1,0:T(8,128)(2,1)}, bf16[1024,1536]{1,0:T(8,128)(2,1)}, u32[]{:S(2)}, u32[]{:S(2)}) collective-permute-start(bf16[1024,1536]{1,0:T(8,128)(2,1)} %all-gather.17.cloned.1.call-done), channel_id=1, source_target_pairs={{0,16},{16,0},{1,17},{17,1},{2,18},{18,2},{3,19},{19,3},{4,20},{20... | collective-permute-start | bytes 9437192 | tf_op jit(solution)/shard_map/ppermute | solution.py:30
  286.6 162.2 %collective-permute-start.11 = (bf16[1024,1536]{1,0:T(8,128)(2,1)}, bf16[1024,1536]{1,0:T(8,128)(2,1)}, u32[]{:S(2)}, u32[]{:S(2)}) collective-permute-start(bf16[1024,1536]{1,0:T(8,128)(2,1)} %all-gather.19.cloned.1.call-done), channel_id=1, source_target_pairs={{0,16},{16,0},{1,17},{17,1},{2,18},{18,2},{3,19},{19,3},{4,20},{20... | collective-permute-start | bytes 9437192 | tf_op jit(solution)/shard_map/ppermute | solution.py:30
  350.4 121.6 %collective-permute-start.12 = (bf16[1024,1536]{1,0:T(8,128)(2,1)}, bf16[1024,1536]{1,0:T(8,128)(2,1)}, u32[]{:S(2)}, u32[]{:S(2)}) collective-permute-start(bf16[1024,1536]{1,0:T(8,128)(2,1)} %all-gather.21.cloned.1.call-done), channel_id=1, source_target_pairs={{0,16},{16,0},{1,17},{17,1},{2,18},{18,2},{3,19},{19,3},{4,20},{20... | collective-permute-start | bytes 9437192 | tf_op jit(solution)/shard_map/ppermute | solution.py:30
  414.1 221.4 %collective-permute-start.13 = (bf16[1024,1536]{1,0:T(8,128)(2,1)}, bf16[1024,1536]{1,0:T(8,128)(2,1)}, u32[]{:S(2)}, u32[]{:S(2)}) collective-permute-start(bf16[1024,1536]{1,0:T(8,128)(2,1)} %all-gather.23.cloned.1.call-done), channel_id=1, source_target_pairs={{0,16},{16,0},{1,17},{17,1},{2,18},{18,2},{3,19},{19,3},{4,20},{20... | collective-permute-start | bytes 9437192 | tf_op jit(solution)/shard_map/ppermute | solution.py:30
  448.4 158.2 %collective-permute-start.34 = (bf16[1024,1536]{0,1:T(8,128)(2,1)S(1)}, bf16[1024,1536]{0,1:T(8,128)(2,1)S(1)}, u32[]{:S(2)}, u32[]{:S(2)}) collective-permute-start(bf16[1024,1536]{0,1:T(8,128)(2,1)S(1)} %pad_maximum_fusion.3), channel_id=1, source_target_pairs={{0,16},{16,0},{1,17},{17,1},{2,18},{18,2},{3,19},{19,3},{4,20},{20... | collective-permute-start | bytes 9437192 | tf_op jit(solution)/shard_map/ppermute | solution.py:35
  463.2 211.0 %collective-permute-start.35 = (bf16[1024,1536]{0,1:T(8,128)(2,1)}, bf16[1024,1536]{0,1:T(8,128)(2,1)}, u32[]{:S(2)}, u32[]{:S(2)}) collective-permute-start(bf16[1024,1536]{0,1:T(8,128)(2,1)} %pad_maximum_fusion.4), channel_id=1, source_target_pairs={{0,16},{16,0},{1,17},{17,1},{2,18},{18,2},{3,19},{19,3},{4,20},{20... | collective-permute-start | bytes 9437192 | tf_op jit(solution)/shard_map/ppermute | solution.py:35
  609.6 556.4 %reduce-scatter.10.cloned.1.call-start = ((), (), s32[]{:S(2)}) async-start(), calls=%async_computation.15 | async-start | bytes 3932160 | tf_op jit(solution)/shard_map/reduce_scatter | solution.py:102
  624.9 116.7 %collective-permute-start.36 = (bf16[1024,1536]{0,1:T(8,128)(2,1)}, bf16[1024,1536]{0,1:T(8,128)(2,1)}, u32[]{:S(2)}, u32[]{:S(2)}) collective-permute-start(bf16[1024,1536]{0,1:T(8,128)(2,1)} %pad_maximum_fusion.5), channel_id=1, source_target_pairs={{0,16},{16,0},{1,17},{17,1},{2,18},{18,2},{3,19},{19,3},{4,20},{20... | collective-permute-start | bytes 9437192 | tf_op jit(solution)/shard_map/ppermute | solution.py:35
  678.2 489.7 %reduce-scatter.12.cloned.1.call-start = ((), (), s32[]{:S(2)}) async-start(), calls=%async_computation.16 | async-start | bytes 3932160 | tf_op jit(solution)/shard_map/reduce_scatter | solution.py:102
  745.6 424.3 %reduce-scatter.14.cloned.1.call-start = ((), (), s32[]{:S(2)}) async-start(), calls=%async_computation.17 | async-start | bytes 3932160 | tf_op jit(solution)/shard_map/reduce_scatter | solution.py:102
  774.1 69.3 %collective-permute-start.37 = (bf16[1024,1536]{0,1:T(8,128)(2,1)}, bf16[1024,1536]{0,1:T(8,128)(2,1)}, u32[]{:S(2)}, u32[]{:S(2)}) collective-permute-start(bf16[1024,1536]{0,1:T(8,128)(2,1)} %pad_maximum_fusion.6), channel_id=1, source_target_pairs={{0,16},{16,0},{1,17},{17,1},{2,18},{18,2},{3,19},{19,3},{4,20},{20... | collective-permute-start | bytes 9437192 | tf_op jit(solution)/shard_map/ppermute | solution.py:35
  847.4 332.5 %reduce-scatter.6.cloned.1.call-start = ((), (), s32[]{:S(2)}) async-start(), calls=%async_computation.13 | async-start | bytes 5242880 | tf_op jit(solution)/shard_map/reduce_scatter | solution.py:102
  915.8 36.4 %collective-permute-start.21 = (bf16[256,1024]{1,0:T(8,128)(2,1)S(1)}, bf16[256,1024]{1,0:T(8,128)(2,1)S(1)}, u32[]{:S(2)}, u32[]{:S(2)}) collective-permute-start(bf16[256,1024]{1,0:T(8,128)(2,1)S(1)} %get-tuple-element.99), channel_id=1, source_target_pairs={{0,8},{4,12},{8,0},{12,4},{1,9},{5,13},{9,1},{13,5},{2,10},{6,14},... | collective-permute-start | bytes 1572872 | tf_op jit(solution)/shard_map/ppermute | solution.py:35
  915.9 36.3 %collective-permute-start.22 = (bf16[256,1024]{1,0:T(8,128)(2,1)S(1)}, bf16[256,1024]{1,0:T(8,128)(2,1)S(1)}, u32[]{:S(2)}, u32[]{:S(2)}) collective-permute-start(bf16[256,1024]{1,0:T(8,128)(2,1)S(1)} %get-tuple-element.98), channel_id=1, source_target_pairs={{0,12},{4,0},{8,4},{12,8},{1,13},{5,1},{9,5},{13,9},{2,14},{6,2},{... | collective-permute-start | bytes 1572872 | tf_op jit(solution)/shard_map/ppermute | solution.py:35
  972.3 90.0 %collective-permute-start.33 = (bf16[1024,2048]{0,1:T(8,128)(2,1)}, bf16[1024,2048]{0,1:T(8,128)(2,1)}, u32[]{:S(2)}, u32[]{:S(2)}) collective-permute-start(bf16[1024,2048]{0,1:T(8,128)(2,1)} %pad_maximum_fusion), channel_id=1, source_target_pairs={{0,16},{16,0},{1,17},{17,1},{2,18},{18,2},{3,19},{19,3},{4,20},{20... | collective-permute-start | bytes 12582920 | tf_op jit(solution)/shard_map/ppermute | solution.py:35
  1106.2 46.8 %collective-permute-start.14 = (bf16[768,512]{1,0:T(8,128)(2,1)}, bf16[768,512]{1,0:T(8,128)(2,1)}, u32[]{:S(2)}, u32[]{:S(2)}) collective-permute-start(bf16[768,512]{1,0:T(8,128)(2,1)} %get-tuple-element.93), channel_id=1, source_target_pairs={{0,1},{1,0},{2,3},{3,2},{4,5},{5,4},{6,7},{7,6},{8,9},{9,8},{10,11... | collective-permute-start | bytes 2359304 | tf_op jit(solution)/shard_map/ppermute | solution.py:25
  1109.3 43.7 %collective-permute-start.16 = (bf16[768,512]{1,0:T(8,128)(2,1)}, bf16[768,512]{1,0:T(8,128)(2,1)}, u32[]{:S(2)}, u32[]{:S(2)}) collective-permute-start(bf16[768,512]{1,0:T(8,128)(2,1)} %add_convert_fusion.15), channel_id=1, source_target_pairs={{0,2},{1,3},{2,0},{3,1},{4,6},{5,7},{6,4},{7,5},{8,10},{9,11},{10,... | collective-permute-start | bytes 2359304 | tf_op jit(solution)/shard_map/ppermute | solution.py:25
  (131 other events, 1889.7 us)
Sparse Core Ops, SparseCore 0:
  9.6 29.8 all-gather.12
  41.1 27.4 all-gather.10
  70.1 27.4 all-gather.8
  99.0 32.2 all-gather.14
  132.7 90.6 all-gather.16
  224.8 61.7 all-gather.18
  288.2 62.1 all-gather.20
  351.9 62.1 all-gather.22
  609.7 58.7 reduce-scatter.7
  678.3 58.7 reduce-scatter.9
  745.7 58.3 reduce-scatter.11
  847.5 59.0 reduce-scatter.13
  1067.5 88.7 reduce-scatter.5

commit v2 on v1

--- a/solution.py
+++ b/solution.py
@@ -14,7 +14,7 @@
 EPS = 1e-05
 ROPE_BASE = 130000.0
 MASKED = -1e30
-FFN_CHUNKS = 4
+FFN_CHUNKS = 2
 BF16 = jnp.bfloat16
 F32 = jnp.float32
 VMEM_LIMIT = 56 * 1024 * 1024
@@ -35,71 +35,24 @@
     return lax.ppermute(values, axis, [(i, (i + shift) % count) for i in range(count)])
 
 
-def add_low(left, right):
-    return (left.astype(F32) + right.astype(F32)).astype(BF16)
-
-
-def sum_over_tp(part):
-    count = lax.axis_size("tp")
-    rows = part.shape[0]
-    half = rows // 2
-    bit = lax.axis_index("tp") & 1
-    keep = lax.dynamic_slice_in_dim(part, bit * half, half)
-    give = lax.dynamic_slice_in_dim(part, (1 - bit) * half, half)
-    total = add_low(keep, swap(give, "tp", 1))
-    mask = 2
-    while mask < count:
-        total = add_low(total, swap(total, "tp", mask))
-        mask *= 2
-    back = swap(total, "tp", 1)
-    first = jnp.where(bit == 0, total, back)
-    last = jnp.where(bit == 0, back, total)
-    return jnp.concatenate([first, last], axis=0)
-
-
-def scatter_over_tp(part, shift):
-    count = lax.axis_size("tp")
-    width = part.shape[1] // count
-    me = lax.axis_index("tp")
-
-    def block(owner):
-        start = lax.rem(owner * width - shift + part.shape[1], part.shape[1])
-        return lax.dynamic_slice_in_dim(part, start, width, 1)
-
-    held = {other: None for other in range(0, count, 2)}
-    for other in held:
-        held[other] = add_low(block(me ^ other), swap(block(me ^ other ^ 1), "tp", 1))
-    mask = count // 2
-    while mask >= 2:
-        for other in [o for o in held if o & mask]:
-            held[other ^ mask] = add_low(held[other ^ mask], swap(held.pop(other), "tp", mask))
-        mask //= 2
-    return held[0]
-
-
-def sum_everywhere(values):
-    for axis in ("tp", "ctx", "dp"):
-        mask = 1
-        while mask < lax.axis_size(axis):
-            values = values + swap(values, axis, mask)
-            mask *= 2
-    return values
-
-
-def gather_rows(weight):
-    own = lax.all_gather(weight, "ctx", axis=0, tiled=True)
+def add(left, right):
+    return left.astype(F32) + right.astype(F32)
+
+
+def low(values):
+    return values.astype(BF16)
+
+
+def gather_dp(own):
     return [own] + [fetch(own, "dp", s) for s in range(1, lax.axis_size("dp"))]
 
 
-def scatter_rows(blocks):
+def scatter_dp(blocks):
     total = blocks[0]
     extra = [send(block, "dp", s) for s, block in enumerate(blocks) if s]
-    if extra:
-        total = total.astype(F32)
-        for term in extra:
-            total = total + term.astype(F32)
-        total = total.astype(BF16)
-    return lax.psum_scatter(total, "ctx", scatter_dimension=0, tiled=True)
+    for term in extra:
+        total = add(total, term)
+    return low(total)
 
 
 def dot(left, right, dims):
@@ -201,8 +154,10 @@
     pieces, order_ref, rank_ref, q_ref, ks_ref, vs_ref, o_ref, lse_ref, do_ref, cos_ref, sin_ref, *refs
 ):
     kp_refs, vp_refs = refs[:pieces], refs[pieces : 2 * pieces]
-    dq_ref, dks_ref, dvs_ref, dkp_ref, dvp_ref = refs[2 * pieces :]
-    step = pl.program_id(1)
+    dq_ref, dks_ref, dvs_ref = refs[2 * pieces : 2 * pieces + 3]
+    piece_refs = refs[2 * pieces + 3 : 3 * pieces + 3]
+    acc_ref = refs[-1]
+    pair, step = pl.program_id(0), pl.program_id(1)
     prompt = step == 0
     q, do = q_ref[...], do_ref[...]
     size = q.shape[0]
@@ -246,17 +201,163 @@
     dks_ref[...] = dk_all[0] * SCALE
     dvs_ref[...] = dv_all[0]
     for s in range(pieces):
+        both = jnp.concatenate([dk_all[s + 1] * SCALE, dv_all[s + 1]], axis=1)
         at = slice(s * size, (s + 1) * size)
 
         @pl.when(prompt)
-        def _():
-            dkp_ref[at, :] = dk_all[s + 1] * SCALE
-            dvp_ref[at, :] = dv_all[s + 1]
+        def _(both=both, at=at):
+            acc_ref[at, :] = both
 
         @pl.when(jnp.logical_not(prompt))
-        def _():
-            dkp_ref[at, :] += dk_all[s + 1] * SCALE
-            dvp_ref[at, :] += dv_all[s + 1]
+        def _(both=both, at=at):
+            acc_ref[at, :] += both
+
+    @pl.when(step == pl.num_programs(1) - 1)
+    def _():
+        wide = piece_refs[0].shape[1] // 2
+        k_at = pl.ds(pl.multiple_of(pair * LANES, LANES), LANES)
+        v_at = pl.ds(pl.multiple_of(wide + pair * LANES, LANES), LANES)
+        for s in range(pieces):
+            both = acc_ref[s * size : (s + 1) * size, :]
+            piece_refs[s][:, k_at] = both[:, :LANES].astype(piece_refs[s].dtype)
+            piece_refs[s][:, v_at] = both[:, LANES:].astype(piece_refs[s].dtype)
+
+
+def merge_kernel(others, mine_ref, dk_ref, dv_ref, own_ref, *refs):
+    got = refs[:others]
+    cos_ref, sin_ref, dk_out, dv_out = refs[others:]
+    width = dk_ref.shape[1]
+    cosine, sine = cos_ref[...], sin_ref[...]
+
+    def write(dk, dv):
+        for at in range(0, width, LANES):
+            part = dk[:, at : at + LANES]
+            dk_out[:, at : at + LANES] = (part * cosine - half_swap(part) * sine).astype(BF16)
+        dv_out[...] = dv.astype(BF16)
+
+    mine = pl.program_id(0) == mine_ref[0]
+
+    @pl.when(mine)
+    def _():
+        extra = own_ref[...]
+        for ref in got:
+            extra = extra + ref[...].astype(F32)
+        write(dk_ref[...] + extra[:, :width], dv_ref[...] + extra[:, width:])
+
+    @pl.when(jnp.logical_not(mine))
+    def _():
+        write(dk_ref[...], dv_ref[...])
+
+
+def merge_keys(mine, dkey, dvalue, own, got, cosine, sine):
+    rows, width = dkey.shape
+    row = lambda i, mine: (i, 0)
+    full = lambda i, mine: (0, 0)
+    return pl.pallas_call(
+        functools.partial(merge_kernel, len(got)),
+        grid_spec=pltpu.PrefetchScalarGridSpec(
+            num_scalar_prefetch=1,
+            grid=(rows // CLEN,),
+            in_specs=[pl.BlockSpec((CLEN, width), row)] * 2
+            + [pl.BlockSpec((CLEN, 2 * width), full)] * (1 + len(got))
+            + [pl.BlockSpec((CLEN, LANES), row)] * 2,
+            out_specs=[pl.BlockSpec((CLEN, width), row)] * 2,
+        ),
+        out_shape=[jax.ShapeDtypeStruct((rows, width), BF16)] * 2,
+        compiler_params=pltpu.CompilerParams(vmem_limit_bytes=VMEM_LIMIT),
+        cost_estimate=pl.CostEstimate(flops=8 * rows * width, bytes_accessed=16 * rows * width, transcendentals=0),
+        name="merge_keys",
+    )(mine, dkey, dvalue, own, *got, cosine, sine)
+
+
+def ffn_kernel(count, second_ref, cot_ref, *refs):
+    w_refs = refs[:count]
+    hidden_ref, dgate_ref, dup_ref = refs[count:]
+    depth = w_refs[0].shape[0]
+    wide = w_refs[0].shape[1] // 3
+    step = min(wide, 256)
+    for at in range(0, wide, step):
+        gate, upward, dhidden = None, None, None
+        for p in range(count):
+            cols = slice(p * depth, (p + 1) * depth)
+            x, g = second_ref[:, cols], cot_ref[:, cols]
+            terms = (
+                dot(x, w_refs[p][:, at : at + step], NN),
+                dot(x, w_refs[p][:, wide + at : wide + at + step], NN),
+                dot(g, w_refs[p][:, 2 * wide + at : 2 * wide + at + step], NN),
+            )
+            if p == 0:
+                gate, upward, dhidden = terms
+            else:
+                gate, upward, dhidden = gate + terms[0], upward + terms[1], dhidden + terms[2]
+        sig = 1.0 / (1.0 + jnp.exp(-gate))
+        silu = gate * sig
+        hidden_ref[:, at : at + step] = (silu * upward).astype(BF16)
+        dup_ref[:, at : at + step] = (dhidden * silu).astype(BF16)
+        dgate_ref[:, at : at + step] = (dhidden * upward * (sig + silu * (1.0 - sig))).astype(BF16)
+
+
+def ffn(second, cotangent, pieces):
+    rows, width = second.shape
+    wide = pieces[0].shape[1] // 3
+    count = len(pieces)
+    row = lambda i: (i, 0)
+    full = lambda i: (0, 0)
+    tile = 256
+    return pl.pallas_call(
+        functools.partial(ffn_kernel, count),
+        grid=(rows // tile,),
+        in_specs=[pl.BlockSpec((tile, width), row)] * 2
+        + [pl.BlockSpec(p.shape, full, pipeline_mode=pl.Buffered(1)) for p in pieces],
+        out_specs=[pl.BlockSpec((tile, wide), row)] * 3,
+        out_shape=[jax.ShapeDtypeStruct((rows, wide), BF16)] * 3,
+        compiler_params=pltpu.CompilerParams(vmem_limit_bytes=VMEM_LIMIT),
+        cost_estimate=pl.CostEstimate(
+            flops=6 * rows * width * wide,
+            bytes_accessed=2 * (2 * rows * width + 3 * width * wide + 3 * rows * wide),
+            transcendentals=rows * wide,
+        ),
+        name="ffn",
+    )(second, cotangent, *pieces)
+
+
+def back_kernel(sides, count, spans, *refs):
+    left_refs = refs[:sides]
+    w_refs = refs[sides:-1]
+    out_ref = refs[-1]
+    depth = w_refs[0].shape[0]
+    for p in range(count):
+        total = None
+        for n, (chunk, start, stop) in enumerate(spans):
+            term = dot(left_refs[n][...], w_refs[chunk * count + p][:, start:stop], NT)
+            total = term if total is None else total + term
+        out_ref[:, p * depth : (p + 1) * depth] = total.astype(BF16)
+
+
+def project_back(lefts, chunks, spans):
+    rows = lefts[0].shape[0]
+    count = len(chunks[0])
+    width = count * chunks[0][0].shape[0]
+    flat = [piece for chunk in chunks for piece in chunk]
+    row = lambda i: (i, 0)
+    full = lambda i: (0, 0)
+    tile = 256
+    depth = sum(left.shape[1] for left in lefts)
+    return pl.pallas_call(
+        functools.partial(back_kernel, len(lefts), count, spans),
+        grid=(rows // tile,),
+        in_specs=[pl.BlockSpec((tile, left.shape[1]), row) for left in lefts]
+        + [pl.BlockSpec(p.shape, full, pipeline_mode=pl.Buffered(1)) for p in flat],
+        out_specs=pl.BlockSpec((tile, width), row),
+        out_shape=jax.ShapeDtypeStruct((rows, width), BF16),
+        compiler_params=pltpu.CompilerParams(vmem_limit_bytes=VMEM_LIMIT),
+        cost_estimate=pl.CostEstimate(
+            flops=2 * rows * width * depth,
+            bytes_accessed=2 * (rows * depth + width * depth + rows * width),
+            transcendentals=0,
+        ),
+        name="project_back",
+    )(*lefts, *flat)
 
 
 def attention_specs(pieces, key_pairs):
@@ -264,7 +365,7 @@
     key = pl.BlockSpec((CLEN, LANES), lambda h, j, order, rank: (0, h))
     value = pl.BlockSpec((CLEN, LANES), lambda h, j, order, rank: (0, key_pairs + h))
     trig = pl.BlockSpec((CLEN, LANES), lambda h, j, order, rank: (order[j], 0))
-    prompt = pl.BlockSpec((pieces * CLEN, LANES), lambda h, j, order, rank: (0, h))
+    prompt = pl.BlockSpec((CLEN, 2 * key_pairs * LANES), lambda h, j, order, rank: (0, 0))
     return own, key, value, trig, prompt
 
 
@@ -301,15 +402,15 @@
             num_scalar_prefetch=2,
             grid=(pairs, rows // CLEN),
             in_specs=[own] * 6 + [trig] * 2 + [key] * pieces + [value] * pieces,
-            out_specs=[own, own, own, prompt, prompt],
+            out_specs=[own, own, own] + [prompt] * pieces,
+            scratch_shapes=[pltpu.VMEM((pieces * CLEN, 2 * LANES), F32)],
         ),
         out_shape=[
             jax.ShapeDtypeStruct((rows, width), BF16),
             jax.ShapeDtypeStruct((rows, width), F32),
             jax.ShapeDtypeStruct((rows, width), F32),
-            jax.ShapeDtypeStruct((pieces * CLEN, width), F32),
-            jax.ShapeDtypeStruct((pieces * CLEN, width), F32),
-        ],
+        ]
+        + [jax.ShapeDtypeStruct((CLEN, 2 * width), BF16 if s else F32) for s in range(pieces)],
         compiler_params=pltpu.CompilerParams(vmem_limit_bytes=VMEM_LIMIT),
         cost_estimate=pl.CostEstimate(
             flops=40 * scores * HEAD_DIM, bytes_accessed=32 * rows * width, transcendentals=scores
@@ -332,15 +433,6 @@
         jnp.concatenate([cosine] * 4, axis=1),
         jnp.concatenate([-sine, sine, -sine, sine], axis=1),
     )
-
-
-def matmul_pieces(left, pieces):
-    depth = pieces[0].shape[0]
-    total = None
-    for s, piece in enumerate(pieces):
-        term = jnp.dot(left[:, s * depth : (s + 1) * depth], piece, preferred_element_type=F32)
-        total = term if total is None else total + term
-    return total
 
 
 def matmul_back(left, pieces):
@@ -376,32 +468,69 @@
 ):
     rows, width = tokens.shape
     head_width = query_weight.shape[1]
-    ffn_width = gate_weight.shape[1]
-    chunk = ffn_width // FFN_CHUNKS
+    own_rows, ffn_width = gate_weight.shape
+    half_units = ffn_width // 2
+    chunk = half_units // FFN_CHUNKS
+    half = rows // 2
     dp_count = lax.axis_size("dp")
     ctx_count = lax.axis_size("ctx")
     tp_count = lax.axis_size("tp")
     dp_index = lax.axis_index("dp")
     ctx_index = lax.axis_index("ctx")
     tp_index = lax.axis_index("tp")
+    bit = tp_index & 1
+    parity = ctx_index & 1
+    upper = (ctx_index // 2) & 1
     shift = dp_index * (width // dp_count)
 
-    def turned(values):
+    def turned(values, amount=shift):
         doubled = jnp.concatenate([values, values], axis=-1)
-        return lax.dynamic_slice_in_dim(doubled, shift, width, values.ndim - 1)
-
-    q_pieces = gather_rows(query_weight)
+        return lax.dynamic_slice_in_dim(doubled, amount, width, values.ndim - 1)
+
+    def natural(values):
+        return turned(values, width - shift)
+
+    def flip(values):
+        split = values.reshape(values.shape[:-1] + (dp_count, 2, width // dp_count // 2))
+        other = split[..., ::-1, :].reshape(values.shape)
+        return jnp.where(upper == 0, values, other)
+
+    def row_half(values):
+        return lax.dynamic_slice_in_dim(values, bit * half, half)
+
+    def assemble(mine, other):
+        first = jnp.where(bit == 0, mine, other)
+        last = jnp.where(bit == 0, other, mine)
+        return jnp.concatenate([first, last], axis=0)
+
+    def gather_rows(weight):
+        return gather_dp(lax.all_gather(weight, "ctx", axis=0, tiled=True))
+
     k_pieces = gather_rows(key_weight)
     v_pieces = gather_rows(value_weight)
+    q_pieces = gather_rows(query_weight)
     o_pieces = gather_rows(out_weight)
     ffn_pieces = []
     for f in range(FFN_CHUNKS):
-        at = slice(f * chunk, (f + 1) * chunk)
-        ffn_pieces.append(
-            gather_rows(
-                jnp.concatenate([gate_weight[:, at], up_weight[:, at], down_weight[:, at]], axis=1)
+
+        def columns(which):
+            start = which * half_units + f * chunk
+            return jnp.concatenate(
+                [
+                    lax.dynamic_slice_in_dim(w, start, chunk, 1)
+                    for w in (gate_weight, up_weight, down_weight)
+                ],
+                axis=1,
             )
+
+        keep = columns(parity)
+        got = swap(columns(1 - parity), "ctx", 1)
+        pair = jnp.concatenate(
+            [jnp.where(parity == 0, keep, got), jnp.where(parity == 0, got, keep)], axis=0
         )
+        near = gather_dp(pair)
+        far = gather_dp(swap(pair, "ctx", 2))
+        ffn_pieces.append([p for both in zip(near, far) for p in both])
 
     group_seq = seq_ids[0].reshape(ctx_count, rows // CLEN, CLEN)[:, :, 0]
     group_pos = positions[0].reshape(ctx_count, rows // CLEN, CLEN)[:, :, 0]
@@ -414,14 +543,13 @@
     own_pos = lax.dynamic_slice_in_dim(positions[0], ctx_index * rows, rows)
     cosine, sine = rope_tables(own_pos)
 
-    inputs = turned(tokens).astype(F32)
+    inputs_low = turned(tokens)
     cotangent_low = turned(out_grad)
     gain_one = turned(attn_gain).astype(F32)
     gain_two = turned(ffn_gain).astype(F32)
-    first_norm, first_scale = normalize(inputs)
-    first = (first_norm * gain_one).astype(BF16)
-
-    query = project(first, q_pieces, cosine, sine, True)
+    first_norm, first_scale = normalize(inputs_low.astype(F32))
+    first = low(first_norm * gain_one)
+
     keys = project(first, k_pieces, cosine, sine, True)
     values = project(first, v_pieces, cosine, sine, False)
     prompt_own = jnp.concatenate(
@@ -432,132 +560,167 @@
         axis=1,
     )
     prompts = [prompt_own] + [fetch(prompt_own, "ctx", s) for s in range(1, ctx_count)]
+    query = project(first, q_pieces, cosine, sine, True)
     mixed, lse = attention_forward(order, rank, query, keys, values, prompts)
-    middle = inputs + sum_over_tp(matmul_back(mixed, o_pieces).astype(BF16)).astype(F32)
+
+    def sum_halves(part):
+        return low(add(row_half(part), swap(lax.dynamic_slice_in_dim(part, (1 - bit) * half, half), "tp", 1)))
+
+    mixed_out = sum_halves(low(matmul_back(mixed, o_pieces)))
+    inputs_half = row_half(inputs_low).astype(F32)
+    middle = inputs_half + add(mixed_out, swap(mixed_out, "tp", 2))
     second_norm, second_scale = normalize(middle)
-    second = (second_norm * gain_two).astype(BF16)
-
-    ffn_part, dsecond_part = None, None
+    second_half = flip(low(second_norm * gain_two))
+
+    def spread(values_half):
+        other = swap(values_half, "tp", 1)
+        far = swap(values_half, "ctx", 1)
+        far_other = swap(far, "tp", 1)
+        return [
+            jnp.concatenate([values_half, other], axis=0),
+            jnp.concatenate([far, far_other], axis=0),
+        ]
+
+    seconds = spread(second_half)
+    cotangent_half = row_half(cotangent_low)
+    cotangents = spread(flip(cotangent_half))
+    hiddens, dgates, dups = [], [], []
+    for side in range(2):
+        made = [ffn(seconds[side], cotangents[side], pieces) for pieces in ffn_pieces]
+        hiddens.append([m[0] for m in made])
+        dgates.append([m[1] for m in made])
+        dups.append([m[2] for m in made])
+    gate_spans = tuple((f, 0, chunk) for f in range(FFN_CHUNKS)) + tuple(
+        (f, chunk, 2 * chunk) for f in range(FFN_CHUNKS)
+    )
+    down_spans = tuple((f, 2 * chunk, 3 * chunk) for f in range(FFN_CHUNKS))
+
+    def collect(parts):
+        near, far = [
+            low(add(part[:half], swap(part[half:], "tp", 1))) for part in parts
+        ]
+        return low(flip(add(near, swap(far, "ctx", 1))))
+
+    dsecond_parts = [
+        project_back(dgates[side] + dups[side], ffn_pieces, gate_spans) for side in (1, 0)
+    ][::-1]
+    dsecond = collect(dsecond_parts)
+    dsecond = add(dsecond, swap(dsecond, "tp", 2))
+
     ffn_grads = []
     for f in range(FFN_CHUNKS):
-        gate_w = [p[:, :chunk] for p in ffn_pieces[f]]
-        up_w = [p[:, chunk : 2 * chunk] for p in ffn_pieces[f]]
-        down_w = [p[:, 2 * chunk :] for p in ffn_pieces[f]]
-        gate = matmul_pieces(second, gate_w)
-        upward = matmul_pieces(second, up_w)
-        dhidden = matmul_pieces(cotangent_low, down_w)
-        sigmoid_gate = jax.nn.sigmoid(gate)
-        silu_gate = gate * sigmoid_gate
-        hidden = (silu_gate * upward).astype(BF16)
-        dgate = (
-            dhidden * upward * (sigmoid_gate + gate * sigmoid_gate * (1.0 - sigmoid_gate))
-        ).astype(BF16)
-        dupward = (dhidden * silu_gate).astype(BF16)
-        part = matmul_back(hidden, down_w)
-        ffn_part = part if ffn_part is None else ffn_part + part
-        part = matmul_back(dgate, gate_w) + matmul_back(dupward, up_w)
-        dsecond_part = part if dsecond_part is None else dsecond_part + part
+        left = jnp.concatenate(seconds, axis=0)
+        left_cot = jnp.concatenate(cotangents, axis=0)
         grads = [
             jnp.concatenate(terms, axis=1)
             for terms in zip(
-                row_grads(second, dgate, dp_count),
-                row_grads(second, dupward, dp_count),
-                row_grads(cotangent_low, hidden, dp_count),
+                row_grads(left, jnp.concatenate([dgates[0][f], dgates[1][f]], axis=0), dp_count),
+                row_grads(left, jnp.concatenate([dups[0][f], dups[1][f]], axis=0), dp_count),
+                row_grads(left_cot, jnp.concatenate([hiddens[0][f], hiddens[1][f]], axis=0), dp_count),
             )
         ]
-        ffn_grads.append(scatter_rows(grads))
-
-    share = width // tp_count
-    ffn_share = scatter_over_tp(ffn_part.astype(BF16), shift).astype(F32)
-
-    def own_share(values):
-        start = lax.rem(tp_index * share - shift + width, width)
-        return lax.dynamic_slice_in_dim(values, start, share, values.ndim - 1)
-
-    block_out = (own_share(middle) + ffn_share).astype(BF16)
-
-    cotangent = cotangent_low.astype(F32)
-    dsecond = sum_over_tp(dsecond_part.astype(BF16)).astype(F32)
+        block = scatter_dp(grads)
+        pair_rows = block.shape[0] // 2
+        pair = add(block[:pair_rows], swap(block[pair_rows:], "ctx", 2))
+        kept = lax.dynamic_slice_in_dim(pair, parity * own_rows, own_rows)
+        given = lax.dynamic_slice_in_dim(low(pair), (1 - parity) * own_rows, own_rows)
+        got = swap(given, "ctx", 1).astype(F32)
+        ffn_grads.append((jnp.where(parity == 0, kept, got), jnp.where(parity == 0, got, kept)))
+
     gain_two_grad = jnp.sum(dsecond * second_norm, axis=0)
     scaled_two = dsecond * gain_two
-    dmiddle = cotangent + second_scale * (
+    dmiddle = cotangent_half.astype(F32) + second_scale * (
         scaled_two - second_norm * jnp.mean(scaled_two * second_norm, axis=-1, keepdims=True)
     )
-    dmiddle_low = dmiddle.astype(BF16)
-    dmixed = matmul_pieces(dmiddle_low, o_pieces).astype(BF16)
-    dquery_low, dkey_own, dvalue_own, dkey_prompt, dvalue_prompt = attention_backward(
+    dmiddle_half = low(dmiddle)
+    dmiddle_low = assemble(dmiddle_half, swap(dmiddle_half, "tp", 1))
+    dmixed = project(dmiddle_low, o_pieces, cosine, sine, False)
+    dquery_low, dkey_own, dvalue_own, dprompt_own, *dprompts = attention_backward(
         order, rank, query, keys, values, mixed, lse, dmixed, cosine, sine, prompts
     )
-    dprompt = jnp.concatenate([dkey_prompt, dvalue_prompt], axis=1)
-    extra = dprompt[:CLEN]
-    for s in range(1, ctx_count):
-        piece = dprompt[s * CLEN : (s + 1) * CLEN].astype(BF16)
-        extra = extra + send(piece, "ctx", s).astype(F32)
-    is_mine = (jnp.arange(rows, dtype=jnp.int32) // CLEN == mine)[:, None]
-    wide = jnp.concatenate([extra] * (rows // CLEN), axis=0)
-    dkey = dkey_own + jnp.where(is_mine, wide[:, :head_width], 0.0)
-    dvalue_low = (dvalue_own + jnp.where(is_mine, wide[:, head_width:], 0.0)).astype(BF16)
-    half = HEAD_DIM // 2
-    turned_key = dkey.reshape(rows, head_width // HEAD_DIM, 2, half)[:, :, ::-1].reshape(rows, head_width)
-    repeats = head_width // LANES
-    dkey_low = (
-        dkey * jnp.concatenate([cosine] * repeats, axis=1)
-        - turned_key * jnp.concatenate([sine] * repeats, axis=1)
-    ).astype(BF16)
-
-    attn_blocks = [
-        jnp.concatenate(terms, axis=1)
-        for terms in zip(
-            row_grads(first, dquery_low, dp_count),
-            row_grads(first, dkey_low, dp_count),
-            row_grads(first, dvalue_low, dp_count),
-            row_grads(dmiddle_low, mixed, dp_count),
-        )
-    ]
-    attn_grads = scatter_rows(attn_blocks)
-
-    dfirst_part = (
-        matmul_back(dquery_low, q_pieces)
-        + matmul_back(dkey_low, k_pieces)
-        + matmul_back(dvalue_low, v_pieces)
-    )
-    dfirst = scatter_over_tp(dfirst_part.astype(BF16), shift).astype(F32)
-    norm_share = own_share(first_norm)
-    gain_one_grad = jnp.sum(dfirst * norm_share, axis=0)
-    scaled_one = dfirst * own_share(gain_one)
-    inner = jnp.sum(scaled_one * norm_share, axis=-1).reshape(1, rows)
-    mask = 1
-    while mask < tp_count:
-        inner = inner + swap(inner, "tp", mask)
-        mask *= 2
-    inner = inner.reshape(rows, 1) / width
-    in_grad = (own_share(dmiddle) + first_scale * (scaled_one - norm_share * inner)).astype(BF16)
-
-    gains = jnp.stack([gain_one_grad, own_share(gain_two_grad)])
-    gains = lax.dynamic_update_slice_in_dim(
-        jnp.zeros((2, width), F32), gains, tp_index * share, 1
-    )
-    gains = sum_everywhere(gains)
+    got = [send(piece, "ctx", s + 1) for s, piece in enumerate(dprompts)]
+    dkey_low, dvalue_low = merge_keys(
+        mine[None], dkey_own, dvalue_own, dprompt_own, got, cosine, sine
+    )
+
+    def attn_grads(pairs):
+        grads = [
+            jnp.concatenate(terms, axis=1)
+            for terms in zip(*[row_grads(left, right, dp_count) for left, right in pairs])
+        ]
+        return lax.psum_scatter(scatter_dp(grads), "ctx", scatter_dimension=0, tiled=True).astype(F32)
+
+    early = attn_grads([(dmiddle_low, mixed), (first, dquery_low)])
+    late = attn_grads([(first, dkey_low), (first, dvalue_low)])
+
+    dfirst_part = project_back(
+        [dquery_low, dkey_low, dvalue_low],
+        [q_pieces, k_pieces, v_pieces],
+        ((0, 0, head_width), (1, 0, head_width), (2, 0, head_width)),
+    )
+    dfirst = sum_halves(dfirst_part)
+    dfirst = add(dfirst, swap(dfirst, "tp", 2))
+    norm_half = row_half(first_norm)
+    gain_one_grad = jnp.sum(dfirst * norm_half, axis=0)
+    scaled_one = dfirst * gain_one
+    dinputs = dmiddle + row_half(first_scale) * (
+        scaled_one - norm_half * jnp.mean(scaled_one * norm_half, axis=-1, keepdims=True)
+    )
+
+    share = width // tp_count
+
+    def deliver(values_half):
+        wide = lax.dynamic_slice_in_dim(values_half, (tp_index // 2) * 2 * share, 2 * share, 1)
+        kept = lax.dynamic_slice_in_dim(wide, bit * share, share, 1)
+        given = lax.dynamic_slice_in_dim(wide, (1 - bit) * share, share, 1)
+        return assemble(kept, swap(given, "tp", 1))
+
+    in_grad = deliver(natural(low(dinputs)))
+
+    ffn_parts = [project_back(hiddens[side], ffn_pieces, down_spans) for side in (1, 0)][::-1]
+    ffn_out = natural(collect(ffn_parts))
+    top = (tp_index // 2) * 2 * share
+    kept = lax.dynamic_slice_in_dim(ffn_out, top, 2 * share, 1)
+    given = lax.dynamic_slice_in_dim(ffn_out, 2 * share - top, 2 * share, 1)
+    ffn_out = add(kept, swap(given, "tp", 2))
+    out_wide = low(lax.dynamic_slice_in_dim(natural(middle), top, 2 * share, 1) + ffn_out)
+    kept = lax.dynamic_slice_in_dim(out_wide, bit * share, share, 1)
+    given = lax.dynamic_slice_in_dim(out_wide, (1 - bit) * share, share, 1)
+    block_out = assemble(kept, swap(given, "tp", 1))
+
+    gains = natural(jnp.stack([gain_one_grad, gain_two_grad]))
+    gains = gains + swap(gains, "tp", 1)
+    for axis in ("ctx", "dp"):
+        mask = 1
+        while mask < lax.axis_size(axis):
+            gains = gains + swap(gains, axis, mask)
+            mask *= 2
     part = width // (dp_count * ctx_count)
     gains = lax.dynamic_slice_in_dim(gains, (dp_index * ctx_count + ctx_index) * part, part, 1)
 
-    attn_grads = attn_grads.astype(F32)
-    ffn_out = [
-        jnp.concatenate([g[:, i * chunk : (i + 1) * chunk].astype(F32) for g in ffn_grads], axis=1)
+    ffn_final = [
+        jnp.concatenate(
+            [
+                ffn_grads[f][side][:, i * chunk : (i + 1) * chunk]
+                for side in range(2)
+                for f in range(FFN_CHUNKS)
+            ],
+            axis=1,
+        )
         for i in range(3)
     ]
     return (
         block_out,
         in_grad,
         gains[0],
-        attn_grads[:, :head_width],
-        attn_grads[:, head_width : 2 * head_width],
-        attn_grads[:, 2 * head_width : 3 * head_width],
-        attn_grads[:, 3 * head_width :],
+        early[:, head_width:],
+        late[:, :head_width],
+        late[:, head_width:],
+        early[:, :head_width],
         gains[1],
-        ffn_out[0],
-        ffn_out[1],
-        ffn_out[2],
+        ffn_final[0],
+        ffn_final[1],
+        ffn_final[2],
     )
 
 

time: 1200 us -> 1130 us (0.942)
  matrix products: 198 us -> 50.2 us
  waiting for transfers between devices: 630 us -> 504 us
  Pallas kernels: 82.9 us -> 192 us
  local copies, waits for them, and re-layouts: 62.7 us -> 161 us
  other arithmetic: 145 us -> 129 us
    ppermute x8 -> x7, waiting for transfers between devices: 271 us -> 84.7 us  [send(): lax.ppermute(values, axis, [(i, (i + shift) % count) for i in range(count)])]
    ppermute x19 -> x33, waiting for transfers between devices: 91.7 us -> 261 us  [swap(): return lax.ppermute(values, axis, [(i, i ^ mask) for i in range(count)])]
    all_gather x8 -> x4, waiting for transfers between devices: 212 us -> 67.6 us  [gather_rows(): return gather_dp(lax.all_gather(weight, 'ctx', axis=0, tiled=True))]
    pallas_call x0 -> x10, Pallas kernels: none -> 102 us  [the longest x5 55.9 us: project_back(): pl.pallas_call(functools.partial(back_kernel, len(lefts), count, spans),...]
    dot_general x32 -> x2, matrix products: 99.9 us -> 3.22 us  [matmul_back(): jnp.einsum('qf,df->qd', left, p, preferred_element_type=F32)]
    dot_general x26 -> x0, matrix products: 59.1 us -> none  [matmul_pieces(): jnp.dot(left[:, s * depth:(s + 1) * depth], piece, preferred_element_type...]
    rev x1 -> x4, local copies, waits for them, and re-layouts: 2.7 us -> 59.3 us  [flip(): other = split[..., ::-1, :].reshape(values.shape)]
    convert_element_type x20 -> x14, other arithmetic: 89.8 us -> 35.3 us  [low(): return values.astype(BF16)]
  transfers between devices with their start and end apart: 51 -> 57, of which waited for: 23 -> 24; matrix products, arithmetic and copies ran while one was open for 32% -> 28% of each run, Pallas kernels for 7% -> 17%
where the time goes in v2:
time: 1130 us; the launch traced here: 1120 us
  waiting for transfers between devices  504 us (45%)
  Pallas kernels  192 us (17%)
  local copies, waits for them, and re-layouts  161 us (14%)
  other arithmetic  129 us (11%)
  starting transfers between devices  65.9 us (6%)
  matrix products  50.2 us (4%)
  between operations  16.3 us (1%)
    ppermute x33, waiting for transfers between devices, swap(): return lax.ppermute(values, axis, [(i, i ^ mask) for i in range(count)])  261 us
    ppermute x7, waiting for transfers between devices, send(): lax.ppermute(values, axis, [(i, (i + shift) % count) for i in range(count)])  84.7 us
    ppermute x11, waiting for transfers between devices, fetch(): lax.ppermute(values, axis, [(i, (i - shift) % count) for i in range(count)])  72.8 us
    all_gather x4, waiting for transfers between devices, gather_rows(): return gather_dp(lax.all_gather(weight, 'ctx', axis=0, tiled=True))  67.6 us
    rev x4, local copies, waits for them, and re-layouts, flip(): other = split[..., ::-1, :].reshape(values.shape)  59.3 us
    pallas_call x5, Pallas kernels, project_back(): pl.pallas_call(functools.partial(back_kernel, len(lefts), count, spans),...  55.9 us
    dot_general x20, matrix products, row_grads(): jnp.einsum('tc,tf->cf', left[:, s * depth:(s + 1) * depth], right, prefer...  47 us
    pallas_call x1, Pallas kernels, attention_backward(): pl.pallas_call(functools.partial(backward_kernel, pieces), grid_spec=pltp...  45.1 us
  transfers between devices with their start and end apart: 57, of which 24 were waited for; matrix products, arithmetic and copies ran while one was open for 28% of the time, Pallas kernels for 17%

profile of v2, /device:TPU:1, one launch (start us, length us, event | category | flops | bytes accessed | tf_op | source)
XLA Modules:
  0.0 1118.2 jit_solution(219601511386479710)
XLA Ops:
  26.9 12.6 %all-gather.9.cloned.1.call-done.refs_0_.refs_7_ = bf16[1024,512]{1,0:T(8,128)(2,1)} async-done(((bf16[256,512]{1,0:T(8,128)(2,1)}), bf16[1024,512]{1,0:T(8,128)(2,1)}) %all-gather.9.cloned.1.call-update) | async-done | bytes 1048592 | tf_op jit(solution)/shard_map/all_gather | solution.py:507
  42.1 26.4 %all-gather.7.cloned.1.call-done.refs_0_.refs_5_ = bf16[1024,512]{1,0:T(8,128)(2,1)} async-done(((bf16[256,512]{1,0:T(8,128)(2,1)}), bf16[1024,512]{1,0:T(8,128)(2,1)}) %all-gather.7.cloned.1.call-update) | async-done | bytes 1048592 | tf_op jit(solution)/shard_map/all_gather | solution.py:507
  76.1 21.4 %all-gather.5.cloned.1.call-done.refs_0_.refs_3_ = bf16[1024,512]{1,0:T(8,128)(2,1)} async-done(((bf16[256,512]{1,0:T(8,128)(2,1)}), bf16[1024,512]{1,0:T(8,128)(2,1)}) %all-gather.5.cloned.1.call-update) | async-done | bytes 1048592 | tf_op jit(solution)/shard_map/all_gather | solution.py:507
  138.7 33.0 %collective-permute-done.4.refs_2_.refs_6_ = bf16[256,1024]{1,0:T(8,128)(2,1)} collective-permute-done((bf16[256,1024]{1,0:T(8,128)(2,1)}, bf16[256,1024]{1,0:T(8,128)(2,1)}, u32[]{:S(2)}, u32[]{:S(2)}) %collective-permute-start.4) | collective-permute-done | bytes 524320 | tf_op jit(solution)/shard_map/ppermute | solution.py:30
  171.8 21.3 %attend.1 = (bf16[768,512]{1,0:T(8,128)(2,1)}, f32[768,512]{1,0:T(8,128)}) custom-call(s32[3]{0:T(128)} %pad_add_fusion.order_ref, s32[4]{0:T(128)} %dynamic_slice.144.rank_ref, bf16[768,512]{1,0:T(8,128)(2,1)} %project.4.q_ref, bf16[768,512]{1,0:T(8,128)(2,1)} %project.5.ks_ref, bf16[768,512]{1,0:T(8,128)(2,1)} %project.6.vs_ref, ...), custom_call_target="tpu_custom_call" | custom-call | flops 8053063680 | bytes 6291456 | tf_op jit(solution)/shard_map/attend/pallas_call | solution.py:377
  207.7 14.8 %rev.13 = bf16[384,2,2,512]{3,2,1,0:T(2,128)(2,1)} reverse(bf16[384,2,2,512]{3,2,1,0:T(2,128)(2,1)} %reshape.106), dimensions={2} | reverse | bytes 3145728 | tf_op jit(solution)/shard_map/rev | solution.py:495
  242.0 39.9 %collective-permute-done.11 = bf16[256,1536]{1,0:T(8,128)(2,1)} collective-permute-done((bf16[256,1536]{1,0:T(8,128)(2,1)}, bf16[256,1536]{1,0:T(8,128)(2,1)}, u32[]{:S(2)}, u32[]{:S(2)}) %collective-permute-start.11) | collective-permute-done | bytes 786464 | tf_op jit(solution)/shard_map/ppermute | solution.py:25
  286.5 25.0 %collective-permute-done.15 = bf16[256,1536]{1,0:T(8,128)(2,1)} collective-permute-done((bf16[256,1536]{1,0:T(8,128)(2,1)}, bf16[256,1536]{1,0:T(8,128)(2,1)}, u32[]{:S(2)}, u32[]{:S(2)}) %collective-permute-start.15) | collective-permute-done | bytes 786464 | tf_op jit(solution)/shard_map/ppermute | solution.py:25
  324.1 14.7 %rev.12 = bf16[384,2,2,512]{3,2,1,0:T(2,128)(2,1)} reverse(bf16[384,2,2,512]{3,2,1,0:T(2,128)(2,1)} %reshape.104), dimensions={2} | reverse | bytes 3145728 | tf_op jit(solution)/shard_map/rev | solution.py:495
  350.3 36.2 %collective-permute-done.12.refs_1_.refs_3_.refs_5_ = bf16[512,1536]{1,0:T(8,128)(2,1)} collective-permute-done((bf16[512,1536]{1,0:T(8,128)(2,1)}, bf16[512,1536]{1,0:T(8,128)(2,1)}, u32[]{:S(2)}, u32[]{:S(2)}) %collective-permute-start.12) | collective-permute-done | bytes 1572896 | tf_op jit(solution)/shard_map/ppermute | solution.py:25
  390.5 29.7 %collective-permute-done.16.refs_1_.refs_7_.refs_9_ = bf16[512,1536]{1,0:T(8,128)(2,1)} collective-permute-done((bf16[512,1536]{1,0:T(8,128)(2,1)}, bf16[512,1536]{1,0:T(8,128)(2,1)}, u32[]{:S(2)}, u32[]{:S(2)}) %collective-permute-start.16) | collective-permute-done | bytes 1572896 | tf_op jit(solution)/shard_map/ppermute | solution.py:25
  436.7 10.0 ffn.4
  452.8 33.7 %collective-permute-done.18.refs_3_.refs_9_.refs_11_ = bf16[512,1536]{1,0:T(8,128)(2,1)} collective-permute-done((bf16[512,1536]{1,0:T(8,128)(2,1)}, bf16[512,1536]{1,0:T(8,128)(2,1)}, u32[]{:S(2)}, u32[]{:S(2)}) %collective-permute-start.18) | collective-permute-done | bytes 1572896 | tf_op jit(solution)/shard_map/ppermute | solution.py:30
  486.5 10.5 ffn.5
  496.9 9.8 project_back.5
  513.0 13.2 %project_back.7 = bf16[768,2048]{1,0:T(8,128)(2,1)} custom-call(bf16[768,512]{1,0:T(8,128)(2,1)} %get-tuple-element.44.refs_0_, bf16[768,512]{1,0:T(8,128)(2,1)} %get-tuple-element.45.refs_1_, bf16[768,512]{1,0:T(8,128)(2,1)} %get-tuple-element.46.refs_2_, bf16[768,512]{1,0:T(8,128)(2,1)} %get-tuple-element.47.refs_3_, ...), custom_call_target="tpu_custom_call" | custom-call | flops 6442450944 | bytes 14680064 | tf_op jit(solution)/shard_map/project_back/pallas_call | solution.py:346
  539.4 10.0 ffn.7
  574.9 10.0 ffn.6
  584.9 9.8 project_back.6
  596.4 13.2 %project_back.8 = bf16[768,2048]{1,0:T(8,128)(2,1)} custom-call(bf16[768,512]{1,0:T(8,128)(2,1)} %get-tuple-element.48.refs_0_, bf16[768,512]{1,0:T(8,128)(2,1)} %get-tuple-element.49.refs_1_, bf16[768,512]{1,0:T(8,128)(2,1)} %get-tuple-element.50.refs_2_, bf16[768,512]{1,0:T(8,128)(2,1)} %get-tuple-element.51.refs_3_, ...), custom_call_target="tpu_custom_call" | custom-call | flops 6442450944 | bytes 14680064 | tf_op jit(solution)/shard_map/project_back/pallas_call | solution.py:346
  639.0 25.2 %collective-permute-done.25 = bf16[384,2048]{1,0:T(8,128)(2,1)S(1)} collective-permute-done((bf16[384,2048]{1,0:T(8,128)(2,1)S(1)}, bf16[384,2048]{1,0:T(8,128)(2,1)S(1)}, u32[]{:S(2)}, u32[]{:S(2)}) %collective-permute-start.25) | collective-permute-done | bytes 1572896 | tf_op jit(solution)/shard_map/ppermute | solution.py:25
  670.0 14.8 %rev.14 = bf16[384,2,2,512]{3,2,1,0:T(2,128)(2,1)} reverse(bf16[384,2,2,512]{3,2,1,0:T(2,128)(2,1)} %reshape.108), dimensions={2} | reverse | bytes 3145728 | tf_op jit(solution)/shard_map/rev | solution.py:495
  705.6 14.9 %rev.15 = bf16[384,2,2,512]{3,2,1,0:T(2,128)(2,1)} reverse(bf16[384,2,2,512]{3,2,1,0:T(2,128)(2,1)} %reshape.110), dimensions={2} | reverse | bytes 3145728 | tf_op jit(solution)/shard_map/rev | solution.py:495
  731.9 19.0 %collective-permute-done.45 = bf16[1024,1536]{1,0:T(8,128)(2,1)} collective-permute-done((bf16[1024,1536]{1,0:T(8,128)(2,1)}, bf16[1024,1536]{1,0:T(8,128)(2,1)}, u32[]{:S(2)}, u32[]{:S(2)}) %collective-permute-start.45) | collective-permute-done | bytes 3145760 | tf_op jit(solution)/shard_map/ppermute | solution.py:35
  767.2 66.7 %collective-permute-done.49 = bf16[512,1536]{1,0:T(8,128)(2,1)S(1)} collective-permute-done((bf16[512,1536]{1,0:T(8,128)(2,1)S(1)}, bf16[512,1536]{1,0:T(8,128)(2,1)S(1)}, u32[]{:S(2)}, u32[]{:S(2)}) %collective-permute-start.49) | collective-permute-done | bytes 1572896 | tf_op jit(solution)/shard_map/ppermute | solution.py:25
  836.0 31.6 %collective-permute-done.46 = bf16[512,1536]{1,0:T(8,128)(2,1)S(1)} collective-permute-done((bf16[512,1536]{1,0:T(8,128)(2,1)S(1)}, bf16[512,1536]{1,0:T(8,128)(2,1)S(1)}, u32[]{:S(2)}, u32[]{:S(2)}) %collective-permute-start.46) | collective-permute-done | bytes 1572896 | tf_op jit(solution)/shard_map/ppermute | solution.py:25
  880.6 45.1 %attend_back.1 = (bf16[768,512]{1,0:T(8,128)(2,1)}, f32[768,512]{1,0:T(8,128)}, f32[768,512]{1,0:T(8,128)}, f32[256,1024]{1,0:T(8,128)}, bf16[256,1024]{1,0:T(8,...) custom-call(s32[3]{0:T(128)} %pad_add_fusion.order_ref, s32[4]{0:T(128)} %dynamic_slice.144.rank_ref, ...), custom_call_target="tpu_custom_call" | custom-call | flops 20132659200 | bytes 12582912 | tf_op jit(solution)/shard_map/attend_back/pallas_call | solution.py:399
  952.3 23.8 %collective-permute-done.34.refs_1_ = bf16[256,1024]{1,0:T(8,128)(2,1)S(1)} collective-permute-done((bf16[256,1024]{1,0:T(8,128)(2,1)S(1)}, bf16[256,1024]{1,0:T(8,128)(2,1)S(1)}, u32[]{:S(2)}, u32[]{:S(2)}) %collective-permute-start.34) | collective-permute-done | bytes 524320 | tf_op jit(solution)/shard_map/ppermute | solution.py:35
  987.1 10.0 project_back.9
  1014.1 36.3 %collective-permute-done.44 = bf16[1024,1024]{0,1:T(8,128)(2,1)S(1)} collective-permute-done((bf16[1024,1024]{0,1:T(8,128)(2,1)S(1)}, bf16[1024,1024]{0,1:T(8,128)(2,1)S(1)}, u32[]{:S(2)}, u32[]{:S(2)}) %collective-permute-start.44) | collective-permute-done | bytes 2097184 | tf_op jit(solution)/shard_map/ppermute | solution.py:35
  1061.9 11.3 %collective-permute-start.40 = (f32[2,2048]{1,0:T(2,128)S(1)}, f32[2,2048]{1,0:T(2,128)S(1)}, u32[]{:S(2)}, u32[]{:S(2)}) collective-permute-start(f32[2,2048]{1,0:T(2,128)S(1)} %fusion.138), channel_id=1, source_target_pairs={{0,4},{4,0},{8,12},{12,8},{1,5},{5,1},{9,13},{13,9},{2,6},{6,2},{1... | collective-permute-start | bytes 49160 | tf_op jit(solution)/shard_map/ppermute | solution.py:25
  1093.3 14.7 %reduce-scatter.5.cloned.1.call-done = bf16[256,1024]{0,1:T(8,128)(2,1)} async-done(((bf16[1024,1024]{0,1:T(8,128)(2,1)}), bf16[256,1024]{0,1:T(8,128)(2,1)}) %reduce-scatter.5.cloned.1.call-update) | async-done | bytes 524304 | tf_op jit(solution)/shard_map/reduce_scatter | solution.py:651
  (477 shorter events, 393.2 us)
Async XLA Ops:
  7.9 60.6 %all-gather.7.cloned.1.call-start = ((), (), s32[]{:S(2)}) async-start(), calls=%async_computation.3 | async-start | bytes 1310720 | tf_op jit(solution)/shard_map/all_gather | solution.py:507
  8.7 88.9 %all-gather.5.cloned.1.call-start = ((), (), s32[]{:S(2)}) async-start(), calls=%async_computation.2 | async-start | bytes 1310720 | tf_op jit(solution)/shard_map/all_gather | solution.py:507
  9.4 119.9 %all-gather.11.cloned.1.call-start = ((), (), s32[]{:S(2)}) async-start(), calls=%async_computation.5 | async-start | bytes 1310720 | tf_op jit(solution)/shard_map/all_gather | solution.py:507
  10.0 1080.2 %reduce-scatter.3.cloned.1.call-start = ((), (), s32[]{:S(2)}) async-start(), calls=%async_computation.6 | async-start | bytes 2621440 | tf_op jit(solution)/shard_map/reduce_scatter | solution.py:651
  39.5 59.3 %collective-permute-start.2 = (bf16[1024,512]{1,0:T(8,128)(2,1)}, bf16[1024,512]{1,0:T(8,128)(2,1)S(1)}, u32[]{:S(2)}, u32[]{:S(2)}) collective-permute-start(bf16[1024,512]{1,0:T(8,128)(2,1)} %all-gather.9.cloned.1.call-done.refs_0_.refs_7_), channel_id=1, source_target_pairs={{0,16},{16,0},{1,17},{17,1},{2,18},{18,2},{3,19},{19,3},{4,20},{20... | collective-permute-start | bytes 3145736 | tf_op jit(solution)/shard_map/ppermute | solution.py:30
  117.2 54.6 %collective-permute-start.4 = (bf16[256,1024]{1,0:T(8,128)(2,1)}, bf16[256,1024]{1,0:T(8,128)(2,1)}, u32[]{:S(2)}, u32[]{:S(2)}) collective-permute-start(bf16[256,1024]{1,0:T(8,128)(2,1)} %pad_maximum_fusion.20.refs_0_.refs_4_), channel_id=1, source_target_pairs={{0,8},{4,12},{8,0},{12,4},{1,9},{5,13},{9,1},{13,5},{2,10},{6,14},... | collective-permute-start | bytes 1572872 | tf_op jit(solution)/shard_map/ppermute | solution.py:30
  117.4 54.3 %collective-permute-start.5 = (bf16[256,1024]{1,0:T(8,128)(2,1)}, bf16[256,1024]{1,0:T(8,128)(2,1)}, u32[]{:S(2)}, u32[]{:S(2)}) collective-permute-start(bf16[256,1024]{1,0:T(8,128)(2,1)} %pad_maximum_fusion.20.refs_0_.refs_4_), channel_id=1, source_target_pairs={{0,4},{4,8},{8,12},{12,0},{1,5},{5,9},{9,13},{13,1},{2,6},{6,10},{... | collective-permute-start | bytes 1572872 | tf_op jit(solution)/shard_map/ppermute | solution.py:30
  129.3 66.1 %collective-permute-start.6 = (bf16[1024,512]{1,0:T(8,128)(2,1)}, bf16[1024,512]{1,0:T(8,128)(2,1)S(1)}, u32[]{:S(2)}, u32[]{:S(2)}) collective-permute-start(bf16[1024,512]{1,0:T(8,128)(2,1)} %all-gather.11.cloned.1.call-done.refs_0_), channel_id=1, source_target_pairs={{0,16},{16,0},{1,17},{17,1},{2,18},{18,2},{3,19},{19,3},{4,20},{20... | collective-permute-start | bytes 3145736 | tf_op jit(solution)/shard_map/ppermute | solution.py:30
  229.6 84.6 %collective-permute-start.22 = (bf16[384,2048]{1,0:T(8,128)(2,1)}, bf16[384,2048]{1,0:T(8,128)(2,1)}, u32[]{:S(2)}, u32[]{:S(2)}) collective-permute-start(bf16[384,2048]{1,0:T(8,128)(2,1)} %broadcast_select_fusion.2), channel_id=1, source_target_pairs={{0,4},{4,0},{8,12},{12,8},{1,5},{5,1},{9,13},{13,9},{2,6},{6,2},{1... | collective-permute-start | bytes 4718600 | tf_op jit(solution)/shard_map/ppermute | solution.py:25
  229.6 115.5 %collective-permute-start.10 = (bf16[384,2048]{1,0:T(8,128)(2,1)}, bf16[384,2048]{1,0:T(8,128)(2,1)}, u32[]{:S(2)}, u32[]{:S(2)}) collective-permute-start(bf16[384,2048]{1,0:T(8,128)(2,1)} %broadcast_select_fusion.2), channel_id=1, source_target_pairs={{0,1},{1,0},{2,3},{3,2},{4,5},{5,4},{6,7},{7,6},{8,9},{9,8},{10,11... | collective-permute-start | bytes 4718600 | tf_op jit(solution)/shard_map/ppermute | solution.py:25
  238.6 72.9 %collective-permute-start.15 = (bf16[256,1536]{1,0:T(8,128)(2,1)}, bf16[256,1536]{1,0:T(8,128)(2,1)}, u32[]{:S(2)}, u32[]{:S(2)}) collective-permute-start(bf16[256,1536]{1,0:T(8,128)(2,1)} %pad_maximum_fusion.17), channel_id=1, source_target_pairs={{0,4},{4,0},{8,12},{12,8},{1,5},{5,1},{9,13},{13,9},{2,6},{6,2},{1... | collective-permute-start | bytes 2359304 | tf_op jit(solution)/shard_map/ppermute | solution.py:25
  240.7 75.0 %collective-permute-start.8 = (bf16[384,2048]{1,0:T(8,128)(2,1)S(1)}, bf16[384,2048]{1,0:T(8,128)(2,1)S(1)}, u32[]{:S(2)}, u32[]{:S(2)}) collective-permute-start(bf16[384,2048]{1,0:T(8,128)(2,1)S(1)} %add_convert_fusion.10), channel_id=1, source_target_pairs={{0,2},{1,3},{2,0},{3,1},{4,6},{5,7},{6,4},{7,5},{8,10},{9,11},{10,... | collective-permute-start | bytes 4718600 | tf_op jit(solution)/shard_map/ppermute | solution.py:25
  284.7 101.8 %collective-permute-start.12 = (bf16[512,1536]{1,0:T(8,128)(2,1)}, bf16[512,1536]{1,0:T(8,128)(2,1)}, u32[]{:S(2)}, u32[]{:S(2)}) collective-permute-start(bf16[512,1536]{1,0:T(8,128)(2,1)} %pad_maximum_fusion.12.refs_0_.refs_2_.refs_4_), channel_id=1, source_target_pairs={{0,8},{4,12},{8,0},{12,4},{1,9},{5,13},{9,1},{13,5},{2,10},{6,14},... | collective-permute-start | bytes 4718600 | tf_op jit(solution)/shard_map/ppermute | solution.py:25
  314.2 106.1 %collective-permute-start.16 = (bf16[512,1536]{1,0:T(8,128)(2,1)}, bf16[512,1536]{1,0:T(8,128)(2,1)}, u32[]{:S(2)}, u32[]{:S(2)}) collective-permute-start(bf16[512,1536]{1,0:T(8,128)(2,1)} %pad_maximum_fusion.13.refs_0_.refs_6_.refs_8_), channel_id=1, source_target_pairs={{0,8},{4,12},{8,0},{12,4},{1,9},{5,13},{9,1},{13,5},{2,10},{6,14},... | collective-permute-start | bytes 4718600 | tf_op jit(solution)/shard_map/ppermute | solution.py:25
  314.2 107.3 %collective-permute-start.23 = (bf16[384,2048]{1,0:T(8,128)(2,1)}, bf16[384,2048]{1,0:T(8,128)(2,1)}, u32[]{:S(2)}, u32[]{:S(2)}) collective-permute-start(bf16[384,2048]{1,0:T(8,128)(2,1)} %collective-permute-done.22), channel_id=1, source_target_pairs={{0,1},{1,0},{2,3},{3,2},{4,5},{5,4},{6,7},{7,6},{8,9},{9,8},{10,11... | collective-permute-start | bytes 4718600 | tf_op jit(solution)/shard_map/ppermute | solution.py:25
  344.4 83.2 %collective-permute-start.9 = (bf16[384,2048]{1,0:T(8,128)(2,1)}, bf16[384,2048]{1,0:T(8,128)(2,1)}, u32[]{:S(2)}, u32[]{:S(2)}) collective-permute-start(bf16[384,2048]{1,0:T(8,128)(2,1)} %broadcast_select_fusion.3), channel_id=1, source_target_pairs={{0,1},{1,0},{2,3},{3,2},{4,5},{5,4},{6,7},{7,6},{8,9},{9,8},{10,11... | collective-permute-start | bytes 4718600 | tf_op jit(solution)/shard_map/ppermute | solution.py:25
  345.1 89.4 %collective-permute-start.13 = (bf16[512,1536]{1,0:T(8,128)(2,1)}, bf16[512,1536]{1,0:T(8,128)(2,1)S(1)}, u32[]{:S(2)}, u32[]{:S(2)}) collective-permute-start(bf16[512,1536]{1,0:T(8,128)(2,1)} %pad_maximum_fusion.12.refs_0_.refs_2_.refs_4_), channel_id=1, source_target_pairs={{0,16},{16,0},{1,17},{17,1},{2,18},{18,2},{3,19},{19,3},{4,20},{20... | collective-permute-start | bytes 4718600 | tf_op jit(solution)/shard_map/ppermute | solution.py:30
  421.5 65.0 %collective-permute-start.18 = (bf16[512,1536]{1,0:T(8,128)(2,1)}, bf16[512,1536]{1,0:T(8,128)(2,1)}, u32[]{:S(2)}, u32[]{:S(2)}) collective-permute-start(bf16[512,1536]{1,0:T(8,128)(2,1)} %collective-permute-done.16.refs_1_.refs_7_.refs_9_), channel_id=1, source_target_pairs={{0,16},{16,0},{1,17},{17,1},{2,18},{18,2},{3,19},{19,3},{4,20},{20... | collective-permute-start | bytes 4718600 | tf_op jit(solution)/shard_map/ppermute | solution.py:30
  427.6 85.4 %collective-permute-start.20 = (bf16[384,2048]{1,0:T(8,128)(2,1)}, bf16[384,2048]{1,0:T(8,128)(2,1)}, u32[]{:S(2)}, u32[]{:S(2)}) collective-permute-start(bf16[384,2048]{1,0:T(8,128)(2,1)} %broadcast_select_fusion.3), channel_id=1, source_target_pairs={{0,4},{4,0},{8,12},{12,8},{1,5},{5,1},{9,13},{13,9},{2,6},{6,2},{1... | collective-permute-start | bytes 4718600 | tf_op jit(solution)/shard_map/ppermute | solution.py:25
  508.3 130.2 %collective-permute-start.19 = (bf16[384,2048]{1,0:T(8,128)(2,1)S(1)}, bf16[384,2048]{1,0:T(8,128)(2,1)S(1)}, u32[]{:S(2)}, u32[]{:S(2)}) collective-permute-start(bf16[384,2048]{1,0:T(8,128)(2,1)S(1)} %slice.179), channel_id=1, source_target_pairs={{0,1},{1,0},{2,3},{3,2},{4,5},{5,4},{6,7},{7,6},{8,9},{9,8},{10,11... | collective-permute-start | bytes 4718600 | tf_op jit(solution)/shard_map/ppermute | solution.py:25
  529.1 165.6 %collective-permute-start.28 = (bf16[384,2048]{1,0:T(8,128)(2,1)}, bf16[384,2048]{1,0:T(8,128)(2,1)}, u32[]{:S(2)}, u32[]{:S(2)}) collective-permute-start(bf16[384,2048]{1,0:T(8,128)(2,1)} %slice.183), channel_id=1, source_target_pairs={{0,1},{1,0},{2,3},{3,2},{4,5},{5,4},{6,7},{7,6},{8,9},{9,8},{10,11... | collective-permute-start | bytes 4718600 | tf_op jit(solution)/shard_map/ppermute | solution.py:25
  613.8 113.5 %collective-permute-start.48 = (bf16[1024,1536]{1,0:T(8,128)(2,1)}, bf16[1024,1536]{1,0:T(8,128)(2,1)}, u32[]{:S(2)}, u32[]{:S(2)}) collective-permute-start(bf16[1024,1536]{1,0:T(8,128)(2,1)} %pad_maximum_fusion.6), channel_id=1, source_target_pairs={{0,16},{16,0},{1,17},{17,1},{2,18},{18,2},{3,19},{19,3},{4,20},{20... | collective-permute-start | bytes 9437192 | tf_op jit(solution)/shard_map/ppermute | solution.py:35
  635.4 62.5 %collective-permute-start.30 = (bf16[384,2048]{1,0:T(8,128)(2,1)}, bf16[384,2048]{1,0:T(8,128)(2,1)}, u32[]{:S(2)}, u32[]{:S(2)}) collective-permute-start(bf16[384,2048]{1,0:T(8,128)(2,1)} %add_convert_fusion.6), channel_id=1, source_target_pairs={{0,4},{4,0},{8,12},{12,8},{1,5},{5,1},{9,13},{13,9},{2,6},{6,2},{1... | collective-permute-start | bytes 4718600 | tf_op jit(solution)/shard_map/ppermute | solution.py:25
  638.5 112.3 %collective-permute-start.45 = (bf16[1024,1536]{1,0:T(8,128)(2,1)}, bf16[1024,1536]{1,0:T(8,128)(2,1)}, u32[]{:S(2)}, u32[]{:S(2)}) collective-permute-start(bf16[1024,1536]{1,0:T(8,128)(2,1)} %pad_maximum_fusion.5), channel_id=1, source_target_pairs={{0,16},{16,0},{1,17},{17,1},{2,18},{18,2},{3,19},{19,3},{4,20},{20... | collective-permute-start | bytes 9437192 | tf_op jit(solution)/shard_map/ppermute | solution.py:35
  693.6 59.8 %collective-permute-start.26 = (bf16[384,1024]{1,0:T(8,128)(2,1)}, bf16[384,1024]{1,0:T(8,128)(2,1)}, u32[]{:S(2)}, u32[]{:S(2)}) collective-permute-start(bf16[384,1024]{1,0:T(8,128)(2,1)} %fusion.87), channel_id=1, source_target_pairs={{0,2},{1,3},{2,0},{3,1},{4,6},{5,7},{6,4},{7,5},{8,10},{9,11},{10,... | collective-permute-start | bytes 2359304 | tf_op jit(solution)/shard_map/ppermute | solution.py:25
  729.8 104.1 %collective-permute-start.49 = (bf16[512,1536]{1,0:T(8,128)(2,1)S(1)}, bf16[512,1536]{1,0:T(8,128)(2,1)S(1)}, u32[]{:S(2)}, u32[]{:S(2)}) collective-permute-start(bf16[512,1536]{1,0:T(8,128)(2,1)S(1)} %slice.206), channel_id=1, source_target_pairs={{0,8},{4,12},{8,0},{12,4},{1,9},{5,13},{9,1},{13,5},{2,10},{6,14},... | collective-permute-start | bytes 4718600 | tf_op jit(solution)/shard_map/ppermute | solution.py:25
  753.3 114.3 %collective-permute-start.46 = (bf16[512,1536]{1,0:T(8,128)(2,1)S(1)}, bf16[512,1536]{1,0:T(8,128)(2,1)S(1)}, u32[]{:S(2)}, u32[]{:S(2)}) collective-permute-start(bf16[512,1536]{1,0:T(8,128)(2,1)S(1)} %slice.203), channel_id=1, source_target_pairs={{0,8},{4,12},{8,0},{12,4},{1,9},{5,13},{9,1},{13,5},{2,10},{6,14},... | collective-permute-start | bytes 4718600 | tf_op jit(solution)/shard_map/ppermute | solution.py:25
  758.1 172.0 %collective-permute-start.27 = (bf16[384,512]{1,0:T(8,128)(2,1)}, bf16[384,512]{1,0:T(8,128)(2,1)S(1)}, u32[]{:S(2)}, u32[]{:S(2)}) collective-permute-start(bf16[384,512]{1,0:T(8,128)(2,1)} %constant_dynamic-slice_fusion.3), channel_id=1, source_target_pairs={{0,1},{1,0},{2,3},{3,2},{4,5},{5,4},{6,7},{7,6},{8,9},{9,8},{10,11... | collective-permute-start | bytes 1179656 | tf_op jit(solution)/shard_map/ppermute | solution.py:25
  764.6 106.1 %collective-permute-start.32 = (bf16[384,2048]{1,0:T(8,128)(2,1)S(1)}, bf16[384,2048]{1,0:T(8,128)(2,1)S(1)}, u32[]{:S(2)}, u32[]{:S(2)}) collective-permute-start(bf16[384,2048]{1,0:T(8,128)(2,1)S(1)} %fusion.105), channel_id=1, source_target_pairs={{0,1},{1,0},{2,3},{3,2},{4,5},{5,4},{6,7},{7,6},{8,9},{9,8},{10,11... | collective-permute-start | bytes 4718600 | tf_op jit(solution)/shard_map/ppermute | solution.py:25
  835.4 95.8 %collective-permute-start.50 = (bf16[256,1536]{1,0:T(8,128)(2,1)}, bf16[256,1536]{1,0:T(8,128)(2,1)}, u32[]{:S(2)}, u32[]{:S(2)}) collective-permute-start(bf16[256,1536]{1,0:T(8,128)(2,1)} %dynamic-slice_convert_fusion), channel_id=1, source_target_pairs={{0,4},{4,0},{8,12},{12,8},{1,5},{5,1},{9,13},{13,9},{2,6},{6,2},{1... | collective-permute-start | bytes 2359304 | tf_op jit(solution)/shard_map/ppermute | solution.py:25
  870.0 64.6 %collective-permute-start.47 = (bf16[256,1536]{1,0:T(8,128)(2,1)}, bf16[256,1536]{1,0:T(8,128)(2,1)}, u32[]{:S(2)}, u32[]{:S(2)}) collective-permute-start(bf16[256,1536]{1,0:T(8,128)(2,1)} %dynamic-slice_convert_fusion.1), channel_id=1, source_target_pairs={{0,4},{4,0},{8,12},{12,8},{1,5},{5,1},{9,13},{13,9},{2,6},{6,2},{1... | collective-permute-start | bytes 2359304 | tf_op jit(solution)/shard_map/ppermute | solution.py:25
  987.0 121.0 %reduce-scatter.5.cloned.1.call-start = ((), (), s32[]{:S(2)}) async-start(), calls=%async_computation.7 | async-start | bytes 2621440 | tf_op jit(solution)/shard_map/reduce_scatter | solution.py:651
  (127 other events, 1719.6 us)
Sparse Core Ops, SparseCore 0:
  9.6 29.8 all-gather.8
  41.1 27.4 all-gather.6
  70.1 27.4 all-gather.4
  99.0 30.2 all-gather.10
  987.2 54.2 reduce-scatter.2
  1052.9 55.0 reduce-scatter.4

commit v3 on v2

v3 whole, which is shorter than its diff:
```python
import functools
import math

import jax
import jax.numpy as jnp
from jax import lax
from jax.experimental import pallas as pl
from jax.experimental.pallas import tpu as pltpu
from jax.sharding import Mesh
from jax.sharding import PartitionSpec as P

HEAD_DIM = 64
CLEN = 256
LANES = 128
EPS = 1e-05
ROPE_BASE = 130000.0
MASKED = -1e30
FFN_CHUNKS = 2
COST_SCALE = 16
BF16 = jnp.bfloat16
F32 = jnp.float32
VMEM_LIMIT = 32 * 1024 * 1024
CTX = ("hi", "lo")


def swap(values, axis, mask=1):
    count = lax.axis_size(axis)
    return lax.ppermute(values, axis, [(i, i ^ mask) for i in range(count)])


def turn(values, axis, shift):
    count = lax.axis_size(axis)
    return lax.ppermute(values, axis, [(i, (i + shift) % count) for i in range(count)])


def add(left, right):
    return left.astype(F32) + right.astype(F32)


def low(values):
    return values.astype(BF16)


def after(values, *needed):
    return lax.optimization_barrier((values,) + needed)[0]


def cost(flops, data, transcendentals=0):
    return pl.CostEstimate(
        flops=flops // COST_SCALE,
        bytes_accessed=data // COST_SCALE,
        transcendentals=transcendentals // COST_SCALE,
    )


def dot(left, right, dims):
    return lax.dot_general(left, right, (dims, ((), ())), preferred_element_type=F32)


NN = ((1,), (0,))
NT = ((1,), (1,))
TN = ((0,), (0,))
VMEM = pl.BlockSpec(memory_space=pltpu.VMEM)
SMEM = pl.BlockSpec(memory_space=pltpu.SMEM)


def at_block(index, size):
    return pl.ds(pl.multiple_of(index * size, size), size)


def half_swap(values):
    lane = lax.broadcasted_iota(jnp.int32, values.shape, 1)
    ahead = pltpu.roll(values, LANES - 32, 1)
    behind = pltpu.roll(values, 32, 1)
    return jnp.where((lane & 63) < 32, ahead, behind)


def call(kernel, operands, out_shape, name, flops, data, scratch=(), smem=(), transcendentals=0):
    many = isinstance(out_shape, list)
    return pl.pallas_call(
        kernel,
        in_specs=[SMEM] * len(smem) + [VMEM] * len(operands),
        out_specs=[VMEM] * len(out_shape) if many else VMEM,
        out_shape=out_shape,
        scratch_shapes=list(scratch),
        compiler_params=pltpu.CompilerParams(vmem_limit_bytes=VMEM_LIMIT),
        cost_estimate=cost(flops, data, transcendentals),
        name=name,
    )(*smem, *operands)


def fill(whole, pieces, place_ref, unit, column, width):
    at = 0
    for piece in pieces:
        for row in range(0, piece.shape[0], unit):
            whole[at_block(place_ref[at], unit), :] = piece[
                row : row + unit, column : column + width
            ]
            at += 1


def project_kernel(parts, column, width, rope_width, bit_ref, place_ref, *refs):
    x_refs = refs[:parts]
    w_refs = refs[parts:-5]
    cos_ref, sin_ref, out_ref, x_all, w_all = refs[-5:]
    fill(w_all, w_refs, place_ref, w_all.shape[0] // place_ref.shape[0], column, width)
    if parts == 2:
        rows = x_refs[0].shape[0]
        x_all[at_block(bit_ref[0], rows), :] = x_refs[0][...]
        x_all[at_block(1 - bit_ref[0], rows), :] = x_refs[1][...]
        x_ref = x_all
    else:
        x_ref = x_refs[0]
    tile = min(width, 256)

    def columns(first, rope):
        def step(t, carry):
            at = pl.multiple_of(first + t * tile, tile)
            total = dot(x_ref[...], w_all[:, pl.ds(at, tile)], NN)
            for c in range(0, tile, LANES):
                part = total[:, c : c + LANES]
                if rope:
                    part = part * cos_ref[...] + half_swap(part) * sin_ref[...]
                out_ref[:, pl.ds(pl.multiple_of(at + c, LANES), LANES)] = part.astype(BF16)
            return carry

        return step

    if rope_width:
        lax.fori_loop(0, rope_width // tile, columns(0, True), 0)
    if rope_width < width:
        lax.fori_loop(0, (width - rope_width) // tile, columns(rope_width, False), 0)


def project(x_parts, stack, places, bit, column, width, cosine, sine, rope_width):
    rows = sum(x.shape[0] for x in x_parts)
    depth = x_parts[0].shape[1]
    return call(
        functools.partial(project_kernel, len(x_parts), column, width, rope_width),
        [*x_parts, *stack, cosine, sine],
        jax.ShapeDtypeStruct((rows, width), BF16),
        "project",
        2 * rows * depth * width,
        2 * (rows * depth + depth * width + rows * width),
        [
            pltpu.VMEM((rows if len(x_parts) == 2 else 16, depth), BF16),
            pltpu.VMEM((depth, width), BF16),
        ],
        [bit, places],
    )


def place_kernel(count, place_ref, *refs):
    out_ref = refs[-1]
    unit = out_ref.shape[0] // count
    at = 0
    for ref in refs[:-1]:
        for row in range(0, ref.shape[0], unit):
            out_ref[at_block(place_ref[at], unit), :] = ref[row : row + unit, :]
            at += 1


def place_rows(pieces, places):
    rows, width = sum(p.shape[0] for p in pieces), pieces[0].shape[1]
    return call(
        functools.partial(place_kernel, places.shape[0]),
        pieces,
        jax.ShapeDtypeStruct((rows, width), BF16),
        "place_rows",
        0,
        4 * rows * width,
        smem=[places],
    )


def ffn_kernel(chunks, *refs):
    x_refs, cot_refs = refs[:2], refs[2:4]
    w_refs = refs[4 : 4 + chunks]
    hidden_ref, dpair_ref = refs[4 + chunks :]
    rows = x_refs[0].shape[0]
    wide = w_refs[0].shape[1] // 3
    tile = min(wide, 256)
    for f, w_ref in enumerate(w_refs):

        def step(t, carry, f=f, w_ref=w_ref):
            for part in range(2):
                x, g = x_refs[part][...], cot_refs[part][...]
                gate = dot(x, w_ref[:, pl.ds(pl.multiple_of(t * tile, tile), tile)], NN)
                upward = dot(x, w_ref[:, pl.ds(pl.multiple_of(wide + t * tile, tile), tile)], NN)
                dhidden = dot(g, w_ref[:, pl.ds(pl.multiple_of(2 * wide + t * tile, tile), tile)], NN)
                sig = 1.0 / (1.0 + jnp.exp(-gate))
                silu = gate * sig
                at = slice(part * rows, (part + 1) * rows)
                hidden_ref[at, pl.ds(pl.multiple_of(f * wide + t * tile, tile), tile)] = (
                    silu * upward
                ).astype(BF16)
                dpair_ref[at, pl.ds(pl.multiple_of(2 * f * wide + t * tile, tile), tile)] = (
                    dhidden * upward * (sig + silu * (1.0 - sig))
                ).astype(BF16)
                dpair_ref[at, pl.ds(pl.multiple_of((2 * f + 1) * wide + t * tile, tile), tile)] = (
                    dhidden * silu
                ).astype(BF16)
            return carry

        lax.fori_loop(0, wide // tile, step, 0)


def ffn(seconds, cotangents, weights):
    rows = 2 * seconds[0].shape[0]
    width = seconds[0].shape[1]
    units = sum(w.shape[1] for w in weights) // 3
    return call(
        functools.partial(ffn_kernel, len(weights)),
        [*seconds, *cotangents, *weights],
        [jax.ShapeDtypeStruct((rows, units), BF16), jax.ShapeDtypeStruct((rows, 2 * units), BF16)],
        "ffn",
        6 * rows * width * units,
        2 * (2 * rows * width + 3 * width * units + 3 * rows * units),
        transcendentals=rows * units,
    )


def back_kernel(spans, *refs):
    count = 1 + max(span[2] for span in spans)
    lefts = refs[: 1 + max(span[0] for span in spans)]
    rights = refs[len(lefts) : len(lefts) + count]
    outs = refs[len(lefts) + count :]
    rows, width = outs[0].shape
    tile = 256

    def step(t, carry):
        for part, out_ref in enumerate(outs):
            total = None
            for left, l_at, right, r_at, wide in spans:
                term = dot(
                    lefts[left][part * rows : (part + 1) * rows, l_at : l_at + wide],
                    rights[right][at_block(t, tile), r_at : r_at + wide],
                    NT,
                )
                total = term if total is None else total + term
            out_ref[:, at_block(t, tile)] = total.astype(BF16)
        return carry

    lax.fori_loop(0, width // tile, step, 0)


def ffn_back(lefts, weights, spans):
    rows = lefts[0].shape[0]
    width = weights[0].shape[0]
    depth = sum(span[4] for span in spans)
    return call(
        functools.partial(back_kernel, spans),
        [*lefts, *weights],
        [jax.ShapeDtypeStruct((rows // 2, width), BF16)] * 2,
        "ffn_back",
        2 * rows * width * depth,
        2 * (rows * depth + width * depth + rows * width),
    )


def project_back_kernel(columns, counts, bit_ref, place_ref, *refs):
    lefts = refs[: len(columns)]
    at, stacks = len(columns), []
    for count in counts:
        stacks.append(refs[at : at + count])
        at += count
    outs, w_all = refs[at : at + 2], refs[at + 2]
    rows, width = outs[0].shape
    unit = width // place_ref.shape[0]
    wide = lefts[0].shape[1]
    for n, (which, column) in enumerate(columns):
        at = 0
        for piece in stacks[which]:
            for row in range(0, piece.shape[0], unit):
                w_all[at_block(place_ref[at], unit), n * wide : (n + 1) * wide] = piece[
                    row : row + unit, column : column + wide
                ]
                at += 1
    tile = 256

    def step(t, carry):
        for part, out_ref in enumerate(outs):
            which = bit_ref[0] if part == 0 else 1 - bit_ref[0]
            total = None
            for n, left in enumerate(lefts):
                term = dot(
                    left[at_block(which, rows), :],
                    w_all[at_block(t, tile), n * wide : (n + 1) * wide],
                    NT,
                )
                total = term if total is None else total + term
            out_ref[:, at_block(t, tile)] = total.astype(BF16)
        return carry

    lax.fori_loop(0, width // tile, step, 0)


def project_back(lefts, columns, stacks, places, bit):
    rows, wide = lefts[0].shape
    width = sum(piece.shape[0] for piece in stacks[0])
    depth = wide * len(lefts)
    return call(
        functools.partial(project_back_kernel, columns, tuple(len(s) for s in stacks)),
        [*lefts, *[piece for stack in stacks for piece in stack]],
        [jax.ShapeDtypeStruct((rows // 2, width), BF16)] * 2,
        "project_back",
        2 * rows * width * depth,
        2 * (rows * depth + width * depth + rows * width),
        [pltpu.VMEM((width, depth), BF16)],
        [bit, places],
    )


def store_blocks(out_ref, values, first, unit, slot_ref, column):
    wide = values.shape[1]
    for row in range(0, values.shape[0], unit):
        slot = slot_ref[(first + row) // unit]
        out_ref[at_block(slot, unit), column : column + wide] = values[row : row + unit]


def ffn_grads_kernel(s, unit, dp_ref, slot_ref, *refs):
    x_refs, cot_refs = refs[:4], refs[4:8]
    hiddens, dpairs, out_ref = refs[8:10], refs[10:12], refs[12]
    rows = x_refs[0].shape[0]
    wide = hiddens[0].shape[1]
    count = out_ref.shape[0]
    tile = 256

    def step(t, carry):
        where = pl.ds(pl.multiple_of(dp_ref[s] * count + t * tile, tile), tile)

        def product(lefts, rights):
            total = None
            for n, left in enumerate(lefts):
                part = slice((n % 2) * rows, (n % 2 + 1) * rows)
                term = dot(left[:, where], rights[n // 2][part, :], TN)
                total = term if total is None else total + term
            return total.astype(BF16)

        store_blocks(out_ref, product(x_refs, dpairs), t * tile, unit, slot_ref, 0)
        store_blocks(out_ref, product(cot_refs, hiddens), t * tile, unit, slot_ref, 2 * wide)
        return carry

    lax.fori_loop(0, count // tile, step, 0)


def ffn_grads(seconds, cotangents, hiddens, dpairs, owners, slots, s, count, unit):
    wide = hiddens[0].shape[1]
    rows = 4 * seconds[0].shape[0]
    return call(
        functools.partial(ffn_grads_kernel, s, unit),
        [*seconds, *cotangents, *hiddens, *dpairs],
        jax.ShapeDtypeStruct((count, 3 * wide), BF16),
        "ffn_grads",
        6 * rows * count * wide,
        2 * (2 * rows * count + 3 * rows * wide + 3 * count * wide),
        smem=[owners, slots],
    )


def attn_grads_kernel(kinds, s, unit, bit_ref, dp_ref, slot_ref, *refs):
    at, pairs = 0, []
    for parts in kinds:
        pairs.append((refs[at : at + parts], refs[at + parts]))
        at += parts + 1
    out_ref = refs[at]
    count = out_ref.shape[0]
    tile = 256

    def step(t, carry):
        where = pl.ds(pl.multiple_of(dp_ref[s] * count + t * tile, tile), tile)
        column = 0
        for lefts, right in pairs:
            if len(lefts) == 1:
                total = dot(lefts[0][:, where], right[...], TN)
            else:
                rows = lefts[0].shape[0]
                total = dot(lefts[0][:, where], right[at_block(bit_ref[0], rows), :], TN) + dot(
                    lefts[1][:, where], right[at_block(1 - bit_ref[0], rows), :], TN
                )
            store_blocks(out_ref, total.astype(BF16), t * tile, unit, slot_ref, column)
            column += right.shape[1]
        return carry

    lax.fori_loop(0, count // tile, step, 0)


def attn_grads_block(pairs, bit, owners, slots, s, count, unit):
    kinds = tuple(len(lefts) for lefts, _ in pairs)
    width = sum(right.shape[1] for _, right in pairs)
    rows = pairs[0][1].shape[0]
    return call(
        functools.partial(attn_grads_kernel, kinds, s, unit),
        [x for lefts, right in pairs for x in (*lefts, right)],
        jax.ShapeDtypeStruct((count, width), BF16),
        "attn_grads",
        2 * rows * width * count,
        2 * (rows * count + rows * width + count * width),
        smem=[bit, owners, slots],
    )


SCALE = HEAD_DIM**-0.5
SCALE_LOG2 = SCALE * math.log2(math.e)


def forward_kernel(pieces, order_ref, rank_ref, q_ref, ks_ref, vs_ref, *refs):
    kp_refs, vp_refs = refs[:pieces], refs[pieces : 2 * pieces]
    o_ref, lse_ref = refs[2 * pieces :]
    q = q_ref[...]
    size = q.shape[0]
    prompt = pl.program_id(1) == 0
    low_lane = lax.broadcasted_iota(jnp.int32, q.shape, 1) < HEAD_DIM
    causal = lax.broadcasted_iota(jnp.int32, (size, size), 0) >= lax.broadcasted_iota(
        jnp.int32, (size, size), 1
    )
    outs = []
    for head in range(2):
        own = low_lane if head == 0 else jnp.logical_not(low_lane)
        qh = jnp.where(own, q, jnp.zeros_like(q))
        raw = [jnp.where(causal, dot(qh, ks_ref[...], NT), MASKED)]
        for s in range(pieces):
            hidden = jnp.logical_and(prompt, rank_ref[s] >= rank_ref[0])
            raw.append(dot(qh, kp_refs[s][...], NT) + jnp.where(hidden, MASKED, 0.0))
        top = raw[0]
        for r in raw[1:]:
            top = jnp.maximum(top, r)
        top = jnp.max(top, axis=-1, keepdims=True) * SCALE_LOG2
        sums, acc = None, None
        for s, r in enumerate(raw):
            e = jnp.exp2(r * SCALE_LOG2 - top)
            v = vs_ref if s == 0 else vp_refs[s - 1]
            term = dot(e.astype(BF16), v[...], NN)
            sums = e if sums is None else sums + e
            acc = term if acc is None else acc + term
        total = jnp.sum(sums, axis=-1, keepdims=True)
        outs.append((acc / total, top + jnp.log2(total)))
    o_ref[...] = jnp.where(low_lane, outs[0][0], outs[1][0]).astype(BF16)
    lse_ref[...] = jnp.where(low_lane, outs[0][1], outs[1][1])


def backward_kernel(
    pieces, order_ref, rank_ref, q_ref, ks_ref, vs_ref, o_ref, lse_ref, do_ref, cos_ref, sin_ref, *refs
):
    kp_refs, vp_refs = refs[:pieces], refs[pieces : 2 * pieces]
    dq_ref, dks_ref, dvs_ref = refs[2 * pieces : 2 * pieces + 3]
    piece_refs = refs[2 * pieces + 3 : 3 * pieces + 3]
    acc_ref = refs[-1]
    pair, step = pl.program_id(0), pl.program_id(1)
    prompt = step == 0
    q, do = q_ref[...], do_ref[...]
    size = q.shape[0]
    low_lane = lax.broadcasted_iota(jnp.int32, q.shape, 1) < HEAD_DIM
    causal = lax.broadcasted_iota(jnp.int32, (size, size), 0) >= lax.broadcasted_iota(
        jnp.int32, (size, size), 1
    )
    product = do.astype(F32) * o_ref[...].astype(F32)
    lse = lse_ref[...]
    dq_heads = []
    dk_all = [None] * (pieces + 1)
    dv_all = [None] * (pieces + 1)
    for head in range(2):
        own = low_lane if head == 0 else jnp.logical_not(low_lane)
        qh = jnp.where(own, q, jnp.zeros_like(q))
        doh = jnp.where(own, do, jnp.zeros_like(do))
        delta = jnp.sum(jnp.where(own, product, 0.0), axis=-1, keepdims=True)
        log_sum = lse[:, head * HEAD_DIM : head * HEAD_DIM + 1]
        dq = None
        for s in range(pieces + 1):
            k = (ks_ref if s == 0 else kp_refs[s - 1])[...]
            v = (vs_ref if s == 0 else vp_refs[s - 1])[...]
            raw = dot(qh, k, NT)
            if s == 0:
                raw = jnp.where(causal, raw, MASKED)
            else:
                hidden = jnp.logical_and(prompt, rank_ref[s - 1] >= rank_ref[0])
                raw = raw + jnp.where(hidden, MASKED, 0.0)
            prob = jnp.exp2(raw * SCALE_LOG2 - log_sum)
            ds = (prob * (dot(doh, v, NT) - delta)).astype(BF16)
            term = dot(ds, k, NN)
            dq = term if dq is None else dq + term
            dk = dot(ds, qh, TN)
            dv = dot(prob.astype(BF16), doh, TN)
            dk_all[s] = dk if dk_all[s] is None else dk_all[s] + dk
            dv_all[s] = dv if dv_all[s] is None else dv_all[s] + dv
        dq_heads.append(dq)
    dq = jnp.where(low_lane, dq_heads[0], dq_heads[1]) * SCALE
    cosine, sine = cos_ref[...], sin_ref[...]
    dq_ref[...] = (dq * cosine - half_swap(dq) * sine).astype(BF16)
    dks_ref[...] = dk_all[0] * SCALE
    dvs_ref[...] = dv_all[0]
    for s in range(pieces):
        both = jnp.concatenate([dk_all[s + 1] * SCALE, dv_all[s + 1]], axis=1)
        at = slice(s * size, (s + 1) * size)

        @pl.when(prompt)
        def _(both=both, at=at):
            acc_ref[at, :] = both

        @pl.when(jnp.logical_not(prompt))
        def _(both=both, at=at):
            acc_ref[at, :] += both

    @pl.when(step == pl.num_programs(1) - 1)
    def _():
        wide = piece_refs[0].shape[1] // 2
        k_at = pl.ds(pl.multiple_of(pair * LANES, LANES), LANES)
        v_at = pl.ds(pl.multiple_of(wide + pair * LANES, LANES), LANES)
        for s in range(pieces):
            both = acc_ref[s * size : (s + 1) * size, :]
            piece_refs[s][:, k_at] = both[:, :LANES].astype(piece_refs[s].dtype)
            piece_refs[s][:, v_at] = both[:, LANES:].astype(piece_refs[s].dtype)


def merge_kernel(others, mine_ref, dk_ref, dv_ref, own_ref, *refs):
    got = refs[:others]
    cos_ref, sin_ref, dk_out, dv_out = refs[others:]
    width = dk_ref.shape[1]
    cosine, sine = cos_ref[...], sin_ref[...]

    def write(dk, dv):
        for at in range(0, width, LANES):
            part = dk[:, at : at + LANES]
            dk_out[:, at : at + LANES] = (part * cosine - half_swap(part) * sine).astype(BF16)
        dv_out[...] = dv.astype(BF16)

    mine = pl.program_id(0) == mine_ref[0]

    @pl.when(mine)
    def _():
        extra = own_ref[...]
        for ref in got:
            extra = extra + ref[...].astype(F32)
        write(dk_ref[...] + extra[:, :width], dv_ref[...] + extra[:, width:])

    @pl.when(jnp.logical_not(mine))
    def _():
        write(dk_ref[...], dv_ref[...])


def merge_keys(mine, dkey, dvalue, own, got, cosine, sine):
    rows, width = dkey.shape
    row = lambda i, mine: (i, 0)
    full = lambda i, mine: (0, 0)
    return pl.pallas_call(
        functools.partial(merge_kernel, len(got)),
        grid_spec=pltpu.PrefetchScalarGridSpec(
            num_scalar_prefetch=1,
            grid=(rows // CLEN,),
            in_specs=[pl.BlockSpec((CLEN, width), row)] * 2
            + [pl.BlockSpec((CLEN, 2 * width), full)] * (1 + len(got))
            + [pl.BlockSpec((CLEN, LANES), row)] * 2,
            out_specs=[pl.BlockSpec((CLEN, width), row)] * 2,
        ),
        out_shape=[jax.ShapeDtypeStruct((rows, width), BF16)] * 2,
        compiler_params=pltpu.CompilerParams(vmem_limit_bytes=VMEM_LIMIT),
        cost_estimate=cost(8 * rows * width, 16 * rows * width, 0),
        name="merge_keys",
    )(mine, dkey, dvalue, own, *got, cosine, sine)


def attention_specs(pieces, key_pairs):
    own = pl.BlockSpec((CLEN, LANES), lambda h, j, order, rank: (order[j], h))
    own_value = pl.BlockSpec((CLEN, LANES), lambda h, j, order, rank: (order[j], key_pairs + h))
    key = pl.BlockSpec((CLEN, LANES), lambda h, j, order, rank: (0, h))
    value = pl.BlockSpec((CLEN, LANES), lambda h, j, order, rank: (0, key_pairs + h))
    trig = pl.BlockSpec((CLEN, LANES), lambda h, j, order, rank: (order[j], 0))
    prompt = pl.BlockSpec((CLEN, 2 * key_pairs * LANES), lambda h, j, order, rank: (0, 0))
    return own, own_value, key, value, trig, prompt


def attention_forward(order, rank, query, kv, prompts):
    rows, width = query.shape
    pieces, pairs = len(prompts), width // LANES
    own, own_value, key, value, _, _ = attention_specs(pieces, pairs)
    scores = rows * (pieces + 1) * CLEN * (width // HEAD_DIM)
    return pl.pallas_call(
        functools.partial(forward_kernel, pieces),
        grid_spec=pltpu.PrefetchScalarGridSpec(
            num_scalar_prefetch=2,
            grid=(pairs, rows // CLEN),
            in_specs=[own, own, own_value] + [key] * pieces + [value] * pieces,
            out_specs=[own, own],
        ),
        out_shape=[jax.ShapeDtypeStruct((rows, width), BF16), jax.ShapeDtypeStruct((rows, width), F32)],
        compiler_params=pltpu.CompilerParams(vmem_limit_bytes=VMEM_LIMIT),
        cost_estimate=cost(
            16 * scores * HEAD_DIM, 16 * rows * width, scores
        ),
        name="attend",
    )(order, rank, query, kv, kv, *prompts, *prompts)


def attention_backward(order, rank, query, kv, mixed, lse, dmixed, cosine, sine, prompts):
    rows, width = query.shape
    pieces, pairs = len(prompts), width // LANES
    own, own_value, key, value, trig, prompt = attention_specs(pieces, pairs)
    scores = rows * (pieces + 1) * CLEN * (width // HEAD_DIM)
    return pl.pallas_call(
        functools.partial(backward_kernel, pieces),
        grid_spec=pltpu.PrefetchScalarGridSpec(
            num_scalar_prefetch=2,
            grid=(pairs, rows // CLEN),
            in_specs=[own, own, own_value, own, own, own] + [trig] * 2 + [key] * pieces + [value] * pieces,
            out_specs=[own, own, own] + [prompt] * pieces,
            scratch_shapes=[pltpu.VMEM((pieces * CLEN, 2 * LANES), F32)],
        ),
        out_shape=[
            jax.ShapeDtypeStruct((rows, width), BF16),
            jax.ShapeDtypeStruct((rows, width), F32),
            jax.ShapeDtypeStruct((rows, width), F32),
        ]
        + [jax.ShapeDtypeStruct((CLEN, 2 * width), BF16 if s else F32) for s in range(pieces)],
        compiler_params=pltpu.CompilerParams(vmem_limit_bytes=VMEM_LIMIT),
        cost_estimate=cost(
            40 * scores * HEAD_DIM, 32 * rows * width, scores
        ),
        name="attend_back",
    )(order, rank, query, kv, kv, mixed, lse, dmixed, cosine, sine, *prompts, *prompts)


def normalize(values):
    factor = lax.rsqrt(jnp.mean(values * values, axis=-1, keepdims=True) + EPS)
    return (values * factor, factor)


def rope_tables(where):
    half = HEAD_DIM // 2
    freqs = ROPE_BASE ** (-(jnp.arange(half).astype(F32) * 2.0) / HEAD_DIM)
    angles = where.astype(F32)[:, None] * freqs[None, :]
    cosine, sine = jnp.cos(angles), jnp.sin(angles)
    return (
        jnp.concatenate([cosine] * 4, axis=1),
        jnp.concatenate([-sine, sine, -sine, sine], axis=1),
    )


def body(
    tokens,
    attn_gain,
    query_weight,
    key_weight,
    value_weight,
    out_weight,
    ffn_gain,
    gate_weight,
    up_weight,
    down_weight,
    seq_ids,
    positions,
    out_grad,
):
    rows, width = tokens.shape
    head_width = query_weight.shape[1]
    own_rows, ffn_width = gate_weight.shape
    half_units = ffn_width // 2
    chunk = half_units // FFN_CHUNKS
    half = rows // 2
    dp_count = lax.axis_size("dp")
    ctx_count = lax.axis_size("hi") * 2
    tp_count = lax.axis_size("tp")
    dp_index = lax.axis_index("dp")
    parity = lax.axis_index("lo")
    ctx_index = lax.axis_index("hi") * 2 + parity
    tp_index = lax.axis_index("tp")
    bit = tp_index & 1
    bit_ref = bit.astype(jnp.int32)[None]

    def row_half(values, which=bit):
        return lax.dynamic_slice_in_dim(values, which * half, half)

    def assemble(mine, other):
        first = jnp.where(bit == 0, mine, other)
        last = jnp.where(bit == 0, other, mine)
        return jnp.concatenate([first, last], axis=0)

    slots = jnp.arange(dp_count * ctx_count, dtype=jnp.int32)

    def places_of(order_k):
        slot_k = jnp.array(order_k, jnp.int32)[slots % ctx_count]
        return (
            lax.rem(dp_index + slots // ctx_count, dp_count) * ctx_count + (ctx_index ^ slot_k)
        ).astype(jnp.int32)

    def slots_of(order_k):
        slot_of = jnp.array([order_k.index(k) for k in range(ctx_count)], jnp.int32)
        return slot_of[ctx_index ^ jnp.arange(ctx_count, dtype=jnp.int32)]

    attn_order, ffn_order = (0, 2, 1, 3), (0, 1, 2, 3)
    places, places_ffn = places_of(attn_order), places_of(ffn_order)
    slots_attn, slots_ffn = slots_of(attn_order), slots_of(ffn_order)
    owners = lax.rem(dp_index + jnp.arange(dp_count, dtype=jnp.int32), dp_count).astype(jnp.int32)
    near_rows = width // dp_count

    def over_dp(blocks):
        return blocks + [turn(x, "dp", -s) for s in range(1, dp_count) for x in blocks]

    kv_weight = jnp.concatenate([key_weight, value_weight], axis=1)
    kv_one, kv_two = swap(kv_weight, "lo"), swap(kv_weight, "hi")
    kv_three = swap(kv_two, "lo")
    kv_stack = over_dp([kv_weight, kv_two, kv_one, kv_three])
    qo_weight = after(jnp.concatenate([query_weight, out_weight], axis=1), kv_three)
    qo_even = jnp.concatenate([qo_weight, swap(qo_weight, "hi")], axis=0)
    qo_odd = swap(qo_even, "lo")
    qo_stack = over_dp([qo_even, qo_odd])

    def ffn_columns(f, which):
        first = which * half_units + f * chunk
        return jnp.concatenate(
            [
                lax.dynamic_slice_in_dim(w, first, chunk, 1)
                for w in (gate_weight, up_weight, down_weight)
            ],
            axis=1,
        )

    def ffn_sends(f, *needed):
        keep, give = after((ffn_columns(f, parity), ffn_columns(f, 1 - parity)), *needed)
        near = jnp.concatenate([keep, swap(give, "lo")], axis=0)
        return near, swap(keep, "hi"), give

    def ffn_stack(near, far):
        stack = [near, far]
        for s in range(1, dp_count):
            stack += [turn(near, "dp", -s), turn(far, "dp", -s)]
        return place_rows(stack, places_ffn)

    group_seq = seq_ids[0].reshape(ctx_count, rows // CLEN, CLEN)[:, :, 0]
    group_pos = positions[0].reshape(ctx_count, rows // CLEN, CLEN)[:, :, 0]
    prompt_at = jnp.argmax(group_seq == 0, axis=1).astype(jnp.int32)
    prompt_rank = jnp.sum(jnp.where(group_seq == 0, group_pos, 0), axis=1).astype(jnp.int32)
    rank = prompt_rank[ctx_index ^ jnp.arange(ctx_count, dtype=jnp.int32)]
    mine = prompt_at[ctx_index]
    pieces = jnp.arange(rows // CLEN, dtype=jnp.int32)
    order = jnp.where(pieces == 0, mine, jnp.where(pieces <= mine, pieces - 1, pieces))
    own_pos = lax.dynamic_slice_in_dim(positions[0], ctx_index * rows, rows)
    cosine, sine = rope_tables(own_pos)

    gain_one = attn_gain[None].astype(F32)
    gain_two = ffn_gain[None].astype(F32)
    first_norm, first_scale = normalize(tokens.astype(F32))
    first = low(first_norm * gain_one)

    kv = project(
        [first], kv_stack, places, bit_ref, 0, 2 * head_width, cosine, sine, head_width
    )
    prompt_own = lax.dynamic_slice_in_dim(kv, mine * CLEN, CLEN)
    prompts = [prompt_own] + [swap(prompt_own, CTX, k) for k in range(1, ctx_count)]
    near_one, two_one, give_one = ffn_sends(0, kv_three)
    query = project(
        [after(first, two_one, near_one)],
        qo_stack,
        places,
        bit_ref,
        0,
        head_width,
        cosine,
        sine,
        head_width,
    )
    mixed, lse = attention_forward(order, rank, query, kv, prompts)
    three_one = swap(after(give_one, *prompts[1:]), CTX, 3)
    near_two, two_two, give_two = ffn_sends(1, *prompts[1:])
    three_two = swap(give_two, CTX, 3)
    ffn_weights = [
        ffn_stack(near_one, jnp.concatenate([two_one, three_one], axis=0)),
        ffn_stack(near_two, jnp.concatenate([two_two, three_two], axis=0)),
    ]

    kept, given = project_back([mixed], ((0, head_width),), [qo_stack], places, bit_ref)
    mixed_out = low(add(kept, swap(given, "tp")))
    mixed_far = after(swap(mixed_out, "tp", 2), three_one, two_two)
    middle = row_half(tokens).astype(F32) + add(mixed_out, mixed_far)
    second_norm, second_scale = normalize(middle)
    second_half = low(second_norm * gain_two)

    cotangent_half = row_half(out_grad)
    cotangent_far = swap(after(cotangent_half, prompts[1]), "lo")
    cotangents = [
        [cotangent_half, row_half(out_grad, 1 - bit)],
        [cotangent_far, swap(cotangent_far, "tp")],
    ]
    second_far = swap(second_half, "lo")
    near = [second_half, swap(second_half, "tp")]
    made = [[ffn(near, cotangents[0], [w]) for w in ffn_weights]]
    second_far = after(second_far, made[0][0][0])
    far = [second_far, swap(second_far, "tp")]
    made.append([ffn(far, cotangents[1], [w]) for w in ffn_weights])
    seconds = [near, far]
    hiddens = [[m[0] for m in side] for side in made]
    dpairs = [[m[1] for m in side] for side in made]
    gate_spans = tuple((f, 0, f, 0, 2 * chunk) for f in range(FFN_CHUNKS))
    down_spans = tuple((f, 0, f, 2 * chunk, chunk) for f in range(FFN_CHUNKS))

    def collect(near, far):
        far = low(add(far[0], swap(far[1], "tp")))
        near = low(add(near[0], swap(near[1], "tp")))
        return low(add(near, swap(far, "lo")))

    dsecond_far = ffn_back(dpairs[1], ffn_weights, gate_spans)
    dsecond_near = ffn_back(dpairs[0], ffn_weights, gate_spans)
    dsecond = collect(dsecond_near, dsecond_far)
    dsecond = add(dsecond, swap(dsecond, "tp", 2))

    lefts, left_cots = after(
        (seconds[0] + seconds[1], cotangents[0] + cotangents[1]), *dsecond_near, *dsecond_far
    )
    ffn_blocks = []
    for f in range(FFN_CHUNKS):

        def part(s, f=f):
            return ffn_grads(
                lefts,
                left_cots,
                [side[f] for side in hiddens],
                [side[f] for side in dpairs],
                owners,
                slots_ffn,
                s,
                near_rows,
                own_rows,
            )

        sent = [turn(part(s), "dp", s) for s in range(1, dp_count)]
        ffn_blocks.append((part(0), sent))

    def ffn_scatter(own, got, first, second, third):
        total = own
        for part in got:
            total = add(total, after(part, first))
        total = low(total)
        pair = add(total[: 2 * own_rows], after(swap(total[2 * own_rows :], "hi"), second))
        kept = pair[:own_rows]
        got = after(swap(low(pair[own_rows:]), "lo"), third).astype(F32)
        return (jnp.where(parity == 0, kept, got), jnp.where(parity == 0, got, kept))

    gain_two_grad = jnp.sum(dsecond * second_norm, axis=0)
    scaled_two = dsecond * gain_two
    dmiddle = cotangent_half.astype(F32) + second_scale * (
        scaled_two - second_norm * jnp.mean(scaled_two * second_norm, axis=-1, keepdims=True)
    )
    dmiddle_low = [low(dmiddle), swap(low(dmiddle), "tp")]
    dmixed = project(dmiddle_low, qo_stack, places, bit_ref, head_width, head_width, cosine, sine, 0)
    dquery_low, dkey_own, dvalue_own, dprompt_own, *dprompts = attention_backward(
        order, rank, query, kv, mixed, lse, dmixed, cosine, sine, prompts
    )
    got = [swap(piece, CTX, k + 1) for k, piece in enumerate(dprompts)]
    dkey_low, dvalue_low = merge_keys(
        mine[None], dkey_own, dvalue_own, dprompt_own, got, cosine, sine
    )

    def attn_grads(pairs):
        parts = [
            attn_grads_block(pairs, bit_ref, owners, slots_attn, s, near_rows, own_rows)
            for s in range(dp_count)
        ]
        total = parts[0]
        for s in range(1, dp_count):
            total = add(total, turn(parts[s], "dp", s))
        total = low(total)
        pair = add(total[: 2 * own_rows], swap(total[2 * own_rows :], "lo"))
        return pair[:own_rows] + swap(low(pair[own_rows:]), "hi").astype(F32)

    early = attn_grads([(dmiddle_low, mixed), ([first], dquery_low)])
    late = attn_grads([([first], dkey_low), ([first], dvalue_low)])
    ffn_sums = [
        ffn_scatter(*ffn_blocks[0], dmiddle, dquery_low, dkey_low),
        ffn_scatter(*ffn_blocks[1], dquery_low, dkey_low, dkey_low),
    ]

    kept, given = project_back(
        [dquery_low, dkey_low, dvalue_low],
        ((0, 0), (1, 0), (1, head_width)),
        [qo_stack, kv_stack],
        places,
        bit_ref,
    )
    norm_half, norm_other = row_half(first_norm), row_half(first_norm, 1 - bit)
    gain_one_grad = jnp.sum(kept.astype(F32) * norm_half, axis=0) + jnp.sum(
        given.astype(F32) * norm_other, axis=0
    )
    dfirst = low(add(kept, swap(given, "tp")))
    dfirst = add(dfirst, swap(dfirst, "tp", 2))
    scaled_one = dfirst * gain_one
    dinputs = dmiddle + row_half(first_scale) * (
        scaled_one - norm_half * jnp.mean(scaled_one * norm_half, axis=-1, keepdims=True)
    )

    share = width // tp_count
    here = tp_index // 2

    def wide_part(values, which):
        return lax.dynamic_slice_in_dim(values, which * 2 * share, 2 * share, 1)

    def deliver(wide):
        kept = lax.dynamic_slice_in_dim(wide, bit * share, share, 1)
        given = lax.dynamic_slice_in_dim(wide, (1 - bit) * share, share, 1)
        return assemble(kept, swap(given, "tp"))

    in_grad = deliver(low(wide_part(dinputs, here)))

    hiddens = after(hiddens, dmixed)
    ffn_out = collect(
        ffn_back(hiddens[0], ffn_weights, down_spans),
        ffn_back(hiddens[1], ffn_weights, down_spans),
    )
    ffn_out = add(wide_part(ffn_out, here), swap(wide_part(ffn_out, 1 - here), "tp", 2))
    block_out = deliver(low(wide_part(middle, here) + ffn_out))

    gains = jnp.stack([gain_one_grad, jnp.where(here == 0, gain_two_grad, 0.0)])
    for axis in ("tp", "lo", "hi", "dp"):
        mask = 1
        while mask < lax.axis_size(axis):
            gains = gains + swap(gains, axis, mask)
            mask *= 2
    part = width // (dp_count * ctx_count)
    gains = lax.dynamic_slice_in_dim(gains, (dp_index * ctx_count + ctx_index) * part, part, 1)

    ffn_final = [
        jnp.concatenate(
            [
                ffn_sums[f][side][:, i * chunk : (i + 1) * chunk]
                for side in range(2)
                for f in range(FFN_CHUNKS)
            ],
            axis=1,
        )
        for i in range(3)
    ]
    return (
        block_out,
        in_grad,
        gains[0],
        early[:, head_width:],
        late[:, :head_width],
        late[:, head_width:],
        early[:, :head_width],
        gains[1],
        ffn_final[0],
        ffn_final[1],
        ffn_final[2],
    )


def solution(mesh):
    dp, ctx, tp = (mesh.shape[name] for name in ("dp", "ctx", "tp"))
    split_mesh = Mesh(mesh.devices.reshape(dp, ctx // 2, 2, tp), ("dp", "hi", "lo", "tp"))
    every = ("dp",) + CTX
    split = P(every, "tp")
    rows = P(every, None)
    vector = P(every)
    return jax.shard_map(
        body,
        mesh=split_mesh,
        in_specs=(rows, P(), split, split, split, split, P(), split, split, split)
        + (P("dp", None), P("dp", None), rows),
        out_specs=(split, split, vector, split, split, split, split, vector, split, split, split),
        check_vma=False,
    )
```

time: 1130 us -> 885 us (0.78)
  waiting for transfers between devices: 504 us -> 370 us
  local copies, waits for them, and re-layouts: 161 us -> 72.4 us
  starting transfers between devices: 65.9 us -> 135 us
  other arithmetic: 129 us -> 63.4 us
  matrix products: 50.2 us -> 0 us
  Pallas kernels: 192 us -> 232 us
  between operations: 16.3 us -> 3.37 us
    ppermute x18 -> x14, waiting for transfers between devices: 158 us -> 54.2 us  [turn(): lax.ppermute(values, axis, [(i, (i + shift) % count) for i in range(count)])]
    ppermute x33 -> x50, starting transfers between devices: 43.4 us -> 128 us  [swap(): return lax.ppermute(values, axis, [(i, i ^ mask) for i in range(count)])]
    all_gather x4 -> x0, waiting for transfers between devices: 67.6 us -> none  [gather_rows(): return gather_dp(lax.all_gather(weight, 'ctx', axis=0, tiled=True))]
    rev x4 -> x0, local copies, waits for them, and re-layouts: 59.3 us -> none  [flip(): other = split[..., ::-1, :].reshape(values.shape)]
    ppermute x33 -> x50, waiting for transfers between devices: 261 us -> 316 us  [swap(): return lax.ppermute(values, axis, [(i, i ^ mask) for i in range(count)])]
    dot_general x22 -> x0, matrix products: 50.2 us -> none  [the longest x20 47 us: row_grads(): jnp.einsum('tc,tf->cf', left[:, s * depth:(s + 1) * depth], right, prefer...]
    pallas_call x13 -> x23, Pallas kernels: 120 us -> 164 us  [call(): pl.pallas_call(kernel, in_specs=[SMEM] * len(smem) + [VMEM] * len(operand...]
    reshape x8 -> x0, local copies, waits for them, and re-layouts: 31.3 us -> none  [the longest x4 15.9 us: flip(): other = split[..., ::-1, :].reshape(values.shape)]
  transfers between devices with their start and end apart: 57 -> 64, of which waited for: 24 -> 28; matrix products, arithmetic and copies ran while one was open for 28% -> 10% of each run, Pallas kernels for 17% -> 20%
where the time goes in v3:
time: 885 us; the launch traced here: 876 us
  waiting for transfers between devices  370 us (42%)
  Pallas kernels  232 us (26%)
  starting transfers between devices  135 us (15%)
  local copies, waits for them, and re-layouts  72.4 us (8%)
  other arithmetic  63.4 us (7%)
    ppermute x50, waiting for transfers between devices, swap(): return lax.ppermute(values, axis, [(i, i ^ mask) for i in range(count)])  316 us
    pallas_call x23, Pallas kernels, call(): pl.pallas_call(kernel, in_specs=[SMEM] * len(smem) + [VMEM] * len(operand...  164 us
    ppermute x50, starting transfers between devices, swap(): return lax.ppermute(values, axis, [(i, i ^ mask) for i in range(count)])  128 us
    ppermute x14, waiting for transfers between devices, turn(): lax.ppermute(values, axis, [(i, (i + shift) % count) for i in range(count)])  54.2 us
    unnamed x257, local copies, waits for them, and re-layouts  49.7 us
    pallas_call x1, Pallas kernels, attention_backward(): pl.pallas_call(functools.partial(backward_kernel, pieces), grid_spec=pltp...  44.7 us
    convert_element_type x14, other arithmetic, low(): return values.astype(BF16)  24.6 us
    pallas_call x1, Pallas kernels, attention_forward(): pl.pallas_call(functools.partial(forward_kernel, pieces), grid_spec=pltpu...  21.1 us
  transfers between devices with their start and end apart: 64, of which 28 were waited for; matrix products, arithmetic and copies ran while one was open for 10% of the time, Pallas kernels for 20%

profile of v3, /device:TPU:1, one launch (start us, length us, event | category | flops | bytes accessed | tf_op | source)
XLA Modules:
  0.0 875.9 jit_solution(9162015035081666884)
XLA Ops:
  17.1 12.3 %collective-permute-done.refs_2_.refs_8_ = bf16[256,1024]{1,0:T(8,128)(2,1)} collective-permute-done((bf16[256,1024]{1,0:T(8,128)(2,1)}, bf16[256,1024]{1,0:T(8,128)(2,1)}, u32[]{:S(2)}, u32[]{:S(2)}) %collective-permute-start) | collective-permute-done | bytes 524320 | tf_op jit(solution)/shard_map/ppermute | solution.py:28
  49.0 17.5 %collective-permute-done.4 = bf16[256,1024]{1,0:T(8,128)(2,1)} collective-permute-done((bf16[256,1024]{1,0:T(8,128)(2,1)}, bf16[256,1024]{1,0:T(8,128)(2,1)}, u32[]{:S(2)}, u32[]{:S(2)}) %collective-permute-start.4) | collective-permute-done | bytes 524320 | tf_op jit(solution)/shard_map/ppermute | solution.py:28
  95.2 12.0 %collective-permute-done.5.refs_2_.refs_3_.refs_4_ = bf16[512,1024]{1,0:T(8,128)(2,1)} collective-permute-done((bf16[512,1024]{1,0:T(8,128)(2,1)}, bf16[512,1024]{1,0:T(8,128)(2,1)}, u32[]{:S(2)}, u32[]{:S(2)}) %collective-permute-start.5) | collective-permute-done | bytes 1048608 | tf_op jit(solution)/shard_map/ppermute | solution.py:28
  132.0 19.1 %collective-permute-done.7.refs_4_.refs_5_.refs_6_ = bf16[512,1024]{1,0:T(8,128)(2,1)} collective-permute-done((bf16[512,1024]{1,0:T(8,128)(2,1)}, bf16[512,1024]{1,0:T(8,128)(2,1)}, u32[]{:S(2)}, u32[]{:S(2)}) %collective-permute-start.7) | collective-permute-done | bytes 1048608 | tf_op jit(solution)/shard_map/ppermute | solution.py:33
  158.8 21.1 %attend.1 = (bf16[768,512]{1,0:T(8,128)(2,1)S(1)}, f32[768,512]{1,0:T(8,128)S(1)}) custom-call(s32[3]{0:T(128)S(1)} %compare_select_fusion.7.order_ref, s32[4]{0:T(128)S(1)} %gather_fusion.1, bf16[768,512]{1,0:T(8,128)(2,1)S(1)} %project.3.q_ref, bf16[768,1024]{1,0:T(8,128)(2,1)S(1)} %copy-done.15, bf16[768,1024]{1,0:T(8,128)(2,1)S(1)} %copy-done.15, ...), custom_call_target="tpu_custom_call" | custom-call | flops 503316480 | bytes 393216 | tf_op jit(solution)/shard_map/attend/pallas_call | solution.py:577
  210.6 11.8 %collective-permute-done.18 = bf16[256,1536]{1,0:T(8,128)(2,1)S(1)} collective-permute-done((bf16[256,1536]{1,0:T(8,128)(2,1)}, bf16[256,1536]{1,0:T(8,128)(2,1)S(1)}, u32[]{:S(2)}, u32[]{:S(2)}) %collective-permute-start.18) | collective-permute-done | bytes 786464 | tf_op jit(solution)/shard_map/ppermute | solution.py:28
  222.4 48.2 %collective-permute-start.23 = (bf16[256,1536]{1,0:T(8,128)(2,1)S(1)}, bf16[256,1536]{1,0:T(8,128)(2,1)S(1)}, u32[]{:S(2)}, u32[]{:S(2)}) collective-permute-start(bf16[256,1536]{1,0:T(8,128)(2,1)S(1)} %pad_maximum_fusion.6), channel_id=1, source_target_pairs={{0,4},{4,0},{1,5},{5,1},{2,6},{6,2},{3,7},{7,3},{8,12},{12,8},{9,1... | collective-permute-start | bytes 2359304 | tf_op jit(solution)/shard_map/ppermute | solution.py:28
  271.6 15.7 %collective-permute-done.19 = bf16[256,1536]{1,0:T(8,128)(2,1)S(1)} collective-permute-done((bf16[256,1536]{1,0:T(8,128)(2,1)S(1)}, bf16[256,1536]{1,0:T(8,128)(2,1)S(1)}, u32[]{:S(2)}, u32[]{:S(2)}) %collective-permute-start.19) | collective-permute-done | bytes 786464 | tf_op jit(solution)/shard_map/ppermute | solution.py:28
  295.9 8.5 collective-permute-done.23
  308.8 29.3 %collective-permute-done.29.refs_2_.refs_6_ = bf16[384,2048]{1,0:T(8,128)(2,1)} collective-permute-done((bf16[384,2048]{1,0:T(8,128)(2,1)S(1)}, bf16[384,2048]{1,0:T(8,128)(2,1)}, u32[]{:S(2)}, u32[]{:S(2)}) %collective-permute-start.29) | collective-permute-done | bytes 1572896 | tf_op jit(solution)/shard_map/ppermute | solution.py:28
  343.4 9.7 %ffn.4 = (bf16[768,512]{1,0:T(8,128)(2,1)S(1)}, bf16[768,1024]{1,0:T(8,128)(2,1)S(1)}) custom-call(bf16[384,2048]{1,0:T(8,128)(2,1)} %multiply_convert_fusion.1.refs_0_, bf16[384,2048]{1,0:T(8,128)(2,1)} %collective-permute-done.20.refs_1_, bf16[384,2048]{1,0:T(8,128)(2,1)S(1)} %get-tuple-element.121.refs_2_.refs_4_, bf16[384,2048]{1,0:T(8,128)(2,1)S(1)} %copy-done.4, ...), custom_call_target="tpu_custom_call" | custom-call | flops 301989888 | bytes 933888 | tf_op jit(solution)/shard_map/ffn/pallas_call | solution.py:80
  354.3 17.5 %collective-permute-done.27.refs_0_.refs_2_ = bf16[384,2048]{1,0:T(8,128)(2,1)} collective-permute-done((bf16[384,2048]{1,0:T(8,128)(2,1)}, bf16[384,2048]{1,0:T(8,128)(2,1)}, u32[]{:S(2)}, u32[]{:S(2)}) %collective-permute-start.27) | collective-permute-done | bytes 1572896 | tf_op jit(solution)/shard_map/ppermute | solution.py:28
  373.9 15.1 %collective-permute-done.26.refs_3_ = bf16[512,1536]{1,0:T(8,128)(2,1)S(1)} collective-permute-done((bf16[512,1536]{1,0:T(8,128)(2,1)S(1)}, bf16[512,1536]{1,0:T(8,128)(2,1)S(1)}, u32[]{:S(2)}, u32[]{:S(2)}) %collective-permute-start.26) | collective-permute-done | bytes 1572896 | tf_op jit(solution)/shard_map/ppermute | solution.py:33
  394.0 9.7 %ffn.6 = (bf16[768,512]{1,0:T(8,128)(2,1)S(1)}, bf16[768,1024]{1,0:T(8,128)(2,1)S(1)}) custom-call(bf16[384,2048]{1,0:T(8,128)(2,1)} %collective-permute-done.27.refs_0_.refs_2_, bf16[384,2048]{1,0:T(8,128)(2,1)S(1)} %collective-permute-done.28.refs_1_.refs_3_, bf16[384,2048]{1,0:T(8,128)(2,1)} %collective-permute-done.29.refs_2_.refs_6_, ...), custom_call_target="tpu_custom_call" | custom-call | flops 301989888 | bytes 933888 | tf_op jit(solution)/shard_map/ffn/pallas_call | solution.py:80
  403.8 8.3 ffn.7
  412.1 8.6 ffn_back.5
  431.9 9.3 %ffn_back.4 = (bf16[384,2048]{1,0:T(8,128)(2,1)S(1)}, bf16[384,2048]{1,0:T(8,128)(2,1)}) custom-call(bf16[768,1024]{1,0:T(8,128)(2,1)S(1)} %copy-done.28, bf16[768,1024]{1,0:T(8,128)(2,1)S(1)} %get-tuple-element.90.refs_1_.refs_10_, bf16[2048,1536]{1,0:T(8,128)(2,1)S(1)} %place_rows.2.refs_4_.refs_2_, bf16[2048,1536]{1,0:T(8,128)(2,1)S(1)} %place_rows.3.refs_4_.refs_3_), custom_call_target="tpu_custom_call" | custom-call | flops 402653184 | bytes 917504 | tf_op jit(solution)/shard_map/ffn_back/pallas_call | solution.py:80
  452.7 10.3 %ffn_grads.5 = bf16[1024,1536]{1,0:T(8,128)(2,1)S(1)} custom-call(s32[2]{0:T(128)S(1)} %compare_select_fusion.2.dp_ref, s32[4]{0:T(128)S(1)} %gather_fusion.4, bf16[384,2048]{1,0:T(8,128)(2,1)} %multiply_convert_fusion.1.refs_0_, bf16[384,2048]{1,0:T(8,128)(2,1)} %collective-permute-done.20.refs_1_, ...), custom_call_target="tpu_custom_call" | custom-call | flops 301989888 | bytes 884736 | tf_op jit(solution)/shard_map/ffn_grads/pallas_call | solution.py:80
  463.4 15.6 %collective-permute-done.33 = bf16[384,2048]{1,0:T(8,128)(2,1)} collective-permute-done((bf16[384,2048]{1,0:T(8,128)(2,1)}, bf16[384,2048]{1,0:T(8,128)(2,1)}, u32[]{:S(2)}, u32[]{:S(2)}) %collective-permute-start.33) | collective-permute-done | bytes 1572896 | tf_op jit(solution)/shard_map/ppermute | solution.py:28
  482.1 12.1 %ffn_grads.7 = bf16[1024,1536]{1,0:T(8,128)(2,1)} custom-call(s32[2]{0:T(128)S(1)} %compare_select_fusion.2.dp_ref, s32[4]{0:T(128)S(1)} %gather_fusion.4, bf16[384,2048]{1,0:T(8,128)(2,1)} %multiply_convert_fusion.1.refs_0_, bf16[384,2048]{1,0:T(8,128)(2,1)} %collective-permute-done.20.refs_1_, bf16[384,2048]{1,0:T(8,128)(2,1)} %collective-permute-done.27.refs_0_.refs_2_, ...), custom_call_target="tpu_custom_call" | custom-call | flops 301989888 | bytes 884736 | tf_op jit(solution)/shard_map/ffn_grads/pallas_call | solution.py:80
  494.5 10.5 %ffn_grads.4 = bf16[1024,1536]{1,0:T(8,128)(2,1)S(1)} custom-call(s32[2]{0:T(128)S(1)} %compare_select_fusion.2.dp_ref, s32[4]{0:T(128)S(1)} %gather_fusion.4, bf16[384,2048]{1,0:T(8,128)(2,1)} %multiply_convert_fusion.1.refs_0_, bf16[384,2048]{1,0:T(8,128)(2,1)} %collective-permute-done.20.refs_1_, ...), custom_call_target="tpu_custom_call" | custom-call | flops 301989888 | bytes 884736 | tf_op jit(solution)/shard_map/ffn_grads/pallas_call | solution.py:80
  505.0 11.6 %collective-permute-done.34 = bf16[384,2048]{1,0:T(8,128)(2,1)S(1)} collective-permute-done((bf16[384,2048]{1,0:T(8,128)(2,1)S(1)}, bf16[384,2048]{1,0:T(8,128)(2,1)S(1)}, u32[]{:S(2)}, u32[]{:S(2)}) %collective-permute-start.34) | collective-permute-done | bytes 1572896 | tf_op jit(solution)/shard_map/ppermute | solution.py:28
  523.5 8.6 collective-permute-done.58
  547.5 10.3 %ffn_grads.6 = bf16[1024,1536]{1,0:T(8,128)(2,1)S(1)} custom-call(s32[2]{0:T(128)S(1)} %compare_select_fusion.2.dp_ref, s32[4]{0:T(128)S(1)} %gather_fusion.4, bf16[384,2048]{1,0:T(8,128)(2,1)} %multiply_convert_fusion.1.refs_0_, bf16[384,2048]{1,0:T(8,128)(2,1)} %collective-permute-done.20.refs_1_, ...), custom_call_target="tpu_custom_call" | custom-call | flops 301989888 | bytes 884736 | tf_op jit(solution)/shard_map/ffn_grads/pallas_call | solution.py:80
  566.2 44.7 %attend_back.1 = (bf16[768,512]{1,0:T(8,128)(2,1)S(1)}, f32[768,512]{1,0:T(8,128)S(1)}, f32[768,512]{1,0:T(8,128)S(1)}, f32[256,1024]{1,0:T(8,128)S(1)}, bf16[25...) custom-call(s32[3]{0:T(128)S(1)} %compare_select_fusion.7.order_ref, s32[4]{0:T(128)S(1)} %gather_fusion.1, ...), custom_call_target="tpu_custom_call" | custom-call | flops 1258291200 | bytes 786432 | tf_op jit(solution)/shard_map/attend_back/pallas_call | solution.py:599
  666.5 10.4 %project_back.3 = (bf16[384,2048]{1,0:T(8,128)(2,1)S(1)}, bf16[384,2048]{1,0:T(8,128)(2,1)S(1)}) custom-call(s32[1]{0:T(128)} %bitcast.bit_ref, s32[8]{0:T(128)S(1)} %xor_add_fusion.1.place_ref, bf16[768,512]{1,0:T(8,128)(2,1)S(1)} %copy-done.60, bf16[768,512]{1,0:T(8,128)(2,1)S(1)} %get-tuple-element.113.refs_1_, ...), custom_call_target="tpu_custom_call" | custom-call | flops 301989888 | bytes 737280 | tf_op jit(solution)/shard_map/project_back/pallas_call | solution.py:80
  689.1 34.2 %collective-permute-done.62 = bf16[512,1536]{1,0:T(8,128)(2,1)S(1)} collective-permute-done((bf16[512,1536]{1,0:T(8,128)(2,1)S(1)}, bf16[512,1536]{1,0:T(8,128)(2,1)S(1)}, u32[]{:S(2)}, u32[]{:S(2)}) %collective-permute-start.62) | collective-permute-done | bytes 1572896 | tf_op jit(solution)/shard_map/ppermute | solution.py:28
  728.7 46.0 %collective-permute-done.63 = bf16[256,1536]{1,0:T(8,128)(2,1)S(1)} collective-permute-done((bf16[256,1536]{1,0:T(8,128)(2,1)S(1)}, bf16[256,1536]{1,0:T(8,128)(2,1)S(1)}, u32[]{:S(2)}, u32[]{:S(2)}) %collective-permute-start.63) | collective-permute-done | bytes 786464 | tf_op jit(solution)/shard_map/ppermute | solution.py:28
  781.3 15.9 %collective-permute-done.53 = bf16[512,1024]{1,0:T(8,128)(2,1)S(1)} collective-permute-done((bf16[512,1024]{1,0:T(8,128)(2,1)S(1)}, bf16[512,1024]{1,0:T(8,128)(2,1)S(1)}, u32[]{:S(2)}, u32[]{:S(2)}) %collective-permute-start.53) | collective-permute-done | bytes 1048608 | tf_op jit(solution)/shard_map/ppermute | solution.py:28
  802.3 28.6 %collective-permute-done.56 = bf16[512,1024]{1,0:T(8,128)(2,1)S(1)} collective-permute-done((bf16[512,1024]{1,0:T(8,128)(2,1)S(1)}, bf16[512,1024]{1,0:T(8,128)(2,1)S(1)}, u32[]{:S(2)}, u32[]{:S(2)}) %collective-permute-start.56) | collective-permute-done | bytes 1048608 | tf_op jit(solution)/shard_map/ppermute | solution.py:28
  842.7 8.7 collective-permute-done.49
  855.2 11.3 %collective-permute-done.50 = f32[2,2048]{1,0:T(2,128)S(1)} collective-permute-done((f32[2,2048]{1,0:T(2,128)S(1)}, f32[2,2048]{1,0:T(2,128)S(1)}, u32[]{:S(2)}, u32[]{:S(2)}) %collective-permute-start.50) | collective-permute-done | bytes 16416 | tf_op jit(solution)/shard_map/ppermute | solution.py:28
  (491 shorter events, 320.0 us)
Async XLA Ops:
  4.2 73.7 %collective-permute-start.9 = (bf16[256,1024]{1,0:T(8,128)(2,1)}, bf16[256,1024]{1,0:T(8,128)(2,1)}, u32[]{:S(2)}, u32[]{:S(2)}) collective-permute-start(bf16[256,1024]{1,0:T(8,128)(2,1)} %constant_dynamic-update-slice_fusion.refs_1_.refs_7_), channel_id=1, source_target_pairs={{0,16},{16,0},{1,17},{17,1},{2,18},{18,2},{3,19},{19,3},{4,20},{20... | collective-permute-start | bytes 1572872 | tf_op jit(solution)/shard_map/ppermute | solution.py:33
  6.2 65.8 %collective-permute-start.8 = (bf16[256,1024]{1,0:T(8,128)(2,1)}, bf16[256,1024]{1,0:T(8,128)(2,1)}, u32[]{:S(2)}, u32[]{:S(2)}) collective-permute-start(bf16[256,1024]{1,0:T(8,128)(2,1)} %constant_dynamic-update-slice_fusion.refs_1_.refs_7_), channel_id=1, source_target_pairs={{0,4},{4,0},{1,5},{5,1},{2,6},{6,2},{3,7},{7,3},{8,12},{12,8},{9,1... | collective-permute-start | bytes 1572872 | tf_op jit(solution)/shard_map/ppermute | solution.py:28
  74.8 45.2 %collective-permute-start.2 = (bf16[256,1536]{1,0:T(8,128)(2,1)}, bf16[256,1536]{1,0:T(8,128)(2,1)}, u32[]{:S(2)}, u32[]{:S(2)}) collective-permute-start(bf16[256,1536]{1,0:T(8,128)(2,1)} %pad_maximum_fusion.3), channel_id=1, source_target_pairs={{0,8},{8,0},{1,9},{9,1},{2,10},{10,2},{3,11},{11,3},{4,12},{12,4},... | collective-permute-start | bytes 2359304 | tf_op jit(solution)/shard_map/ppermute | solution.py:28
  77.9 46.7 %collective-permute-start.3 = (bf16[256,1536]{1,0:T(8,128)(2,1)}, bf16[256,1536]{1,0:T(8,128)(2,1)}, u32[]{:S(2)}, u32[]{:S(2)}) collective-permute-start(bf16[256,1536]{1,0:T(8,128)(2,1)} %pad_maximum_fusion.4), channel_id=1, source_target_pairs={{0,4},{4,0},{1,5},{5,1},{2,6},{6,2},{3,7},{7,3},{8,12},{12,8},{9,1... | collective-permute-start | bytes 2359304 | tf_op jit(solution)/shard_map/ppermute | solution.py:28
  197.9 89.3 %collective-permute-start.17 = (bf16[384,2048]{1,0:T(8,128)(2,1)S(1)}, bf16[384,2048]{1,0:T(8,128)(2,1)}, u32[]{:S(2)}, u32[]{:S(2)}) collective-permute-start(bf16[384,2048]{1,0:T(8,128)(2,1)S(1)} %add_convert_fusion.10), channel_id=1, source_target_pairs={{0,2},{1,3},{2,0},{3,1},{4,6},{5,7},{6,4},{7,5},{8,10},{9,11},{10,... | collective-permute-start | bytes 4718600 | tf_op jit(solution)/shard_map/ppermute | solution.py:28
  205.4 81.8 %collective-permute-start.19 = (bf16[256,1536]{1,0:T(8,128)(2,1)S(1)}, bf16[256,1536]{1,0:T(8,128)(2,1)S(1)}, u32[]{:S(2)}, u32[]{:S(2)}) collective-permute-start(bf16[256,1536]{1,0:T(8,128)(2,1)S(1)} %pad_maximum_fusion.5), channel_id=1, source_target_pairs={{0,8},{8,0},{1,9},{9,1},{2,10},{10,2},{3,11},{11,3},{4,12},{12,4},... | collective-permute-start | bytes 2359304 | tf_op jit(solution)/shard_map/ppermute | solution.py:28
  207.0 101.4 %collective-permute-start.21 = (bf16[512,1536]{1,0:T(8,128)(2,1)}, bf16[512,1536]{1,0:T(8,128)(2,1)}, u32[]{:S(2)}, u32[]{:S(2)}) collective-permute-start(bf16[512,1536]{1,0:T(8,128)(2,1)} %constant_dynamic-update-slice_fusion.2.refs_0_), channel_id=1, source_target_pairs={{0,16},{16,0},{1,17},{17,1},{2,18},{18,2},{3,19},{19,3},{4,20},{20... | collective-permute-start | bytes 4718600 | tf_op jit(solution)/shard_map/ppermute | solution.py:33
  209.6 83.3 %collective-permute-start.24 = (bf16[256,1536]{1,0:T(8,128)(2,1)S(1)}, bf16[256,1536]{1,0:T(8,128)(2,1)S(1)}, u32[]{:S(2)}, u32[]{:S(2)}) collective-permute-start(bf16[256,1536]{1,0:T(8,128)(2,1)S(1)} %pad_maximum_fusion.6), channel_id=1, source_target_pairs={{0,12},{4,8},{8,4},{12,0},{1,13},{5,9},{9,5},{13,1},{2,14},{6,10},... | collective-permute-start | bytes 2359304 | tf_op jit(solution)/shard_map/ppermute | solution.py:28
  222.4 82.0 %collective-permute-start.23 = (bf16[256,1536]{1,0:T(8,128)(2,1)S(1)}, bf16[256,1536]{1,0:T(8,128)(2,1)S(1)}, u32[]{:S(2)}, u32[]{:S(2)}) collective-permute-start(bf16[256,1536]{1,0:T(8,128)(2,1)S(1)} %pad_maximum_fusion.6), channel_id=1, source_target_pairs={{0,4},{4,0},{1,5},{5,1},{2,6},{6,2},{3,7},{7,3},{8,12},{12,8},{9,1... | collective-permute-start | bytes 2359304 | tf_op jit(solution)/shard_map/ppermute | solution.py:28
  287.2 50.8 %collective-permute-start.29 = (bf16[384,2048]{1,0:T(8,128)(2,1)S(1)}, bf16[384,2048]{1,0:T(8,128)(2,1)}, u32[]{:S(2)}, u32[]{:S(2)}) collective-permute-start(bf16[384,2048]{1,0:T(8,128)(2,1)S(1)} %get-tuple-element.121.refs_2_.refs_4_), channel_id=1, source_target_pairs={{0,4},{4,0},{1,5},{5,1},{2,6},{6,2},{3,7},{7,3},{8,12},{12,8},{9,1... | collective-permute-start | bytes 4718600 | tf_op jit(solution)/shard_map/ppermute | solution.py:28
  288.1 50.3 %collective-permute-start.22 = (bf16[512,1536]{1,0:T(8,128)(2,1)}, bf16[512,1536]{1,0:T(8,128)(2,1)}, u32[]{:S(2)}, u32[]{:S(2)}) collective-permute-start(bf16[512,1536]{1,0:T(8,128)(2,1)} %constant_dynamic-update-slice_fusion.6.refs_1_), channel_id=1, source_target_pairs={{0,16},{16,0},{1,17},{17,1},{2,18},{18,2},{3,19},{19,3},{4,20},{20... | collective-permute-start | bytes 4718600 | tf_op jit(solution)/shard_map/ppermute | solution.py:33
  292.9 50.5 %collective-permute-start.20 = (bf16[384,2048]{1,0:T(8,128)(2,1)}, bf16[384,2048]{1,0:T(8,128)(2,1)}, u32[]{:S(2)}, u32[]{:S(2)}) collective-permute-start(bf16[384,2048]{1,0:T(8,128)(2,1)} %multiply_convert_fusion.1.refs_0_), channel_id=1, source_target_pairs={{0,1},{1,0},{2,3},{3,2},{4,5},{5,4},{6,7},{7,6},{8,9},{9,8},{10,11... | collective-permute-start | bytes 4718600 | tf_op jit(solution)/shard_map/ppermute | solution.py:28
  304.4 67.4 %collective-permute-start.27 = (bf16[384,2048]{1,0:T(8,128)(2,1)}, bf16[384,2048]{1,0:T(8,128)(2,1)}, u32[]{:S(2)}, u32[]{:S(2)}) collective-permute-start(bf16[384,2048]{1,0:T(8,128)(2,1)} %multiply_convert_fusion.1.refs_0_), channel_id=1, source_target_pairs={{0,4},{4,0},{1,5},{5,1},{2,6},{6,2},{3,7},{7,3},{8,12},{12,8},{9,1... | collective-permute-start | bytes 4718600 | tf_op jit(solution)/shard_map/ppermute | solution.py:28
  308.4 64.3 %collective-permute-start.25 = (bf16[512,1536]{1,0:T(8,128)(2,1)S(1)}, bf16[512,1536]{1,0:T(8,128)(2,1)S(1)}, u32[]{:S(2)}, u32[]{:S(2)}) collective-permute-start(bf16[512,1536]{1,0:T(8,128)(2,1)S(1)} %constant_dynamic-update-slice_fusion.8.refs_0_), channel_id=1, source_target_pairs={{0,16},{16,0},{1,17},{17,1},{2,18},{18,2},{3,19},{19,3},{4,20},{20... | collective-permute-start | bytes 4718600 | tf_op jit(solution)/shard_map/ppermute | solution.py:33
  338.1 50.9 %collective-permute-start.26 = (bf16[512,1536]{1,0:T(8,128)(2,1)S(1)}, bf16[512,1536]{1,0:T(8,128)(2,1)S(1)}, u32[]{:S(2)}, u32[]{:S(2)}) collective-permute-start(bf16[512,1536]{1,0:T(8,128)(2,1)S(1)} %constant_dynamic-update-slice_fusion.10.refs_1_), channel_id=1, source_target_pairs={{0,16},{16,0},{1,17},{17,1},{2,18},{18,2},{3,19},{19,3},{4,20},{20... | collective-permute-start | bytes 4718600 | tf_op jit(solution)/shard_map/ppermute | solution.py:33
  338.4 55.5 %collective-permute-start.30 = (bf16[384,2048]{1,0:T(8,128)(2,1)}, bf16[384,2048]{1,0:T(8,128)(2,1)S(1)}, u32[]{:S(2)}, u32[]{:S(2)}) collective-permute-start(bf16[384,2048]{1,0:T(8,128)(2,1)} %collective-permute-done.29.refs_2_.refs_6_), channel_id=1, source_target_pairs={{0,1},{1,0},{2,3},{3,2},{4,5},{5,4},{6,7},{7,6},{8,9},{9,8},{10,11... | collective-permute-start | bytes 4718600 | tf_op jit(solution)/shard_map/ppermute | solution.py:28
  463.0 69.2 %collective-permute-start.58 = (bf16[1024,1536]{1,0:T(8,128)(2,1)S(1)}, bf16[1024,1536]{1,0:T(8,128)(2,1)}, u32[]{:S(2)}, u32[]{:S(2)}) collective-permute-start(bf16[1024,1536]{1,0:T(8,128)(2,1)S(1)} %ffn_grads.5), channel_id=1, source_target_pairs={{0,16},{16,0},{1,17},{17,1},{2,18},{18,2},{3,19},{19,3},{4,20},{20... | collective-permute-start | bytes 9437192 | tf_op jit(solution)/shard_map/ppermute | solution.py:33
  494.2 132.4 %collective-permute-start.61 = (bf16[1024,1536]{1,0:T(8,128)(2,1)}, bf16[1024,1536]{1,0:T(8,128)(2,1)}, u32[]{:S(2)}, u32[]{:S(2)}) collective-permute-start(bf16[1024,1536]{1,0:T(8,128)(2,1)} %ffn_grads.7), channel_id=1, source_target_pairs={{0,16},{16,0},{1,17},{17,1},{2,18},{18,2},{3,19},{19,3},{4,20},{20... | collective-permute-start | bytes 9437192 | tf_op jit(solution)/shard_map/ppermute | solution.py:33
  537.9 82.7 %collective-permute-start.59 = (bf16[512,1536]{1,0:T(8,128)(2,1)}, bf16[512,1536]{1,0:T(8,128)(2,1)}, u32[]{:S(2)}, u32[]{:S(2)}) collective-permute-start(bf16[512,1536]{1,0:T(8,128)(2,1)} %slice.175), channel_id=1, source_target_pairs={{0,8},{8,0},{1,9},{9,1},{2,10},{10,2},{3,11},{11,3},{4,12},{12,4},... | collective-permute-start | bytes 4718600 | tf_op jit(solution)/shard_map/ppermute | solution.py:28
  620.6 65.1 %collective-permute-start.37 = (bf16[384,2048]{1,0:T(8,128)(2,1)}, bf16[384,2048]{1,0:T(8,128)(2,1)}, u32[]{:S(2)}, u32[]{:S(2)}) collective-permute-start(bf16[384,2048]{1,0:T(8,128)(2,1)} %get-tuple-element.104), channel_id=1, source_target_pairs={{0,1},{1,0},{2,3},{3,2},{4,5},{5,4},{6,7},{7,6},{8,9},{9,8},{10,11... | collective-permute-start | bytes 4718600 | tf_op jit(solution)/shard_map/ppermute | solution.py:28
  626.6 50.4 %collective-permute-start.60 = (bf16[256,1536]{1,0:T(8,128)(2,1)S(1)}, bf16[256,1536]{1,0:T(8,128)(2,1)S(1)}, u32[]{:S(2)}, u32[]{:S(2)}) collective-permute-start(bf16[256,1536]{1,0:T(8,128)(2,1)S(1)} %slice.213), channel_id=1, source_target_pairs={{0,4},{4,0},{1,5},{5,1},{2,6},{6,2},{3,7},{7,3},{8,12},{12,8},{9,1... | collective-permute-start | bytes 2359304 | tf_op jit(solution)/shard_map/ppermute | solution.py:28
  653.6 71.8 %collective-permute-start.52 = (bf16[1024,1024]{1,0:T(8,128)(2,1)}, bf16[1024,1024]{1,0:T(8,128)(2,1)S(1)}, u32[]{:S(2)}, u32[]{:S(2)}) collective-permute-start(bf16[1024,1024]{1,0:T(8,128)(2,1)} %attn_grads.5), channel_id=1, source_target_pairs={{0,16},{16,0},{1,17},{17,1},{2,18},{18,2},{3,19},{19,3},{4,20},{20... | collective-permute-start | bytes 6291464 | tf_op jit(solution)/shard_map/ppermute | solution.py:33
  653.9 145.6 %collective-permute-start.36 = (bf16[384,2048]{1,0:T(8,128)(2,1)}, bf16[384,2048]{1,0:T(8,128)(2,1)}, u32[]{:S(2)}, u32[]{:S(2)}) collective-permute-start(bf16[384,2048]{1,0:T(8,128)(2,1)} %get-tuple-element.100), channel_id=1, source_target_pairs={{0,1},{1,0},{2,3},{3,2},{4,5},{5,4},{6,7},{7,6},{8,9},{9,8},{10,11... | collective-permute-start | bytes 4718600 | tf_op jit(solution)/shard_map/ppermute | solution.py:28
  654.6 68.7 %collective-permute-start.62 = (bf16[512,1536]{1,0:T(8,128)(2,1)S(1)}, bf16[512,1536]{1,0:T(8,128)(2,1)S(1)}, u32[]{:S(2)}, u32[]{:S(2)}) collective-permute-start(bf16[512,1536]{1,0:T(8,128)(2,1)S(1)} %copy-done.98), channel_id=1, source_target_pairs={{0,8},{8,0},{1,9},{9,1},{2,10},{10,2},{3,11},{11,3},{4,12},{12,4},... | collective-permute-start | bytes 4718600 | tf_op jit(solution)/shard_map/ppermute | solution.py:28
  677.0 50.5 %collective-permute-start.44 = (bf16[384,2048]{1,0:T(8,128)(2,1)S(1)}, bf16[384,2048]{1,0:T(8,128)(2,1)S(1)}, u32[]{:S(2)}, u32[]{:S(2)}) collective-permute-start(bf16[384,2048]{1,0:T(8,128)(2,1)S(1)} %get-tuple-element.116), channel_id=1, source_target_pairs={{0,1},{1,0},{2,3},{3,2},{4,5},{5,4},{6,7},{7,6},{8,9},{9,8},{10,11... | collective-permute-start | bytes 4718600 | tf_op jit(solution)/shard_map/ppermute | solution.py:28
  685.7 94.4 %collective-permute-start.55 = (bf16[1024,1024]{1,0:T(8,128)(2,1)S(1)}, bf16[1024,1024]{1,0:T(8,128)(2,1)S(1)}, u32[]{:S(2)}, u32[]{:S(2)}) collective-permute-start(bf16[1024,1024]{1,0:T(8,128)(2,1)S(1)} %attn_grads.7), channel_id=1, source_target_pairs={{0,16},{16,0},{1,17},{17,1},{2,18},{18,2},{3,19},{19,3},{4,20},{20... | collective-permute-start | bytes 6291464 | tf_op jit(solution)/shard_map/ppermute | solution.py:33
  723.4 76.2 %collective-permute-start.38 = (bf16[384,2048]{1,0:T(8,128)(2,1)S(1)}, bf16[384,2048]{1,0:T(8,128)(2,1)S(1)}, u32[]{:S(2)}, u32[]{:S(2)}) collective-permute-start(bf16[384,2048]{1,0:T(8,128)(2,1)S(1)} %add_convert_fusion.5), channel_id=1, source_target_pairs={{0,4},{4,0},{1,5},{5,1},{2,6},{6,2},{3,7},{7,3},{8,12},{12,8},{9,1... | collective-permute-start | bytes 4718600 | tf_op jit(solution)/shard_map/ppermute | solution.py:28
  725.4 49.3 %collective-permute-start.63 = (bf16[256,1536]{1,0:T(8,128)(2,1)S(1)}, bf16[256,1536]{1,0:T(8,128)(2,1)S(1)}, u32[]{:S(2)}, u32[]{:S(2)}) collective-permute-start(bf16[256,1536]{1,0:T(8,128)(2,1)S(1)} %slice.212), channel_id=1, source_target_pairs={{0,4},{4,0},{1,5},{5,1},{2,6},{6,2},{3,7},{7,3},{8,12},{12,8},{9,1... | collective-permute-start | bytes 2359304 | tf_op jit(solution)/shard_map/ppermute | solution.py:28
  727.5 69.7 %collective-permute-start.53 = (bf16[512,1024]{1,0:T(8,128)(2,1)S(1)}, bf16[512,1024]{1,0:T(8,128)(2,1)S(1)}, u32[]{:S(2)}, u32[]{:S(2)}) collective-permute-start(bf16[512,1024]{1,0:T(8,128)(2,1)S(1)} %slice.162), channel_id=1, source_target_pairs={{0,4},{4,0},{1,5},{5,1},{2,6},{6,2},{3,7},{7,3},{8,12},{12,8},{9,1... | collective-permute-start | bytes 3145736 | tf_op jit(solution)/shard_map/ppermute | solution.py:28
  774.7 56.6 %collective-permute-start.45 = (bf16[384,2048]{1,0:T(8,128)(2,1)S(1)}, bf16[384,2048]{1,0:T(8,128)(2,1)S(1)}, u32[]{:S(2)}, u32[]{:S(2)}) collective-permute-start(bf16[384,2048]{1,0:T(8,128)(2,1)S(1)} %fusion.1), channel_id=1, source_target_pairs={{0,2},{1,3},{2,0},{3,1},{4,6},{5,7},{6,4},{7,5},{8,10},{9,11},{10,... | collective-permute-start | bytes 4718600 | tf_op jit(solution)/shard_map/ppermute | solution.py:28
  781.2 49.6 %collective-permute-start.56 = (bf16[512,1024]{1,0:T(8,128)(2,1)S(1)}, bf16[512,1024]{1,0:T(8,128)(2,1)S(1)}, u32[]{:S(2)}, u32[]{:S(2)}) collective-permute-start(bf16[512,1024]{1,0:T(8,128)(2,1)S(1)} %slice.167), channel_id=1, source_target_pairs={{0,4},{4,0},{1,5},{5,1},{2,6},{6,2},{3,7},{7,3},{8,12},{12,8},{9,1... | collective-permute-start | bytes 3145736 | tf_op jit(solution)/shard_map/ppermute | solution.py:28
  802.0 67.8 %collective-permute-start.39 = (bf16[384,1024]{1,0:T(8,128)(2,1)S(1)}, bf16[384,1024]{1,0:T(8,128)(2,1)S(1)}, u32[]{:S(2)}, u32[]{:S(2)}) collective-permute-start(bf16[384,1024]{1,0:T(8,128)(2,1)S(1)} %constant_dynamic-slice_fusion.4), channel_id=1, source_target_pairs={{0,2},{1,3},{2,0},{3,1},{4,6},{5,7},{6,4},{7,5},{8,10},{9,11},{10,... | collective-permute-start | bytes 2359304 | tf_op jit(solution)/shard_map/ppermute | solution.py:28
  (157 other events, 2673.5 us)

commit v4 on v3

--- a/solution.py
+++ b/solution.py
@@ -20,6 +20,7 @@
 BF16 = jnp.bfloat16
 F32 = jnp.float32
 VMEM_LIMIT = 32 * 1024 * 1024
+VMEM_WHOLE = 60 * 1024 * 1024
 CTX = ("hi", "lo")
 
 
@@ -318,44 +319,48 @@
         out_ref[at_block(slot, unit), column : column + wide] = values[row : row + unit]
 
 
-def ffn_grads_kernel(s, unit, dp_ref, slot_ref, *refs):
+def ffn_grads_kernel(tile, unit, dp_ref, slot_ref, *refs):
+    del dp_ref
     x_refs, cot_refs = refs[:4], refs[4:8]
     hiddens, dpairs, out_ref = refs[8:10], refs[10:12], refs[12]
     rows = x_refs[0].shape[0]
     wide = hiddens[0].shape[1]
-    count = out_ref.shape[0]
+
+    def product(lefts, rights):
+        total = None
+        for n, left in enumerate(lefts):
+            part = slice((n % 2) * rows, (n % 2 + 1) * rows)
+            term = dot(left[...], rights[n // 2][part, :], TN)
+            total = term if total is None else total + term
+        return total.astype(BF16)
+
+    first = pl.program_id(0) * tile
+    store_blocks(out_ref, product(x_refs, dpairs), first, unit, slot_ref, 0)
+    store_blocks(out_ref, product(cot_refs, hiddens), first, unit, slot_ref, 2 * wide)
+
+
+def ffn_grads(seconds, cotangents, hiddens, dpairs, owners, slots, s, count, unit):
+    half, wide = seconds[0].shape[0], hiddens[0].shape[1]
+    rows = 4 * half
     tile = 256
-
-    def step(t, carry):
-        where = pl.ds(pl.multiple_of(dp_ref[s] * count + t * tile, tile), tile)
-
-        def product(lefts, rights):
-            total = None
-            for n, left in enumerate(lefts):
-                part = slice((n % 2) * rows, (n % 2 + 1) * rows)
-                term = dot(left[:, where], rights[n // 2][part, :], TN)
-                total = term if total is None else total + term
-            return total.astype(BF16)
-
-        store_blocks(out_ref, product(x_refs, dpairs), t * tile, unit, slot_ref, 0)
-        store_blocks(out_ref, product(cot_refs, hiddens), t * tile, unit, slot_ref, 2 * wide)
-        return carry
-
-    lax.fori_loop(0, count // tile, step, 0)
-
-
-def ffn_grads(seconds, cotangents, hiddens, dpairs, owners, slots, s, count, unit):
-    wide = hiddens[0].shape[1]
-    rows = 4 * seconds[0].shape[0]
-    return call(
-        functools.partial(ffn_grads_kernel, s, unit),
-        [*seconds, *cotangents, *hiddens, *dpairs],
-        jax.ShapeDtypeStruct((count, 3 * wide), BF16),
-        "ffn_grads",
-        6 * rows * count * wide,
-        2 * (2 * rows * count + 3 * rows * wide + 3 * count * wide),
-        smem=[owners, slots],
-    )
+    left = pl.BlockSpec((half, tile), lambda t, dp, slot: (0, dp[s] * (count // tile) + t))
+    whole = lambda x: pl.BlockSpec(x.shape, lambda t, dp, slot: (0, 0))
+    return pl.pallas_call(
+        functools.partial(ffn_grads_kernel, tile, unit),
+        grid_spec=pltpu.PrefetchScalarGridSpec(
+            num_scalar_prefetch=2,
+            grid=(count // tile,),
+            in_specs=[left] * 8 + [whole(x) for x in (*hiddens, *dpairs)],
+            out_specs=pl.BlockSpec((count, 3 * wide), lambda t, dp, slot: (0, 0)),
+        ),
+        out_shape=jax.ShapeDtypeStruct((count, 3 * wide), BF16),
+        compiler_params=pltpu.CompilerParams(vmem_limit_bytes=VMEM_WHOLE),
+        cost_estimate=cost(
+            6 * rows * count * wide,
+            2 * (2 * rows * count + 3 * rows * wide + 3 * count * wide),
+        ),
+        name="ffn_grads",
+    )(owners, slots, *seconds, *cotangents, *hiddens, *dpairs)
 
 
 def attn_grads_kernel(kinds, s, unit, bit_ref, dp_ref, slot_ref, *refs):
@@ -719,11 +724,13 @@
         near = jnp.concatenate([keep, swap(give, "lo")], axis=0)
         return near, swap(keep, "hi"), give
 
-    def ffn_stack(near, far):
-        stack = [near, far]
-        for s in range(1, dp_count):
-            stack += [turn(near, "dp", -s), turn(far, "dp", -s)]
-        return place_rows(stack, places_ffn)
+    def ffn_stack(near_blocks, far):
+        return place_rows(
+            [x for both in zip(near_blocks, gather_dp(far)) for x in both], places_ffn
+        )
+
+    def gather_dp(own):
+        return [own] + [turn(own, "dp", -s) for s in range(1, dp_count)]
 
     group_seq = seq_ids[0].reshape(ctx_count, rows // CLEN, CLEN)[:, :, 0]
     group_pos = positions[0].reshape(ctx_count, rows // CLEN, CLEN)[:, :, 0]
@@ -758,24 +765,32 @@
         sine,
         head_width,
     )
+    near_one = gather_dp(near_one)
+    cotangent_half = row_half(out_grad)
+    cotangent_far = swap(after(cotangent_half, *prompts[1:]), "lo")
+    three_one = swap(after(give_one, kv_stack[-1]), CTX, 3)
+    query = after(query, *near_one[1:], three_one)
     mixed, lse = attention_forward(order, rank, query, kv, prompts)
-    three_one = swap(after(give_one, *prompts[1:]), CTX, 3)
     near_two, two_two, give_two = ffn_sends(1, *prompts[1:])
-    three_two = swap(give_two, CTX, 3)
+    mixed = after(mixed, two_two, near_two)
+    near_two = gather_dp(near_two)
+    three_two = swap(after(give_two, three_one), CTX, 3)
     ffn_weights = [
         ffn_stack(near_one, jnp.concatenate([two_one, three_one], axis=0)),
         ffn_stack(near_two, jnp.concatenate([two_two, three_two], axis=0)),
     ]
 
-    kept, given = project_back([mixed], ((0, head_width),), [qo_stack], places, bit_ref)
+    kept, given = project_back(
+        [mixed], ((0, head_width),), [qo_stack], places, bit_ref
+    )
     mixed_out = low(add(kept, swap(given, "tp")))
-    mixed_far = after(swap(mixed_out, "tp", 2), three_one, two_two)
+    mixed_far = after(
+        swap(mixed_out, "tp", 2), three_two, ffn_weights[0], *near_two[1:], cotangent_far
+    )
     middle = row_half(tokens).astype(F32) + add(mixed_out, mixed_far)
     second_norm, second_scale = normalize(middle)
     second_half = low(second_norm * gain_two)
 
-    cotangent_half = row_half(out_grad)
-    cotangent_far = swap(after(cotangent_half, prompts[1]), "lo")
     cotangents = [
         [cotangent_half, row_half(out_grad, 1 - bit)],
         [cotangent_far, swap(cotangent_far, "tp")],
@@ -792,20 +807,17 @@
     gate_spans = tuple((f, 0, f, 0, 2 * chunk) for f in range(FFN_CHUNKS))
     down_spans = tuple((f, 0, f, 2 * chunk, chunk) for f in range(FFN_CHUNKS))
 
-    def collect(near, far):
-        far = low(add(far[0], swap(far[1], "tp")))
-        near = low(add(near[0], swap(near[1], "tp")))
-        return low(add(near, swap(far, "lo")))
+    def cores(part):
+        return low(add(part[0], swap(part[1], "tp")))
 
     dsecond_far = ffn_back(dpairs[1], ffn_weights, gate_spans)
     dsecond_near = ffn_back(dpairs[0], ffn_weights, gate_spans)
-    dsecond = collect(dsecond_near, dsecond_far)
-    dsecond = add(dsecond, swap(dsecond, "tp", 2))
+    dsecond_got, dsecond_half = swap(cores(dsecond_far), "lo"), cores(dsecond_near)
 
     lefts, left_cots = after(
         (seconds[0] + seconds[1], cotangents[0] + cotangents[1]), *dsecond_near, *dsecond_far
     )
-    ffn_blocks = []
+    ffn_given, ffn_own = [], []
     for f in range(FFN_CHUNKS):
 
         def part(s, f=f):
@@ -821,30 +833,56 @@
                 own_rows,
             )
 
-        sent = [turn(part(s), "dp", s) for s in range(1, dp_count)]
-        ffn_blocks.append((part(0), sent))
-
-    def ffn_scatter(own, got, first, second, third):
-        total = own
-        for part in got:
-            total = add(total, after(part, first))
-        total = low(total)
-        pair = add(total[: 2 * own_rows], after(swap(total[2 * own_rows :], "hi"), second))
+        ffn_given.append([part(s) for s in range(1, dp_count)])
+        ffn_own.append(part(0))
+    pair_rows = 2 * own_rows
+
+    def over_dp_rows(f, first, *needed):
+        return [
+            turn(after(x[first : first + pair_rows], *needed), "dp", s + 1)
+            for s, x in enumerate(ffn_given[f])
+        ]
+
+    def total_rows(f, first, got):
+        total = ffn_own[f][first : first + pair_rows]
+        for x in got:
+            total = add(total, x)
+        return low(total)
+
+    far_one = over_dp_rows(0, pair_rows)
+    near_one_got = over_dp_rows(0, 0, *far_one)
+    far_two = over_dp_rows(1, pair_rows, *near_one_got)
+    near_two_got = over_dp_rows(1, 0, *far_two)
+    dsecond_got = after(dsecond_got, *ffn_given[1], ffn_own[0], *far_one)
+    dsecond = low(add(dsecond_half, dsecond_got))
+    hi_one = swap(total_rows(0, pair_rows, far_one), "hi")
+    hiddens_late = after(hiddens, dsecond)
+    out_far = ffn_back(hiddens_late[1], ffn_weights, down_spans)
+    out_near = ffn_back(hiddens_late[0], ffn_weights, down_spans)
+
+    def ffn_deliver(near, hi_got, needed):
+        pair = add(near, hi_got)
         kept = pair[:own_rows]
-        got = after(swap(low(pair[own_rows:]), "lo"), third).astype(F32)
+        got = after(swap(low(pair[own_rows:]), "lo"), needed).astype(F32)
         return (jnp.where(parity == 0, kept, got), jnp.where(parity == 0, got, kept))
 
+    dsecond = add(dsecond, after(
+        swap(dsecond, "tp", 2), *ffn_own, *out_far, *out_near, *near_one_got
+    ))
     gain_two_grad = jnp.sum(dsecond * second_norm, axis=0)
     scaled_two = dsecond * gain_two
     dmiddle = cotangent_half.astype(F32) + second_scale * (
         scaled_two - second_norm * jnp.mean(scaled_two * second_norm, axis=-1, keepdims=True)
     )
-    dmiddle_low = [low(dmiddle), swap(low(dmiddle), "tp")]
+    out_half, out_far_got = cores(out_near), swap(cores(out_far), "lo")
+    dmiddle_low = [low(dmiddle), after(swap(low(dmiddle), "tp"), out_half)]
     dmixed = project(dmiddle_low, qo_stack, places, bit_ref, head_width, head_width, cosine, sine, 0)
     dquery_low, dkey_own, dvalue_own, dprompt_own, *dprompts = attention_backward(
         order, rank, query, kv, mixed, lse, dmixed, cosine, sine, prompts
     )
     got = [swap(piece, CTX, k + 1) for k, piece in enumerate(dprompts)]
+    far_two = after(far_two, dquery_low)
+    hi_two = swap(total_rows(1, pair_rows, far_two), "hi")
     dkey_low, dvalue_low = merge_keys(
         mine[None], dkey_own, dvalue_own, dprompt_own, got, cosine, sine
     )
@@ -859,13 +897,17 @@
             total = add(total, turn(parts[s], "dp", s))
         total = low(total)
         pair = add(total[: 2 * own_rows], swap(total[2 * own_rows :], "lo"))
-        return pair[:own_rows] + swap(low(pair[own_rows:]), "hi").astype(F32)
-
-    early = attn_grads([(dmiddle_low, mixed), ([first], dquery_low)])
-    late = attn_grads([([first], dkey_low), ([first], dvalue_low)])
+        return total, pair[:own_rows] + swap(low(pair[own_rows:]), "hi").astype(F32)
+
+    _, early = attn_grads([(dmiddle_low, mixed), ([first], dquery_low)])
+    late_total, late = attn_grads([([first], dkey_low), ([first], dvalue_low)])
     ffn_sums = [
-        ffn_scatter(*ffn_blocks[0], dmiddle, dquery_low, dkey_low),
-        ffn_scatter(*ffn_blocks[1], dquery_low, dkey_low, dkey_low),
+        ffn_deliver(total_rows(0, 0, near_one_got), after(hi_one, dquery_low), dkey_low),
+        ffn_deliver(
+            total_rows(1, 0, after(near_two_got, dquery_low)),
+            after(hi_two, late_total),
+            late_total,
+        ),
     ]
 
     kept, given = project_back(
@@ -879,7 +921,7 @@
     gain_one_grad = jnp.sum(kept.astype(F32) * norm_half, axis=0) + jnp.sum(
         given.astype(F32) * norm_other, axis=0
     )
-    dfirst = low(add(kept, swap(given, "tp")))
+    dfirst = after(low(add(kept, swap(given, "tp"))), gain_one_grad)
     dfirst = add(dfirst, swap(dfirst, "tp", 2))
     scaled_one = dfirst * gain_one
     dinputs = dmiddle + row_half(first_scale) * (
@@ -888,31 +930,27 @@
 
     share = width // tp_count
     here = tp_index // 2
-
-    def wide_part(values, which):
-        return lax.dynamic_slice_in_dim(values, which * 2 * share, 2 * share, 1)
-
-    def deliver(wide):
-        kept = lax.dynamic_slice_in_dim(wide, bit * share, share, 1)
-        given = lax.dynamic_slice_in_dim(wide, (1 - bit) * share, share, 1)
-        return assemble(kept, swap(given, "tp"))
-
-    in_grad = deliver(low(wide_part(dinputs, here)))
-
-    hiddens = after(hiddens, dmixed)
-    ffn_out = collect(
-        ffn_back(hiddens[0], ffn_weights, down_spans),
-        ffn_back(hiddens[1], ffn_weights, down_spans),
-    )
-    ffn_out = add(wide_part(ffn_out, here), swap(wide_part(ffn_out, 1 - here), "tp", 2))
-    block_out = deliver(low(wide_part(middle, here) + ffn_out))
-
     gains = jnp.stack([gain_one_grad, jnp.where(here == 0, gain_two_grad, 0.0)])
     for axis in ("tp", "lo", "hi", "dp"):
         mask = 1
         while mask < lax.axis_size(axis):
             gains = gains + swap(gains, axis, mask)
             mask *= 2
+
+    def wide_part(values, which):
+        return lax.dynamic_slice_in_dim(values, which * 2 * share, 2 * share, 1)
+
+    def deliver(wide):
+        kept = lax.dynamic_slice_in_dim(wide, bit * share, share, 1)
+        given = lax.dynamic_slice_in_dim(wide, (1 - bit) * share, share, 1)
+        return assemble(kept, swap(given, "tp"))
+
+    in_grad = deliver(after(low(wide_part(dinputs, here)), gains))
+
+    ffn_out = low(add(out_half, after(out_far_got, dquery_low)))
+    ffn_out = add(wide_part(ffn_out, here), swap(wide_part(ffn_out, 1 - here), "tp", 2))
+    block_out = deliver(low(wide_part(middle, here) + ffn_out))
+
     part = width // (dp_count * ctx_count)
     gains = lax.dynamic_slice_in_dim(gains, (dp_index * ctx_count + ctx_index) * part, part, 1)
 

time: 885 us -> 840 us (0.949)
  waiting for transfers between devices: 370 us -> 328 us
  starting transfers between devices: 135 us -> 103 us
  other arithmetic: 63.4 us -> 82.7 us
  local copies, waits for them, and re-layouts: 72.4 us -> 82.6 us
    ppermute x50, waiting for transfers between devices: 316 us -> 191 us  [swap(): return lax.ppermute(values, axis, [(i, i ^ mask) for i in range(count)])]
    ppermute x14 -> x16, waiting for transfers between devices: 54.2 us -> 137 us  [turn(): lax.ppermute(values, axis, [(i, (i + shift) % count) for i in range(count)])]
    pallas_call x23 -> x19, Pallas kernels: 164 us -> 111 us  [call(): pl.pallas_call(kernel, in_specs=[SMEM] * len(smem) + [VMEM] * len(operand...]
    pallas_call x0 -> x4, Pallas kernels: none -> 52.8 us  [ffn_grads(): pl.pallas_call(functools.partial(ffn_grads_kernel, tile, unit), grid_spec...]
    ppermute x50, starting transfers between devices: 128 us -> 89.8 us  [swap(): return lax.ppermute(values, axis, [(i, i ^ mask) for i in range(count)])]
    convert_element_type x14 -> x15, other arithmetic: 24.6 us -> 32.9 us  [low(): return values.astype(BF16)]
    unnamed x257 -> x211, local copies, waits for them, and re-layouts: 49.7 us -> 44.8 us
  transfers between devices with their start and end apart: 64 -> 66, of which waited for: 28 -> 28; matrix products, arithmetic and copies ran while one was open for 10% -> 15% of each run, Pallas kernels for 20% -> 24%
where the time goes in v4:
time: 840 us; the launch traced here: 830 us
  waiting for transfers between devices  328 us (39%)
  Pallas kernels  230 us (27%)
  starting transfers between devices  103 us (12%)
  other arithmetic  82.7 us (10%)
  local copies, waits for them, and re-layouts  82.6 us (10%)
    ppermute x50, waiting for transfers between devices, swap(): return lax.ppermute(values, axis, [(i, i ^ mask) for i in range(count)])  191 us
    ppermute x16, waiting for transfers between devices, turn(): lax.ppermute(values, axis, [(i, (i + shift) % count) for i in range(count)])  137 us
    pallas_call x19, Pallas kernels, call(): pl.pallas_call(kernel, in_specs=[SMEM] * len(smem) + [VMEM] * len(operand...  111 us
    ppermute x50, starting transfers between devices, swap(): return lax.ppermute(values, axis, [(i, i ^ mask) for i in range(count)])  89.8 us
    pallas_call x4, Pallas kernels, ffn_grads(): pl.pallas_call(functools.partial(ffn_grads_kernel, tile, unit), grid_spec...  52.8 us
    unnamed x211, local copies, waits for them, and re-layouts  44.8 us
    pallas_call x1, Pallas kernels, attention_backward(): pl.pallas_call(functools.partial(backward_kernel, pieces), grid_spec=pltp...  42.9 us
    convert_element_type x15, other arithmetic, low(): return values.astype(BF16)  32.9 us
  transfers between devices with their start and end apart: 66, of which 28 were waited for; matrix products, arithmetic and copies ran while one was open for 15% of the time, Pallas kernels for 24%

profile of v4, /device:TPU:1, one launch (start us, length us, event | category | flops | bytes accessed | tf_op | source)
XLA Modules:
  0.0 829.7 jit_solution(2373466647029390412)
XLA Ops:
  58.2 11.2 %collective-permute-done.9.refs_8_.refs_14_ = bf16[256,1024]{1,0:T(8,128)(2,1)} collective-permute-done((bf16[256,1024]{1,0:T(8,128)(2,1)}, bf16[256,1024]{1,0:T(8,128)(2,1)}, u32[]{:S(2)}, u32[]{:S(2)}) %collective-permute-start.9) | collective-permute-done | bytes 524320 | tf_op jit(solution)/shard_map/ppermute | solution.py:34
  69.4 7.2 project.4.ks_ref.vs_ref
  90.0 19.7 %collective-permute-start.2 = (bf16[256,1536]{1,0:T(8,128)(2,1)}, bf16[256,1536]{1,0:T(8,128)(2,1)}, u32[]{:S(2)}, u32[]{:S(2)}) collective-permute-start(bf16[256,1536]{1,0:T(8,128)(2,1)} %pad_maximum_fusion.3), channel_id=1, source_target_pairs={{0,8},{8,0},{1,9},{9,1},{2,10},{10,2},{3,11},{11,3},{4,12},{12,4},... | collective-permute-start | bytes 2359304 | tf_op jit(solution)/shard_map/ppermute | solution.py:29
  109.7 9.8 %collective-permute-done.16.refs_2_.refs_6_ = bf16[256,1024]{1,0:T(8,128)(2,1)S(1)} collective-permute-done((bf16[256,1024]{1,0:T(8,128)(2,1)S(1)}, bf16[256,1024]{1,0:T(8,128)(2,1)S(1)}, u32[]{:S(2)}, u32[]{:S(2)}) %collective-permute-start.16) | collective-permute-done | bytes 524320 | tf_op jit(solution)/shard_map/ppermute | solution.py:29
  126.8 26.8 %collective-permute-done.5.refs_2_.refs_3_.refs_4_ = bf16[512,1024]{1,0:T(8,128)(2,1)} collective-permute-done((bf16[512,1024]{1,0:T(8,128)(2,1)}, bf16[512,1024]{1,0:T(8,128)(2,1)}, u32[]{:S(2)}, u32[]{:S(2)}) %collective-permute-start.5) | collective-permute-done | bytes 1048608 | tf_op jit(solution)/shard_map/ppermute | solution.py:29
  155.5 19.3 %collective-permute-done.19 = bf16[256,1536]{1,0:T(8,128)(2,1)} collective-permute-done((bf16[256,1536]{1,0:T(8,128)(2,1)}, bf16[256,1536]{1,0:T(8,128)(2,1)}, u32[]{:S(2)}, u32[]{:S(2)}) %collective-permute-start.19) | collective-permute-done | bytes 786464 | tf_op jit(solution)/shard_map/ppermute | solution.py:29
  181.2 14.5 %collective-permute-done.7.refs_4_.refs_5_.refs_6_ = bf16[512,1024]{1,0:T(8,128)(2,1)} collective-permute-done((bf16[512,1024]{1,0:T(8,128)(2,1)}, bf16[512,1024]{1,0:T(8,128)(2,1)}, u32[]{:S(2)}, u32[]{:S(2)}) %collective-permute-start.7) | collective-permute-done | bytes 1048608 | tf_op jit(solution)/shard_map/ppermute | solution.py:34
  200.7 20.6 %attend.1 = (bf16[768,512]{1,0:T(8,128)(2,1)S(1)}, f32[768,512]{1,0:T(8,128)S(1)}) custom-call(s32[3]{0:T(128)S(1)} %compare_select_fusion.7.order_ref, s32[4]{0:T(128)S(1)} %gather_fusion.1, bf16[768,512]{1,0:T(8,128)(2,1)S(1)} %project.3.q_ref, bf16[768,1024]{1,0:T(8,128)(2,1)S(1)} %copy-done.21, bf16[768,1024]{1,0:T(8,128)(2,1)S(1)} %copy-done.21, ...), custom_call_target="tpu_custom_call" | custom-call | flops 503316480 | bytes 393216 | tf_op jit(solution)/shard_map/attend/pallas_call | solution.py:582
  222.4 7.1 project_back.2
  229.6 8.4 %collective-permute-start.20 = (bf16[384,2048]{1,0:T(8,128)(2,1)}, bf16[384,2048]{1,0:T(8,128)(2,1)}, u32[]{:S(2)}, u32[]{:S(2)}) collective-permute-start(bf16[384,2048]{1,0:T(8,128)(2,1)} %get-tuple-element.94), channel_id=1, source_target_pairs={{0,1},{1,0},{2,3},{3,2},{4,5},{5,4},{6,7},{7,6},{8,9},{9,8},{10,11... | collective-permute-start | bytes 4718600 | tf_op jit(solution)/shard_map/ppermute | solution.py:29
  258.2 25.7 %collective-permute-done.23.refs_3_ = bf16[512,1536]{1,0:T(8,128)(2,1)} collective-permute-done((bf16[512,1536]{1,0:T(8,128)(2,1)}, bf16[512,1536]{1,0:T(8,128)(2,1)}, u32[]{:S(2)}, u32[]{:S(2)}) %collective-permute-start.23) | collective-permute-done | bytes 1572896 | tf_op jit(solution)/shard_map/ppermute | solution.py:34
  287.2 11.9 %collective-permute-done.22 = bf16[256,1536]{1,0:T(8,128)(2,1)} collective-permute-done((bf16[256,1536]{1,0:T(8,128)(2,1)}, bf16[256,1536]{1,0:T(8,128)(2,1)}, u32[]{:S(2)}, u32[]{:S(2)}) %collective-permute-start.22) | collective-permute-done | bytes 786464 | tf_op jit(solution)/shard_map/ppermute | solution.py:29
  299.1 18.5 %collective-permute-done.24.refs_2_ = bf16[512,1536]{1,0:T(8,128)(2,1)} collective-permute-done((bf16[512,1536]{1,0:T(8,128)(2,1)}, bf16[512,1536]{1,0:T(8,128)(2,1)}, u32[]{:S(2)}, u32[]{:S(2)}) %collective-permute-start.24) | collective-permute-done | bytes 1572896 | tf_op jit(solution)/shard_map/ppermute | solution.py:34
  333.4 25.3 %collective-permute-done.28.refs_0_.refs_2_ = bf16[384,2048]{1,0:T(8,128)(2,1)S(1)} collective-permute-done((bf16[384,2048]{1,0:T(8,128)(2,1)S(1)}, bf16[384,2048]{1,0:T(8,128)(2,1)S(1)}, u32[]{:S(2)}, u32[]{:S(2)}) %collective-permute-start.28) | collective-permute-done | bytes 1572896 | tf_op jit(solution)/shard_map/ppermute | solution.py:29
  370.2 7.5 ffn.6
  378.6 7.5 ffn.7
  386.2 9.3 %ffn_back.5 = (bf16[384,2048]{1,0:T(8,128)(2,1)S(1)}, bf16[384,2048]{1,0:T(8,128)(2,1)}) custom-call(bf16[768,1024]{1,0:T(8,128)(2,1)S(1)} %get-tuple-element.107.refs_0_.refs_11_, bf16[768,1024]{1,0:T(8,128)(2,1)S(1)} %get-tuple-element.108.refs_1_.refs_11_, bf16[2048,1536]{1,0:T(8,128)(2,1)S(1)} %place_rows.2.refs_4_.refs_2_, ...), custom_call_target="tpu_custom_call" | custom-call | flops 402653184 | bytes 917504 | tf_op jit(solution)/shard_map/ffn_back/pallas_call | solution.py:81
  412.5 9.3 %ffn_back.4 = (bf16[384,2048]{1,0:T(8,128)(2,1)S(1)}, bf16[384,2048]{1,0:T(8,128)(2,1)}) custom-call(bf16[768,1024]{1,0:T(8,128)(2,1)S(1)} %copy-done.28, bf16[768,1024]{1,0:T(8,128)(2,1)S(1)} %get-tuple-element.104.refs_1_.refs_10_, bf16[2048,1536]{1,0:T(8,128)(2,1)S(1)} %bitcast.11, bf16[2048,1536]{1,0:T(8,128)(2,1)S(1)} %copy-done.3), custom_call_target="tpu_custom_call" | custom-call | flops 402653184 | bytes 917504 | tf_op jit(solution)/shard_map/ffn_back/pallas_call | solution.py:81
  421.8 13.2 %ffn_grads.6 = bf16[1024,1536]{1,0:T(8,128)(2,1)} custom-call(s32[2]{0:T(128)} %compare_select_fusion.2.dp_ref, s32[4]{0:T(128)} %gather_fusion.3, bf16[384,2048]{1,0:T(8,128)(2,1)} %copy-done.10, bf16[384,2048]{1,0:T(8,128)(2,1)} %copy-done.14, bf16[384,2048]{1,0:T(8,128)(2,1)} %copy-done.16, bf16[384,2048]{1,0:T(8,128)(2,1)} %copy-done.19, ...), custom_call_target="tpu_custom_call" | custom-call | flops 301989888 | bytes 884736 | tf_op jit(solution)/shard_map/ffn_grads/pallas_call | solution.py:348
  445.3 13.2 %ffn_grads.5 = bf16[1024,1536]{1,0:T(8,128)(2,1)} custom-call(s32[2]{0:T(128)} %compare_select_fusion.2.dp_ref, s32[4]{0:T(128)} %gather_fusion.3, bf16[384,2048]{1,0:T(8,128)(2,1)} %copy-done.10, bf16[384,2048]{1,0:T(8,128)(2,1)} %copy-done.14, bf16[384,2048]{1,0:T(8,128)(2,1)} %copy-done.16, bf16[384,2048]{1,0:T(8,128)(2,1)} %copy-done.19, ...), custom_call_target="tpu_custom_call" | custom-call | flops 301989888 | bytes 884736 | tf_op jit(solution)/shard_map/ffn_grads/pallas_call | solution.py:348
  458.5 13.1 %ffn_grads.4 = bf16[1024,1536]{1,0:T(8,128)(2,1)} custom-call(s32[2]{0:T(128)} %compare_select_fusion.2.dp_ref, s32[4]{0:T(128)} %gather_fusion.3, bf16[384,2048]{1,0:T(8,128)(2,1)} %copy-done.10, bf16[384,2048]{1,0:T(8,128)(2,1)} %copy-done.14, bf16[384,2048]{1,0:T(8,128)(2,1)} %copy-done.16, bf16[384,2048]{1,0:T(8,128)(2,1)} %copy-done.19, ...), custom_call_target="tpu_custom_call" | custom-call | flops 301989888 | bytes 884736 | tf_op jit(solution)/shard_map/ffn_grads/pallas_call | solution.py:348
  483.8 13.3 %ffn_grads.7 = bf16[1024,1536]{1,0:T(8,128)(2,1)} custom-call(s32[2]{0:T(128)} %compare_select_fusion.2.dp_ref, s32[4]{0:T(128)} %gather_fusion.3, bf16[384,2048]{1,0:T(8,128)(2,1)} %copy-done.10, bf16[384,2048]{1,0:T(8,128)(2,1)} %copy-done.14, bf16[384,2048]{1,0:T(8,128)(2,1)} %copy-done.16, bf16[384,2048]{1,0:T(8,128)(2,1)} %copy-done.19, ...), custom_call_target="tpu_custom_call" | custom-call | flops 301989888 | bytes 884736 | tf_op jit(solution)/shard_map/ffn_grads/pallas_call | solution.py:348
  518.7 6.2 ffn_back.6
  539.4 22.2 %collective-permute-done.62 = bf16[512,1536]{1,0:T(8,128)(2,1)} collective-permute-done((bf16[512,1536]{1,0:T(8,128)(2,1)}, bf16[512,1536]{1,0:T(8,128)(2,1)}, u32[]{:S(2)}, u32[]{:S(2)}) %collective-permute-start.62) | collective-permute-done | bytes 1572896 | tf_op jit(solution)/shard_map/ppermute | solution.py:34
  569.9 42.9 %attend_back.1 = (bf16[768,512]{1,0:T(8,128)(2,1)S(1)}, f32[768,512]{1,0:T(8,128)S(1)}, f32[768,512]{1,0:T(8,128)S(1)}, f32[256,1024]{1,0:T(8,128)S(1)}, bf16[25...) custom-call(s32[3]{0:T(128)S(1)} %compare_select_fusion.7.order_ref, ...), custom_call_target="tpu_custom_call" | custom-call | flops 1258291200 | bytes 786432 | tf_op jit(solution)/shard_map/attend_back/pallas_call | solution.py:604
  628.8 6.9 collective-permute-done.43.refs_0_
  649.9 10.3 %project_back.3 = (bf16[384,2048]{1,0:T(8,128)(2,1)S(1)}, bf16[384,2048]{1,0:T(8,128)(2,1)S(1)}) custom-call(s32[1]{0:T(128)} %bitcast.bit_ref, s32[8]{0:T(128)S(1)} %xor_add_fusion.1.place_ref, bf16[768,512]{1,0:T(8,128)(2,1)S(1)} %get-tuple-element.132.refs_0_.refs_4_, bf16[768,512]{1,0:T(8,128)(2,1)S(1)} %get-tuple-element.140.refs_1_, ...), custom_call_target="tpu_custom_call" | custom-call | flops 301989888 | bytes 737280 | tf_op jit(solution)/shard_map/project_back/pallas_call | solution.py:81
  680.1 9.9 %collective-permute-start.55 = (bf16[512,1024]{1,0:T(8,128)(2,1)S(1)}, bf16[512,1024]{1,0:T(8,128)(2,1)S(1)}, u32[]{:S(2)}, u32[]{:S(2)}) collective-permute-start(bf16[512,1024]{1,0:T(8,128)(2,1)S(1)} %slice.179), channel_id=1, source_target_pairs={{0,4},{4,0},{1,5},{5,1},{2,6},{6,2},{3,7},{7,3},{8,12},{12,8},{9,1... | collective-permute-start | bytes 3145736 | tf_op jit(solution)/shard_map/ppermute | solution.py:29
  690.0 33.9 %collective-permute-done.57 = bf16[1024,1024]{1,0:T(8,128)(2,1)S(1)} collective-permute-done((bf16[1024,1024]{1,0:T(8,128)(2,1)S(1)}, bf16[1024,1024]{1,0:T(8,128)(2,1)S(1)}, u32[]{:S(2)}, u32[]{:S(2)}) %collective-permute-start.57) | collective-permute-done | bytes 2097184 | tf_op jit(solution)/shard_map/ppermute | solution.py:34
  742.7 26.8 %collective-permute-done.65 = bf16[256,1536]{1,0:T(8,128)(2,1)S(1)} collective-permute-done((bf16[256,1536]{1,0:T(8,128)(2,1)S(1)}, bf16[256,1536]{1,0:T(8,128)(2,1)S(1)}, u32[]{:S(2)}, u32[]{:S(2)}) %collective-permute-start.65) | collective-permute-done | bytes 786464 | tf_op jit(solution)/shard_map/ppermute | solution.py:29
  782.9 9.3 %collective-permute-done.58 = bf16[512,1024]{1,0:T(8,128)(2,1)} collective-permute-done((bf16[512,1024]{1,0:T(8,128)(2,1)}, bf16[512,1024]{1,0:T(8,128)(2,1)}, u32[]{:S(2)}, u32[]{:S(2)}) %collective-permute-start.58) | collective-permute-done | bytes 1048608 | tf_op jit(solution)/shard_map/ppermute | solution.py:29
  796.5 23.2 %collective-permute-done.51 = f32[2,2048]{1,0:T(2,128)S(1)} collective-permute-done((f32[2,2048]{1,0:T(2,128)S(1)}, f32[2,2048]{1,0:T(2,128)S(1)}, u32[]{:S(2)}, u32[]{:S(2)}) %collective-permute-start.51) | collective-permute-done | bytes 16416 | tf_op jit(solution)/shard_map/ppermute | solution.py:29
  (449 shorter events, 322.4 us)
Async XLA Ops:
  4.0 46.3 %collective-permute-start.12 = (bf16[256,1024]{1,0:T(8,128)(2,1)}, bf16[256,1024]{1,0:T(8,128)(2,1)}, u32[]{:S(2)}, u32[]{:S(2)}) collective-permute-start(bf16[256,1024]{1,0:T(8,128)(2,1)} %constant_dynamic-update-slice_fusion.refs_1_.refs_7_), channel_id=1, source_target_pairs={{0,16},{16,0},{1,17},{17,1},{2,18},{18,2},{3,19},{19,3},{4,20},{20... | collective-permute-start | bytes 1572872 | tf_op jit(solution)/shard_map/ppermute | solution.py:34
  50.3 70.8 %collective-permute-start.3 = (bf16[256,1536]{1,0:T(8,128)(2,1)S(1)}, bf16[256,1536]{1,0:T(8,128)(2,1)S(1)}, u32[]{:S(2)}, u32[]{:S(2)}) collective-permute-start(bf16[256,1536]{1,0:T(8,128)(2,1)S(1)} %copy-done.81), channel_id=1, source_target_pairs={{0,4},{4,0},{1,5},{5,1},{2,6},{6,2},{3,7},{7,3},{8,12},{12,8},{9,1... | collective-permute-start | bytes 2359304 | tf_op jit(solution)/shard_map/ppermute | solution.py:29
  77.1 42.4 %collective-permute-start.16 = (bf16[256,1024]{1,0:T(8,128)(2,1)S(1)}, bf16[256,1024]{1,0:T(8,128)(2,1)S(1)}, u32[]{:S(2)}, u32[]{:S(2)}) collective-permute-start(bf16[256,1024]{1,0:T(8,128)(2,1)S(1)} %constant_dynamic-slice_fusion.12.refs_0_.refs_4_), channel_id=1, source_target_pairs={{0,8},{4,12},{8,0},{12,4},{1,9},{5,13},{9,1},{13,5},{2,10},{6,14},... | collective-permute-start | bytes 1572872 | tf_op jit(solution)/shard_map/ppermute | solution.py:29
  77.1 43.1 %collective-permute-start.15 = (bf16[256,1024]{1,0:T(8,128)(2,1)S(1)}, bf16[256,1024]{1,0:T(8,128)(2,1)S(1)}, u32[]{:S(2)}, u32[]{:S(2)}) collective-permute-start(bf16[256,1024]{1,0:T(8,128)(2,1)S(1)} %constant_dynamic-slice_fusion.12.refs_0_.refs_4_), channel_id=1, source_target_pairs={{0,4},{4,0},{8,12},{12,8},{1,5},{5,1},{9,13},{13,9},{2,6},{6,2},{1... | collective-permute-start | bytes 1572872 | tf_op jit(solution)/shard_map/ppermute | solution.py:29
  82.3 71.3 %collective-permute-start.5 = (bf16[512,1024]{1,0:T(8,128)(2,1)}, bf16[512,1024]{1,0:T(8,128)(2,1)}, u32[]{:S(2)}, u32[]{:S(2)}) collective-permute-start(bf16[512,1024]{1,0:T(8,128)(2,1)} %constant_dynamic-update-slice_fusion.4.refs_1_.refs_2_.refs_3_), channel_id=1, source_target_pairs={{0,4},{4,0},{1,5},{5,1},{2,6},{6,2},{3,7},{7,3},{8,12},{12,8},{9,1... | collective-permute-start | bytes 3145736 | tf_op jit(solution)/shard_map/ppermute | solution.py:29
  90.0 64.7 %collective-permute-start.2 = (bf16[256,1536]{1,0:T(8,128)(2,1)}, bf16[256,1536]{1,0:T(8,128)(2,1)}, u32[]{:S(2)}, u32[]{:S(2)}) collective-permute-start(bf16[256,1536]{1,0:T(8,128)(2,1)} %pad_maximum_fusion.3), channel_id=1, source_target_pairs={{0,8},{8,0},{1,9},{9,1},{2,10},{10,2},{3,11},{11,3},{4,12},{12,4},... | collective-permute-start | bytes 2359304 | tf_op jit(solution)/shard_map/ppermute | solution.py:29
  121.1 53.7 %collective-permute-start.19 = (bf16[256,1536]{1,0:T(8,128)(2,1)}, bf16[256,1536]{1,0:T(8,128)(2,1)}, u32[]{:S(2)}, u32[]{:S(2)}) collective-permute-start(bf16[256,1536]{1,0:T(8,128)(2,1)} %pad_maximum_fusion.6), channel_id=1, source_target_pairs={{0,4},{4,0},{1,5},{5,1},{2,6},{6,2},{3,7},{7,3},{8,12},{12,8},{9,1... | collective-permute-start | bytes 2359304 | tf_op jit(solution)/shard_map/ppermute | solution.py:29
  122.0 78.6 %collective-permute-start.8 = (bf16[512,1536]{1,0:T(8,128)(2,1)}, bf16[512,1536]{1,0:T(8,128)(2,1)}, u32[]{:S(2)}, u32[]{:S(2)}) collective-permute-start(bf16[512,1536]{1,0:T(8,128)(2,1)} %constant_dynamic-update-slice_fusion.2.refs_0_), channel_id=1, source_target_pairs={{0,16},{16,0},{1,17},{17,1},{2,18},{18,2},{3,19},{19,3},{4,20},{20... | collective-permute-start | bytes 4718600 | tf_op jit(solution)/shard_map/ppermute | solution.py:34
  125.6 55.6 %collective-permute-start.6 = (bf16[512,1024]{1,0:T(8,128)(2,1)}, bf16[512,1024]{1,0:T(8,128)(2,1)}, u32[]{:S(2)}, u32[]{:S(2)}) collective-permute-start(bf16[512,1024]{1,0:T(8,128)(2,1)} %constant_dynamic-update-slice_fusion.4.refs_1_.refs_2_.refs_3_), channel_id=1, source_target_pairs={{0,16},{16,0},{1,17},{17,1},{2,18},{18,2},{3,19},{19,3},{4,20},{20... | collective-permute-start | bytes 3145736 | tf_op jit(solution)/shard_map/ppermute | solution.py:34
  153.6 42.1 %collective-permute-start.7 = (bf16[512,1024]{1,0:T(8,128)(2,1)}, bf16[512,1024]{1,0:T(8,128)(2,1)}, u32[]{:S(2)}, u32[]{:S(2)}) collective-permute-start(bf16[512,1024]{1,0:T(8,128)(2,1)} %collective-permute-done.5.refs_2_.refs_3_.refs_4_), channel_id=1, source_target_pairs={{0,16},{16,0},{1,17},{17,1},{2,18},{18,2},{3,19},{19,3},{4,20},{20... | collective-permute-start | bytes 3145736 | tf_op jit(solution)/shard_map/ppermute | solution.py:34
  154.7 45.9 %collective-permute-start.10 = (bf16[256,1536]{1,0:T(8,128)(2,1)}, bf16[256,1536]{1,0:T(8,128)(2,1)}, u32[]{:S(2)}, u32[]{:S(2)}) collective-permute-start(bf16[256,1536]{1,0:T(8,128)(2,1)} %pad_maximum_fusion.4), channel_id=1, source_target_pairs={{0,12},{4,8},{8,4},{12,0},{1,13},{5,9},{9,5},{13,1},{2,14},{6,10},... | collective-permute-start | bytes 2359304 | tf_op jit(solution)/shard_map/ppermute | solution.py:29
  174.8 47.6 %collective-permute-start.18 = (bf16[256,1536]{1,0:T(8,128)(2,1)}, bf16[256,1536]{1,0:T(8,128)(2,1)}, u32[]{:S(2)}, u32[]{:S(2)}) collective-permute-start(bf16[256,1536]{1,0:T(8,128)(2,1)} %pad_maximum_fusion.5), channel_id=1, source_target_pairs={{0,8},{8,0},{1,9},{9,1},{2,10},{10,2},{3,11},{11,3},{4,12},{12,4},... | collective-permute-start | bytes 2359304 | tf_op jit(solution)/shard_map/ppermute | solution.py:29
  244.0 55.1 %collective-permute-start.25 = (bf16[384,2048]{1,0:T(8,128)(2,1)S(1)}, bf16[384,2048]{1,0:T(8,128)(2,1)}, u32[]{:S(2)}, u32[]{:S(2)}) collective-permute-start(bf16[384,2048]{1,0:T(8,128)(2,1)S(1)} %get-tuple-element.115.refs_2_.refs_4_), channel_id=1, source_target_pairs={{0,4},{4,0},{1,5},{5,1},{2,6},{6,2},{3,7},{7,3},{8,12},{12,8},{9,1... | collective-permute-start | bytes 4718600 | tf_op jit(solution)/shard_map/ppermute | solution.py:29
  249.1 68.5 %collective-permute-start.24 = (bf16[512,1536]{1,0:T(8,128)(2,1)}, bf16[512,1536]{1,0:T(8,128)(2,1)}, u32[]{:S(2)}, u32[]{:S(2)}) collective-permute-start(bf16[512,1536]{1,0:T(8,128)(2,1)} %constant_dynamic-update-slice_fusion.6.refs_0_), channel_id=1, source_target_pairs={{0,16},{16,0},{1,17},{17,1},{2,18},{18,2},{3,19},{19,3},{4,20},{20... | collective-permute-start | bytes 4718600 | tf_op jit(solution)/shard_map/ppermute | solution.py:34
  252.6 65.1 %collective-permute-start.21 = (bf16[384,2048]{1,0:T(8,128)(2,1)}, bf16[384,2048]{1,0:T(8,128)(2,1)S(1)}, u32[]{:S(2)}, u32[]{:S(2)}) collective-permute-start(bf16[384,2048]{1,0:T(8,128)(2,1)} %add_convert_fusion.12), channel_id=1, source_target_pairs={{0,2},{1,3},{2,0},{3,1},{4,6},{5,7},{6,4},{7,5},{8,10},{9,11},{10,... | collective-permute-start | bytes 4718600 | tf_op jit(solution)/shard_map/ppermute | solution.py:29
  253.8 45.3 %collective-permute-start.22 = (bf16[256,1536]{1,0:T(8,128)(2,1)}, bf16[256,1536]{1,0:T(8,128)(2,1)}, u32[]{:S(2)}, u32[]{:S(2)}) collective-permute-start(bf16[256,1536]{1,0:T(8,128)(2,1)} %pad_maximum_fusion.6), channel_id=1, source_target_pairs={{0,12},{4,8},{8,4},{12,0},{1,13},{5,9},{9,5},{13,1},{2,14},{6,10},... | collective-permute-start | bytes 2359304 | tf_op jit(solution)/shard_map/ppermute | solution.py:29
  395.5 44.5 %collective-permute-start.32 = (bf16[384,2048]{1,0:T(8,128)(2,1)}, bf16[384,2048]{1,0:T(8,128)(2,1)}, u32[]{:S(2)}, u32[]{:S(2)}) collective-permute-start(bf16[384,2048]{1,0:T(8,128)(2,1)} %get-tuple-element.110), channel_id=1, source_target_pairs={{0,1},{1,0},{2,3},{3,2},{4,5},{5,4},{6,7},{7,6},{8,9},{9,8},{10,11... | collective-permute-start | bytes 4718600 | tf_op jit(solution)/shard_map/ppermute | solution.py:29
  475.1 50.2 %collective-permute-start.39 = (bf16[512,1536]{1,0:T(8,128)(2,1)}, bf16[512,1536]{1,0:T(8,128)(2,1)}, u32[]{:S(2)}, u32[]{:S(2)}) collective-permute-start(bf16[512,1536]{1,0:T(8,128)(2,1)} %get-tuple-element.129), channel_id=1, source_target_pairs={{0,16},{16,0},{1,17},{17,1},{2,18},{18,2},{3,19},{19,3},{4,20},{20... | collective-permute-start | bytes 4718600 | tf_op jit(solution)/shard_map/ppermute | solution.py:34
  482.6 43.0 %collective-permute-start.38 = (bf16[384,2048]{1,0:T(8,128)(2,1)}, bf16[384,2048]{1,0:T(8,128)(2,1)}, u32[]{:S(2)}, u32[]{:S(2)}) collective-permute-start(bf16[384,2048]{1,0:T(8,128)(2,1)} %add_convert_fusion.9), channel_id=1, source_target_pairs={{0,2},{1,3},{2,0},{3,1},{4,6},{5,7},{6,4},{7,5},{8,10},{9,11},{10,... | collective-permute-start | bytes 4718600 | tf_op jit(solution)/shard_map/ppermute | solution.py:29
  513.9 98.9 %collective-permute-start.60 = (bf16[512,1536]{1,0:T(8,128)(2,1)}, bf16[512,1536]{1,0:T(8,128)(2,1)}, u32[]{:S(2)}, u32[]{:S(2)}) collective-permute-start(bf16[512,1536]{1,0:T(8,128)(2,1)} %add_convert_fusion.4), channel_id=1, source_target_pairs={{0,8},{8,0},{1,9},{9,1},{2,10},{10,2},{3,11},{11,3},{4,12},{12,4},... | collective-permute-start | bytes 4718600 | tf_op jit(solution)/shard_map/ppermute | solution.py:29
  536.6 76.2 %collective-permute-start.37 = (bf16[384,2048]{1,0:T(8,128)(2,1)}, bf16[384,2048]{1,0:T(8,128)(2,1)}, u32[]{:S(2)}, u32[]{:S(2)}) collective-permute-start(bf16[384,2048]{1,0:T(8,128)(2,1)} %add_convert_fusion.7), channel_id=1, source_target_pairs={{0,4},{4,0},{1,5},{5,1},{2,6},{6,2},{3,7},{7,3},{8,12},{12,8},{9,1... | collective-permute-start | bytes 4718600 | tf_op jit(solution)/shard_map/ppermute | solution.py:29
  561.6 66.0 %collective-permute-start.63 = (bf16[512,1536]{1,0:T(8,128)(2,1)}, bf16[512,1536]{1,0:T(8,128)(2,1)S(1)}, u32[]{:S(2)}, u32[]{:S(2)}) collective-permute-start(bf16[512,1536]{1,0:T(8,128)(2,1)} %get-tuple-element.148), channel_id=1, source_target_pairs={{0,16},{16,0},{1,17},{17,1},{2,18},{18,2},{3,19},{19,3},{4,20},{20... | collective-permute-start | bytes 4718600 | tf_op jit(solution)/shard_map/ppermute | solution.py:34
  619.6 51.6 %collective-permute-start.41 = (bf16[384,1024]{1,0:T(8,128)(2,1)}, bf16[384,1024]{1,0:T(8,128)(2,1)}, u32[]{:S(2)}, u32[]{:S(2)}) collective-permute-start(bf16[384,1024]{1,0:T(8,128)(2,1)} %constant_dynamic-slice_fusion.3), channel_id=1, source_target_pairs={{0,2},{1,3},{2,0},{3,1},{4,6},{5,7},{6,4},{7,5},{8,10},{9,11},{10,... | collective-permute-start | bytes 2359304 | tf_op jit(solution)/shard_map/ppermute | solution.py:29
  627.6 46.3 %collective-permute-start.61 = (bf16[256,1536]{1,0:T(8,128)(2,1)}, bf16[256,1536]{1,0:T(8,128)(2,1)}, u32[]{:S(2)}, u32[]{:S(2)}) collective-permute-start(bf16[256,1536]{1,0:T(8,128)(2,1)} %slice.233), channel_id=1, source_target_pairs={{0,4},{4,0},{1,5},{5,1},{2,6},{6,2},{3,7},{7,3},{8,12},{12,8},{9,1... | collective-permute-start | bytes 2359304 | tf_op jit(solution)/shard_map/ppermute | solution.py:29
  635.7 43.3 %collective-permute-start.54 = (bf16[1024,1024]{1,0:T(8,128)(2,1)S(1)}, bf16[1024,1024]{1,0:T(8,128)(2,1)S(1)}, u32[]{:S(2)}, u32[]{:S(2)}) collective-permute-start(bf16[1024,1024]{1,0:T(8,128)(2,1)S(1)} %attn_grads.5), channel_id=1, source_target_pairs={{0,16},{16,0},{1,17},{17,1},{2,18},{18,2},{3,19},{19,3},{4,20},{20... | collective-permute-start | bytes 6291464 | tf_op jit(solution)/shard_map/ppermute | solution.py:34
  644.1 83.2 %collective-permute-start.64 = (bf16[512,1536]{1,0:T(8,128)(2,1)}, bf16[512,1536]{1,0:T(8,128)(2,1)}, u32[]{:S(2)}, u32[]{:S(2)}) collective-permute-start(bf16[512,1536]{1,0:T(8,128)(2,1)} %add_convert_fusion.2), channel_id=1, source_target_pairs={{0,8},{8,0},{1,9},{9,1},{2,10},{10,2},{3,11},{11,3},{4,12},{12,4},... | collective-permute-start | bytes 4718600 | tf_op jit(solution)/shard_map/ppermute | solution.py:29
  660.2 73.0 %collective-permute-start.46 = (bf16[384,2048]{1,0:T(8,128)(2,1)S(1)}, bf16[384,2048]{1,0:T(8,128)(2,1)}, u32[]{:S(2)}, u32[]{:S(2)}) collective-permute-start(bf16[384,2048]{1,0:T(8,128)(2,1)S(1)} %get-tuple-element.143), channel_id=1, source_target_pairs={{0,1},{1,0},{2,3},{3,2},{4,5},{5,4},{6,7},{7,6},{8,9},{9,8},{10,11... | collective-permute-start | bytes 4718600 | tf_op jit(solution)/shard_map/ppermute | solution.py:29
  671.2 52.8 %collective-permute-start.57 = (bf16[1024,1024]{1,0:T(8,128)(2,1)S(1)}, bf16[1024,1024]{1,0:T(8,128)(2,1)S(1)}, u32[]{:S(2)}, u32[]{:S(2)}) collective-permute-start(bf16[1024,1024]{1,0:T(8,128)(2,1)S(1)} %attn_grads.7), channel_id=1, source_target_pairs={{0,16},{16,0},{1,17},{17,1},{2,18},{18,2},{3,19},{19,3},{4,20},{20... | collective-permute-start | bytes 6291464 | tf_op jit(solution)/shard_map/ppermute | solution.py:34
  680.1 61.4 %collective-permute-start.55 = (bf16[512,1024]{1,0:T(8,128)(2,1)S(1)}, bf16[512,1024]{1,0:T(8,128)(2,1)S(1)}, u32[]{:S(2)}, u32[]{:S(2)}) collective-permute-start(bf16[512,1024]{1,0:T(8,128)(2,1)S(1)} %slice.179), channel_id=1, source_target_pairs={{0,4},{4,0},{1,5},{5,1},{2,6},{6,2},{3,7},{7,3},{8,12},{12,8},{9,1... | collective-permute-start | bytes 3145736 | tf_op jit(solution)/shard_map/ppermute | solution.py:29
  729.4 40.1 %collective-permute-start.65 = (bf16[256,1536]{1,0:T(8,128)(2,1)S(1)}, bf16[256,1536]{1,0:T(8,128)(2,1)S(1)}, u32[]{:S(2)}, u32[]{:S(2)}) collective-permute-start(bf16[256,1536]{1,0:T(8,128)(2,1)S(1)} %slice.232), channel_id=1, source_target_pairs={{0,4},{4,0},{1,5},{5,1},{2,6},{6,2},{3,7},{7,3},{8,12},{12,8},{9,1... | collective-permute-start | bytes 2359304 | tf_op jit(solution)/shard_map/ppermute | solution.py:29
  736.5 55.6 %collective-permute-start.58 = (bf16[512,1024]{1,0:T(8,128)(2,1)}, bf16[512,1024]{1,0:T(8,128)(2,1)}, u32[]{:S(2)}, u32[]{:S(2)}) collective-permute-start(bf16[512,1024]{1,0:T(8,128)(2,1)} %slice.184), channel_id=1, source_target_pairs={{0,4},{4,0},{1,5},{5,1},{2,6},{6,2},{3,7},{7,3},{8,12},{12,8},{9,1... | collective-permute-start | bytes 3145736 | tf_op jit(solution)/shard_map/ppermute | solution.py:29
  742.7 81.4 %collective-permute-start.56 = (bf16[256,1024]{1,0:T(8,128)(2,1)}, bf16[256,1024]{1,0:T(8,128)(2,1)}, u32[]{:S(2)}, u32[]{:S(2)}) collective-permute-start(bf16[256,1024]{1,0:T(8,128)(2,1)} %slice.235), channel_id=1, source_target_pairs={{0,8},{8,0},{1,9},{9,1},{2,10},{10,2},{3,11},{11,3},{4,12},{12,4},... | collective-permute-start | bytes 1572872 | tf_op jit(solution)/shard_map/ppermute | solution.py:29
  (136 other events, 2145.3 us)

commit v5 on v4

--- a/solution.py
+++ b/solution.py
@@ -705,7 +705,8 @@
     kv_three = swap(kv_two, "lo")
     kv_stack = over_dp([kv_weight, kv_two, kv_one, kv_three])
     qo_weight = after(jnp.concatenate([query_weight, out_weight], axis=1), kv_three)
-    qo_even = jnp.concatenate([qo_weight, swap(qo_weight, "hi")], axis=0)
+    qo_two = swap(qo_weight, "hi")
+    qo_even = jnp.concatenate([qo_weight, qo_two], axis=0)
     qo_odd = swap(qo_even, "lo")
     qo_stack = over_dp([qo_even, qo_odd])
 
@@ -724,10 +725,8 @@
         near = jnp.concatenate([keep, swap(give, "lo")], axis=0)
         return near, swap(keep, "hi"), give
 
-    def ffn_stack(near_blocks, far):
-        return place_rows(
-            [x for both in zip(near_blocks, gather_dp(far)) for x in both], places_ffn
-        )
+    def ffn_stack(near_blocks, far_blocks):
+        return place_rows([x for both in zip(near_blocks, far_blocks) for x in both], places_ffn)
 
     def gather_dp(own):
         return [own] + [turn(own, "dp", -s) for s in range(1, dp_count)]
@@ -749,7 +748,7 @@
     first = low(first_norm * gain_one)
 
     kv = project(
-        [first], kv_stack, places, bit_ref, 0, 2 * head_width, cosine, sine, head_width
+        [after(first, qo_two)], kv_stack, places, bit_ref, 0, 2 * head_width, cosine, sine, head_width
     )
     prompt_own = lax.dynamic_slice_in_dim(kv, mine * CLEN, CLEN)
     prompts = [prompt_own] + [swap(prompt_own, CTX, k) for k in range(1, ctx_count)]
@@ -772,20 +771,19 @@
     query = after(query, *near_one[1:], three_one)
     mixed, lse = attention_forward(order, rank, query, kv, prompts)
     near_two, two_two, give_two = ffn_sends(1, *prompts[1:])
-    mixed = after(mixed, two_two, near_two)
-    near_two = gather_dp(near_two)
+    near_two = gather_dp(after(near_two, two_one, *qo_stack[2:]))
+    mixed = after(mixed, two_two, *near_two[1:])
     three_two = swap(after(give_two, three_one), CTX, 3)
-    ffn_weights = [
-        ffn_stack(near_one, jnp.concatenate([two_one, three_one], axis=0)),
-        ffn_stack(near_two, jnp.concatenate([two_two, three_two], axis=0)),
-    ]
+    far_one_blocks = gather_dp(jnp.concatenate([two_one, three_one], axis=0))
+    far_two_blocks = gather_dp(jnp.concatenate([two_two, three_two], axis=0))
+    ffn_weights = [ffn_stack(near_one, far_one_blocks), ffn_stack(near_two, far_two_blocks)]
 
     kept, given = project_back(
         [mixed], ((0, head_width),), [qo_stack], places, bit_ref
     )
-    mixed_out = low(add(kept, swap(given, "tp")))
+    mixed_out = low(add(kept, after(swap(given, "tp"), three_two)))
     mixed_far = after(
-        swap(mixed_out, "tp", 2), three_two, ffn_weights[0], *near_two[1:], cotangent_far
+        swap(mixed_out, "tp", 2), ffn_weights[0], cotangent_far
     )
     middle = row_half(tokens).astype(F32) + add(mixed_out, mixed_far)
     second_norm, second_scale = normalize(middle)
@@ -796,22 +794,22 @@
         [cotangent_far, swap(cotangent_far, "tp")],
     ]
     second_far = swap(second_half, "lo")
-    near = [second_half, swap(second_half, "tp")]
+    near = [second_half, after(swap(second_half, "tp"), *far_two_blocks[1:])]
     made = [[ffn(near, cotangents[0], [w]) for w in ffn_weights]]
-    second_far = after(second_far, made[0][0][0])
+    gate_spans = tuple((f, 0, f, 0, 2 * chunk) for f in range(FFN_CHUNKS))
+    down_spans = tuple((f, 0, f, 2 * chunk, chunk) for f in range(FFN_CHUNKS))
+    dsecond_near = ffn_back([m[1] for m in made[0]], ffn_weights, gate_spans)
+    second_far = after(second_far, *dsecond_near)
     far = [second_far, swap(second_far, "tp")]
     made.append([ffn(far, cotangents[1], [w]) for w in ffn_weights])
     seconds = [near, far]
     hiddens = [[m[0] for m in side] for side in made]
     dpairs = [[m[1] for m in side] for side in made]
-    gate_spans = tuple((f, 0, f, 0, 2 * chunk) for f in range(FFN_CHUNKS))
-    down_spans = tuple((f, 0, f, 2 * chunk, chunk) for f in range(FFN_CHUNKS))
 
     def cores(part):
         return low(add(part[0], swap(part[1], "tp")))
 
     dsecond_far = ffn_back(dpairs[1], ffn_weights, gate_spans)
-    dsecond_near = ffn_back(dpairs[0], ffn_weights, gate_spans)
     dsecond_got, dsecond_half = swap(cores(dsecond_far), "lo"), cores(dsecond_near)
 
     lefts, left_cots = after(
@@ -852,7 +850,7 @@
     far_one = over_dp_rows(0, pair_rows)
     near_one_got = over_dp_rows(0, 0, *far_one)
     far_two = over_dp_rows(1, pair_rows, *near_one_got)
-    near_two_got = over_dp_rows(1, 0, *far_two)
+    near_two_got = over_dp_rows(1, 0, *near_one_got)
     dsecond_got = after(dsecond_got, *ffn_given[1], ffn_own[0], *far_one)
     dsecond = low(add(dsecond_half, dsecond_got))
     hi_one = swap(total_rows(0, pair_rows, far_one), "hi")

time: 840 us -> 818 us (0.974)
  local copies, waits for them, and re-layouts: 82.6 us -> 64.9 us
    ppermute x16, waiting for transfers between devices: 137 us -> 81.5 us  [turn(): lax.ppermute(values, axis, [(i, (i + shift) % count) for i in range(count)])]
    ppermute x50, waiting for transfers between devices: 191 us -> 241 us  [swap(): return lax.ppermute(values, axis, [(i, i ^ mask) for i in range(count)])]
    unnamed x211 -> x232, local copies, waits for them, and re-layouts: 44.8 us -> 31.4 us
  transfers between devices with their start and end apart: 66 -> 66, of which waited for: 28 -> 31; matrix products, arithmetic and copies ran while one was open for 15% -> 15% of each run, Pallas kernels for 24% -> 24%
where the time goes in v5:
time: 818 us; the launch traced here: 808 us
  waiting for transfers between devices  322 us (39%)
  Pallas kernels  228 us (28%)
  starting transfers between devices  105 us (13%)
  other arithmetic  84.8 us (10%)
  local copies, waits for them, and re-layouts  64.9 us (8%)
    ppermute x50, waiting for transfers between devices, swap(): return lax.ppermute(values, axis, [(i, i ^ mask) for i in range(count)])  241 us
    pallas_call x19, Pallas kernels, call(): pl.pallas_call(kernel, in_specs=[SMEM] * len(smem) + [VMEM] * len(operand...  110 us
    ppermute x50, starting transfers between devices, swap(): return lax.ppermute(values, axis, [(i, i ^ mask) for i in range(count)])  92.3 us
    ppermute x16, waiting for transfers between devices, turn(): lax.ppermute(values, axis, [(i, (i + shift) % count) for i in range(count)])  81.5 us
    pallas_call x4, Pallas kernels, ffn_grads(): pl.pallas_call(functools.partial(ffn_grads_kernel, tile, unit), grid_spec...  52.8 us
    pallas_call x1, Pallas kernels, attention_backward(): pl.pallas_call(functools.partial(backward_kernel, pieces), grid_spec=pltp...  42.9 us
    convert_element_type x15, other arithmetic, low(): return values.astype(BF16)  33 us
    unnamed x232, local copies, waits for them, and re-layouts  31.4 us
  transfers between devices with their start and end apart: 66, of which 31 were waited for; matrix products, arithmetic and copies ran while one was open for 15% of the time, Pallas kernels for 24%

profile of v5, /device:TPU:1, one launch (start us, length us, event | category | flops | bytes accessed | tf_op | source)
XLA Modules:
  0.0 808.4 jit_solution(6188763610307187956)
XLA Ops:
  22.3 6.9 collective-permute-done.refs_2_.refs_8_
  34.6 7.5 collective-permute-done.1.refs_4_.refs_10_
  51.5 14.8 %collective-permute-done.4 = bf16[256,1024]{1,0:T(8,128)(2,1)} collective-permute-done((bf16[256,1024]{1,0:T(8,128)(2,1)}, bf16[256,1024]{1,0:T(8,128)(2,1)}, u32[]{:S(2)}, u32[]{:S(2)}) %collective-permute-start.4) | collective-permute-done | bytes 524320 | tf_op jit(solution)/shard_map/ppermute | solution.py:29
  72.8 7.4 collective-permute-done.9.refs_8_.refs_14_
  80.2 7.3 project.4.ks_ref.vs_ref
  94.7 9.8 %collective-permute-done.17.refs_3_.refs_7_ = bf16[256,1024]{1,0:T(8,128)(2,1)S(1)} collective-permute-done((bf16[256,1024]{1,0:T(8,128)(2,1)S(1)}, bf16[256,1024]{1,0:T(8,128)(2,1)S(1)}, u32[]{:S(2)}, u32[]{:S(2)}) %collective-permute-start.17) | collective-permute-done | bytes 524320 | tf_op jit(solution)/shard_map/ppermute | solution.py:29
  104.5 27.3 %collective-permute-done.16.refs_2_.refs_6_ = bf16[256,1024]{1,0:T(8,128)(2,1)S(1)} collective-permute-done((bf16[256,1024]{1,0:T(8,128)(2,1)S(1)}, bf16[256,1024]{1,0:T(8,128)(2,1)S(1)}, u32[]{:S(2)}, u32[]{:S(2)}) %collective-permute-start.16) | collective-permute-done | bytes 524320 | tf_op jit(solution)/shard_map/ppermute | solution.py:29
  136.6 23.0 %collective-permute-done.3 = bf16[256,1536]{1,0:T(8,128)(2,1)S(1)} collective-permute-done((bf16[256,1536]{1,0:T(8,128)(2,1)}, bf16[256,1536]{1,0:T(8,128)(2,1)S(1)}, u32[]{:S(2)}, u32[]{:S(2)}) %collective-permute-start.3) | collective-permute-done | bytes 786464 | tf_op jit(solution)/shard_map/ppermute | solution.py:29
  160.9 15.6 %collective-permute-done.19 = bf16[256,1536]{1,0:T(8,128)(2,1)S(1)} collective-permute-done((bf16[256,1536]{1,0:T(8,128)(2,1)S(1)}, bf16[256,1536]{1,0:T(8,128)(2,1)S(1)}, u32[]{:S(2)}, u32[]{:S(2)}) %collective-permute-start.19) | collective-permute-done | bytes 786464 | tf_op jit(solution)/shard_map/ppermute | solution.py:29
  199.9 8.5 %collective-permute-done.8.refs_2_ = bf16[512,1536]{1,0:T(8,128)(2,1)} collective-permute-done((bf16[512,1536]{1,0:T(8,128)(2,1)}, bf16[512,1536]{1,0:T(8,128)(2,1)}, u32[]{:S(2)}, u32[]{:S(2)}) %collective-permute-start.8) | collective-permute-done | bytes 1572896 | tf_op jit(solution)/shard_map/ppermute | solution.py:34
  208.5 20.6 %attend.1 = (bf16[768,512]{1,0:T(8,128)(2,1)S(1)}, f32[768,512]{1,0:T(8,128)S(1)}) custom-call(s32[3]{0:T(128)S(1)} %compare_select_fusion.7.order_ref, s32[4]{0:T(128)S(1)} %gather_fusion.1, bf16[768,512]{1,0:T(8,128)(2,1)S(1)} %project.3.q_ref, bf16[768,1024]{1,0:T(8,128)(2,1)S(1)} %copy-done.16, bf16[768,1024]{1,0:T(8,128)(2,1)S(1)} %copy-done.16, ...), custom_call_target="tpu_custom_call" | custom-call | flops 503316480 | bytes 393216 | tf_op jit(solution)/shard_map/attend/pallas_call | solution.py:582
  229.1 21.0 %collective-permute-done.18 = bf16[256,1536]{1,0:T(8,128)(2,1)} collective-permute-done((bf16[256,1536]{1,0:T(8,128)(2,1)}, bf16[256,1536]{1,0:T(8,128)(2,1)}, u32[]{:S(2)}, u32[]{:S(2)}) %collective-permute-start.18) | collective-permute-done | bytes 786464 | tf_op jit(solution)/shard_map/ppermute | solution.py:29
  266.9 6.9 collective-permute-start.25
  289.3 22.2 %collective-permute-done.24.refs_3_ = bf16[512,1536]{1,0:T(8,128)(2,1)} collective-permute-done((bf16[512,1536]{1,0:T(8,128)(2,1)}, bf16[512,1536]{1,0:T(8,128)(2,1)}, u32[]{:S(2)}, u32[]{:S(2)}) %collective-permute-start.24) | collective-permute-done | bytes 1572896 | tf_op jit(solution)/shard_map/ppermute | solution.py:34
  326.1 17.6 %collective-permute-start.28 = (bf16[384,2048]{1,0:T(8,128)(2,1)S(1)}, bf16[384,2048]{1,0:T(8,128)(2,1)S(1)}, u32[]{:S(2)}, u32[]{:S(2)}) collective-permute-start(bf16[384,2048]{1,0:T(8,128)(2,1)S(1)} %multiply_convert_fusion.1.refs_0_), channel_id=1, source_target_pairs={{0,4},{4,0},{1,5},{5,1},{2,6},{6,2},{3,7},{7,3},{8,12},{12,8},{9,1... | collective-permute-start | bytes 4718600 | tf_op jit(solution)/shard_map/ppermute | solution.py:29
  359.6 9.2 %ffn_back.4 = (bf16[384,2048]{1,0:T(8,128)(2,1)S(1)}, bf16[384,2048]{1,0:T(8,128)(2,1)}) custom-call(bf16[768,1024]{1,0:T(8,128)(2,1)S(1)} %get-tuple-element.108.refs_0_.refs_10_, bf16[768,1024]{1,0:T(8,128)(2,1)S(1)} %get-tuple-element.109.refs_1_.refs_10_, bf16[2048,1536]{1,0:T(8,128)(2,1)S(1)} %place_rows.2.refs_4_.refs_2_, ...), custom_call_target="tpu_custom_call" | custom-call | flops 402653184 | bytes 917504 | tf_op jit(solution)/shard_map/ffn_back/pallas_call | solution.py:81
  370.0 8.4 %collective-permute-done.28.refs_0_.refs_2_ = bf16[384,2048]{1,0:T(8,128)(2,1)S(1)} collective-permute-done((bf16[384,2048]{1,0:T(8,128)(2,1)S(1)}, bf16[384,2048]{1,0:T(8,128)(2,1)S(1)}, u32[]{:S(2)}, u32[]{:S(2)}) %collective-permute-start.28) | collective-permute-done | bytes 1572896 | tf_op jit(solution)/shard_map/ppermute | solution.py:29
  382.1 8.0 ffn.7
  392.7 8.6 %ffn.6 = (bf16[768,512]{1,0:T(8,128)(2,1)S(1)}, bf16[768,1024]{1,0:T(8,128)(2,1)S(1)}) custom-call(bf16[384,2048]{1,0:T(8,128)(2,1)S(1)} %copy-done.13, bf16[384,2048]{1,0:T(8,128)(2,1)S(1)} %collective-permute-done.29.refs_1_.refs_3_, bf16[384,2048]{1,0:T(8,128)(2,1)} %collective-permute-done.25.refs_2_.refs_6_, ...), custom_call_target="tpu_custom_call" | custom-call | flops 301989888 | bytes 933888 | tf_op jit(solution)/shard_map/ffn/pallas_call | solution.py:81
  401.4 9.3 %ffn_back.5 = (bf16[384,2048]{1,0:T(8,128)(2,1)S(1)}, bf16[384,2048]{1,0:T(8,128)(2,1)}) custom-call(bf16[768,1024]{1,0:T(8,128)(2,1)S(1)} %get-tuple-element.115.refs_0_.refs_11_, bf16[768,1024]{1,0:T(8,128)(2,1)S(1)} %get-tuple-element.116.refs_1_.refs_11_, bf16[2048,1536]{1,0:T(8,128)(2,1)S(1)} %place_rows.2.refs_4_.refs_2_, ...), custom_call_target="tpu_custom_call" | custom-call | flops 402653184 | bytes 917504 | tf_op jit(solution)/shard_map/ffn_back/pallas_call | solution.py:81
  412.8 13.2 %ffn_grads.6 = bf16[1024,1536]{1,0:T(8,128)(2,1)} custom-call(s32[2]{0:T(128)} %compare_select_fusion.2.dp_ref, s32[4]{0:T(128)} %gather_fusion.3, bf16[384,2048]{1,0:T(8,128)(2,1)} %copy-done.9, bf16[384,2048]{1,0:T(8,128)(2,1)} %copy-done.11, bf16[384,2048]{1,0:T(8,128)(2,1)} %copy-done.12, bf16[384,2048]{1,0:T(8,128)(2,1)} %copy-done.14, ...), custom_call_target="tpu_custom_call" | custom-call | flops 301989888 | bytes 884736 | tf_op jit(solution)/shard_map/ffn_grads/pallas_call | solution.py:348
  436.3 13.2 %ffn_grads.5 = bf16[1024,1536]{1,0:T(8,128)(2,1)} custom-call(s32[2]{0:T(128)} %compare_select_fusion.2.dp_ref, s32[4]{0:T(128)} %gather_fusion.3, bf16[384,2048]{1,0:T(8,128)(2,1)} %copy-done.9, bf16[384,2048]{1,0:T(8,128)(2,1)} %copy-done.11, bf16[384,2048]{1,0:T(8,128)(2,1)} %copy-done.12, bf16[384,2048]{1,0:T(8,128)(2,1)} %copy-done.14, ...), custom_call_target="tpu_custom_call" | custom-call | flops 301989888 | bytes 884736 | tf_op jit(solution)/shard_map/ffn_grads/pallas_call | solution.py:348
  449.5 13.3 %ffn_grads.4 = bf16[1024,1536]{1,0:T(8,128)(2,1)} custom-call(s32[2]{0:T(128)} %compare_select_fusion.2.dp_ref, s32[4]{0:T(128)} %gather_fusion.3, bf16[384,2048]{1,0:T(8,128)(2,1)} %copy-done.9, bf16[384,2048]{1,0:T(8,128)(2,1)} %copy-done.11, bf16[384,2048]{1,0:T(8,128)(2,1)} %copy-done.12, bf16[384,2048]{1,0:T(8,128)(2,1)} %copy-done.14, ...), custom_call_target="tpu_custom_call" | custom-call | flops 301989888 | bytes 884736 | tf_op jit(solution)/shard_map/ffn_grads/pallas_call | solution.py:348
  474.7 13.1 %ffn_grads.7 = bf16[1024,1536]{1,0:T(8,128)(2,1)} custom-call(s32[2]{0:T(128)} %compare_select_fusion.2.dp_ref, s32[4]{0:T(128)} %gather_fusion.3, bf16[384,2048]{1,0:T(8,128)(2,1)} %copy-done.9, bf16[384,2048]{1,0:T(8,128)(2,1)} %copy-done.11, bf16[384,2048]{1,0:T(8,128)(2,1)} %copy-done.12, bf16[384,2048]{1,0:T(8,128)(2,1)} %copy-done.14, ...), custom_call_target="tpu_custom_call" | custom-call | flops 301989888 | bytes 884736 | tf_op jit(solution)/shard_map/ffn_grads/pallas_call | solution.py:348
  538.0 42.9 %attend_back.1 = (bf16[768,512]{1,0:T(8,128)(2,1)S(1)}, f32[768,512]{1,0:T(8,128)S(1)}, f32[768,512]{1,0:T(8,128)S(1)}, f32[256,1024]{1,0:T(8,128)S(1)}, bf16[25...) custom-call(s32[3]{0:T(128)S(1)} %compare_select_fusion.7.order_ref, ...), custom_call_target="tpu_custom_call" | custom-call | flops 1258291200 | bytes 786432 | tf_op jit(solution)/shard_map/attend_back/pallas_call | solution.py:604
  581.0 12.9 %collective-permute-done.37 = bf16[384,2048]{1,0:T(8,128)(2,1)} collective-permute-done((bf16[384,2048]{1,0:T(8,128)(2,1)}, bf16[384,2048]{1,0:T(8,128)(2,1)}, u32[]{:S(2)}, u32[]{:S(2)}) %collective-permute-start.37) | collective-permute-done | bytes 1572896 | tf_op jit(solution)/shard_map/ppermute | solution.py:29
  607.9 8.6 %collective-permute-done.43.refs_0_ = bf16[256,1024]{1,0:T(8,128)(2,1)S(1)} collective-permute-done((bf16[256,1024]{1,0:T(8,128)(2,1)S(1)}, bf16[256,1024]{1,0:T(8,128)(2,1)S(1)}, u32[]{:S(2)}, u32[]{:S(2)}) %collective-permute-start.43) | collective-permute-done | bytes 524320 | tf_op jit(solution)/shard_map/ppermute | solution.py:29
  631.4 9.6 %project_back.3 = (bf16[384,2048]{1,0:T(8,128)(2,1)S(1)}, bf16[384,2048]{1,0:T(8,128)(2,1)S(1)}) custom-call(s32[1]{0:T(128)} %bitcast.bit_ref, s32[8]{0:T(128)S(1)} %xor_add_fusion.1.place_ref, bf16[768,512]{1,0:T(8,128)(2,1)S(1)} %get-tuple-element.140.refs_0_.refs_4_, bf16[768,512]{1,0:T(8,128)(2,1)S(1)} %get-tuple-element.148.refs_1_, ...), custom_call_target="tpu_custom_call" | custom-call | flops 301989888 | bytes 737280 | tf_op jit(solution)/shard_map/project_back/pallas_call | solution.py:81
  662.9 7.3 collective-permute-start.55
  670.3 35.0 %collective-permute-done.57 = bf16[1024,1024]{1,0:T(8,128)(2,1)S(1)} collective-permute-done((bf16[1024,1024]{1,0:T(8,128)(2,1)S(1)}, bf16[1024,1024]{1,0:T(8,128)(2,1)S(1)}, u32[]{:S(2)}, u32[]{:S(2)}) %collective-permute-start.57) | collective-permute-done | bytes 2097184 | tf_op jit(solution)/shard_map/ppermute | solution.py:34
  722.1 26.8 %collective-permute-done.65 = bf16[256,1536]{1,0:T(8,128)(2,1)S(1)} collective-permute-done((bf16[256,1536]{1,0:T(8,128)(2,1)S(1)}, bf16[256,1536]{1,0:T(8,128)(2,1)S(1)}, u32[]{:S(2)}, u32[]{:S(2)}) %collective-permute-start.65) | collective-permute-done | bytes 786464 | tf_op jit(solution)/shard_map/ppermute | solution.py:29
  775.8 23.2 %collective-permute-done.51 = f32[2,2048]{1,0:T(2,128)S(1)} collective-permute-done((f32[2,2048]{1,0:T(2,128)S(1)}, f32[2,2048]{1,0:T(2,128)S(1)}, u32[]{:S(2)}, u32[]{:S(2)}) %collective-permute-start.51) | collective-permute-done | bytes 16416 | tf_op jit(solution)/shard_map/ppermute | solution.py:29
  (469 shorter events, 326.2 us)
Async XLA Ops:
  4.0 68.8 %collective-permute-start.12 = (bf16[256,1024]{1,0:T(8,128)(2,1)}, bf16[256,1024]{1,0:T(8,128)(2,1)}, u32[]{:S(2)}, u32[]{:S(2)}) collective-permute-start(bf16[256,1024]{1,0:T(8,128)(2,1)} %constant_dynamic-update-slice_fusion.refs_1_.refs_7_), channel_id=1, source_target_pairs={{0,16},{16,0},{1,17},{17,1},{2,18},{18,2},{3,19},{19,3},{4,20},{20... | collective-permute-start | bytes 1572872 | tf_op jit(solution)/shard_map/ppermute | solution.py:34
  6.0 42.1 %collective-permute-start.11 = (bf16[256,1024]{1,0:T(8,128)(2,1)}, bf16[256,1024]{1,0:T(8,128)(2,1)}, u32[]{:S(2)}, u32[]{:S(2)}) collective-permute-start(bf16[256,1024]{1,0:T(8,128)(2,1)} %constant_dynamic-update-slice_fusion.refs_1_.refs_7_), channel_id=1, source_target_pairs={{0,4},{4,0},{1,5},{5,1},{2,6},{6,2},{3,7},{7,3},{8,12},{12,8},{9,1... | collective-permute-start | bytes 1572872 | tf_op jit(solution)/shard_map/ppermute | solution.py:29
  68.2 64.0 %collective-permute-start.5 = (bf16[512,1024]{1,0:T(8,128)(2,1)}, bf16[512,1024]{1,0:T(8,128)(2,1)}, u32[]{:S(2)}, u32[]{:S(2)}) collective-permute-start(bf16[512,1024]{1,0:T(8,128)(2,1)} %constant_dynamic-update-slice_fusion.4.refs_1_.refs_2_.refs_3_), channel_id=1, source_target_pairs={{0,4},{4,0},{1,5},{5,1},{2,6},{6,2},{3,7},{7,3},{8,12},{12,8},{9,1... | collective-permute-start | bytes 3145736 | tf_op jit(solution)/shard_map/ppermute | solution.py:29
  91.2 40.6 %collective-permute-start.16 = (bf16[256,1024]{1,0:T(8,128)(2,1)S(1)}, bf16[256,1024]{1,0:T(8,128)(2,1)S(1)}, u32[]{:S(2)}, u32[]{:S(2)}) collective-permute-start(bf16[256,1024]{1,0:T(8,128)(2,1)S(1)} %constant_dynamic-slice_fusion.12.refs_0_.refs_4_), channel_id=1, source_target_pairs={{0,8},{4,12},{8,0},{12,4},{1,9},{5,13},{9,1},{13,5},{2,10},{6,14},... | collective-permute-start | bytes 1572872 | tf_op jit(solution)/shard_map/ppermute | solution.py:29
  91.2 40.6 %collective-permute-start.15 = (bf16[256,1024]{1,0:T(8,128)(2,1)S(1)}, bf16[256,1024]{1,0:T(8,128)(2,1)S(1)}, u32[]{:S(2)}, u32[]{:S(2)}) collective-permute-start(bf16[256,1024]{1,0:T(8,128)(2,1)S(1)} %constant_dynamic-slice_fusion.12.refs_0_.refs_4_), channel_id=1, source_target_pairs={{0,4},{4,0},{8,12},{12,8},{1,5},{5,1},{9,13},{13,9},{2,6},{6,2},{1... | collective-permute-start | bytes 1572872 | tf_op jit(solution)/shard_map/ppermute | solution.py:29
  92.6 67.0 %collective-permute-start.3 = (bf16[256,1536]{1,0:T(8,128)(2,1)}, bf16[256,1536]{1,0:T(8,128)(2,1)S(1)}, u32[]{:S(2)}, u32[]{:S(2)}) collective-permute-start(bf16[256,1536]{1,0:T(8,128)(2,1)} %pad_maximum_fusion.5), channel_id=1, source_target_pairs={{0,4},{4,0},{1,5},{5,1},{2,6},{6,2},{3,7},{7,3},{8,12},{12,8},{9,1... | collective-permute-start | bytes 2359304 | tf_op jit(solution)/shard_map/ppermute | solution.py:29
  131.8 44.6 %collective-permute-start.19 = (bf16[256,1536]{1,0:T(8,128)(2,1)S(1)}, bf16[256,1536]{1,0:T(8,128)(2,1)S(1)}, u32[]{:S(2)}, u32[]{:S(2)}) collective-permute-start(bf16[256,1536]{1,0:T(8,128)(2,1)S(1)} %copy-done.90), channel_id=1, source_target_pairs={{0,4},{4,0},{1,5},{5,1},{2,6},{6,2},{3,7},{7,3},{8,12},{12,8},{9,1... | collective-permute-start | bytes 2359304 | tf_op jit(solution)/shard_map/ppermute | solution.py:29
  131.9 47.0 %collective-permute-start.6 = (bf16[512,1024]{1,0:T(8,128)(2,1)}, bf16[512,1024]{1,0:T(8,128)(2,1)S(1)}, u32[]{:S(2)}, u32[]{:S(2)}) collective-permute-start(bf16[512,1024]{1,0:T(8,128)(2,1)} %constant_dynamic-update-slice_fusion.4.refs_1_.refs_2_.refs_3_), channel_id=1, source_target_pairs={{0,16},{16,0},{1,17},{17,1},{2,18},{18,2},{3,19},{19,3},{4,20},{20... | collective-permute-start | bytes 3145736 | tf_op jit(solution)/shard_map/ppermute | solution.py:34
  132.2 47.7 %collective-permute-start.7 = (bf16[512,1024]{1,0:T(8,128)(2,1)}, bf16[512,1024]{1,0:T(8,128)(2,1)S(1)}, u32[]{:S(2)}, u32[]{:S(2)}) collective-permute-start(bf16[512,1024]{1,0:T(8,128)(2,1)} %collective-permute-done.5.refs_2_.refs_3_.refs_4_), channel_id=1, source_target_pairs={{0,16},{16,0},{1,17},{17,1},{2,18},{18,2},{3,19},{19,3},{4,20},{20... | collective-permute-start | bytes 3145736 | tf_op jit(solution)/shard_map/ppermute | solution.py:34
  133.4 45.4 %collective-permute-start.2 = (bf16[256,1536]{1,0:T(8,128)(2,1)S(1)}, bf16[256,1536]{1,0:T(8,128)(2,1)S(1)}, u32[]{:S(2)}, u32[]{:S(2)}) collective-permute-start(bf16[256,1536]{1,0:T(8,128)(2,1)S(1)} %pad_maximum_fusion.4), channel_id=1, source_target_pairs={{0,8},{8,0},{1,9},{9,1},{2,10},{10,2},{3,11},{11,3},{4,12},{12,4},... | collective-permute-start | bytes 2359304 | tf_op jit(solution)/shard_map/ppermute | solution.py:29
  160.5 47.9 %collective-permute-start.8 = (bf16[512,1536]{1,0:T(8,128)(2,1)}, bf16[512,1536]{1,0:T(8,128)(2,1)}, u32[]{:S(2)}, u32[]{:S(2)}) collective-permute-start(bf16[512,1536]{1,0:T(8,128)(2,1)} %constant_dynamic-update-slice_fusion.2.refs_0_), channel_id=1, source_target_pairs={{0,16},{16,0},{1,17},{17,1},{2,18},{18,2},{3,19},{19,3},{4,20},{20... | collective-permute-start | bytes 4718600 | tf_op jit(solution)/shard_map/ppermute | solution.py:34
  181.1 69.0 %collective-permute-start.20 = (bf16[512,1536]{1,0:T(8,128)(2,1)}, bf16[512,1536]{1,0:T(8,128)(2,1)}, u32[]{:S(2)}, u32[]{:S(2)}) collective-permute-start(bf16[512,1536]{1,0:T(8,128)(2,1)} %pad_maximum_fusion.3.refs_0_), channel_id=1, source_target_pairs={{0,16},{16,0},{1,17},{17,1},{2,18},{18,2},{3,19},{19,3},{4,20},{20... | collective-permute-start | bytes 4718600 | tf_op jit(solution)/shard_map/ppermute | solution.py:34
  185.1 65.0 %collective-permute-start.18 = (bf16[256,1536]{1,0:T(8,128)(2,1)}, bf16[256,1536]{1,0:T(8,128)(2,1)}, u32[]{:S(2)}, u32[]{:S(2)}) collective-permute-start(bf16[256,1536]{1,0:T(8,128)(2,1)} %pad_maximum_fusion.6), channel_id=1, source_target_pairs={{0,8},{8,0},{1,9},{9,1},{2,10},{10,2},{3,11},{11,3},{4,12},{12,4},... | collective-permute-start | bytes 2359304 | tf_op jit(solution)/shard_map/ppermute | solution.py:29
  266.9 48.4 %collective-permute-start.25 = (bf16[384,2048]{1,0:T(8,128)(2,1)S(1)}, bf16[384,2048]{1,0:T(8,128)(2,1)}, u32[]{:S(2)}, u32[]{:S(2)}) collective-permute-start(bf16[384,2048]{1,0:T(8,128)(2,1)S(1)} %get-tuple-element.123.refs_2_.refs_4_), channel_id=1, source_target_pairs={{0,4},{4,0},{1,5},{5,1},{2,6},{6,2},{3,7},{7,3},{8,12},{12,8},{9,1... | collective-permute-start | bytes 4718600 | tf_op jit(solution)/shard_map/ppermute | solution.py:29
  288.0 57.1 %collective-permute-start.27 = (bf16[512,1536]{1,0:T(8,128)(2,1)S(1)}, bf16[512,1536]{1,0:T(8,128)(2,1)S(1)}, u32[]{:S(2)}, u32[]{:S(2)}) collective-permute-start(bf16[512,1536]{1,0:T(8,128)(2,1)S(1)} %constant_dynamic-update-slice_fusion.8.refs_1_), channel_id=1, source_target_pairs={{0,16},{16,0},{1,17},{17,1},{2,18},{18,2},{3,19},{19,3},{4,20},{20... | collective-permute-start | bytes 4718600 | tf_op jit(solution)/shard_map/ppermute | solution.py:34
  326.1 52.3 %collective-permute-start.28 = (bf16[384,2048]{1,0:T(8,128)(2,1)S(1)}, bf16[384,2048]{1,0:T(8,128)(2,1)S(1)}, u32[]{:S(2)}, u32[]{:S(2)}) collective-permute-start(bf16[384,2048]{1,0:T(8,128)(2,1)S(1)} %multiply_convert_fusion.1.refs_0_), channel_id=1, source_target_pairs={{0,4},{4,0},{1,5},{5,1},{2,6},{6,2},{3,7},{7,3},{8,12},{12,8},{9,1... | collective-permute-start | bytes 4718600 | tf_op jit(solution)/shard_map/ppermute | solution.py:29
  465.9 48.9 %collective-permute-start.39 = (bf16[512,1536]{1,0:T(8,128)(2,1)}, bf16[512,1536]{1,0:T(8,128)(2,1)}, u32[]{:S(2)}, u32[]{:S(2)}) collective-permute-start(bf16[512,1536]{1,0:T(8,128)(2,1)} %get-tuple-element.137), channel_id=1, source_target_pairs={{0,16},{16,0},{1,17},{17,1},{2,18},{18,2},{3,19},{19,3},{4,20},{20... | collective-permute-start | bytes 4718600 | tf_op jit(solution)/shard_map/ppermute | solution.py:34
  473.4 41.4 %collective-permute-start.38 = (bf16[384,2048]{1,0:T(8,128)(2,1)}, bf16[384,2048]{1,0:T(8,128)(2,1)S(1)}, u32[]{:S(2)}, u32[]{:S(2)}) collective-permute-start(bf16[384,2048]{1,0:T(8,128)(2,1)} %add_convert_fusion.9), channel_id=1, source_target_pairs={{0,2},{1,3},{2,0},{3,1},{4,6},{5,7},{6,4},{7,5},{8,10},{9,11},{10,... | collective-permute-start | bytes 4718600 | tf_op jit(solution)/shard_map/ppermute | solution.py:29
  502.8 78.2 %collective-permute-start.60 = (bf16[512,1536]{1,0:T(8,128)(2,1)}, bf16[512,1536]{1,0:T(8,128)(2,1)}, u32[]{:S(2)}, u32[]{:S(2)}) collective-permute-start(bf16[512,1536]{1,0:T(8,128)(2,1)} %add_convert_fusion.4), channel_id=1, source_target_pairs={{0,8},{8,0},{1,9},{9,1},{2,10},{10,2},{3,11},{11,3},{4,12},{12,4},... | collective-permute-start | bytes 4718600 | tf_op jit(solution)/shard_map/ppermute | solution.py:29
  524.9 69.0 %collective-permute-start.37 = (bf16[384,2048]{1,0:T(8,128)(2,1)}, bf16[384,2048]{1,0:T(8,128)(2,1)}, u32[]{:S(2)}, u32[]{:S(2)}) collective-permute-start(bf16[384,2048]{1,0:T(8,128)(2,1)} %add_convert_fusion.7), channel_id=1, source_target_pairs={{0,4},{4,0},{1,5},{5,1},{2,6},{6,2},{3,7},{7,3},{8,12},{12,8},{9,1... | collective-permute-start | bytes 4718600 | tf_op jit(solution)/shard_map/ppermute | solution.py:29
  529.6 71.6 %collective-permute-start.63 = (bf16[512,1536]{1,0:T(8,128)(2,1)}, bf16[512,1536]{1,0:T(8,128)(2,1)S(1)}, u32[]{:S(2)}, u32[]{:S(2)}) collective-permute-start(bf16[512,1536]{1,0:T(8,128)(2,1)} %get-tuple-element.157), channel_id=1, source_target_pairs={{0,16},{16,0},{1,17},{17,1},{2,18},{18,2},{3,19},{19,3},{4,20},{20... | collective-permute-start | bytes 4718600 | tf_op jit(solution)/shard_map/ppermute | solution.py:34
  529.9 77.9 %collective-permute-start.62 = (bf16[512,1536]{1,0:T(8,128)(2,1)}, bf16[512,1536]{1,0:T(8,128)(2,1)}, u32[]{:S(2)}, u32[]{:S(2)}) collective-permute-start(bf16[512,1536]{1,0:T(8,128)(2,1)} %get-tuple-element.155), channel_id=1, source_target_pairs={{0,16},{16,0},{1,17},{17,1},{2,18},{18,2},{3,19},{19,3},{4,20},{20... | collective-permute-start | bytes 4718600 | tf_op jit(solution)/shard_map/ppermute | solution.py:34
  598.2 52.7 %collective-permute-start.41 = (bf16[384,1024]{1,0:T(8,128)(2,1)}, bf16[384,1024]{1,0:T(8,128)(2,1)}, u32[]{:S(2)}, u32[]{:S(2)}) collective-permute-start(bf16[384,1024]{1,0:T(8,128)(2,1)} %constant_dynamic-slice_fusion.3), channel_id=1, source_target_pairs={{0,2},{1,3},{2,0},{3,1},{4,6},{5,7},{6,4},{7,5},{8,10},{9,11},{10,... | collective-permute-start | bytes 2359304 | tf_op jit(solution)/shard_map/ppermute | solution.py:29
  607.8 44.9 %collective-permute-start.61 = (bf16[256,1536]{1,0:T(8,128)(2,1)S(1)}, bf16[256,1536]{1,0:T(8,128)(2,1)}, u32[]{:S(2)}, u32[]{:S(2)}) collective-permute-start(bf16[256,1536]{1,0:T(8,128)(2,1)S(1)} %slice.233), channel_id=1, source_target_pairs={{0,4},{4,0},{1,5},{5,1},{2,6},{6,2},{3,7},{7,3},{8,12},{12,8},{9,1... | collective-permute-start | bytes 2359304 | tf_op jit(solution)/shard_map/ppermute | solution.py:29
  616.5 43.8 %collective-permute-start.54 = (bf16[1024,1024]{1,0:T(8,128)(2,1)S(1)}, bf16[1024,1024]{1,0:T(8,128)(2,1)}, u32[]{:S(2)}, u32[]{:S(2)}) collective-permute-start(bf16[1024,1024]{1,0:T(8,128)(2,1)S(1)} %attn_grads.5), channel_id=1, source_target_pairs={{0,16},{16,0},{1,17},{17,1},{2,18},{18,2},{3,19},{19,3},{4,20},{20... | collective-permute-start | bytes 6291464 | tf_op jit(solution)/shard_map/ppermute | solution.py:34
  629.3 79.5 %collective-permute-start.64 = (bf16[512,1536]{1,0:T(8,128)(2,1)}, bf16[512,1536]{1,0:T(8,128)(2,1)}, u32[]{:S(2)}, u32[]{:S(2)}) collective-permute-start(bf16[512,1536]{1,0:T(8,128)(2,1)} %add_convert_fusion.2), channel_id=1, source_target_pairs={{0,8},{8,0},{1,9},{9,1},{2,10},{10,2},{3,11},{11,3},{4,12},{12,4},... | collective-permute-start | bytes 4718600 | tf_op jit(solution)/shard_map/ppermute | solution.py:29
  641.1 72.3 %collective-permute-start.46 = (bf16[384,2048]{1,0:T(8,128)(2,1)S(1)}, bf16[384,2048]{1,0:T(8,128)(2,1)}, u32[]{:S(2)}, u32[]{:S(2)}) collective-permute-start(bf16[384,2048]{1,0:T(8,128)(2,1)S(1)} %get-tuple-element.151), channel_id=1, source_target_pairs={{0,1},{1,0},{2,3},{3,2},{4,5},{5,4},{6,7},{7,6},{8,9},{9,8},{10,11... | collective-permute-start | bytes 4718600 | tf_op jit(solution)/shard_map/ppermute | solution.py:29
  650.9 54.3 %collective-permute-start.57 = (bf16[1024,1024]{1,0:T(8,128)(2,1)S(1)}, bf16[1024,1024]{1,0:T(8,128)(2,1)S(1)}, u32[]{:S(2)}, u32[]{:S(2)}) collective-permute-start(bf16[1024,1024]{1,0:T(8,128)(2,1)S(1)} %attn_grads.7), channel_id=1, source_target_pairs={{0,16},{16,0},{1,17},{17,1},{2,18},{18,2},{3,19},{19,3},{4,20},{20... | collective-permute-start | bytes 6291464 | tf_op jit(solution)/shard_map/ppermute | solution.py:34
  662.9 57.9 %collective-permute-start.55 = (bf16[512,1024]{1,0:T(8,128)(2,1)S(1)}, bf16[512,1024]{1,0:T(8,128)(2,1)S(1)}, u32[]{:S(2)}, u32[]{:S(2)}) collective-permute-start(bf16[512,1024]{1,0:T(8,128)(2,1)S(1)} %slice.179), channel_id=1, source_target_pairs={{0,4},{4,0},{1,5},{5,1},{2,6},{6,2},{3,7},{7,3},{8,12},{12,8},{9,1... | collective-permute-start | bytes 3145736 | tf_op jit(solution)/shard_map/ppermute | solution.py:29
  711.4 37.6 %collective-permute-start.65 = (bf16[256,1536]{1,0:T(8,128)(2,1)S(1)}, bf16[256,1536]{1,0:T(8,128)(2,1)S(1)}, u32[]{:S(2)}, u32[]{:S(2)}) collective-permute-start(bf16[256,1536]{1,0:T(8,128)(2,1)S(1)} %slice.232), channel_id=1, source_target_pairs={{0,4},{4,0},{1,5},{5,1},{2,6},{6,2},{3,7},{7,3},{8,12},{12,8},{9,1... | collective-permute-start | bytes 2359304 | tf_op jit(solution)/shard_map/ppermute | solution.py:29
  716.5 54.9 %collective-permute-start.58 = (bf16[512,1024]{1,0:T(8,128)(2,1)}, bf16[512,1024]{1,0:T(8,128)(2,1)}, u32[]{:S(2)}, u32[]{:S(2)}) collective-permute-start(bf16[512,1024]{1,0:T(8,128)(2,1)} %slice.184), channel_id=1, source_target_pairs={{0,4},{4,0},{1,5},{5,1},{2,6},{6,2},{3,7},{7,3},{8,12},{12,8},{9,1... | collective-permute-start | bytes 3145736 | tf_op jit(solution)/shard_map/ppermute | solution.py:29
  722.1 81.7 %collective-permute-start.56 = (bf16[256,1024]{1,0:T(8,128)(2,1)}, bf16[256,1024]{1,0:T(8,128)(2,1)S(1)}, u32[]{:S(2)}, u32[]{:S(2)}) collective-permute-start(bf16[256,1024]{1,0:T(8,128)(2,1)} %slice.235), channel_id=1, source_target_pairs={{0,8},{8,0},{1,9},{9,1},{2,10},{10,2},{3,11},{11,3},{4,12},{12,4},... | collective-permute-start | bytes 1572872 | tf_op jit(solution)/shard_map/ppermute | solution.py:29
  (147 other events, 2205.6 us)

commit v6 on v5

--- a/solution.py
+++ b/solution.py
@@ -16,7 +16,7 @@
 ROPE_BASE = 130000.0
 MASKED = -1e30
 FFN_CHUNKS = 2
-COST_SCALE = 16
+COST_SCALE = 4
 BF16 = jnp.bfloat16
 F32 = jnp.float32
 VMEM_LIMIT = 32 * 1024 * 1024

time: 818 us -> 813 us (level)
    unnamed x232 -> x264, local copies, waits for them, and re-layouts: 31.4 us -> 37.4 us
  transfers between devices with their start and end apart: 66 -> 66, of which waited for: 31 -> 32; matrix products, arithmetic and copies ran while one was open for 15% -> 14% of each run, Pallas kernels for 24% -> 24%
where the time goes in v6:
time: 813 us; the launch traced here: 803 us
  waiting for transfers between devices  320 us (39%)
  Pallas kernels  220 us (27%)
  starting transfers between devices  111 us (14%)
  other arithmetic  80.6 us (10%)
  local copies, waits for them, and re-layouts  68.3 us (8%)
    ppermute x50, waiting for transfers between devices, swap(): return lax.ppermute(values, axis, [(i, i ^ mask) for i in range(count)])  240 us
    pallas_call x19, Pallas kernels, call(): pl.pallas_call(kernel, in_specs=[SMEM] * len(smem) + [VMEM] * len(operand...  102 us
    ppermute x50, starting transfers between devices, swap(): return lax.ppermute(values, axis, [(i, i ^ mask) for i in range(count)])  98.3 us
    ppermute x16, waiting for transfers between devices, turn(): lax.ppermute(values, axis, [(i, (i + shift) % count) for i in range(count)])  79.8 us
    pallas_call x4, Pallas kernels, ffn_grads(): pl.pallas_call(functools.partial(ffn_grads_kernel, tile, unit), grid_spec...  52.9 us
    pallas_call x1, Pallas kernels, attention_backward(): pl.pallas_call(functools.partial(backward_kernel, pieces), grid_spec=pltp...  42.9 us
    unnamed x264, local copies, waits for them, and re-layouts  37.4 us
    convert_element_type x15, other arithmetic, low(): return values.astype(BF16)  33.4 us
  transfers between devices with their start and end apart: 66, of which 32 were waited for; matrix products, arithmetic and copies ran while one was open for 14% of the time, Pallas kernels for 24%

profile of v6, /device:TPU:1, one launch (start us, length us, event | category | flops | bytes accessed | tf_op | source)
XLA Modules:
  0.0 803.1 jit_solution(4966721140619820087)
XLA Ops:
  20.3 8.9 %collective-permute-done.refs_2_.refs_8_ = bf16[256,1024]{1,0:T(8,128)(2,1)} collective-permute-done((bf16[256,1024]{1,0:T(8,128)(2,1)}, bf16[256,1024]{1,0:T(8,128)(2,1)}, u32[]{:S(2)}, u32[]{:S(2)}) %collective-permute-start) | collective-permute-done | bytes 524320 | tf_op jit(solution)/shard_map/ppermute | solution.py:29
  46.3 20.0 %collective-permute-done.4 = bf16[256,1024]{1,0:T(8,128)(2,1)S(1)} collective-permute-done((bf16[256,1024]{1,0:T(8,128)(2,1)}, bf16[256,1024]{1,0:T(8,128)(2,1)S(1)}, u32[]{:S(2)}, u32[]{:S(2)}) %collective-permute-start.4) | collective-permute-done | bytes 524320 | tf_op jit(solution)/shard_map/ppermute | solution.py:29
  67.6 9.1 %collective-permute-done.9.refs_8_.refs_14_ = bf16[256,1024]{1,0:T(8,128)(2,1)S(1)} collective-permute-done((bf16[256,1024]{1,0:T(8,128)(2,1)}, bf16[256,1024]{1,0:T(8,128)(2,1)S(1)}, u32[]{:S(2)}, u32[]{:S(2)}) %collective-permute-start.9) | collective-permute-done | bytes 524320 | tf_op jit(solution)/shard_map/ppermute | solution.py:34
  76.7 7.0 project.4.ks_ref.vs_ref
  91.7 11.5 %collective-permute-done.17.refs_3_.refs_7_ = bf16[256,1024]{1,0:T(8,128)(2,1)S(1)} collective-permute-done((bf16[256,1024]{1,0:T(8,128)(2,1)S(1)}, bf16[256,1024]{1,0:T(8,128)(2,1)S(1)}, u32[]{:S(2)}, u32[]{:S(2)}) %collective-permute-start.17) | collective-permute-done | bytes 524320 | tf_op jit(solution)/shard_map/ppermute | solution.py:29
  103.2 25.1 %collective-permute-done.16.refs_2_.refs_6_ = bf16[256,1024]{1,0:T(8,128)(2,1)S(1)} collective-permute-done((bf16[256,1024]{1,0:T(8,128)(2,1)S(1)}, bf16[256,1024]{1,0:T(8,128)(2,1)S(1)}, u32[]{:S(2)}, u32[]{:S(2)}) %collective-permute-start.16) | collective-permute-done | bytes 524320 | tf_op jit(solution)/shard_map/ppermute | solution.py:29
  132.7 24.2 %collective-permute-done.3 = bf16[256,1536]{1,0:T(8,128)(2,1)S(1)} collective-permute-done((bf16[256,1536]{1,0:T(8,128)(2,1)}, bf16[256,1536]{1,0:T(8,128)(2,1)S(1)}, u32[]{:S(2)}, u32[]{:S(2)}) %collective-permute-start.3) | collective-permute-done | bytes 786464 | tf_op jit(solution)/shard_map/ppermute | solution.py:29
  158.2 15.5 %collective-permute-done.19 = bf16[256,1536]{1,0:T(8,128)(2,1)S(1)} collective-permute-done((bf16[256,1536]{1,0:T(8,128)(2,1)S(1)}, bf16[256,1536]{1,0:T(8,128)(2,1)S(1)}, u32[]{:S(2)}, u32[]{:S(2)}) %collective-permute-start.19) | collective-permute-done | bytes 786464 | tf_op jit(solution)/shard_map/ppermute | solution.py:29
  198.5 5.7 collective-permute-done.8.refs_2_
  204.3 20.6 %attend.1 = (bf16[768,512]{1,0:T(8,128)(2,1)S(1)}, f32[768,512]{1,0:T(8,128)S(1)}) custom-call(s32[3]{0:T(128)S(1)} %compare_select_fusion.7.order_ref, s32[4]{0:T(128)S(1)} %gather_fusion.1, bf16[768,512]{1,0:T(8,128)(2,1)S(1)} %project.3.q_ref, bf16[768,1024]{1,0:T(8,128)(2,1)S(1)} %copy-done.20, bf16[768,1024]{1,0:T(8,128)(2,1)S(1)} %copy-done.20, ...), custom_call_target="tpu_custom_call" | custom-call | flops 2013265920 | bytes 1572864 | tf_op jit(solution)/shard_map/attend/pallas_call | solution.py:582
  226.1 21.2 %collective-permute-done.18 = bf16[256,1536]{1,0:T(8,128)(2,1)} collective-permute-done((bf16[256,1536]{1,0:T(8,128)(2,1)}, bf16[256,1536]{1,0:T(8,128)(2,1)}, u32[]{:S(2)}, u32[]{:S(2)}) %collective-permute-start.18) | collective-permute-done | bytes 786464 | tf_op jit(solution)/shard_map/ppermute | solution.py:29
  263.0 7.4 collective-permute-start.25
  285.4 22.7 %collective-permute-done.24.refs_3_ = bf16[512,1536]{1,0:T(8,128)(2,1)} collective-permute-done((bf16[512,1536]{1,0:T(8,128)(2,1)}, bf16[512,1536]{1,0:T(8,128)(2,1)}, u32[]{:S(2)}, u32[]{:S(2)}) %collective-permute-start.24) | collective-permute-done | bytes 1572896 | tf_op jit(solution)/shard_map/ppermute | solution.py:34
  322.2 17.6 %collective-permute-start.28 = (bf16[384,2048]{1,0:T(8,128)(2,1)S(1)}, bf16[384,2048]{1,0:T(8,128)(2,1)S(1)}, u32[]{:S(2)}, u32[]{:S(2)}) collective-permute-start(bf16[384,2048]{1,0:T(8,128)(2,1)S(1)} %multiply_convert_fusion.1.refs_0_), channel_id=1, source_target_pairs={{0,4},{4,0},{1,5},{5,1},{2,6},{6,2},{3,7},{7,3},{8,12},{12,8},{9,1... | collective-permute-start | bytes 4718600 | tf_op jit(solution)/shard_map/ppermute | solution.py:29
  356.1 9.3 %ffn_back.4 = (bf16[384,2048]{1,0:T(8,128)(2,1)S(1)}, bf16[384,2048]{1,0:T(8,128)(2,1)}) custom-call(bf16[768,1024]{1,0:T(8,128)(2,1)S(1)} %get-tuple-element.108.refs_0_.refs_10_, bf16[768,1024]{1,0:T(8,128)(2,1)S(1)} %get-tuple-element.109.refs_1_.refs_10_, bf16[2048,1536]{1,0:T(8,128)(2,1)S(1)} %place_rows.2.refs_4_.refs_2_, ...), custom_call_target="tpu_custom_call" | custom-call | flops 1610612736 | bytes 3670016 | tf_op jit(solution)/shard_map/ffn_back/pallas_call | solution.py:81
  366.6 7.9 collective-permute-done.28.refs_0_.refs_2_
  378.1 8.0 ffn.7
  388.7 8.6 %ffn.6 = (bf16[768,512]{1,0:T(8,128)(2,1)S(1)}, bf16[768,1024]{1,0:T(8,128)(2,1)S(1)}) custom-call(bf16[384,2048]{1,0:T(8,128)(2,1)S(1)} %copy-done.13, bf16[384,2048]{1,0:T(8,128)(2,1)S(1)} %collective-permute-done.29.refs_1_.refs_3_, bf16[384,2048]{1,0:T(8,128)(2,1)} %collective-permute-done.25.refs_2_.refs_6_, ...), custom_call_target="tpu_custom_call" | custom-call | flops 1207959552 | bytes 3735552 | tf_op jit(solution)/shard_map/ffn/pallas_call | solution.py:81
  397.4 9.2 %ffn_back.5 = (bf16[384,2048]{1,0:T(8,128)(2,1)S(1)}, bf16[384,2048]{1,0:T(8,128)(2,1)}) custom-call(bf16[768,1024]{1,0:T(8,128)(2,1)S(1)} %get-tuple-element.115.refs_0_.refs_11_, bf16[768,1024]{1,0:T(8,128)(2,1)S(1)} %get-tuple-element.116.refs_1_.refs_11_, bf16[2048,1536]{1,0:T(8,128)(2,1)S(1)} %place_rows.2.refs_4_.refs_2_, ...), custom_call_target="tpu_custom_call" | custom-call | flops 1610612736 | bytes 3670016 | tf_op jit(solution)/shard_map/ffn_back/pallas_call | solution.py:81
  408.9 13.1 %ffn_grads.6 = bf16[1024,1536]{1,0:T(8,128)(2,1)} custom-call(s32[2]{0:T(128)} %compare_select_fusion.2.dp_ref, s32[4]{0:T(128)} %gather_fusion.3, bf16[384,2048]{1,0:T(8,128)(2,1)} %copy-done.9, bf16[384,2048]{1,0:T(8,128)(2,1)} %copy-done.11, bf16[384,2048]{1,0:T(8,128)(2,1)} %copy-done.12, bf16[384,2048]{1,0:T(8,128)(2,1)} %copy-done.14, ...), custom_call_target="tpu_custom_call" | custom-call | flops 1207959552 | bytes 3538944 | tf_op jit(solution)/shard_map/ffn_grads/pallas_call | solution.py:348
  432.4 13.1 %ffn_grads.5 = bf16[1024,1536]{1,0:T(8,128)(2,1)} custom-call(s32[2]{0:T(128)} %compare_select_fusion.2.dp_ref, s32[4]{0:T(128)} %gather_fusion.3, bf16[384,2048]{1,0:T(8,128)(2,1)} %copy-done.9, bf16[384,2048]{1,0:T(8,128)(2,1)} %copy-done.11, bf16[384,2048]{1,0:T(8,128)(2,1)} %copy-done.12, bf16[384,2048]{1,0:T(8,128)(2,1)} %copy-done.14, ...), custom_call_target="tpu_custom_call" | custom-call | flops 1207959552 | bytes 3538944 | tf_op jit(solution)/shard_map/ffn_grads/pallas_call | solution.py:348
  445.6 13.3 %ffn_grads.4 = bf16[1024,1536]{1,0:T(8,128)(2,1)} custom-call(s32[2]{0:T(128)} %compare_select_fusion.2.dp_ref, s32[4]{0:T(128)} %gather_fusion.3, bf16[384,2048]{1,0:T(8,128)(2,1)} %copy-done.9, bf16[384,2048]{1,0:T(8,128)(2,1)} %copy-done.11, bf16[384,2048]{1,0:T(8,128)(2,1)} %copy-done.12, bf16[384,2048]{1,0:T(8,128)(2,1)} %copy-done.14, ...), custom_call_target="tpu_custom_call" | custom-call | flops 1207959552 | bytes 3538944 | tf_op jit(solution)/shard_map/ffn_grads/pallas_call | solution.py:348
  471.6 13.3 %ffn_grads.7 = bf16[1024,1536]{1,0:T(8,128)(2,1)} custom-call(s32[2]{0:T(128)} %compare_select_fusion.2.dp_ref, s32[4]{0:T(128)} %gather_fusion.3, bf16[384,2048]{1,0:T(8,128)(2,1)} %copy-done.9, bf16[384,2048]{1,0:T(8,128)(2,1)} %copy-done.11, bf16[384,2048]{1,0:T(8,128)(2,1)} %copy-done.12, bf16[384,2048]{1,0:T(8,128)(2,1)} %copy-done.14, ...), custom_call_target="tpu_custom_call" | custom-call | flops 1207959552 | bytes 3538944 | tf_op jit(solution)/shard_map/ffn_grads/pallas_call | solution.py:348
  530.5 42.9 %attend_back.1 = (bf16[768,512]{1,0:T(8,128)(2,1)S(1)}, f32[768,512]{1,0:T(8,128)S(1)}, f32[768,512]{1,0:T(8,128)S(1)}, f32[256,1024]{1,0:T(8,128)S(1)}, bf16[25...) custom-call(s32[3]{0:T(128)S(1)} %compare_select_fusion.7.order_ref, ...), custom_call_target="tpu_custom_call" | custom-call | flops 5033164800 | bytes 3145728 | tf_op jit(solution)/shard_map/attend_back/pallas_call | solution.py:604
  573.4 16.2 %collective-permute-done.37 = bf16[384,2048]{1,0:T(8,128)(2,1)} collective-permute-done((bf16[384,2048]{1,0:T(8,128)(2,1)}, bf16[384,2048]{1,0:T(8,128)(2,1)}, u32[]{:S(2)}, u32[]{:S(2)}) %collective-permute-start.37) | collective-permute-done | bytes 1572896 | tf_op jit(solution)/shard_map/ppermute | solution.py:29
  614.2 9.5 %collective-permute-done.45.refs_2_ = bf16[256,1024]{1,0:T(8,128)(2,1)S(1)} collective-permute-done((bf16[256,1024]{1,0:T(8,128)(2,1)S(1)}, bf16[256,1024]{1,0:T(8,128)(2,1)S(1)}, u32[]{:S(2)}, u32[]{:S(2)}) %collective-permute-start.45) | collective-permute-done | bytes 524320 | tf_op jit(solution)/shard_map/ppermute | solution.py:29
  626.0 8.6 %project_back.3 = (bf16[384,2048]{1,0:T(8,128)(2,1)S(1)}, bf16[384,2048]{1,0:T(8,128)(2,1)S(1)}) custom-call(s32[1]{0:T(128)} %bitcast.bit_ref, s32[8]{0:T(128)S(1)} %xor_add_fusion.1.place_ref, bf16[768,512]{1,0:T(8,128)(2,1)S(1)} %get-tuple-element.140.refs_0_.refs_4_, bf16[768,512]{1,0:T(8,128)(2,1)S(1)} %get-tuple-element.148.refs_1_, ...), custom_call_target="tpu_custom_call" | custom-call | flops 1207959552 | bytes 2949120 | tf_op jit(solution)/shard_map/project_back/pallas_call | solution.py:81
  657.8 8.1 %collective-permute-start.55 = (bf16[512,1024]{1,0:T(8,128)(2,1)S(1)}, bf16[512,1024]{1,0:T(8,128)(2,1)S(1)}, u32[]{:S(2)}, u32[]{:S(2)}) collective-permute-start(bf16[512,1024]{1,0:T(8,128)(2,1)S(1)} %slice.179), channel_id=1, source_target_pairs={{0,4},{4,0},{1,5},{5,1},{2,6},{6,2},{3,7},{7,3},{8,12},{12,8},{9,1... | collective-permute-start | bytes 3145736 | tf_op jit(solution)/shard_map/ppermute | solution.py:29
  665.9 34.2 %collective-permute-done.57 = bf16[1024,1024]{1,0:T(8,128)(2,1)S(1)} collective-permute-done((bf16[1024,1024]{1,0:T(8,128)(2,1)S(1)}, bf16[1024,1024]{1,0:T(8,128)(2,1)S(1)}, u32[]{:S(2)}, u32[]{:S(2)}) %collective-permute-start.57) | collective-permute-done | bytes 2097184 | tf_op jit(solution)/shard_map/ppermute | solution.py:34
  717.1 26.8 %collective-permute-done.65 = bf16[256,1536]{1,0:T(8,128)(2,1)S(1)} collective-permute-done((bf16[256,1536]{1,0:T(8,128)(2,1)S(1)}, bf16[256,1536]{1,0:T(8,128)(2,1)S(1)}, u32[]{:S(2)}, u32[]{:S(2)}) %collective-permute-start.65) | collective-permute-done | bytes 786464 | tf_op jit(solution)/shard_map/ppermute | solution.py:29
  750.9 7.8 collective-permute-start.48
  770.9 23.2 %collective-permute-done.51 = f32[2,2048]{1,0:T(2,128)S(1)} collective-permute-done((f32[2,2048]{1,0:T(2,128)S(1)}, f32[2,2048]{1,0:T(2,128)S(1)}, u32[]{:S(2)}, u32[]{:S(2)}) %collective-permute-start.51) | collective-permute-done | bytes 16416 | tf_op jit(solution)/shard_map/ppermute | solution.py:29
  (501 shorter events, 310.2 us)
Async XLA Ops:
  4.0 63.6 %collective-permute-start.12 = (bf16[256,1024]{1,0:T(8,128)(2,1)}, bf16[256,1024]{1,0:T(8,128)(2,1)}, u32[]{:S(2)}, u32[]{:S(2)}) collective-permute-start(bf16[256,1024]{1,0:T(8,128)(2,1)} %constant_dynamic-update-slice_fusion.refs_1_.refs_7_), channel_id=1, source_target_pairs={{0,16},{16,0},{1,17},{17,1},{2,18},{18,2},{3,19},{19,3},{4,20},{20... | collective-permute-start | bytes 1572872 | tf_op jit(solution)/shard_map/ppermute | solution.py:34
  6.0 38.7 %collective-permute-start.11 = (bf16[256,1024]{1,0:T(8,128)(2,1)}, bf16[256,1024]{1,0:T(8,128)(2,1)}, u32[]{:S(2)}, u32[]{:S(2)}) collective-permute-start(bf16[256,1024]{1,0:T(8,128)(2,1)} %constant_dynamic-update-slice_fusion.refs_1_.refs_7_), channel_id=1, source_target_pairs={{0,4},{4,0},{1,5},{5,1},{2,6},{6,2},{3,7},{7,3},{8,12},{12,8},{9,1... | collective-permute-start | bytes 1572872 | tf_op jit(solution)/shard_map/ppermute | solution.py:29
  66.3 62.4 %collective-permute-start.5 = (bf16[512,1024]{1,0:T(8,128)(2,1)S(1)}, bf16[512,1024]{1,0:T(8,128)(2,1)S(1)}, u32[]{:S(2)}, u32[]{:S(2)}) collective-permute-start(bf16[512,1024]{1,0:T(8,128)(2,1)S(1)} %constant_dynamic-update-slice_fusion.4.refs_1_.refs_2_.refs_3_), channel_id=1, source_target_pairs={{0,4},{4,0},{1,5},{5,1},{2,6},{6,2},{3,7},{7,3},{8,12},{12,8},{9,1... | collective-permute-start | bytes 3145736 | tf_op jit(solution)/shard_map/ppermute | solution.py:29
  88.2 40.1 %collective-permute-start.16 = (bf16[256,1024]{1,0:T(8,128)(2,1)S(1)}, bf16[256,1024]{1,0:T(8,128)(2,1)S(1)}, u32[]{:S(2)}, u32[]{:S(2)}) collective-permute-start(bf16[256,1024]{1,0:T(8,128)(2,1)S(1)} %constant_dynamic-slice_fusion.12.refs_0_.refs_4_), channel_id=1, source_target_pairs={{0,8},{4,12},{8,0},{12,4},{1,9},{5,13},{9,1},{13,5},{2,10},{6,14},... | collective-permute-start | bytes 1572872 | tf_op jit(solution)/shard_map/ppermute | solution.py:29
  88.2 40.1 %collective-permute-start.15 = (bf16[256,1024]{1,0:T(8,128)(2,1)S(1)}, bf16[256,1024]{1,0:T(8,128)(2,1)S(1)}, u32[]{:S(2)}, u32[]{:S(2)}) collective-permute-start(bf16[256,1024]{1,0:T(8,128)(2,1)S(1)} %constant_dynamic-slice_fusion.12.refs_0_.refs_4_), channel_id=1, source_target_pairs={{0,4},{4,0},{8,12},{12,8},{1,5},{5,1},{9,13},{13,9},{2,6},{6,2},{1... | collective-permute-start | bytes 1572872 | tf_op jit(solution)/shard_map/ppermute | solution.py:29
  89.6 67.4 %collective-permute-start.3 = (bf16[256,1536]{1,0:T(8,128)(2,1)}, bf16[256,1536]{1,0:T(8,128)(2,1)S(1)}, u32[]{:S(2)}, u32[]{:S(2)}) collective-permute-start(bf16[256,1536]{1,0:T(8,128)(2,1)} %pad_maximum_fusion.5), channel_id=1, source_target_pairs={{0,4},{4,0},{1,5},{5,1},{2,6},{6,2},{3,7},{7,3},{8,12},{12,8},{9,1... | collective-permute-start | bytes 2359304 | tf_op jit(solution)/shard_map/ppermute | solution.py:29
  128.3 45.5 %collective-permute-start.19 = (bf16[256,1536]{1,0:T(8,128)(2,1)S(1)}, bf16[256,1536]{1,0:T(8,128)(2,1)S(1)}, u32[]{:S(2)}, u32[]{:S(2)}) collective-permute-start(bf16[256,1536]{1,0:T(8,128)(2,1)S(1)} %pad_maximum_fusion.7), channel_id=1, source_target_pairs={{0,4},{4,0},{1,5},{5,1},{2,6},{6,2},{3,7},{7,3},{8,12},{12,8},{9,1... | collective-permute-start | bytes 2359304 | tf_op jit(solution)/shard_map/ppermute | solution.py:29
  128.4 47.9 %collective-permute-start.6 = (bf16[512,1024]{1,0:T(8,128)(2,1)S(1)}, bf16[512,1024]{1,0:T(8,128)(2,1)S(1)}, u32[]{:S(2)}, u32[]{:S(2)}) collective-permute-start(bf16[512,1024]{1,0:T(8,128)(2,1)S(1)} %constant_dynamic-update-slice_fusion.4.refs_1_.refs_2_.refs_3_), channel_id=1, source_target_pairs={{0,16},{16,0},{1,17},{17,1},{2,18},{18,2},{3,19},{19,3},{4,20},{20... | collective-permute-start | bytes 3145736 | tf_op jit(solution)/shard_map/ppermute | solution.py:34
  128.7 48.6 %collective-permute-start.7 = (bf16[512,1024]{1,0:T(8,128)(2,1)S(1)}, bf16[512,1024]{1,0:T(8,128)(2,1)S(1)}, u32[]{:S(2)}, u32[]{:S(2)}) collective-permute-start(bf16[512,1024]{1,0:T(8,128)(2,1)S(1)} %collective-permute-done.5.refs_2_.refs_3_.refs_4_), channel_id=1, source_target_pairs={{0,16},{16,0},{1,17},{17,1},{2,18},{18,2},{3,19},{19,3},{4,20},{20... | collective-permute-start | bytes 3145736 | tf_op jit(solution)/shard_map/ppermute | solution.py:34
  129.9 46.3 %collective-permute-start.2 = (bf16[256,1536]{1,0:T(8,128)(2,1)S(1)}, bf16[256,1536]{1,0:T(8,128)(2,1)S(1)}, u32[]{:S(2)}, u32[]{:S(2)}) collective-permute-start(bf16[256,1536]{1,0:T(8,128)(2,1)S(1)} %pad_maximum_fusion.4), channel_id=1, source_target_pairs={{0,8},{8,0},{1,9},{9,1},{2,10},{10,2},{3,11},{11,3},{4,12},{12,4},... | collective-permute-start | bytes 2359304 | tf_op jit(solution)/shard_map/ppermute | solution.py:29
  157.9 46.3 %collective-permute-start.8 = (bf16[512,1536]{1,0:T(8,128)(2,1)}, bf16[512,1536]{1,0:T(8,128)(2,1)}, u32[]{:S(2)}, u32[]{:S(2)}) collective-permute-start(bf16[512,1536]{1,0:T(8,128)(2,1)} %constant_dynamic-update-slice_fusion.2.refs_0_), channel_id=1, source_target_pairs={{0,16},{16,0},{1,17},{17,1},{2,18},{18,2},{3,19},{19,3},{4,20},{20... | collective-permute-start | bytes 4718600 | tf_op jit(solution)/shard_map/ppermute | solution.py:34
  178.5 68.8 %collective-permute-start.20 = (bf16[512,1536]{1,0:T(8,128)(2,1)}, bf16[512,1536]{1,0:T(8,128)(2,1)}, u32[]{:S(2)}, u32[]{:S(2)}) collective-permute-start(bf16[512,1536]{1,0:T(8,128)(2,1)} %pad_maximum_fusion.3.refs_0_), channel_id=1, source_target_pairs={{0,16},{16,0},{1,17},{17,1},{2,18},{18,2},{3,19},{19,3},{4,20},{20... | collective-permute-start | bytes 4718600 | tf_op jit(solution)/shard_map/ppermute | solution.py:34
  185.6 61.6 %collective-permute-start.18 = (bf16[256,1536]{1,0:T(8,128)(2,1)}, bf16[256,1536]{1,0:T(8,128)(2,1)}, u32[]{:S(2)}, u32[]{:S(2)}) collective-permute-start(bf16[256,1536]{1,0:T(8,128)(2,1)} %pad_maximum_fusion.6), channel_id=1, source_target_pairs={{0,8},{8,0},{1,9},{9,1},{2,10},{10,2},{3,11},{11,3},{4,12},{12,4},... | collective-permute-start | bytes 2359304 | tf_op jit(solution)/shard_map/ppermute | solution.py:29
  263.0 48.5 %collective-permute-start.25 = (bf16[384,2048]{1,0:T(8,128)(2,1)S(1)}, bf16[384,2048]{1,0:T(8,128)(2,1)}, u32[]{:S(2)}, u32[]{:S(2)}) collective-permute-start(bf16[384,2048]{1,0:T(8,128)(2,1)S(1)} %get-tuple-element.123.refs_2_.refs_4_), channel_id=1, source_target_pairs={{0,4},{4,0},{1,5},{5,1},{2,6},{6,2},{3,7},{7,3},{8,12},{12,8},{9,1... | collective-permute-start | bytes 4718600 | tf_op jit(solution)/shard_map/ppermute | solution.py:29
  284.1 57.5 %collective-permute-start.27 = (bf16[512,1536]{1,0:T(8,128)(2,1)S(1)}, bf16[512,1536]{1,0:T(8,128)(2,1)S(1)}, u32[]{:S(2)}, u32[]{:S(2)}) collective-permute-start(bf16[512,1536]{1,0:T(8,128)(2,1)S(1)} %constant_dynamic-update-slice_fusion.8.refs_1_), channel_id=1, source_target_pairs={{0,16},{16,0},{1,17},{17,1},{2,18},{18,2},{3,19},{19,3},{4,20},{20... | collective-permute-start | bytes 4718600 | tf_op jit(solution)/shard_map/ppermute | solution.py:34
  322.2 52.4 %collective-permute-start.28 = (bf16[384,2048]{1,0:T(8,128)(2,1)S(1)}, bf16[384,2048]{1,0:T(8,128)(2,1)S(1)}, u32[]{:S(2)}, u32[]{:S(2)}) collective-permute-start(bf16[384,2048]{1,0:T(8,128)(2,1)S(1)} %multiply_convert_fusion.1.refs_0_), channel_id=1, source_target_pairs={{0,4},{4,0},{1,5},{5,1},{2,6},{6,2},{3,7},{7,3},{8,12},{12,8},{9,1... | collective-permute-start | bytes 4718600 | tf_op jit(solution)/shard_map/ppermute | solution.py:29
  462.0 48.9 %collective-permute-start.39 = (bf16[512,1536]{1,0:T(8,128)(2,1)}, bf16[512,1536]{1,0:T(8,128)(2,1)}, u32[]{:S(2)}, u32[]{:S(2)}) collective-permute-start(bf16[512,1536]{1,0:T(8,128)(2,1)} %get-tuple-element.137), channel_id=1, source_target_pairs={{0,16},{16,0},{1,17},{17,1},{2,18},{18,2},{3,19},{19,3},{4,20},{20... | collective-permute-start | bytes 4718600 | tf_op jit(solution)/shard_map/ppermute | solution.py:34
  469.5 41.3 %collective-permute-start.38 = (bf16[384,2048]{1,0:T(8,128)(2,1)}, bf16[384,2048]{1,0:T(8,128)(2,1)}, u32[]{:S(2)}, u32[]{:S(2)}) collective-permute-start(bf16[384,2048]{1,0:T(8,128)(2,1)} %add_convert_fusion.9), channel_id=1, source_target_pairs={{0,2},{1,3},{2,0},{3,1},{4,6},{5,7},{6,4},{7,5},{8,10},{9,11},{10,... | collective-permute-start | bytes 4718600 | tf_op jit(solution)/shard_map/ppermute | solution.py:29
  499.9 73.5 %collective-permute-start.60 = (bf16[512,1536]{1,0:T(8,128)(2,1)}, bf16[512,1536]{1,0:T(8,128)(2,1)}, u32[]{:S(2)}, u32[]{:S(2)}) collective-permute-start(bf16[512,1536]{1,0:T(8,128)(2,1)} %add_convert_fusion.4), channel_id=1, source_target_pairs={{0,8},{8,0},{1,9},{9,1},{2,10},{10,2},{3,11},{11,3},{4,12},{12,4},... | collective-permute-start | bytes 4718600 | tf_op jit(solution)/shard_map/ppermute | solution.py:29
  521.0 68.6 %collective-permute-start.37 = (bf16[384,2048]{1,0:T(8,128)(2,1)}, bf16[384,2048]{1,0:T(8,128)(2,1)}, u32[]{:S(2)}, u32[]{:S(2)}) collective-permute-start(bf16[384,2048]{1,0:T(8,128)(2,1)} %add_convert_fusion.7), channel_id=1, source_target_pairs={{0,4},{4,0},{1,5},{5,1},{2,6},{6,2},{3,7},{7,3},{8,12},{12,8},{9,1... | collective-permute-start | bytes 4718600 | tf_op jit(solution)/shard_map/ppermute | solution.py:29
  523.4 73.4 %collective-permute-start.63 = (bf16[512,1536]{1,0:T(8,128)(2,1)}, bf16[512,1536]{1,0:T(8,128)(2,1)S(1)}, u32[]{:S(2)}, u32[]{:S(2)}) collective-permute-start(bf16[512,1536]{1,0:T(8,128)(2,1)} %get-tuple-element.157), channel_id=1, source_target_pairs={{0,16},{16,0},{1,17},{17,1},{2,18},{18,2},{3,19},{19,3},{4,20},{20... | collective-permute-start | bytes 4718600 | tf_op jit(solution)/shard_map/ppermute | solution.py:34
  523.7 85.0 %collective-permute-start.62 = (bf16[512,1536]{1,0:T(8,128)(2,1)}, bf16[512,1536]{1,0:T(8,128)(2,1)}, u32[]{:S(2)}, u32[]{:S(2)}) collective-permute-start(bf16[512,1536]{1,0:T(8,128)(2,1)} %get-tuple-element.155), channel_id=1, source_target_pairs={{0,16},{16,0},{1,17},{17,1},{2,18},{18,2},{3,19},{19,3},{4,20},{20... | collective-permute-start | bytes 4718600 | tf_op jit(solution)/shard_map/ppermute | solution.py:34
  598.8 49.3 %collective-permute-start.61 = (bf16[256,1536]{1,0:T(8,128)(2,1)}, bf16[256,1536]{1,0:T(8,128)(2,1)}, u32[]{:S(2)}, u32[]{:S(2)}) collective-permute-start(bf16[256,1536]{1,0:T(8,128)(2,1)} %slice.233), channel_id=1, source_target_pairs={{0,4},{4,0},{1,5},{5,1},{2,6},{6,2},{3,7},{7,3},{8,12},{12,8},{9,1... | collective-permute-start | bytes 2359304 | tf_op jit(solution)/shard_map/ppermute | solution.py:29
  608.7 37.4 %collective-permute-start.41 = (bf16[384,1024]{1,0:T(8,128)(2,1)}, bf16[384,1024]{1,0:T(8,128)(2,1)}, u32[]{:S(2)}, u32[]{:S(2)}) collective-permute-start(bf16[384,1024]{1,0:T(8,128)(2,1)} %constant_dynamic-slice_fusion.3), channel_id=1, source_target_pairs={{0,2},{1,3},{2,0},{3,1},{4,6},{5,7},{6,4},{7,5},{8,10},{9,11},{10,... | collective-permute-start | bytes 2359304 | tf_op jit(solution)/shard_map/ppermute | solution.py:29
  611.9 43.2 %collective-permute-start.54 = (bf16[1024,1024]{1,0:T(8,128)(2,1)S(1)}, bf16[1024,1024]{1,0:T(8,128)(2,1)}, u32[]{:S(2)}, u32[]{:S(2)}) collective-permute-start(bf16[1024,1024]{1,0:T(8,128)(2,1)S(1)} %attn_grads.5), channel_id=1, source_target_pairs={{0,16},{16,0},{1,17},{17,1},{2,18},{18,2},{3,19},{19,3},{4,20},{20... | collective-permute-start | bytes 6291464 | tf_op jit(solution)/shard_map/ppermute | solution.py:34
  612.2 91.8 %collective-permute-start.64 = (bf16[512,1536]{1,0:T(8,128)(2,1)}, bf16[512,1536]{1,0:T(8,128)(2,1)}, u32[]{:S(2)}, u32[]{:S(2)}) collective-permute-start(bf16[512,1536]{1,0:T(8,128)(2,1)} %add_convert_fusion.2), channel_id=1, source_target_pairs={{0,8},{8,0},{1,9},{9,1},{2,10},{10,2},{3,11},{11,3},{4,12},{12,4},... | collective-permute-start | bytes 4718600 | tf_op jit(solution)/shard_map/ppermute | solution.py:29
  634.5 74.0 %collective-permute-start.46 = (bf16[384,2048]{1,0:T(8,128)(2,1)S(1)}, bf16[384,2048]{1,0:T(8,128)(2,1)S(1)}, u32[]{:S(2)}, u32[]{:S(2)}) collective-permute-start(bf16[384,2048]{1,0:T(8,128)(2,1)S(1)} %get-tuple-element.151), channel_id=1, source_target_pairs={{0,1},{1,0},{2,3},{3,2},{4,5},{5,4},{6,7},{7,6},{8,9},{9,8},{10,11... | collective-permute-start | bytes 4718600 | tf_op jit(solution)/shard_map/ppermute | solution.py:29
  646.1 53.9 %collective-permute-start.57 = (bf16[1024,1024]{1,0:T(8,128)(2,1)S(1)}, bf16[1024,1024]{1,0:T(8,128)(2,1)S(1)}, u32[]{:S(2)}, u32[]{:S(2)}) collective-permute-start(bf16[1024,1024]{1,0:T(8,128)(2,1)S(1)} %attn_grads.7), channel_id=1, source_target_pairs={{0,16},{16,0},{1,17},{17,1},{2,18},{18,2},{3,19},{19,3},{4,20},{20... | collective-permute-start | bytes 6291464 | tf_op jit(solution)/shard_map/ppermute | solution.py:34
  657.8 58.1 %collective-permute-start.55 = (bf16[512,1024]{1,0:T(8,128)(2,1)S(1)}, bf16[512,1024]{1,0:T(8,128)(2,1)S(1)}, u32[]{:S(2)}, u32[]{:S(2)}) collective-permute-start(bf16[512,1024]{1,0:T(8,128)(2,1)S(1)} %slice.179), channel_id=1, source_target_pairs={{0,4},{4,0},{1,5},{5,1},{2,6},{6,2},{3,7},{7,3},{8,12},{12,8},{9,1... | collective-permute-start | bytes 3145736 | tf_op jit(solution)/shard_map/ppermute | solution.py:29
  706.5 37.4 %collective-permute-start.65 = (bf16[256,1536]{1,0:T(8,128)(2,1)S(1)}, bf16[256,1536]{1,0:T(8,128)(2,1)S(1)}, u32[]{:S(2)}, u32[]{:S(2)}) collective-permute-start(bf16[256,1536]{1,0:T(8,128)(2,1)S(1)} %slice.232), channel_id=1, source_target_pairs={{0,4},{4,0},{1,5},{5,1},{2,6},{6,2},{3,7},{7,3},{8,12},{12,8},{9,1... | collective-permute-start | bytes 2359304 | tf_op jit(solution)/shard_map/ppermute | solution.py:29
  713.4 53.1 %collective-permute-start.58 = (bf16[512,1024]{1,0:T(8,128)(2,1)}, bf16[512,1024]{1,0:T(8,128)(2,1)}, u32[]{:S(2)}, u32[]{:S(2)}) collective-permute-start(bf16[512,1024]{1,0:T(8,128)(2,1)} %slice.184), channel_id=1, source_target_pairs={{0,4},{4,0},{1,5},{5,1},{2,6},{6,2},{3,7},{7,3},{8,12},{12,8},{9,1... | collective-permute-start | bytes 3145736 | tf_op jit(solution)/shard_map/ppermute | solution.py:29
  717.1 81.4 %collective-permute-start.56 = (bf16[256,1024]{1,0:T(8,128)(2,1)}, bf16[256,1024]{1,0:T(8,128)(2,1)S(1)}, u32[]{:S(2)}, u32[]{:S(2)}) collective-permute-start(bf16[256,1024]{1,0:T(8,128)(2,1)} %slice.235), channel_id=1, source_target_pairs={{0,8},{8,0},{1,9},{9,1},{2,10},{10,2},{3,11},{11,3},{4,12},{12,4},... | collective-permute-start | bytes 1572872 | tf_op jit(solution)/shard_map/ppermute | solution.py:29
  (163 other events, 2420.6 us)

commit v7 on v6

--- a/solution.py
+++ b/solution.py
@@ -456,40 +456,46 @@
     q, do = q_ref[...], do_ref[...]
     size = q.shape[0]
     low_lane = lax.broadcasted_iota(jnp.int32, q.shape, 1) < HEAD_DIM
-    causal = lax.broadcasted_iota(jnp.int32, (size, size), 0) >= lax.broadcasted_iota(
+    causal = lax.broadcasted_iota(jnp.int32, (size, size), 0) <= lax.broadcasted_iota(
         jnp.int32, (size, size), 1
     )
-    product = do.astype(F32) * o_ref[...].astype(F32)
-    lse = lse_ref[...]
-    dq_heads = []
+    product = (do.astype(F32) * o_ref[...].astype(F32)).T
+    lse = lse_ref[...].T
+    dq_heads = [None, None]
     dk_all = [None] * (pieces + 1)
     dv_all = [None] * (pieces + 1)
+    heads = []
     for head in range(2):
         own = low_lane if head == 0 else jnp.logical_not(low_lane)
-        qh = jnp.where(own, q, jnp.zeros_like(q))
-        doh = jnp.where(own, do, jnp.zeros_like(do))
-        delta = jnp.sum(jnp.where(own, product, 0.0), axis=-1, keepdims=True)
-        log_sum = lse[:, head * HEAD_DIM : head * HEAD_DIM + 1]
-        dq = None
-        for s in range(pieces + 1):
-            k = (ks_ref if s == 0 else kp_refs[s - 1])[...]
-            v = (vs_ref if s == 0 else vp_refs[s - 1])[...]
-            raw = dot(qh, k, NT)
+        at = slice(head * HEAD_DIM, (head + 1) * HEAD_DIM)
+        heads.append(
+            (
+                jnp.where(own, q, jnp.zeros_like(q)),
+                jnp.where(own, do, jnp.zeros_like(do)),
+                jnp.sum(product[at], axis=0, keepdims=True),
+                lse[head * HEAD_DIM : head * HEAD_DIM + 1],
+            )
+        )
+    for s in range(pieces + 1):
+        k = (ks_ref if s == 0 else kp_refs[s - 1])[...]
+        v = (vs_ref if s == 0 else vp_refs[s - 1])[...]
+        k_turned = k.T
+        for head, (qh, doh, delta, log_sum) in enumerate(heads):
+            raw = dot(k, qh, NT)
             if s == 0:
                 raw = jnp.where(causal, raw, MASKED)
             else:
                 hidden = jnp.logical_and(prompt, rank_ref[s - 1] >= rank_ref[0])
                 raw = raw + jnp.where(hidden, MASKED, 0.0)
             prob = jnp.exp2(raw * SCALE_LOG2 - log_sum)
-            ds = (prob * (dot(doh, v, NT) - delta)).astype(BF16)
-            term = dot(ds, k, NN)
-            dq = term if dq is None else dq + term
-            dk = dot(ds, qh, TN)
-            dv = dot(prob.astype(BF16), doh, TN)
+            ds = (prob * (dot(v, doh, NT) - delta)).astype(BF16)
+            term = dot(k_turned[head * HEAD_DIM : (head + 1) * HEAD_DIM], ds, NN)
+            dq_heads[head] = term if dq_heads[head] is None else dq_heads[head] + term
+            dk = dot(ds, qh, NN)
+            dv = dot(prob.astype(BF16), doh, NN)
             dk_all[s] = dk if dk_all[s] is None else dk_all[s] + dk
             dv_all[s] = dv if dv_all[s] is None else dv_all[s] + dv
-        dq_heads.append(dq)
-    dq = jnp.where(low_lane, dq_heads[0], dq_heads[1]) * SCALE
+    dq = jnp.concatenate(dq_heads, axis=0).T * SCALE
     cosine, sine = cos_ref[...], sin_ref[...]
     dq_ref[...] = (dq * cosine - half_swap(dq) * sine).astype(BF16)
     dks_ref[...] = dk_all[0] * SCALE

time: 813 us -> 813 us (level)
  transfers between devices with their start and end apart: 66 -> 66, of which waited for: 32 -> 32; matrix products, arithmetic and copies ran while one was open for 14% -> 14% of each run, Pallas kernels for 24% -> 23%
where the time goes in v7:
time: 813 us; the launch traced here: 803 us
  waiting for transfers between devices  321 us (39%)
  Pallas kernels  219 us (27%)
  starting transfers between devices  111 us (14%)
  other arithmetic  80.6 us (10%)
  local copies, waits for them, and re-layouts  68.3 us (8%)
    ppermute x50, waiting for transfers between devices, swap(): return lax.ppermute(values, axis, [(i, i ^ mask) for i in range(count)])  241 us
    pallas_call x19, Pallas kernels, call(): pl.pallas_call(kernel, in_specs=[SMEM] * len(smem) + [VMEM] * len(operand...  102 us
    ppermute x50, starting transfers between devices, swap(): return lax.ppermute(values, axis, [(i, i ^ mask) for i in range(count)])  98.3 us
    ppermute x16, waiting for transfers between devices, turn(): lax.ppermute(values, axis, [(i, (i + shift) % count) for i in range(count)])  79.8 us
    pallas_call x4, Pallas kernels, ffn_grads(): pl.pallas_call(functools.partial(ffn_grads_kernel, tile, unit), grid_spec...  52.9 us
    pallas_call x1, Pallas kernels, attention_backward(): pl.pallas_call(functools.partial(backward_kernel, pieces), grid_spec=pltp...  41.5 us
    unnamed x264, local copies, waits for them, and re-layouts  37.4 us
    convert_element_type x15, other arithmetic, low(): return values.astype(BF16)  33.4 us
  transfers between devices with their start and end apart: 66, of which 32 were waited for; matrix products, arithmetic and copies ran while one was open for 14% of the time, Pallas kernels for 23%

profile of v7, /device:TPU:1, one launch (start us, length us, event | category | flops | bytes accessed | tf_op | source)
XLA Modules:
  0.0 803.1 jit_solution(10115555136023409942)
XLA Ops:
  20.3 8.9 %collective-permute-done.refs_2_.refs_8_ = bf16[256,1024]{1,0:T(8,128)(2,1)} collective-permute-done((bf16[256,1024]{1,0:T(8,128)(2,1)}, bf16[256,1024]{1,0:T(8,128)(2,1)}, u32[]{:S(2)}, u32[]{:S(2)}) %collective-permute-start) | collective-permute-done | bytes 524320 | tf_op jit(solution)/shard_map/ppermute | solution.py:29
  46.3 20.0 %collective-permute-done.4 = bf16[256,1024]{1,0:T(8,128)(2,1)S(1)} collective-permute-done((bf16[256,1024]{1,0:T(8,128)(2,1)}, bf16[256,1024]{1,0:T(8,128)(2,1)S(1)}, u32[]{:S(2)}, u32[]{:S(2)}) %collective-permute-start.4) | collective-permute-done | bytes 524320 | tf_op jit(solution)/shard_map/ppermute | solution.py:29
  67.6 9.1 %collective-permute-done.9.refs_8_.refs_14_ = bf16[256,1024]{1,0:T(8,128)(2,1)S(1)} collective-permute-done((bf16[256,1024]{1,0:T(8,128)(2,1)}, bf16[256,1024]{1,0:T(8,128)(2,1)S(1)}, u32[]{:S(2)}, u32[]{:S(2)}) %collective-permute-start.9) | collective-permute-done | bytes 524320 | tf_op jit(solution)/shard_map/ppermute | solution.py:34
  76.7 7.0 project.4.ks_ref.vs_ref
  91.7 11.5 %collective-permute-done.17.refs_3_.refs_7_ = bf16[256,1024]{1,0:T(8,128)(2,1)S(1)} collective-permute-done((bf16[256,1024]{1,0:T(8,128)(2,1)S(1)}, bf16[256,1024]{1,0:T(8,128)(2,1)S(1)}, u32[]{:S(2)}, u32[]{:S(2)}) %collective-permute-start.17) | collective-permute-done | bytes 524320 | tf_op jit(solution)/shard_map/ppermute | solution.py:29
  103.2 25.1 %collective-permute-done.16.refs_2_.refs_6_ = bf16[256,1024]{1,0:T(8,128)(2,1)S(1)} collective-permute-done((bf16[256,1024]{1,0:T(8,128)(2,1)S(1)}, bf16[256,1024]{1,0:T(8,128)(2,1)S(1)}, u32[]{:S(2)}, u32[]{:S(2)}) %collective-permute-start.16) | collective-permute-done | bytes 524320 | tf_op jit(solution)/shard_map/ppermute | solution.py:29
  132.7 24.2 %collective-permute-done.3 = bf16[256,1536]{1,0:T(8,128)(2,1)S(1)} collective-permute-done((bf16[256,1536]{1,0:T(8,128)(2,1)}, bf16[256,1536]{1,0:T(8,128)(2,1)S(1)}, u32[]{:S(2)}, u32[]{:S(2)}) %collective-permute-start.3) | collective-permute-done | bytes 786464 | tf_op jit(solution)/shard_map/ppermute | solution.py:29
  158.2 15.5 %collective-permute-done.19 = bf16[256,1536]{1,0:T(8,128)(2,1)S(1)} collective-permute-done((bf16[256,1536]{1,0:T(8,128)(2,1)S(1)}, bf16[256,1536]{1,0:T(8,128)(2,1)S(1)}, u32[]{:S(2)}, u32[]{:S(2)}) %collective-permute-start.19) | collective-permute-done | bytes 786464 | tf_op jit(solution)/shard_map/ppermute | solution.py:29
  198.5 5.7 collective-permute-done.8.refs_2_
  204.3 20.6 %attend.1 = (bf16[768,512]{1,0:T(8,128)(2,1)S(1)}, f32[768,512]{1,0:T(8,128)S(1)}) custom-call(s32[3]{0:T(128)S(1)} %compare_select_fusion.7.order_ref, s32[4]{0:T(128)S(1)} %gather_fusion.1, bf16[768,512]{1,0:T(8,128)(2,1)S(1)} %project.3.q_ref, bf16[768,1024]{1,0:T(8,128)(2,1)S(1)} %copy-done.20, bf16[768,1024]{1,0:T(8,128)(2,1)S(1)} %copy-done.20, ...), custom_call_target="tpu_custom_call" | custom-call | flops 2013265920 | bytes 1572864 | tf_op jit(solution)/shard_map/attend/pallas_call | solution.py:588
  226.1 21.2 %collective-permute-done.18 = bf16[256,1536]{1,0:T(8,128)(2,1)} collective-permute-done((bf16[256,1536]{1,0:T(8,128)(2,1)}, bf16[256,1536]{1,0:T(8,128)(2,1)}, u32[]{:S(2)}, u32[]{:S(2)}) %collective-permute-start.18) | collective-permute-done | bytes 786464 | tf_op jit(solution)/shard_map/ppermute | solution.py:29
  263.0 7.4 collective-permute-start.25
  285.4 22.7 %collective-permute-done.24.refs_3_ = bf16[512,1536]{1,0:T(8,128)(2,1)} collective-permute-done((bf16[512,1536]{1,0:T(8,128)(2,1)}, bf16[512,1536]{1,0:T(8,128)(2,1)}, u32[]{:S(2)}, u32[]{:S(2)}) %collective-permute-start.24) | collective-permute-done | bytes 1572896 | tf_op jit(solution)/shard_map/ppermute | solution.py:34
  322.2 17.6 %collective-permute-start.28 = (bf16[384,2048]{1,0:T(8,128)(2,1)S(1)}, bf16[384,2048]{1,0:T(8,128)(2,1)S(1)}, u32[]{:S(2)}, u32[]{:S(2)}) collective-permute-start(bf16[384,2048]{1,0:T(8,128)(2,1)S(1)} %multiply_convert_fusion.1.refs_0_), channel_id=1, source_target_pairs={{0,4},{4,0},{1,5},{5,1},{2,6},{6,2},{3,7},{7,3},{8,12},{12,8},{9,1... | collective-permute-start | bytes 4718600 | tf_op jit(solution)/shard_map/ppermute | solution.py:29
  356.1 9.3 %ffn_back.4 = (bf16[384,2048]{1,0:T(8,128)(2,1)S(1)}, bf16[384,2048]{1,0:T(8,128)(2,1)}) custom-call(bf16[768,1024]{1,0:T(8,128)(2,1)S(1)} %get-tuple-element.108.refs_0_.refs_10_, bf16[768,1024]{1,0:T(8,128)(2,1)S(1)} %get-tuple-element.109.refs_1_.refs_10_, bf16[2048,1536]{1,0:T(8,128)(2,1)S(1)} %place_rows.2.refs_4_.refs_2_, ...), custom_call_target="tpu_custom_call" | custom-call | flops 1610612736 | bytes 3670016 | tf_op jit(solution)/shard_map/ffn_back/pallas_call | solution.py:81
  366.6 7.9 collective-permute-done.28.refs_0_.refs_2_
  378.1 8.0 ffn.7
  388.7 8.6 %ffn.6 = (bf16[768,512]{1,0:T(8,128)(2,1)S(1)}, bf16[768,1024]{1,0:T(8,128)(2,1)S(1)}) custom-call(bf16[384,2048]{1,0:T(8,128)(2,1)S(1)} %copy-done.13, bf16[384,2048]{1,0:T(8,128)(2,1)S(1)} %collective-permute-done.29.refs_1_.refs_3_, bf16[384,2048]{1,0:T(8,128)(2,1)} %collective-permute-done.25.refs_2_.refs_6_, ...), custom_call_target="tpu_custom_call" | custom-call | flops 1207959552 | bytes 3735552 | tf_op jit(solution)/shard_map/ffn/pallas_call | solution.py:81
  397.4 9.2 %ffn_back.5 = (bf16[384,2048]{1,0:T(8,128)(2,1)S(1)}, bf16[384,2048]{1,0:T(8,128)(2,1)}) custom-call(bf16[768,1024]{1,0:T(8,128)(2,1)S(1)} %get-tuple-element.115.refs_0_.refs_11_, bf16[768,1024]{1,0:T(8,128)(2,1)S(1)} %get-tuple-element.116.refs_1_.refs_11_, bf16[2048,1536]{1,0:T(8,128)(2,1)S(1)} %place_rows.2.refs_4_.refs_2_, ...), custom_call_target="tpu_custom_call" | custom-call | flops 1610612736 | bytes 3670016 | tf_op jit(solution)/shard_map/ffn_back/pallas_call | solution.py:81
  408.9 13.1 %ffn_grads.6 = bf16[1024,1536]{1,0:T(8,128)(2,1)} custom-call(s32[2]{0:T(128)} %compare_select_fusion.2.dp_ref, s32[4]{0:T(128)} %gather_fusion.3, bf16[384,2048]{1,0:T(8,128)(2,1)} %copy-done.9, bf16[384,2048]{1,0:T(8,128)(2,1)} %copy-done.11, bf16[384,2048]{1,0:T(8,128)(2,1)} %copy-done.12, bf16[384,2048]{1,0:T(8,128)(2,1)} %copy-done.14, ...), custom_call_target="tpu_custom_call" | custom-call | flops 1207959552 | bytes 3538944 | tf_op jit(solution)/shard_map/ffn_grads/pallas_call | solution.py:348
  432.4 13.1 %ffn_grads.5 = bf16[1024,1536]{1,0:T(8,128)(2,1)} custom-call(s32[2]{0:T(128)} %compare_select_fusion.2.dp_ref, s32[4]{0:T(128)} %gather_fusion.3, bf16[384,2048]{1,0:T(8,128)(2,1)} %copy-done.9, bf16[384,2048]{1,0:T(8,128)(2,1)} %copy-done.11, bf16[384,2048]{1,0:T(8,128)(2,1)} %copy-done.12, bf16[384,2048]{1,0:T(8,128)(2,1)} %copy-done.14, ...), custom_call_target="tpu_custom_call" | custom-call | flops 1207959552 | bytes 3538944 | tf_op jit(solution)/shard_map/ffn_grads/pallas_call | solution.py:348
  445.6 13.3 %ffn_grads.4 = bf16[1024,1536]{1,0:T(8,128)(2,1)} custom-call(s32[2]{0:T(128)} %compare_select_fusion.2.dp_ref, s32[4]{0:T(128)} %gather_fusion.3, bf16[384,2048]{1,0:T(8,128)(2,1)} %copy-done.9, bf16[384,2048]{1,0:T(8,128)(2,1)} %copy-done.11, bf16[384,2048]{1,0:T(8,128)(2,1)} %copy-done.12, bf16[384,2048]{1,0:T(8,128)(2,1)} %copy-done.14, ...), custom_call_target="tpu_custom_call" | custom-call | flops 1207959552 | bytes 3538944 | tf_op jit(solution)/shard_map/ffn_grads/pallas_call | solution.py:348
  471.6 13.3 %ffn_grads.7 = bf16[1024,1536]{1,0:T(8,128)(2,1)} custom-call(s32[2]{0:T(128)} %compare_select_fusion.2.dp_ref, s32[4]{0:T(128)} %gather_fusion.3, bf16[384,2048]{1,0:T(8,128)(2,1)} %copy-done.9, bf16[384,2048]{1,0:T(8,128)(2,1)} %copy-done.11, bf16[384,2048]{1,0:T(8,128)(2,1)} %copy-done.12, bf16[384,2048]{1,0:T(8,128)(2,1)} %copy-done.14, ...), custom_call_target="tpu_custom_call" | custom-call | flops 1207959552 | bytes 3538944 | tf_op jit(solution)/shard_map/ffn_grads/pallas_call | solution.py:348
  530.5 41.5 %attend_back.1 = (bf16[768,512]{1,0:T(8,128)(2,1)S(1)}, f32[768,512]{1,0:T(8,128)S(1)}, f32[768,512]{1,0:T(8,128)S(1)}, f32[256,1024]{1,0:T(8,128)S(1)}, bf16[25...) custom-call(s32[3]{0:T(128)S(1)} %compare_select_fusion.7.order_ref, ...), custom_call_target="tpu_custom_call" | custom-call | flops 5033164800 | bytes 3145728 | tf_op jit(solution)/shard_map/attend_back/pallas_call | solution.py:610
  572.0 17.5 %collective-permute-done.37 = bf16[384,2048]{1,0:T(8,128)(2,1)} collective-permute-done((bf16[384,2048]{1,0:T(8,128)(2,1)}, bf16[384,2048]{1,0:T(8,128)(2,1)}, u32[]{:S(2)}, u32[]{:S(2)}) %collective-permute-start.37) | collective-permute-done | bytes 1572896 | tf_op jit(solution)/shard_map/ppermute | solution.py:29
  614.2 9.5 %collective-permute-done.45.refs_2_ = bf16[256,1024]{1,0:T(8,128)(2,1)S(1)} collective-permute-done((bf16[256,1024]{1,0:T(8,128)(2,1)S(1)}, bf16[256,1024]{1,0:T(8,128)(2,1)S(1)}, u32[]{:S(2)}, u32[]{:S(2)}) %collective-permute-start.45) | collective-permute-done | bytes 524320 | tf_op jit(solution)/shard_map/ppermute | solution.py:29
  626.0 8.6 %project_back.3 = (bf16[384,2048]{1,0:T(8,128)(2,1)S(1)}, bf16[384,2048]{1,0:T(8,128)(2,1)S(1)}) custom-call(s32[1]{0:T(128)} %bitcast.bit_ref, s32[8]{0:T(128)S(1)} %xor_add_fusion.1.place_ref, bf16[768,512]{1,0:T(8,128)(2,1)S(1)} %get-tuple-element.140.refs_0_.refs_4_, bf16[768,512]{1,0:T(8,128)(2,1)S(1)} %get-tuple-element.148.refs_1_, ...), custom_call_target="tpu_custom_call" | custom-call | flops 1207959552 | bytes 2949120 | tf_op jit(solution)/shard_map/project_back/pallas_call | solution.py:81
  657.8 8.1 %collective-permute-start.55 = (bf16[512,1024]{1,0:T(8,128)(2,1)S(1)}, bf16[512,1024]{1,0:T(8,128)(2,1)S(1)}, u32[]{:S(2)}, u32[]{:S(2)}) collective-permute-start(bf16[512,1024]{1,0:T(8,128)(2,1)S(1)} %slice.179), channel_id=1, source_target_pairs={{0,4},{4,0},{1,5},{5,1},{2,6},{6,2},{3,7},{7,3},{8,12},{12,8},{9,1... | collective-permute-start | bytes 3145736 | tf_op jit(solution)/shard_map/ppermute | solution.py:29
  665.9 34.2 %collective-permute-done.57 = bf16[1024,1024]{1,0:T(8,128)(2,1)S(1)} collective-permute-done((bf16[1024,1024]{1,0:T(8,128)(2,1)S(1)}, bf16[1024,1024]{1,0:T(8,128)(2,1)S(1)}, u32[]{:S(2)}, u32[]{:S(2)}) %collective-permute-start.57) | collective-permute-done | bytes 2097184 | tf_op jit(solution)/shard_map/ppermute | solution.py:34
  717.1 26.8 %collective-permute-done.65 = bf16[256,1536]{1,0:T(8,128)(2,1)S(1)} collective-permute-done((bf16[256,1536]{1,0:T(8,128)(2,1)S(1)}, bf16[256,1536]{1,0:T(8,128)(2,1)S(1)}, u32[]{:S(2)}, u32[]{:S(2)}) %collective-permute-start.65) | collective-permute-done | bytes 786464 | tf_op jit(solution)/shard_map/ppermute | solution.py:29
  750.9 7.8 collective-permute-start.48
  770.9 23.2 %collective-permute-done.51 = f32[2,2048]{1,0:T(2,128)S(1)} collective-permute-done((f32[2,2048]{1,0:T(2,128)S(1)}, f32[2,2048]{1,0:T(2,128)S(1)}, u32[]{:S(2)}, u32[]{:S(2)}) %collective-permute-start.51) | collective-permute-done | bytes 16416 | tf_op jit(solution)/shard_map/ppermute | solution.py:29
  (501 shorter events, 310.2 us)
Async XLA Ops:
  4.0 63.6 %collective-permute-start.12 = (bf16[256,1024]{1,0:T(8,128)(2,1)}, bf16[256,1024]{1,0:T(8,128)(2,1)}, u32[]{:S(2)}, u32[]{:S(2)}) collective-permute-start(bf16[256,1024]{1,0:T(8,128)(2,1)} %constant_dynamic-update-slice_fusion.refs_1_.refs_7_), channel_id=1, source_target_pairs={{0,16},{16,0},{1,17},{17,1},{2,18},{18,2},{3,19},{19,3},{4,20},{20... | collective-permute-start | bytes 1572872 | tf_op jit(solution)/shard_map/ppermute | solution.py:34
  6.0 38.7 %collective-permute-start.11 = (bf16[256,1024]{1,0:T(8,128)(2,1)}, bf16[256,1024]{1,0:T(8,128)(2,1)}, u32[]{:S(2)}, u32[]{:S(2)}) collective-permute-start(bf16[256,1024]{1,0:T(8,128)(2,1)} %constant_dynamic-update-slice_fusion.refs_1_.refs_7_), channel_id=1, source_target_pairs={{0,4},{4,0},{1,5},{5,1},{2,6},{6,2},{3,7},{7,3},{8,12},{12,8},{9,1... | collective-permute-start | bytes 1572872 | tf_op jit(solution)/shard_map/ppermute | solution.py:29
  66.3 62.4 %collective-permute-start.5 = (bf16[512,1024]{1,0:T(8,128)(2,1)S(1)}, bf16[512,1024]{1,0:T(8,128)(2,1)S(1)}, u32[]{:S(2)}, u32[]{:S(2)}) collective-permute-start(bf16[512,1024]{1,0:T(8,128)(2,1)S(1)} %constant_dynamic-update-slice_fusion.4.refs_1_.refs_2_.refs_3_), channel_id=1, source_target_pairs={{0,4},{4,0},{1,5},{5,1},{2,6},{6,2},{3,7},{7,3},{8,12},{12,8},{9,1... | collective-permute-start | bytes 3145736 | tf_op jit(solution)/shard_map/ppermute | solution.py:29
  88.2 40.1 %collective-permute-start.16 = (bf16[256,1024]{1,0:T(8,128)(2,1)S(1)}, bf16[256,1024]{1,0:T(8,128)(2,1)S(1)}, u32[]{:S(2)}, u32[]{:S(2)}) collective-permute-start(bf16[256,1024]{1,0:T(8,128)(2,1)S(1)} %constant_dynamic-slice_fusion.12.refs_0_.refs_4_), channel_id=1, source_target_pairs={{0,8},{4,12},{8,0},{12,4},{1,9},{5,13},{9,1},{13,5},{2,10},{6,14},... | collective-permute-start | bytes 1572872 | tf_op jit(solution)/shard_map/ppermute | solution.py:29
  88.2 40.1 %collective-permute-start.15 = (bf16[256,1024]{1,0:T(8,128)(2,1)S(1)}, bf16[256,1024]{1,0:T(8,128)(2,1)S(1)}, u32[]{:S(2)}, u32[]{:S(2)}) collective-permute-start(bf16[256,1024]{1,0:T(8,128)(2,1)S(1)} %constant_dynamic-slice_fusion.12.refs_0_.refs_4_), channel_id=1, source_target_pairs={{0,4},{4,0},{8,12},{12,8},{1,5},{5,1},{9,13},{13,9},{2,6},{6,2},{1... | collective-permute-start | bytes 1572872 | tf_op jit(solution)/shard_map/ppermute | solution.py:29
  89.6 67.4 %collective-permute-start.3 = (bf16[256,1536]{1,0:T(8,128)(2,1)}, bf16[256,1536]{1,0:T(8,128)(2,1)S(1)}, u32[]{:S(2)}, u32[]{:S(2)}) collective-permute-start(bf16[256,1536]{1,0:T(8,128)(2,1)} %pad_maximum_fusion.5), channel_id=1, source_target_pairs={{0,4},{4,0},{1,5},{5,1},{2,6},{6,2},{3,7},{7,3},{8,12},{12,8},{9,1... | collective-permute-start | bytes 2359304 | tf_op jit(solution)/shard_map/ppermute | solution.py:29
  128.3 45.5 %collective-permute-start.19 = (bf16[256,1536]{1,0:T(8,128)(2,1)S(1)}, bf16[256,1536]{1,0:T(8,128)(2,1)S(1)}, u32[]{:S(2)}, u32[]{:S(2)}) collective-permute-start(bf16[256,1536]{1,0:T(8,128)(2,1)S(1)} %pad_maximum_fusion.7), channel_id=1, source_target_pairs={{0,4},{4,0},{1,5},{5,1},{2,6},{6,2},{3,7},{7,3},{8,12},{12,8},{9,1... | collective-permute-start | bytes 2359304 | tf_op jit(solution)/shard_map/ppermute | solution.py:29
  128.4 47.9 %collective-permute-start.6 = (bf16[512,1024]{1,0:T(8,128)(2,1)S(1)}, bf16[512,1024]{1,0:T(8,128)(2,1)S(1)}, u32[]{:S(2)}, u32[]{:S(2)}) collective-permute-start(bf16[512,1024]{1,0:T(8,128)(2,1)S(1)} %constant_dynamic-update-slice_fusion.4.refs_1_.refs_2_.refs_3_), channel_id=1, source_target_pairs={{0,16},{16,0},{1,17},{17,1},{2,18},{18,2},{3,19},{19,3},{4,20},{20... | collective-permute-start | bytes 3145736 | tf_op jit(solution)/shard_map/ppermute | solution.py:34
  128.7 48.6 %collective-permute-start.7 = (bf16[512,1024]{1,0:T(8,128)(2,1)S(1)}, bf16[512,1024]{1,0:T(8,128)(2,1)S(1)}, u32[]{:S(2)}, u32[]{:S(2)}) collective-permute-start(bf16[512,1024]{1,0:T(8,128)(2,1)S(1)} %collective-permute-done.5.refs_2_.refs_3_.refs_4_), channel_id=1, source_target_pairs={{0,16},{16,0},{1,17},{17,1},{2,18},{18,2},{3,19},{19,3},{4,20},{20... | collective-permute-start | bytes 3145736 | tf_op jit(solution)/shard_map/ppermute | solution.py:34
  129.9 46.3 %collective-permute-start.2 = (bf16[256,1536]{1,0:T(8,128)(2,1)S(1)}, bf16[256,1536]{1,0:T(8,128)(2,1)S(1)}, u32[]{:S(2)}, u32[]{:S(2)}) collective-permute-start(bf16[256,1536]{1,0:T(8,128)(2,1)S(1)} %pad_maximum_fusion.4), channel_id=1, source_target_pairs={{0,8},{8,0},{1,9},{9,1},{2,10},{10,2},{3,11},{11,3},{4,12},{12,4},... | collective-permute-start | bytes 2359304 | tf_op jit(solution)/shard_map/ppermute | solution.py:29
  157.9 46.3 %collective-permute-start.8 = (bf16[512,1536]{1,0:T(8,128)(2,1)}, bf16[512,1536]{1,0:T(8,128)(2,1)}, u32[]{:S(2)}, u32[]{:S(2)}) collective-permute-start(bf16[512,1536]{1,0:T(8,128)(2,1)} %constant_dynamic-update-slice_fusion.2.refs_0_), channel_id=1, source_target_pairs={{0,16},{16,0},{1,17},{17,1},{2,18},{18,2},{3,19},{19,3},{4,20},{20... | collective-permute-start | bytes 4718600 | tf_op jit(solution)/shard_map/ppermute | solution.py:34
  178.5 68.8 %collective-permute-start.20 = (bf16[512,1536]{1,0:T(8,128)(2,1)}, bf16[512,1536]{1,0:T(8,128)(2,1)}, u32[]{:S(2)}, u32[]{:S(2)}) collective-permute-start(bf16[512,1536]{1,0:T(8,128)(2,1)} %pad_maximum_fusion.3.refs_0_), channel_id=1, source_target_pairs={{0,16},{16,0},{1,17},{17,1},{2,18},{18,2},{3,19},{19,3},{4,20},{20... | collective-permute-start | bytes 4718600 | tf_op jit(solution)/shard_map/ppermute | solution.py:34
  185.6 61.6 %collective-permute-start.18 = (bf16[256,1536]{1,0:T(8,128)(2,1)}, bf16[256,1536]{1,0:T(8,128)(2,1)}, u32[]{:S(2)}, u32[]{:S(2)}) collective-permute-start(bf16[256,1536]{1,0:T(8,128)(2,1)} %pad_maximum_fusion.6), channel_id=1, source_target_pairs={{0,8},{8,0},{1,9},{9,1},{2,10},{10,2},{3,11},{11,3},{4,12},{12,4},... | collective-permute-start | bytes 2359304 | tf_op jit(solution)/shard_map/ppermute | solution.py:29
  263.0 48.5 %collective-permute-start.25 = (bf16[384,2048]{1,0:T(8,128)(2,1)S(1)}, bf16[384,2048]{1,0:T(8,128)(2,1)}, u32[]{:S(2)}, u32[]{:S(2)}) collective-permute-start(bf16[384,2048]{1,0:T(8,128)(2,1)S(1)} %get-tuple-element.123.refs_2_.refs_4_), channel_id=1, source_target_pairs={{0,4},{4,0},{1,5},{5,1},{2,6},{6,2},{3,7},{7,3},{8,12},{12,8},{9,1... | collective-permute-start | bytes 4718600 | tf_op jit(solution)/shard_map/ppermute | solution.py:29
  284.1 57.5 %collective-permute-start.27 = (bf16[512,1536]{1,0:T(8,128)(2,1)S(1)}, bf16[512,1536]{1,0:T(8,128)(2,1)S(1)}, u32[]{:S(2)}, u32[]{:S(2)}) collective-permute-start(bf16[512,1536]{1,0:T(8,128)(2,1)S(1)} %constant_dynamic-update-slice_fusion.8.refs_1_), channel_id=1, source_target_pairs={{0,16},{16,0},{1,17},{17,1},{2,18},{18,2},{3,19},{19,3},{4,20},{20... | collective-permute-start | bytes 4718600 | tf_op jit(solution)/shard_map/ppermute | solution.py:34
  322.2 52.4 %collective-permute-start.28 = (bf16[384,2048]{1,0:T(8,128)(2,1)S(1)}, bf16[384,2048]{1,0:T(8,128)(2,1)S(1)}, u32[]{:S(2)}, u32[]{:S(2)}) collective-permute-start(bf16[384,2048]{1,0:T(8,128)(2,1)S(1)} %multiply_convert_fusion.1.refs_0_), channel_id=1, source_target_pairs={{0,4},{4,0},{1,5},{5,1},{2,6},{6,2},{3,7},{7,3},{8,12},{12,8},{9,1... | collective-permute-start | bytes 4718600 | tf_op jit(solution)/shard_map/ppermute | solution.py:29
  462.0 48.9 %collective-permute-start.39 = (bf16[512,1536]{1,0:T(8,128)(2,1)}, bf16[512,1536]{1,0:T(8,128)(2,1)}, u32[]{:S(2)}, u32[]{:S(2)}) collective-permute-start(bf16[512,1536]{1,0:T(8,128)(2,1)} %get-tuple-element.137), channel_id=1, source_target_pairs={{0,16},{16,0},{1,17},{17,1},{2,18},{18,2},{3,19},{19,3},{4,20},{20... | collective-permute-start | bytes 4718600 | tf_op jit(solution)/shard_map/ppermute | solution.py:34
  469.5 41.3 %collective-permute-start.38 = (bf16[384,2048]{1,0:T(8,128)(2,1)}, bf16[384,2048]{1,0:T(8,128)(2,1)}, u32[]{:S(2)}, u32[]{:S(2)}) collective-permute-start(bf16[384,2048]{1,0:T(8,128)(2,1)} %add_convert_fusion.9), channel_id=1, source_target_pairs={{0,2},{1,3},{2,0},{3,1},{4,6},{5,7},{6,4},{7,5},{8,10},{9,11},{10,... | collective-permute-start | bytes 4718600 | tf_op jit(solution)/shard_map/ppermute | solution.py:29
  499.9 72.1 %collective-permute-start.60 = (bf16[512,1536]{1,0:T(8,128)(2,1)}, bf16[512,1536]{1,0:T(8,128)(2,1)}, u32[]{:S(2)}, u32[]{:S(2)}) collective-permute-start(bf16[512,1536]{1,0:T(8,128)(2,1)} %add_convert_fusion.4), channel_id=1, source_target_pairs={{0,8},{8,0},{1,9},{9,1},{2,10},{10,2},{3,11},{11,3},{4,12},{12,4},... | collective-permute-start | bytes 4718600 | tf_op jit(solution)/shard_map/ppermute | solution.py:29
  521.0 68.6 %collective-permute-start.37 = (bf16[384,2048]{1,0:T(8,128)(2,1)}, bf16[384,2048]{1,0:T(8,128)(2,1)}, u32[]{:S(2)}, u32[]{:S(2)}) collective-permute-start(bf16[384,2048]{1,0:T(8,128)(2,1)} %add_convert_fusion.7), channel_id=1, source_target_pairs={{0,4},{4,0},{1,5},{5,1},{2,6},{6,2},{3,7},{7,3},{8,12},{12,8},{9,1... | collective-permute-start | bytes 4718600 | tf_op jit(solution)/shard_map/ppermute | solution.py:29
  523.4 73.4 %collective-permute-start.63 = (bf16[512,1536]{1,0:T(8,128)(2,1)}, bf16[512,1536]{1,0:T(8,128)(2,1)S(1)}, u32[]{:S(2)}, u32[]{:S(2)}) collective-permute-start(bf16[512,1536]{1,0:T(8,128)(2,1)} %get-tuple-element.157), channel_id=1, source_target_pairs={{0,16},{16,0},{1,17},{17,1},{2,18},{18,2},{3,19},{19,3},{4,20},{20... | collective-permute-start | bytes 4718600 | tf_op jit(solution)/shard_map/ppermute | solution.py:34
  523.7 85.0 %collective-permute-start.62 = (bf16[512,1536]{1,0:T(8,128)(2,1)}, bf16[512,1536]{1,0:T(8,128)(2,1)}, u32[]{:S(2)}, u32[]{:S(2)}) collective-permute-start(bf16[512,1536]{1,0:T(8,128)(2,1)} %get-tuple-element.155), channel_id=1, source_target_pairs={{0,16},{16,0},{1,17},{17,1},{2,18},{18,2},{3,19},{19,3},{4,20},{20... | collective-permute-start | bytes 4718600 | tf_op jit(solution)/shard_map/ppermute | solution.py:34
  598.8 49.3 %collective-permute-start.61 = (bf16[256,1536]{1,0:T(8,128)(2,1)}, bf16[256,1536]{1,0:T(8,128)(2,1)}, u32[]{:S(2)}, u32[]{:S(2)}) collective-permute-start(bf16[256,1536]{1,0:T(8,128)(2,1)} %slice.233), channel_id=1, source_target_pairs={{0,4},{4,0},{1,5},{5,1},{2,6},{6,2},{3,7},{7,3},{8,12},{12,8},{9,1... | collective-permute-start | bytes 2359304 | tf_op jit(solution)/shard_map/ppermute | solution.py:29
  608.7 37.4 %collective-permute-start.41 = (bf16[384,1024]{1,0:T(8,128)(2,1)}, bf16[384,1024]{1,0:T(8,128)(2,1)}, u32[]{:S(2)}, u32[]{:S(2)}) collective-permute-start(bf16[384,1024]{1,0:T(8,128)(2,1)} %constant_dynamic-slice_fusion.3), channel_id=1, source_target_pairs={{0,2},{1,3},{2,0},{3,1},{4,6},{5,7},{6,4},{7,5},{8,10},{9,11},{10,... | collective-permute-start | bytes 2359304 | tf_op jit(solution)/shard_map/ppermute | solution.py:29
  611.9 43.2 %collective-permute-start.54 = (bf16[1024,1024]{1,0:T(8,128)(2,1)S(1)}, bf16[1024,1024]{1,0:T(8,128)(2,1)}, u32[]{:S(2)}, u32[]{:S(2)}) collective-permute-start(bf16[1024,1024]{1,0:T(8,128)(2,1)S(1)} %attn_grads.5), channel_id=1, source_target_pairs={{0,16},{16,0},{1,17},{17,1},{2,18},{18,2},{3,19},{19,3},{4,20},{20... | collective-permute-start | bytes 6291464 | tf_op jit(solution)/shard_map/ppermute | solution.py:34
  612.2 91.8 %collective-permute-start.64 = (bf16[512,1536]{1,0:T(8,128)(2,1)}, bf16[512,1536]{1,0:T(8,128)(2,1)}, u32[]{:S(2)}, u32[]{:S(2)}) collective-permute-start(bf16[512,1536]{1,0:T(8,128)(2,1)} %add_convert_fusion.2), channel_id=1, source_target_pairs={{0,8},{8,0},{1,9},{9,1},{2,10},{10,2},{3,11},{11,3},{4,12},{12,4},... | collective-permute-start | bytes 4718600 | tf_op jit(solution)/shard_map/ppermute | solution.py:29
  634.5 74.0 %collective-permute-start.46 = (bf16[384,2048]{1,0:T(8,128)(2,1)S(1)}, bf16[384,2048]{1,0:T(8,128)(2,1)S(1)}, u32[]{:S(2)}, u32[]{:S(2)}) collective-permute-start(bf16[384,2048]{1,0:T(8,128)(2,1)S(1)} %get-tuple-element.151), channel_id=1, source_target_pairs={{0,1},{1,0},{2,3},{3,2},{4,5},{5,4},{6,7},{7,6},{8,9},{9,8},{10,11... | collective-permute-start | bytes 4718600 | tf_op jit(solution)/shard_map/ppermute | solution.py:29
  646.1 53.9 %collective-permute-start.57 = (bf16[1024,1024]{1,0:T(8,128)(2,1)S(1)}, bf16[1024,1024]{1,0:T(8,128)(2,1)S(1)}, u32[]{:S(2)}, u32[]{:S(2)}) collective-permute-start(bf16[1024,1024]{1,0:T(8,128)(2,1)S(1)} %attn_grads.7), channel_id=1, source_target_pairs={{0,16},{16,0},{1,17},{17,1},{2,18},{18,2},{3,19},{19,3},{4,20},{20... | collective-permute-start | bytes 6291464 | tf_op jit(solution)/shard_map/ppermute | solution.py:34
  657.8 58.1 %collective-permute-start.55 = (bf16[512,1024]{1,0:T(8,128)(2,1)S(1)}, bf16[512,1024]{1,0:T(8,128)(2,1)S(1)}, u32[]{:S(2)}, u32[]{:S(2)}) collective-permute-start(bf16[512,1024]{1,0:T(8,128)(2,1)S(1)} %slice.179), channel_id=1, source_target_pairs={{0,4},{4,0},{1,5},{5,1},{2,6},{6,2},{3,7},{7,3},{8,12},{12,8},{9,1... | collective-permute-start | bytes 3145736 | tf_op jit(solution)/shard_map/ppermute | solution.py:29
  706.5 37.4 %collective-permute-start.65 = (bf16[256,1536]{1,0:T(8,128)(2,1)S(1)}, bf16[256,1536]{1,0:T(8,128)(2,1)S(1)}, u32[]{:S(2)}, u32[]{:S(2)}) collective-permute-start(bf16[256,1536]{1,0:T(8,128)(2,1)S(1)} %slice.232), channel_id=1, source_target_pairs={{0,4},{4,0},{1,5},{5,1},{2,6},{6,2},{3,7},{7,3},{8,12},{12,8},{9,1... | collective-permute-start | bytes 2359304 | tf_op jit(solution)/shard_map/ppermute | solution.py:29
  713.4 53.1 %collective-permute-start.58 = (bf16[512,1024]{1,0:T(8,128)(2,1)}, bf16[512,1024]{1,0:T(8,128)(2,1)}, u32[]{:S(2)}, u32[]{:S(2)}) collective-permute-start(bf16[512,1024]{1,0:T(8,128)(2,1)} %slice.184), channel_id=1, source_target_pairs={{0,4},{4,0},{1,5},{5,1},{2,6},{6,2},{3,7},{7,3},{8,12},{12,8},{9,1... | collective-permute-start | bytes 3145736 | tf_op jit(solution)/shard_map/ppermute | solution.py:29
  717.1 81.4 %collective-permute-start.56 = (bf16[256,1024]{1,0:T(8,128)(2,1)}, bf16[256,1024]{1,0:T(8,128)(2,1)S(1)}, u32[]{:S(2)}, u32[]{:S(2)}) collective-permute-start(bf16[256,1024]{1,0:T(8,128)(2,1)} %slice.235), channel_id=1, source_target_pairs={{0,8},{8,0},{1,9},{9,1},{2,10},{10,2},{3,11},{11,3},{4,12},{12,4},... | collective-permute-start | bytes 1572872 | tf_op jit(solution)/shard_map/ppermute | solution.py:29
  (163 other events, 2420.6 us)
